TPU v7x, 512 devices: a whole 4x8x8 slice. The times are simulated.
512 devices in a mesh: blk: 64 (over x, y_hi, z), head: 8 (over y_lo, core).
Axes of the slice: x: 4, y: 8 (y_hi: 2, y_lo: 4; y = y_hi * 4 + y_lo), z: 8, core: 2. Of those that a mesh axis runs over, the one named last changes fastest.
Arguments:
- query_rows: bfloat16 [16384, 2048], P('blk', 'head'), may hold values from -10 to 10
- key_rows: bfloat16 [16384, 2048], P('blk', 'head'), may hold values from -10 to 10
- value_rows: bfloat16 [16384, 2048], P('blk', 'head'), may hold values from -6 to 6
- grad_out: bfloat16 [16384, 4096], P('blk', 'head'), may hold values from -6 to 6
- out_weight: bfloat16 [2048, 4096], P('head'), may hold values from -0.09375 to 0.09375
- mask_types: int32 [128, 128], replicated, may hold values from 0 to 2, as said below
- drop_seed: int32 [1], replicated, may hold values from 0 to 1048575
Outputs:
- grad_query: bfloat16 [16384, 2048], P('blk', 'head')
- grad_key: bfloat16 [16384, 2048], P('blk', 'head')
- grad_value: bfloat16 [16384, 2048], P('blk', 'head')
Inputs may be any that keep to these rules, and one draw needn't show every extreme that they name: Blocks are runs of 128 positions. The sequence is cut into documents of whole blocks, each 1 to 4 blocks long, and some document has exactly 4 blocks. Images are pairs of blocks 2m and 2m + 1 of one document. mask_types[a, b] is 0 where blocks a and b lie in different documents; inside a document it is 2 for b < a, 2 for b = a in an image, 1 for b = a in text, 2 for b = a + 1 in one image, and 0 for other b > a. So a position sees keys only of its own shard of 256 positions and of up to 2 earlier ones.
All inputs are finite; a program needn't handle non-finite values.
Results may differ from a plain program's by a relative error of at most 0.029.
Values may be sent and summed in bfloat16 or wider, within the bound.
No kernel may reach another device: no remote copies, remote signals or barrier semaphores. Data moves between devices by JAX's collectives and lax.ppermute only.
A program may use at most 64 MiB of HBM per device.

v0:
```python
import jax
import jax.numpy as jnp
from jax import lax
from jax.sharding import PartitionSpec as P

DH = 128
HEADS_DEV = 2
MB = 128
REACH = 2


drop_level = 6554
keep_scale = 65536.0 / 58982.0
mix_one = 73244475
mix_two = 295559667
mix_three = 668265263


def shifted(value, axis, steps):
    count = lax.axis_size(axis)
    leading, last = (max(0, -steps), min(count, count - steps))
    return lax.ppermute(value, axis, [(source, source + steps) for source in range(leading, last)])


def mixhash(seed_word, head_index, query_pos, key_pos):
    hashed = query_pos * mix_one + key_pos * mix_two + head_index * mix_three + seed_word
    hashed = hashed ^ lax.shift_right_logical(hashed, jnp.int32(16))
    hashed = hashed * mix_one
    hashed = hashed ^ lax.shift_right_logical(hashed, jnp.int32(16))
    hashed = hashed * mix_one
    hashed = hashed ^ lax.shift_right_logical(hashed, jnp.int32(16))
    return (hashed & 65535 >= drop_level).astype(jnp.float32)


def visible(table_tile, query_pos, key_pos):
    return (table_tile == 2) | (table_tile == 1) & (key_pos[None, :] <= query_pos[:, None])


def expand(block_table):
    count_rows, count_cols = block_table.shape
    spread = jnp.broadcast_to(block_table[:, None, :, None], (count_rows, MB, count_cols, MB))
    return spread.reshape(count_rows * MB, count_cols * MB)


def contract_first(left, right):
    return lax.dot_general(
        left, right, (((0,), (0,)), ((), ())), preferred_element_type=jnp.float32
    )


def contract_last(left, right):
    return lax.dot_general(
        left, right, (((1,), (1,)), ((), ())), preferred_element_type=jnp.float32
    )


def on_device(query_rows, key_rows, value_rows, grad_out, out_weight, mask_types, drop_seed):
    row_count = query_rows.shape[0]
    span_rows = (REACH + 1) * row_count
    block_rows = row_count // MB
    margin_blocks = REACH * block_rows
    span_blocks = span_rows // MB
    score_scale = DH ** (-0.5)
    seed_word = drop_seed[0]
    device = lax.axis_index("blk")
    head_base = lax.axis_index("head") * HEADS_DEV
    own_pos = device * row_count + jnp.arange(row_count, dtype=jnp.int32)
    window_pos = (device - REACH) * row_count + jnp.arange(span_rows, dtype=jnp.int32)
    padded_table = jnp.pad(mask_types, margin_blocks)
    near_table = lax.dynamic_slice(
        padded_table,
        (device * block_rows + margin_blocks, device * block_rows),
        (block_rows, span_blocks),
    )
    allowed = visible(expand(near_table), own_pos, window_pos)
    grad_attn = contract_last(
        lax.all_gather(grad_out, "head", axis=1, tiled=True), out_weight
    ).astype(jnp.bfloat16)
    offsets = [distance for distance in range(1, REACH + 1)]
    stacked = jnp.stack((key_rows, value_rows))
    key_slots = [stacked for slot_index in range(REACH + 1)]
    for distance in offsets:
        key_slots[REACH - distance] = shifted(stacked, "blk", distance)
    windowed = jnp.concatenate(key_slots, axis=1)
    query_grads = []
    key_parts = []
    value_parts = []
    total_cols = []
    dot_cols = []
    for local_head in range(HEADS_DEV):
        head_index = head_base + local_head
        first_col = local_head * DH
        last_col = first_col + DH
        query_head = query_rows[:, first_col:last_col]
        grad_head = grad_attn[:, first_col:last_col]
        key_window = windowed[0, :, first_col:last_col]
        value_window = windowed[1, :, first_col:last_col]
        scores = contract_last(query_head, key_window) * score_scale
        masked = jnp.where(allowed, scores, -jnp.inf)
        row_max = jnp.max(masked, axis=1, keepdims=True)
        log_total = row_max + jnp.log(jnp.sum(jnp.exp(masked - row_max), axis=1, keepdims=True))
        attn_prob = jnp.where(allowed, jnp.exp(scores - log_total), 0.0)
        keep_mask = (
            mixhash(seed_word, head_index, own_pos[:, None], window_pos[None, :]) * keep_scale
        )
        dropped = (attn_prob * keep_mask).astype(jnp.bfloat16)
        attended = jnp.dot(dropped, value_window, preferred_element_type=jnp.float32).astype(
            jnp.bfloat16
        )
        row_dot = jnp.sum(
            grad_head.astype(jnp.float32) * attended.astype(jnp.float32), axis=1, keepdims=True
        )
        grad_prob = contract_last(grad_head, value_window)
        dscore = (attn_prob * (grad_prob * keep_mask - row_dot)).astype(jnp.bfloat16)
        query_grads.append(
            jnp.dot(dscore, key_window, preferred_element_type=jnp.float32) * score_scale
        )
        total_cols.append(log_total)
        dot_cols.append(row_dot)
        key_parts.append(contract_first(dscore, query_head) * score_scale)
        value_parts.append(contract_first(dropped, grad_head))
    grad_query = jnp.concatenate(query_grads, axis=1).astype(jnp.bfloat16)
    partials = jnp.stack((jnp.concatenate(key_parts, axis=1), jnp.concatenate(value_parts, axis=1)))
    summed = partials[:, REACH * row_count : (REACH + 1) * row_count]
    for distance in offsets:
        slot_index = REACH - distance
        outgoing = partials[:, slot_index * row_count : (slot_index + 1) * row_count]
        summed = summed + shifted(outgoing, "blk", -distance)
    grad_key = summed[0].astype(jnp.bfloat16)
    grad_value = summed[1].astype(jnp.bfloat16)
    return (grad_query, grad_key, grad_value)


def solution(mesh):
    in_specs = (
        P("blk", "head"),
        P("blk", "head"),
        P("blk", "head"),
        P("blk", "head"),
        P("head", None),
        P(),
        P(),
    )
    out_specs = (P("blk", "head"), P("blk", "head"), P("blk", "head"))
    return jax.shard_map(
        on_device, mesh=mesh, in_specs=in_specs, out_specs=out_specs, check_vma=False
    )
```

profile of v0, /device:TPU:6, one launch (start us, length us, event | category | flops | bytes accessed | tf_op | source)
XLA Modules:
  0.0 147.7 jit_solution(5357728235868405602)
XLA Ops:
  7.2 0.0 copy-start
  7.2 0.0 all-gather.2.cloned.1.call-start
  7.2 0.7 all-gather.2.cloned.1.call-update
  7.9 1.0 pad_maximum_fusion.1
  8.9 4.3 %collective-permute-start.1 = (bf16[2,256,256]{2,1,0:T(8,128)(2,1)S(1)}, bf16[2,256,256]{2,1,0:T(8,128)(2,1)S(1)}, u32[]{:S(2)}, u32[]{:S(2)}) collective-permute-start(bf16[2,256,256]{2,1,0:T(8,128)(2,1)S(1)} %pad_maximum_fusion.1), channel_id=1, source_target_pairs={{0,8},{8,16},{16,24},{24,32},{32,40},{40,48},{48,56},{56,64},{64,7... | collective-permute-start | bytes 786440 | tf_op jit(solution)/shard_map/ppermute | solution.py:22
  13.2 6.1 %collective-permute-start = (bf16[2,256,256]{2,1,0:T(8,128)(2,1)S(1)}, bf16[2,256,256]{2,1,0:T(8,128)(2,1)S(1)}, u32[]{:S(2)}, u32[]{:S(2)}) collective-permute-start(bf16[2,256,256]{2,1,0:T(8,128)(2,1)S(1)} %pad_maximum_fusion.1), channel_id=1, source_target_pairs={{0,16},{8,24},{16,32},{24,40},{32,48},{40,56},{48,64},{56,72},{64,... | collective-permute-start | bytes 786440 | tf_op jit(solution)/shard_map/ppermute | solution.py:22
  19.3 0.8 broadcast_compare_fusion
  20.8 0.1 broadcast_in_dim.13
  20.9 0.1 copy.31
  21.1 0.0 copy-start.8
  21.1 0.3 copy.18
  21.4 0.1 broadcast_in_dim.14
  21.5 0.1 copy.30
  21.6 1.0 copy.17
  22.6 13.1 %collective-permute-done.1 = bf16[2,256,256]{2,1,0:T(8,128)(2,1)S(1)} collective-permute-done((bf16[2,256,256]{2,1,0:T(8,128)(2,1)S(1)}, bf16[2,256,256]{2,1,0:T(8,128)(2,1)S(1)}, u32[]{:S(2)}, u32[]{:S(2)}) %collective-permute-start.1) | collective-permute-done | bytes 262176 | tf_op jit(solution)/shard_map/ppermute | solution.py:22
  35.7 5.8 %collective-permute-done = bf16[2,256,256]{2,1,0:T(8,128)(2,1)S(1)} collective-permute-done((bf16[2,256,256]{2,1,0:T(8,128)(2,1)S(1)}, bf16[2,256,256]{2,1,0:T(8,128)(2,1)S(1)}, u32[]{:S(2)}, u32[]{:S(2)}) %collective-permute-start) | collective-permute-done | bytes 262176 | tf_op jit(solution)/shard_map/ppermute | solution.py:22
  41.5 0.0 copy-done.6
  41.5 0.1 maximum_maximum_fusion
  41.6 0.0 copy-done.8
  41.6 0.0 copy-start.2
  41.6 0.3 fusion.4
  41.9 0.5 fusion.33
  42.4 0.1 copy-done.2
  42.5 0.9 copy-done.4
  43.4 0.3 exponential_reduce_fusion.1
  43.7 12.8 %all-gather.2.cloned.1.call-done = bf16[256,4096]{1,0:T(8,128)(2,1)} async-done(((bf16[256,512]{1,0:T(8,128)(2,1)}), bf16[256,4096]{1,0:T(8,128)(2,1)}) %all-gather.2.cloned.1.call-update) | async-done | bytes 2097168 | tf_op jit(solution)/shard_map/all_gather | solution.py:77
  56.6 2.4 %convolution_convert_fusion = bf16[256,256]{0,1:T(8,128)(2,1)S(1)} fusion(bf16[256,4096]{1,0:T(8,128)(2,1)} %all-gather.2.cloned.1.call-done, bf16[256,4096]{1,0:T(8,128)(2,1)S(1)} %copy-done), kind=kOutput, calls=%fused_computation.24 | convolution fusion | flops 536936448 | bytes 4325376 | tf_op jit(solution)/shard_map/dot_general | solution.py:52
  59.0 0.8 fusion.15
  59.9 0.8 fusion.42
  60.6 0.7 fusion.6
  61.4 0.3 convolution_multiply_fusion.5
  61.6 0.8 fusion.14
  62.5 0.8 fusion.39
  63.2 0.7 fusion.7
  64.0 0.3 convolution_multiply_fusion.4
  64.2 0.1 maximum_bitcast_fusion.1
  64.3 0.1 maximum_bitcast_fusion
  64.4 1.0 fusion.28
  65.4 18.8 %collective-permute-start.2 = (f32[2,256,256]{1,2,0:T(8,128)}, f32[2,256,256]{1,2,0:T(8,128)}, u32[]{:S(2)}, u32[]{:S(2)}) collective-permute-start(f32[2,256,256]{1,2,0:T(8,128)} %get-tuple-element.16), channel_id=1, source_target_pairs={{8,0},{16,8},{24,16},{32,24},{40,32},{48,40},{56,48},{64,56},{72,6... | collective-permute-start | bytes 1572872 | tf_op jit(solution)/shard_map/ppermute | solution.py:22
  84.2 1.9 %collective-permute-start.3 = (f32[2,256,256]{1,2,0:T(8,128)S(1)}, f32[2,256,256]{1,2,0:T(8,128)}, u32[]{:S(2)}, u32[]{:S(2)}) collective-permute-start(f32[2,256,256]{1,2,0:T(8,128)S(1)} %get-tuple-element.17), channel_id=1, source_target_pairs={{16,0},{24,8},{32,16},{40,24},{48,32},{56,40},{64,48},{72,56},{80,... | collective-permute-start | bytes 1572872 | tf_op jit(solution)/shard_map/ppermute | solution.py:22
  86.2 0.3 fusion.8
  86.5 0.3 fusion.9
  86.7 0.8 copy.21
  87.5 40.2 %collective-permute-done.2 = f32[2,256,256]{1,2,0:T(8,128)} collective-permute-done((f32[2,256,256]{1,2,0:T(8,128)}, f32[2,256,256]{1,2,0:T(8,128)}, u32[]{:S(2)}, u32[]{:S(2)}) %collective-permute-start.2) | collective-permute-done | bytes 524320 | tf_op jit(solution)/shard_map/ppermute | solution.py:22
  127.7 10.3 %collective-permute-done.3 = f32[2,256,256]{1,2,0:T(8,128)} collective-permute-done((f32[2,256,256]{1,2,0:T(8,128)S(1)}, f32[2,256,256]{1,2,0:T(8,128)}, u32[]{:S(2)}, u32[]{:S(2)}) %collective-permute-start.3) | collective-permute-done | bytes 524320 | tf_op jit(solution)/shard_map/ppermute | solution.py:22
  138.0 1.3 fusion.32
  139.3 0.8 copy.23
  140.1 0.8 copy.22
  (21 shorter events, 0.1 us)
Async XLA Ops:
  7.2 49.4 %copy-start = (bf16[256,4096]{1,0:T(8,128)(2,1)S(1)}, bf16[256,4096]{1,0:T(8,128)(2,1)}, u32[]{:S(2)}) copy-start(bf16[256,4096]{1,0:T(8,128)(2,1)} %param.11) | copy-start | bytes 6291460
  7.2 34.4 %copy-start.6 = (bf16[256,256]{1,0:T(8,128)(2,1)S(1)}, bf16[256,256]{1,0:T(8,128)(2,1)}, u32[]{:S(2)}) copy-start(bf16[256,256]{1,0:T(8,128)(2,1)} %param.9) | copy-start | bytes 393220
  7.2 34.4 %copy-start.7 = (bf16[256,256]{1,0:T(8,128)(2,1)S(1)}, bf16[256,256]{1,0:T(8,128)(2,1)}, u32[]{:S(2)}) copy-start(bf16[256,256]{1,0:T(8,128)(2,1)} %param.8) | copy-start | bytes 393220
  7.2 49.4 %all-gather.2.cloned.1.call-start = ((), (), s32[]{:S(2)}) async-start(), calls=%async_computation | async-start | bytes 2359296 | tf_op jit(solution)/shard_map/all_gather | solution.py:77
  8.9 26.8 %collective-permute-start.1 = (bf16[2,256,256]{2,1,0:T(8,128)(2,1)S(1)}, bf16[2,256,256]{2,1,0:T(8,128)(2,1)S(1)}, u32[]{:S(2)}, u32[]{:S(2)}) collective-permute-start(bf16[2,256,256]{2,1,0:T(8,128)(2,1)S(1)} %pad_maximum_fusion.1), channel_id=1, source_target_pairs={{0,8},{8,16},{16,24},{24,32},{32,40},{40,48},{48,56},{56,64},{64,7... | collective-permute-start | bytes 786440 | tf_op jit(solution)/shard_map/ppermute | solution.py:22
  13.2 28.3 %collective-permute-start = (bf16[2,256,256]{2,1,0:T(8,128)(2,1)S(1)}, bf16[2,256,256]{2,1,0:T(8,128)(2,1)S(1)}, u32[]{:S(2)}, u32[]{:S(2)}) collective-permute-start(bf16[2,256,256]{2,1,0:T(8,128)(2,1)S(1)} %pad_maximum_fusion.1), channel_id=1, source_target_pairs={{0,16},{8,24},{16,32},{24,40},{32,48},{40,56},{48,64},{56,72},{64,... | collective-permute-start | bytes 786440 | tf_op jit(solution)/shard_map/ppermute | solution.py:22
  21.1 20.6 %copy-start.8 = (bf16[256,256]{1,0:T(8,128)(2,1)S(1)}, bf16[256,256]{1,0:T(8,128)(2,1)}, u32[]{:S(2)}) copy-start(bf16[256,256]{1,0:T(8,128)(2,1)} %param.7) | copy-start | bytes 393220
  22.6 19.3 %copy-start.9 = (pred[256,768]{0,1:T(32,128)(4,1)S(1)}, pred[256,768]{0,1:T(32,128)(4,1)}, u32[]{:S(2)}) copy-start(pred[256,768]{0,1:T(32,128)(4,1)} %copy.17) | copy-start | bytes 589828
  41.6 0.9 copy-start.2
  42.5 0.9 copy-start.4
  56.6 2.5 %copy-start.3 = (bf16[2,768,256]{2,1,0:T(8,128)(2,1)S(1)}, bf16[2,768,256]{2,1,0:T(8,128)(2,1)}, u32[]{:S(2)}) copy-start(bf16[2,768,256]{2,1,0:T(8,128)(2,1)} %copy-done.2) | copy-start | bytes 2359300
  56.6 2.5 %copy-start.5 = (f32[256,768]{0,1:T(8,128)S(1)}, f32[256,768]{0,1:T(8,128)}, u32[]{:S(2)}) copy-start(f32[256,768]{0,1:T(8,128)} %copy-done.4) | copy-start | bytes 2359300
  64.4 22.1 %copy-start.1 = (f32[1,768,256]{1,2,0:T(8,128)}, f32[1,768,256]{1,2,0:T(8,128)S(1)}, u32[]{:S(2)}) copy-start(f32[1,768,256]{1,2,0:T(8,128)S(1)} %maximum_bitcast_fusion) | copy-start | bytes 2359300
  65.4 62.3 %collective-permute-start.2 = (f32[2,256,256]{1,2,0:T(8,128)}, f32[2,256,256]{1,2,0:T(8,128)}, u32[]{:S(2)}, u32[]{:S(2)}) collective-permute-start(f32[2,256,256]{1,2,0:T(8,128)} %get-tuple-element.16), channel_id=1, source_target_pairs={{8,0},{16,8},{24,16},{32,24},{40,32},{48,40},{56,48},{64,56},{72,6... | collective-permute-start | bytes 1572872 | tf_op jit(solution)/shard_map/ppermute | solution.py:22
  84.2 53.7 %collective-permute-start.3 = (f32[2,256,256]{1,2,0:T(8,128)S(1)}, f32[2,256,256]{1,2,0:T(8,128)}, u32[]{:S(2)}, u32[]{:S(2)}) collective-permute-start(f32[2,256,256]{1,2,0:T(8,128)S(1)} %get-tuple-element.17), channel_id=1, source_target_pairs={{16,0},{24,8},{32,16},{40,24},{48,32},{56,40},{64,48},{72,56},{80,... | collective-permute-start | bytes 1572872 | tf_op jit(solution)/shard_map/ppermute | solution.py:22
Sparse Core Ops, SparseCore 0:
  10.1 46.3 all-gather.1
where the time goes:
time: 148 us
  waiting for transfers between devices  82.9 us (56%)
  starting transfers between devices  31.2 us (21%)
  between operations  15 us (10%)
  matrix products  8.92 us (6%)
  local copies, waits for them, and re-layouts  5.06 us (3%)
  other arithmetic  4.67 us (3%)
    ppermute x4, waiting for transfers between devices, shifted(): lax.ppermute(value, axis, [(source, source + steps) for source in range(l...  69.4 us
    ppermute x4, starting transfers between devices, shifted(): lax.ppermute(value, axis, [(source, source + steps) for source in range(l...  31.1 us
    all_gather x1, waiting for transfers between devices, on_device(): lax.all_gather(grad_out, 'head', axis=1, tiled=True)  12.8 us
    dot_general x5, matrix products, contract_last(): lax.dot_general(left, right, (((1,), (1,)), ((), ())), preferred_element_...  4.61 us
    unnamed x25, local copies, waits for them, and re-layouts  3.5 us
  transfers between devices with their start and end apart: 5, of which 5 were waited for; matrix products, arithmetic and copies ran while one was open for 4% of the time, Pallas kernels for 0%

commit v1 on v0

v1 whole, which is shorter than its diff:
```python
import jax
import jax.numpy as jnp
from jax import lax
from jax.experimental import pallas as pl
from jax.experimental.pallas import tpu as pltpu
from jax.sharding import PartitionSpec as P

DH = 128
MB = 128
HEADS = 2
ROWS = 256
SLOTS = 5
WIN = SLOTS * MB
FAR = 3 * MB
WIDE = HEADS * DH

drop_level = 6554
keep_scale = 65536.0 / 58982.0
mix_one = 73244475
mix_two = 295559667
mix_three = 668265263
score_scale = DH**-0.5
hidden = -1e30

VMEM = pl.BlockSpec(memory_space=pltpu.VMEM)
SMEM = pl.BlockSpec(memory_space=pltpu.SMEM)


def bf16(value):
    return value.astype(jnp.bfloat16)


def f32(value):
    return value.astype(jnp.float32)


def dot_last(left, right):
    return lax.dot_general(
        left, right, (((1,), (1,)), ((), ())), preferred_element_type=jnp.float32
    )


def dot_first(left, right):
    return lax.dot_general(
        left, right, (((0,), (0,)), ((), ())), preferred_element_type=jnp.float32
    )


def dot(left, right):
    return jnp.dot(left, right, preferred_element_type=jnp.float32)


def bound_of(table, query_block, key_block):
    last = table.shape[0] - 1
    inside = (key_block >= 0) & (query_block <= last)
    kind = table[jnp.minimum(query_block, last), jnp.maximum(key_block, 0)]
    far = jnp.int32(1 << 20)
    bound = jnp.where(kind == 2, far, jnp.where(kind == 1, (query_block - key_block) * MB, -far))
    return jnp.where(inside, bound, -far)


def kept(seed, head, query_block, key_block):
    base = query_block * MB * mix_one + key_block * MB * mix_two + head * mix_three + seed
    rows = lax.broadcasted_iota(jnp.int32, (MB, MB), 0) * mix_one
    cols = lax.broadcasted_iota(jnp.int32, (MB, MB), 1) * mix_two
    hashed = (rows + cols) + base
    for _ in range(2):
        hashed = hashed ^ lax.shift_right_logical(hashed, jnp.int32(16))
        hashed = hashed * mix_one
    hashed = hashed ^ lax.shift_right_logical(hashed, jnp.int32(16))
    return (hashed & 65535) >= drop_level


def column_minus_row():
    return lax.broadcasted_iota(jnp.int32, (MB, MB), 1) - lax.broadcasted_iota(
        jnp.int32, (MB, MB), 0
    )


def forward_kernel(
    table, seed, query, key, value, near, far, signed, message, key_win, value_win
):
    shard = lax.axis_index("blk")
    first_head = lax.axis_index("head") * HEADS
    key_win[0:MB] = far[0:MB]
    key_win[MB:FAR] = near[0:ROWS]
    key_win[FAR:] = key[...]
    value_win[0:MB] = far[MB:]
    value_win[MB:FAR] = near[ROWS:]
    value_win[FAR:] = value[...]
    message[:, 0:WIDE] = query[...]
    ahead = column_minus_row()
    lane = lax.broadcasted_iota(jnp.int32, (MB, MB), 1)
    for block in range(2):
        rows = pl.ds(block * MB, MB)
        query_block = shard * 2 + block
        stats = jnp.zeros((MB, MB), jnp.float32)
        for head in range(HEADS):
            cols = pl.ds(head * DH, DH)
            scores = dot_last(query[rows, cols], key_win[:, cols])
            tiles = []
            for slot in range(block, SLOTS):
                bound = bound_of(table, query_block, shard * 2 - 3 + slot)
                tile = scores[:, slot * MB : (slot + 1) * MB] * score_scale
                tiles.append(jnp.where(ahead <= bound, tile, hidden))
            top = tiles[0]
            for tile in tiles[1:]:
                top = jnp.maximum(top, tile)
            top = jnp.max(top, axis=1, keepdims=True)
            tiles = [jnp.exp(tile - top) for tile in tiles]
            total = tiles[0]
            for tile in tiles[1:]:
                total = total + tile
            total = jnp.sum(total, axis=1, keepdims=True)
            inverse = 1.0 / total
            log_total = top + jnp.log(total)
            drops = []
            for slot in range(block, SLOTS):
                prob = tiles[slot - block] * inverse
                keep = kept(seed[0], first_head + head, query_block, shard * 2 - 3 + slot)
                signed[head, rows, slot * MB : (slot + 1) * MB] = jnp.where(keep, prob, -prob)
                drops.append(bf16(jnp.where(keep, prob * keep_scale, 0.0)))
            if block > 0:
                signed[head, rows, 0:MB] = jnp.zeros((MB, MB), jnp.float32)
            attended = dot(jnp.concatenate(drops, axis=1), value_win[block * MB :, cols])
            message[rows, WIDE + head * DH : WIDE + (head + 1) * DH] = bf16(attended)
            rest = log_total
            for part in range(3):
                piece = f32(bf16(rest))
                stats = jnp.where(lane == head * 3 + part, piece, stats)
                rest = rest - piece
        message[rows, 2 * WIDE :] = bf16(stats)


def later_kernel(table, seed, key, near, far, signed):
    shard = lax.axis_index("blk")
    first_head = lax.axis_index("head") * HEADS
    ahead = column_minus_row()
    for block in range(3):
        source, first = (near, block * MB) if block < 2 else (far, 0)
        query_block = shard * 2 + 2 + block
        for head in range(HEADS):
            cols = pl.ds(head * DH, DH)
            scores = dot_last(source[first : first + MB, cols], key[:, cols]) * score_scale
            stats = f32(source[first : first + MB, 2 * WIDE :])
            log_total = stats[:, 3 * head : 3 * head + 1]
            log_total = log_total + stats[:, 3 * head + 1 : 3 * head + 2]
            log_total = log_total + stats[:, 3 * head + 2 : 3 * head + 3]
            for slot in range(2):
                bound = bound_of(table, query_block, shard * 2 + slot)
                tile = scores[:, slot * MB : (slot + 1) * MB] - log_total
                prob = jnp.exp(jnp.where(ahead <= bound, tile, hidden))
                keep = kept(seed[0], first_head + head, query_block, shard * 2 + slot)
                signed[head, block * MB : (block + 1) * MB, slot * MB : (slot + 1) * MB] = (
                    jnp.where(keep, prob, -prob)
                )


def project_other_kernel(gathered, weight, out):
    width = gathered.shape[2]
    total = dot_last(gathered[0], weight[:, 0:width])
    for part in range(1, gathered.shape[0]):
        total = total + dot_last(gathered[part], weight[:, part * width : (part + 1) * width])
    out[...] = total


def project_own_kernel(gathered, weight, out):
    width = gathered.shape[2]
    core = lax.rem(lax.axis_index("head"), 2)
    total = None
    for part in range(gathered.shape[0]):
        first = pl.multiple_of((part * 2 + core) * width, width)
        term = dot_last(gathered[part], weight[:, pl.ds(first, width)])
        total = term if total is None else total + term
    out[...] = total


def dscore_of(signed, grad_prob, row_dot):
    scaled = jnp.where(signed > 0.0, grad_prob * keep_scale, 0.0)
    return bf16(jnp.abs(signed) * (scaled - row_dot))


def dropped_of(signed):
    return bf16(jnp.maximum(signed, 0.0) * keep_scale)


def own_kernel(signed, message, grad, key_win, value_win, grad_query, key_part, value_part):
    for head in range(HEADS):
        cols = pl.ds(head * DH, DH)
        grad_head = grad[:, cols]
        attended = message[:, WIDE + head * DH : WIDE + (head + 1) * DH]
        row_dot = jnp.sum(f32(grad_head) * f32(attended), axis=1, keepdims=True)
        grad_prob = dot_last(grad_head, value_win[:, cols])
        probs = signed[head]
        dscore = dscore_of(probs, grad_prob, row_dot)
        grad_query[:, cols] = bf16(dot(dscore, key_win[:, cols]) * score_scale)
        key_part[:, cols] = dot_first(dscore[:, FAR:], message[:, cols])
        value_part[:, cols] = dot_first(dropped_of(probs[:, FAR:]), grad_head)


def finish_kernel(
    signed, key, value, near, far, grad_near, grad_far, key_part, value_part, grad_key, grad_value
):
    for head in range(HEADS):
        cols = pl.ds(head * DH, DH)
        key_sum = key_part[:, cols]
        value_sum = value_part[:, cols]
        for source, grads, first, count in ((near, grad_near, 0, ROWS), (far, grad_far, ROWS, MB)):
            grad_head = grads[:, cols]
            attended = source[:, WIDE + head * DH : WIDE + (head + 1) * DH]
            row_dot = jnp.sum(f32(grad_head) * f32(attended), axis=1, keepdims=True)
            grad_prob = dot_last(grad_head, value[:, cols])
            probs = signed[head, first : first + count]
            dscore = dscore_of(probs, grad_prob, row_dot)
            key_sum = key_sum + dot_first(dscore, source[:, cols])
            value_sum = value_sum + dot_first(dropped_of(probs), grad_head)
        grad_key[:, cols] = bf16(key_sum * score_scale)
        grad_value[:, cols] = bf16(value_sum)


def call(kernel, specs, outs, flops, *args):
    shapes = [jax.ShapeDtypeStruct(shape, dtype) for shape, dtype in outs]
    moved = sum(a.size * a.dtype.itemsize for a in args)
    moved += sum(s.size * s.dtype.itemsize for s in shapes)
    return pl.pallas_call(
        kernel,
        out_shape=shapes,
        in_specs=specs,
        out_specs=[VMEM] * len(shapes),
        compiler_params=pltpu.CompilerParams(vmem_limit_bytes=32 << 20),
        cost_estimate=pl.CostEstimate(flops=flops, bytes_accessed=moved, transcendentals=0),
    )(*args)


def shifted(value, steps):
    count = lax.axis_size("blk")
    pairs = [(source, source + steps) for source in range(count) if 0 <= source + steps < count]
    return lax.ppermute(value, "blk", pairs)


def other_core(value):
    count = lax.axis_size("head")
    return lax.ppermute(value, "head", [(source, source ^ 1) for source in range(count)])


def on_device(query_rows, key_rows, value_rows, grad_out, out_weight, mask_types, drop_seed):
    half, full = jnp.bfloat16, jnp.float32
    count = lax.axis_size("head")
    core = lax.rem(lax.axis_index("head"), 2)
    groups = [list(range(first, count, 2)) for first in range(2)]
    gathered = lax.all_gather(grad_out, "head", axis=0, axis_index_groups=groups)
    width = grad_out.shape[1]
    far_keys = shifted(jnp.concatenate((key_rows[MB:], value_rows[MB:])), 2)
    near_keys = shifted(jnp.concatenate((key_rows, value_rows)), 1)
    by_part = out_weight.reshape(WIDE, count // 2, 2, width)
    theirs = lax.dynamic_index_in_dim(by_part, 1 - core, 2, keepdims=False)
    other_weight = other_core(theirs.reshape(WIDE, (count // 2) * width))
    tile = 2 * MB * MB * DH
    signed, message, key_win, value_win = call(
        forward_kernel,
        [SMEM, SMEM] + [VMEM] * 5,
        [
            ((HEADS, ROWS, WIN), full),
            ((ROWS, 2 * WIDE + MB), half),
            ((WIN, WIDE), half),
            ((WIN, WIDE), half),
        ],
        40 * tile,
        mask_types, drop_seed, query_rows, key_rows, value_rows, near_keys, far_keys,
    )
    far_message = shifted(message[:MB], -2)
    near_message = shifted(message, -1)
    (later,) = call(
        later_kernel,
        [SMEM, SMEM] + [VMEM] * 3,
        [((HEADS, FAR, ROWS), full)],
        24 * tile,
        mask_types, drop_seed, key_rows, near_message, far_message,
    )
    flops = 2 * ROWS * WIDE * width * (count // 2)
    shape = [((ROWS, WIDE), full)]
    (sent,) = call(project_other_kernel, [VMEM] * 2, shape, flops, gathered, other_weight)
    received = other_core(sent)
    (own,) = call(project_own_kernel, [VMEM] * 2, shape, flops, gathered, out_weight)
    grad_attn = (own + received).astype(half)
    grad_far = shifted(grad_attn[:MB], -2)
    grad_near = shifted(grad_attn, -1)
    grad_query, key_part, value_part = call(
        own_kernel,
        [VMEM] * 5,
        [((ROWS, WIDE), half), ((ROWS, WIDE), full), ((ROWS, WIDE), full)],
        80 * tile,
        signed, message, grad_attn, key_win, value_win,
    )
    grad_key, grad_value = call(
        finish_kernel,
        [VMEM] * 9,
        [((ROWS, WIDE), half), ((ROWS, WIDE), half)],
        40 * tile,
        later, key_rows, value_rows, near_message, far_message, grad_near, grad_far,
        key_part, value_part,
    )
    return (grad_query, grad_key, grad_value)


def solution(mesh):
    split = P("blk", "head")
    return jax.shard_map(
        on_device,
        mesh=mesh,
        in_specs=(split, split, split, split, P("head", None), P(), P()),
        out_specs=(split, split, split),
        check_vma=False,
    )
```

time: 148 us -> 129 us (0.87)
  the two profiles are of different devices: /device:TPU:6 before, /device:TPU:22 now
where the time goes in v1:
time: 129 us
  waiting for transfers between devices  58.5 us (45%)
  starting transfers between devices  31.5 us (24%)
  between operations  14.9 us (12%)
  local copies, waits for them, and re-layouts  13.1 us (10%)
  Pallas kernels  10.1 us (8%)
    ppermute x6, waiting for transfers between devices, shifted(): return lax.ppermute(value, 'blk', pairs)  33.8 us
    ppermute x6, starting transfers between devices, shifted(): return lax.ppermute(value, 'blk', pairs)  27.5 us
    all_gather x1, waiting for transfers between devices, on_device(): lax.all_gather(grad_out, 'head', axis=0, axis_index_groups=groups)  24 us
    pallas_call x6, Pallas kernels, call(): pl.pallas_call(kernel, out_shape=shapes, in_specs=specs, out_specs=[VMEM]...  10.1 us
    dynamic_slice x1, local copies, waits for them, and re-layouts, on_device(): theirs = lax.dynamic_index_in_dim(by_part, 1 - core, 2, keepdims=False)  6.55 us
    ppermute x2, starting transfers between devices, other_core(): lax.ppermute(value, 'head', [(source, source ^ 1) for source in range(cou...  3.97 us
    reshape x1, local copies, waits for them, and re-layouts, on_device(): by_part = out_weight.reshape(WIDE, count // 2, 2, width)  3.3 us
    unnamed x17, local copies, waits for them, and re-layouts  3.26 us
  transfers between devices with their start and end apart: 9, of which 3 were waited for; matrix products, arithmetic and copies ran while one was open for 8% of the time, Pallas kernels for 6%

profile of v1, /device:TPU:22, one launch (start us, length us, event | category | flops | bytes accessed | tf_op | source)
XLA Modules:
  0.0 128.9 jit_solution(10371936225921398092)
XLA Ops:
  7.2 0.0 all-gather.3.cloned.1.call-start
  7.2 0.7 all-gather.3.cloned.1.call-update
  7.9 3.3 %reshape.13 = bf16[256,4,2,512]{3,2,1,0:T(2,128)(2,1)S(1)} reshape(bf16[256,4096]{1,0:T(8,128)(2,1)} %weight.1) | data formatting | bytes 4194304 | tf_op jit(solution)/shard_map/reshape | solution.py:255
  11.2 0.0 copy-start.3
  11.2 0.0 copy-start.4
  11.2 6.5 %dynamic-slice_reduce_fusion = bf16[256,4,512]{2,1,0:T(4,128)(2,1)S(1)} fusion(bf16[256,4,2,512]{3,2,1,0:T(2,128)(2,1)S(1)} %reshape.13, s32[]{:T(128)S(6)} %select_n.4), kind=kLoop, calls=%fused_computation | loop fusion | bytes 2097156 | tf_op jit(solution)/shard_map/jit(dynamic_index_in_dim)/dynamic_slice | solution.py:256
  17.8 0.3 copy.12
  18.1 0.0 slice-start
  18.1 0.0 slice-start.1
  18.1 2.1 %collective-permute-start.2 = (bf16[256,2048]{1,0:T(8,128)(2,1)S(1)}, bf16[256,2048]{1,0:T(8,128)(2,1)S(1)}, u32[]{:S(2)}, u32[]{:S(2)}) collective-permute-start(bf16[256,2048]{1,0:T(8,128)(2,1)S(1)} %bitcast.6), channel_id=1, source_target_pairs={{0,1},{1,0},{2,3},{3,2},{4,5},{5,4},{6,7},{7,6},{8,9},{9,8},{10,11... | collective-permute-start | bytes 3145736 | tf_op jit(solution)/shard_map/ppermute | solution.py:243
  20.2 0.0 copy-done.3
  20.2 0.0 copy-done.4
  20.2 0.7 pad_maximum_fusion
  20.9 0.0 copy-start
  20.9 4.4 %collective-permute-start = (bf16[512,256]{1,0:T(8,128)(2,1)}, bf16[512,256]{1,0:T(8,128)(2,1)}, u32[]{:S(2)}, u32[]{:S(2)}) collective-permute-start(bf16[512,256]{1,0:T(8,128)(2,1)} %pad_maximum_fusion), channel_id=1, source_target_pairs={{0,8},{8,16},{16,24},{24,32},{32,40},{40,48},{48,56},{56,64},{64,7... | collective-permute-start | bytes 786440 | tf_op jit(solution)/shard_map/ppermute | solution.py:238
  25.3 0.0 collective-permute-done.2.weight
  25.3 24.0 %all-gather.3.cloned.1.call-done = bf16[1024,512]{1,0:T(8,128)(2,1)} async-done(((bf16[256,512]{1,0:T(8,128)(2,1)}), bf16[1024,512]{1,0:T(8,128)(2,1)}) %all-gather.3.cloned.1.call-update) | async-done | bytes 1048592 | tf_op jit(solution)/shard_map/all_gather | solution.py:251
  49.3 0.0 copy-start.1
  49.3 1.2 copy-done.1
  50.5 0.0 copy-start.2
  50.5 0.5 shard_map.96
  51.0 1.9 %collective-permute-start.3 = (f32[256,256]{1,0:T(8,128)S(1)}, f32[256,256]{1,0:T(8,128)S(1)}, u32[]{:S(2)}, u32[]{:S(2)}) collective-permute-start(f32[256,256]{1,0:T(8,128)S(1)} %shard_map.96), channel_id=1, source_target_pairs={{0,1},{1,0},{2,3},{3,2},{4,5},{5,4},{6,7},{7,6},{8,9},{9,8},{10,11... | collective-permute-start | bytes 786440 | tf_op jit(solution)/shard_map/ppermute | solution.py:243
  52.9 0.0 slice-done
  52.9 0.0 slice-done.1
  52.9 4.6 %collective-permute-start.1 = (bf16[256,256]{1,0:T(8,128)(2,1)S(1)}, bf16[256,256]{1,0:T(8,128)(2,1)S(1)}, u32[]{:S(2)}, u32[]{:S(2)}) collective-permute-start(bf16[256,256]{1,0:T(8,128)(2,1)S(1)} %pad_maximum_fusion.1), channel_id=1, source_target_pairs={{0,16},{8,24},{16,32},{24,40},{32,48},{40,56},{48,64},{56,72},{64,... | collective-permute-start | bytes 393224 | tf_op jit(solution)/shard_map/ppermute | solution.py:238
  58.2 10.7 %collective-permute-done.1.far = bf16[256,256]{1,0:T(8,128)(2,1)S(1)} collective-permute-done((bf16[256,256]{1,0:T(8,128)(2,1)S(1)}, bf16[256,256]{1,0:T(8,128)(2,1)S(1)}, u32[]{:S(2)}, u32[]{:S(2)}) %collective-permute-start.1) | collective-permute-done | bytes 131104 | tf_op jit(solution)/shard_map/ppermute | solution.py:238
  69.0 0.0 collective-permute-done.near
  69.0 0.8 copy-done.5
  69.8 0.0 copy-start.7
  69.8 0.9 copy-done.7
  70.7 3.6 %shard_map.94 = (f32[2,256,640]{2,1,0:T(8,128)S(1)}, bf16[256,640]{1,0:T(8,128)(2,1)S(1)}, bf16[640,256]{1,0:T(8,128)(2,1)S(1)}, bf16[640,256]{1,0:T(8,128)(2,1)S(1)}) custom-call(s32[128,128]{1,0:T(8,128)S(1)} %copy-done.5, s32[1]{0:T(128)S(6)} %copy.13.seed, bf16[256,256]{1,0:T(8,128)(2,1)S(1)} %copy-done.7, bf16[256,256]{1,0:T(8,128)(2,1)S(1)} %copy-done.3, ...), custom_call_target="tpu_custom_call" | custom-call | flops 167772160 | bytes 3145732 | tf_op jit(solution)/shard_map/pallas_call | solution.py:225
  74.4 12.4 %collective-permute-start.4 = (bf16[256,640]{1,0:T(8,128)(2,1)S(1)}, bf16[256,640]{1,0:T(8,128)(2,1)S(1)}, u32[]{:S(2)}, u32[]{:S(2)}) collective-permute-start(bf16[256,640]{1,0:T(8,128)(2,1)S(1)} %get-tuple-element.13.message), channel_id=1, source_target_pairs={{8,0},{16,8},{24,16},{32,24},{40,32},{48,40},{56,48},{64,56},{72,6... | collective-permute-start | bytes 983048 | tf_op jit(solution)/shard_map/ppermute | solution.py:238
  86.8 0.0 copy-start.6
  86.8 2.1 %collective-permute-start.5 = (bf16[128,640]{1,0:T(8,128)(2,1)S(1)}, bf16[128,640]{1,0:T(8,128)(2,1)S(1)}, u32[]{:S(2)}, u32[]{:S(2)}) collective-permute-start(bf16[128,640]{1,0:T(8,128)(2,1)S(1)} %slice.14), channel_id=1, source_target_pairs={{16,0},{24,8},{32,16},{40,24},{48,32},{56,40},{64,48},{72,56},{80,... | collective-permute-start | bytes 491528 | tf_op jit(solution)/shard_map/ppermute | solution.py:238
  88.9 0.0 copy-done
  88.9 0.0 copy-done.2
  88.9 0.5 shard_map.95
  89.4 0.0 collective-permute-done.3
  89.4 1.9 %collective-permute-start.6 = (bf16[256,256]{1,0:T(8,128)(2,1)S(1)}, bf16[256,256]{1,0:T(8,128)(2,1)S(1)}, u32[]{:S(2)}, u32[]{:S(2)}) collective-permute-start(bf16[256,256]{1,0:T(8,128)(2,1)S(1)} %add_convert_fusion.grad), channel_id=1, source_target_pairs={{8,0},{16,8},{24,16},{32,24},{40,32},{48,40},{56,48},{64,56},{72,6... | collective-permute-start | bytes 393224 | tf_op jit(solution)/shard_map/ppermute | solution.py:238
  91.4 2.1 %collective-permute-start.7 = (bf16[128,256]{1,0:T(8,128)(2,1)S(1)}, bf16[128,256]{1,0:T(8,128)(2,1)S(1)}, u32[]{:S(2)}, u32[]{:S(2)}) collective-permute-start(bf16[128,256]{1,0:T(8,128)(2,1)S(1)} %slice.16), channel_id=1, source_target_pairs={{16,0},{24,8},{32,16},{40,24},{48,32},{56,40},{64,48},{72,56},{80,... | collective-permute-start | bytes 196616 | tf_op jit(solution)/shard_map/ppermute | solution.py:238
  93.5 23.1 %collective-permute-done.5.far = bf16[128,640]{1,0:T(8,128)(2,1)S(1)} collective-permute-done((bf16[128,640]{1,0:T(8,128)(2,1)S(1)}, bf16[128,640]{1,0:T(8,128)(2,1)S(1)}, u32[]{:S(2)}, u32[]{:S(2)}) %collective-permute-start.5) | collective-permute-done | bytes 163872 | tf_op jit(solution)/shard_map/ppermute | solution.py:238
  116.5 0.0 collective-permute-done.4.near
  116.5 0.0 copy-done.6
  116.5 2.3 %shard_map.98.signed = f32[2,384,256]{2,1,0:T(8,128)S(1)} custom-call(s32[128,128]{1,0:T(8,128)S(1)} %copy-done.6, s32[1]{0:T(128)S(6)} %copy.13.seed, bf16[256,256]{1,0:T(8,128)(2,1)S(1)} %copy-done.3, bf16[256,640]{1,0:T(8,128)(2,1)S(1)} %collective-permute-done.4.near, bf16[128,640]{1,0:T(8,128)(2,1)S(1)} %collective-permute-done.5.far), custom_call_target="tpu_custom_call" | custom-call | flops 100663296 | bytes 1474564 | tf_op jit(solution)/shard_map/pallas_call | solution.py:225
  118.9 1.4 %shard_map.97 = (bf16[256,256]{1,0:T(8,128)(2,1)}, f32[256,256]{1,0:T(8,128)S(1)}, f32[256,256]{1,0:T(8,128)S(1)}) custom-call(f32[2,256,640]{2,1,0:T(8,128)S(1)} %get-tuple-element.12.signed, bf16[256,640]{1,0:T(8,128)(2,1)S(1)} %get-tuple-element.13.message, bf16[256,256]{1,0:T(8,128)(2,1)S(1)} %add_convert_fusion.grad, ...), custom_call_target="tpu_custom_call" | custom-call | flops 335544320 | bytes 3080192 | tf_op jit(solution)/shard_map/pallas_call | solution.py:225
  120.3 0.0 collective-permute-done.7.grad_far
  120.3 0.0 collective-permute-done.6.grad_near
  120.3 1.7 %shard_map.99 = (bf16[256,256]{1,0:T(8,128)(2,1)}, bf16[256,256]{1,0:T(8,128)(2,1)}) custom-call(f32[2,384,256]{2,1,0:T(8,128)S(1)} %shard_map.98.signed, bf16[256,256]{1,0:T(8,128)(2,1)S(1)} %copy-done.3, bf16[256,256]{1,0:T(8,128)(2,1)S(1)} %copy-done.4, bf16[256,640]{1,0:T(8,128)(2,1)S(1)} %collective-permute-done.4.near, ...), custom_call_target="tpu_custom_call" | custom-call | flops 167772160 | bytes 2523136 | tf_op jit(solution)/shard_map/pallas_call | solution.py:225
  (5 shorter events, 0.1 us)
Async XLA Ops:
  7.2 42.1 %all-gather.3.cloned.1.call-start = ((), (), s32[]{:S(2)}) async-start(), calls=%async_computation | async-start | bytes 1310720 | tf_op jit(solution)/shard_map/all_gather | solution.py:251
  11.2 8.9 %copy-start.3 = (bf16[256,256]{1,0:T(8,128)(2,1)S(1)}, bf16[256,256]{1,0:T(8,128)(2,1)}, u32[]{:S(2)}) copy-start(bf16[256,256]{1,0:T(8,128)(2,1)} %key.5) | copy-start | bytes 393220
  11.2 8.9 %copy-start.4 = (bf16[256,256]{1,0:T(8,128)(2,1)S(1)}, bf16[256,256]{1,0:T(8,128)(2,1)}, u32[]{:S(2)}) copy-start(bf16[256,256]{1,0:T(8,128)(2,1)} %value.3) | copy-start | bytes 393220
  18.1 34.8 %slice-start = ((bf16[256,256]{1,0:T(8,128)(2,1)}), bf16[128,256]{1,0:T(8,128)(2,1)S(1)}, s32[]{:S(2)}) async-start(bf16[256,256]{1,0:T(8,128)(2,1)} %key.5), calls=%async_computation.1 | async-start | bytes 131072 | tf_op jit(solution)/shard_map/slice | solution.py:253
  18.1 34.8 %slice-start.1 = ((bf16[256,256]{1,0:T(8,128)(2,1)}), bf16[128,256]{1,0:T(8,128)(2,1)S(1)}, s32[]{:S(2)}) async-start(bf16[256,256]{1,0:T(8,128)(2,1)} %value.3), calls=%async_computation.2 | async-start | bytes 131072 | tf_op jit(solution)/shard_map/slice | solution.py:253
  18.1 7.2 %collective-permute-start.2 = (bf16[256,2048]{1,0:T(8,128)(2,1)S(1)}, bf16[256,2048]{1,0:T(8,128)(2,1)S(1)}, u32[]{:S(2)}, u32[]{:S(2)}) collective-permute-start(bf16[256,2048]{1,0:T(8,128)(2,1)S(1)} %bitcast.6), channel_id=1, source_target_pairs={{0,1},{1,0},{2,3},{3,2},{4,5},{5,4},{6,7},{7,6},{8,9},{9,8},{10,11... | collective-permute-start | bytes 3145736 | tf_op jit(solution)/shard_map/ppermute | solution.py:243
  20.9 68.0 %copy-start = (bf16[256,4096]{1,0:T(8,128)(2,1)S(1)}, bf16[256,4096]{1,0:T(8,128)(2,1)}, u32[]{:S(2)}) copy-start(bf16[256,4096]{1,0:T(8,128)(2,1)} %weight.1) | copy-start | bytes 6291460
  20.9 48.1 %collective-permute-start = (bf16[512,256]{1,0:T(8,128)(2,1)}, bf16[512,256]{1,0:T(8,128)(2,1)}, u32[]{:S(2)}, u32[]{:S(2)}) collective-permute-start(bf16[512,256]{1,0:T(8,128)(2,1)} %pad_maximum_fusion), channel_id=1, source_target_pairs={{0,8},{8,16},{16,24},{24,32},{32,40},{40,48},{48,56},{56,64},{64,7... | collective-permute-start | bytes 786440 | tf_op jit(solution)/shard_map/ppermute | solution.py:238
  49.3 1.2 copy-start.1
  50.5 38.4 %copy-start.2 = (bf16[1024,512]{1,0:T(8,128)(2,1)S(1)}, bf16[1024,512]{1,0:T(8,128)(2,1)}, u32[]{:S(2)}) copy-start(bf16[1024,512]{1,0:T(8,128)(2,1)} %all-gather.3.cloned.1.call-done) | copy-start | bytes 3145732
  51.0 38.4 %collective-permute-start.3 = (f32[256,256]{1,0:T(8,128)S(1)}, f32[256,256]{1,0:T(8,128)S(1)}, u32[]{:S(2)}, u32[]{:S(2)}) collective-permute-start(f32[256,256]{1,0:T(8,128)S(1)} %shard_map.96), channel_id=1, source_target_pairs={{0,1},{1,0},{2,3},{3,2},{4,5},{5,4},{6,7},{7,6},{8,9},{9,8},{10,11... | collective-permute-start | bytes 786440 | tf_op jit(solution)/shard_map/ppermute | solution.py:243
  52.9 16.0 %collective-permute-start.1 = (bf16[256,256]{1,0:T(8,128)(2,1)S(1)}, bf16[256,256]{1,0:T(8,128)(2,1)S(1)}, u32[]{:S(2)}, u32[]{:S(2)}) collective-permute-start(bf16[256,256]{1,0:T(8,128)(2,1)S(1)} %pad_maximum_fusion.1), channel_id=1, source_target_pairs={{0,16},{8,24},{16,32},{24,40},{32,48},{40,56},{48,64},{56,72},{64,... | collective-permute-start | bytes 393224 | tf_op jit(solution)/shard_map/ppermute | solution.py:238
  69.0 0.8 copy-start.5
  69.8 0.9 copy-start.7
  74.4 42.2 %collective-permute-start.4 = (bf16[256,640]{1,0:T(8,128)(2,1)S(1)}, bf16[256,640]{1,0:T(8,128)(2,1)S(1)}, u32[]{:S(2)}, u32[]{:S(2)}) collective-permute-start(bf16[256,640]{1,0:T(8,128)(2,1)S(1)} %get-tuple-element.13.message), channel_id=1, source_target_pairs={{8,0},{16,8},{24,16},{32,24},{40,32},{48,40},{56,48},{64,56},{72,6... | collective-permute-start | bytes 983048 | tf_op jit(solution)/shard_map/ppermute | solution.py:238
  86.8 29.8 %copy-start.6 = (s32[128,128]{1,0:T(8,128)S(1)}, s32[128,128]{1,0:T(8,128)}, u32[]{:S(2)}) copy-start(s32[128,128]{1,0:T(8,128)} %table.3) | copy-start | bytes 196612
  86.8 29.7 %collective-permute-start.5 = (bf16[128,640]{1,0:T(8,128)(2,1)S(1)}, bf16[128,640]{1,0:T(8,128)(2,1)S(1)}, u32[]{:S(2)}, u32[]{:S(2)}) collective-permute-start(bf16[128,640]{1,0:T(8,128)(2,1)S(1)} %slice.14), channel_id=1, source_target_pairs={{16,0},{24,8},{32,16},{40,24},{48,32},{56,40},{64,48},{72,56},{80,... | collective-permute-start | bytes 491528 | tf_op jit(solution)/shard_map/ppermute | solution.py:238
  89.4 30.9 %collective-permute-start.6 = (bf16[256,256]{1,0:T(8,128)(2,1)S(1)}, bf16[256,256]{1,0:T(8,128)(2,1)S(1)}, u32[]{:S(2)}, u32[]{:S(2)}) collective-permute-start(bf16[256,256]{1,0:T(8,128)(2,1)S(1)} %add_convert_fusion.grad), channel_id=1, source_target_pairs={{8,0},{16,8},{24,16},{32,24},{40,32},{48,40},{56,48},{64,56},{72,6... | collective-permute-start | bytes 393224 | tf_op jit(solution)/shard_map/ppermute | solution.py:238
  91.4 29.0 %collective-permute-start.7 = (bf16[128,256]{1,0:T(8,128)(2,1)S(1)}, bf16[128,256]{1,0:T(8,128)(2,1)S(1)}, u32[]{:S(2)}, u32[]{:S(2)}) collective-permute-start(bf16[128,256]{1,0:T(8,128)(2,1)S(1)} %slice.16), channel_id=1, source_target_pairs={{16,0},{24,8},{32,16},{40,24},{48,32},{56,40},{64,48},{72,56},{80,... | collective-permute-start | bytes 196616 | tf_op jit(solution)/shard_map/ppermute | solution.py:238
Sparse Core Ops, SparseCore 0:
  10.1 39.1 all-gather.2

commit v2 on v1

--- a/solution.py
+++ b/solution.py
@@ -156,6 +156,15 @@
                 )
 
 
+def cut_kernel(weight, out):
+    core = lax.rem(lax.axis_index("head"), 2)
+    parts = lax.axis_size("head") // 2
+    width = out.shape[1] // parts
+    for part in range(parts):
+        first = pl.multiple_of((part * 2 + 1 - core) * width, width)
+        out[:, part * width : (part + 1) * width] = weight[:, pl.ds(first, width)]
+
+
 def project_other_kernel(gathered, weight, out):
     width = gathered.shape[2]
     total = dot_last(gathered[0], weight[:, 0:width])
@@ -227,7 +236,7 @@
         out_shape=shapes,
         in_specs=specs,
         out_specs=[VMEM] * len(shapes),
-        compiler_params=pltpu.CompilerParams(vmem_limit_bytes=32 << 20),
+        compiler_params=pltpu.CompilerParams(vmem_limit_bytes=16 << 20),
         cost_estimate=pl.CostEstimate(flops=flops, bytes_accessed=moved, transcendentals=0),
     )(*args)
 
@@ -246,15 +255,14 @@
 def on_device(query_rows, key_rows, value_rows, grad_out, out_weight, mask_types, drop_seed):
     half, full = jnp.bfloat16, jnp.float32
     count = lax.axis_size("head")
-    core = lax.rem(lax.axis_index("head"), 2)
     groups = [list(range(first, count, 2)) for first in range(2)]
     gathered = lax.all_gather(grad_out, "head", axis=0, axis_index_groups=groups)
     width = grad_out.shape[1]
+    near_keys = shifted(jnp.concatenate((key_rows, value_rows)), 1)
     far_keys = shifted(jnp.concatenate((key_rows[MB:], value_rows[MB:])), 2)
-    near_keys = shifted(jnp.concatenate((key_rows, value_rows)), 1)
-    by_part = out_weight.reshape(WIDE, count // 2, 2, width)
-    theirs = lax.dynamic_index_in_dim(by_part, 1 - core, 2, keepdims=False)
-    other_weight = other_core(theirs.reshape(WIDE, (count // 2) * width))
+    (theirs,) = call(
+        cut_kernel, [VMEM], [((WIDE, (count // 2) * width), half)], 0, out_weight
+    )
     tile = 2 * MB * MB * DH
     signed, message, key_win, value_win = call(
         forward_kernel,
@@ -268,8 +276,12 @@
         40 * tile,
         mask_types, drop_seed, query_rows, key_rows, value_rows, near_keys, far_keys,
     )
+    near_message = shifted(message, -1)
     far_message = shifted(message[:MB], -2)
-    near_message = shifted(message, -1)
+    other_weight = other_core(theirs)
+    gathered, near_message, far_message = lax.optimization_barrier(
+        (gathered, near_message, far_message)
+    )
     (later,) = call(
         later_kernel,
         [SMEM, SMEM] + [VMEM] * 3,

time: 129 us -> 115 us (0.89)
  the two profiles are of different devices: /device:TPU:22 before, /device:TPU:15 now
where the time goes in v2:
time: 115 us; the launch traced here: 114 us
  starting transfers between devices  43.5 us (38%)
  waiting for transfers between devices  38.9 us (34%)
  between operations  15 us (13%)
  Pallas kernels  12.3 us (11%)
  local copies, waits for them, and re-layouts  4.7 us (4%)
    ppermute x6, starting transfers between devices, shifted(): return lax.ppermute(value, 'blk', pairs)  38.3 us
    ppermute x6, waiting for transfers between devices, shifted(): return lax.ppermute(value, 'blk', pairs)  37.6 us
    pallas_call x7, Pallas kernels, call(): pl.pallas_call(kernel, out_shape=shapes, in_specs=specs, out_specs=[VMEM]...  12.3 us
    ppermute x2, starting transfers between devices, other_core(): lax.ppermute(value, 'head', [(source, source ^ 1) for source in range(cou...  5.1 us
    unnamed x26, local copies, waits for them, and re-layouts  4.67 us
  transfers between devices with their start and end apart: 9, of which 4 were waited for; matrix products, arithmetic and copies ran while one was open for 0% of the time, Pallas kernels for 8%

profile of v2, /device:TPU:15, one launch (start us, length us, event | category | flops | bytes accessed | tf_op | source)
XLA Modules:
  0.0 114.5 jit_solution(3158929756974097732)
XLA Ops:
  7.2 0.0 copy-start.3
  7.2 0.0 slice-start
  7.2 0.0 slice-start.1
  7.2 0.0 all-gather.3.cloned.1.call-start
  7.2 0.7 all-gather.3.cloned.1.call-update
  7.9 0.0 copy-start
  7.9 1.6 %copy-done = bf16[256,4096]{1,0:T(8,128)(2,1)S(1)} copy-done((bf16[256,4096]{1,0:T(8,128)(2,1)S(1)}, bf16[256,4096]{1,0:T(8,128)(2,1)}, u32[]{:S(2)}) %copy-start) | copy-done | bytes 2097176
  9.5 1.1 shard_map.96
  10.6 2.6 %collective-permute-start.4 = (bf16[256,2048]{1,0:T(8,128)(2,1)}, bf16[256,2048]{1,0:T(8,128)(2,1)}, u32[]{:S(2)}, u32[]{:S(2)}) collective-permute-start(bf16[256,2048]{1,0:T(8,128)(2,1)} %shard_map.96), channel_id=1, source_target_pairs={{0,1},{1,0},{2,3},{3,2},{4,5},{5,4},{6,7},{7,6},{8,9},{9,8},{10,11... | collective-permute-start | bytes 3145736 | tf_op jit(solution)/shard_map/ppermute | solution.py:252
  13.2 0.0 copy-done.3
  13.2 0.0 copy-done.4
  13.2 0.0 copy-start.1
  13.2 4.1 %collective-permute-start = (bf16[512,256]{1,0:T(8,128)(2,1)S(1)}, bf16[512,256]{1,0:T(8,128)(2,1)S(1)}, u32[]{:S(2)}, u32[]{:S(2)}) collective-permute-start(bf16[512,256]{1,0:T(8,128)(2,1)S(1)} %pad_maximum_fusion), channel_id=1, source_target_pairs={{0,8},{8,16},{16,24},{24,32},{32,40},{40,48},{48,56},{56,64},{64,7... | collective-permute-start | bytes 786440 | tf_op jit(solution)/shard_map/ppermute | solution.py:247
  17.4 0.0 slice-done
  17.4 0.0 slice-done.1
  17.4 5.8 %collective-permute-start.1 = (bf16[256,256]{1,0:T(8,128)(2,1)S(1)}, bf16[256,256]{1,0:T(8,128)(2,1)S(1)}, u32[]{:S(2)}, u32[]{:S(2)}) collective-permute-start(bf16[256,256]{1,0:T(8,128)(2,1)S(1)} %pad_maximum_fusion.1), channel_id=1, source_target_pairs={{0,16},{8,24},{16,32},{24,40},{32,48},{40,56},{48,64},{56,72},{64,... | collective-permute-start | bytes 393224 | tf_op jit(solution)/shard_map/ppermute | solution.py:247
  23.9 14.5 %collective-permute-done.1.far = bf16[256,256]{1,0:T(8,128)(2,1)S(1)} collective-permute-done((bf16[256,256]{1,0:T(8,128)(2,1)S(1)}, bf16[256,256]{1,0:T(8,128)(2,1)S(1)}, u32[]{:S(2)}, u32[]{:S(2)}) %collective-permute-start.1) | collective-permute-done | bytes 131104 | tf_op jit(solution)/shard_map/ppermute | solution.py:247
  38.4 0.7 collective-permute-done.near
  39.0 0.0 copy-done.11
  39.0 0.0 copy-done.12
  39.0 3.6 %shard_map.94 = (f32[2,256,640]{2,1,0:T(8,128)S(1)}, bf16[256,640]{1,0:T(8,128)(2,1)S(1)}, bf16[640,256]{1,0:T(8,128)(2,1)S(1)}, bf16[640,256]{1,0:T(8,128)(2,1)S(1)}) custom-call(s32[128,128]{1,0:T(8,128)S(1)} %copy-done.11, s32[1]{0:T(128)S(6)} %copy.10.seed, bf16[256,256]{1,0:T(8,128)(2,1)S(1)} %copy-done.12, bf16[256,256]{1,0:T(8,128)(2,1)S(1)} %copy-done.3, ...), custom_call_target="tpu_custom_call" | custom-call | flops 167772160 | bytes 3145732 | tf_op jit(solution)/shard_map/pallas_call | solution.py:234
  42.7 0.0 copy-start.5
  42.7 1.1 copy-done.5
  43.8 0.7 copy-done.7
  44.5 12.5 %collective-permute-start.2 = (bf16[256,640]{1,0:T(8,128)(2,1)S(1)}, bf16[256,640]{1,0:T(8,128)(2,1)S(1)}, u32[]{:S(2)}, u32[]{:S(2)}) collective-permute-start(bf16[256,640]{1,0:T(8,128)(2,1)S(1)} %get-tuple-element.16.message), channel_id=1, source_target_pairs={{8,0},{16,8},{24,16},{32,24},{40,32},{48,40},{56,48},{64,56},{72,6... | collective-permute-start | bytes 983048 | tf_op jit(solution)/shard_map/ppermute | solution.py:247
  57.0 1.9 %collective-permute-start.3 = (bf16[128,640]{1,0:T(8,128)(2,1)S(1)}, bf16[128,640]{1,0:T(8,128)(2,1)S(1)}, u32[]{:S(2)}, u32[]{:S(2)}) collective-permute-start(bf16[128,640]{1,0:T(8,128)(2,1)S(1)} %slice.14), channel_id=1, source_target_pairs={{16,0},{24,8},{32,16},{40,24},{48,32},{56,40},{64,48},{72,56},{80,... | collective-permute-start | bytes 491528 | tf_op jit(solution)/shard_map/ppermute | solution.py:247
  59.0 22.5 %collective-permute-done.3.far = bf16[128,640]{1,0:T(8,128)(2,1)S(1)} collective-permute-done((bf16[128,640]{1,0:T(8,128)(2,1)S(1)}, bf16[128,640]{1,0:T(8,128)(2,1)S(1)}, u32[]{:S(2)}, u32[]{:S(2)}) %collective-permute-start.3) | collective-permute-done | bytes 163872 | tf_op jit(solution)/shard_map/ppermute | solution.py:247
  81.4 0.0 copy-done.9
  81.4 0.0 collective-permute-done.2.near
  81.4 0.0 collective-permute-done.4.weight
  81.5 1.2 %copy-done.2 = bf16[1024,512]{1,0:T(8,128)(2,1)S(1)} copy-done((bf16[1024,512]{1,0:T(8,128)(2,1)S(1)}, bf16[1024,512]{1,0:T(8,128)(2,1)}, u32[]{:S(2)}) %copy-start.2) | copy-done | bytes 1048600
  82.7 1.7 %shard_map.97 = f32[256,256]{1,0:T(8,128)S(1)} custom-call(bf16[4,256,512]{2,1,0:T(8,128)(2,1)S(1)} %bitcast.1, bf16[256,2048]{1,0:T(8,128)(2,1)} %collective-permute-done.4.weight), custom_call_target="tpu_custom_call" | custom-call | flops 268435456 | bytes 2359296 | tf_op jit(solution)/shard_map/pallas_call | solution.py:234
  84.4 0.0 copy-start.6
  84.4 0.0 copy-start.8
  84.4 0.0 copy-start.10
  84.4 2.5 %collective-permute-start.5 = (f32[256,256]{1,0:T(8,128)S(1)}, f32[256,256]{1,0:T(8,128)S(1)}, u32[]{:S(2)}, u32[]{:S(2)}) collective-permute-start(f32[256,256]{1,0:T(8,128)S(1)} %shard_map.97), channel_id=1, source_target_pairs={{0,1},{1,0},{2,3},{3,2},{4,5},{5,4},{6,7},{7,6},{8,9},{9,8},{10,11... | collective-permute-start | bytes 786440 | tf_op jit(solution)/shard_map/ppermute | solution.py:252
  86.9 0.5 shard_map.95
  87.4 0.6 collective-permute-done.5
  88.1 7.7 %collective-permute-start.6 = (bf16[256,256]{1,0:T(8,128)(2,1)S(1)}, bf16[256,256]{1,0:T(8,128)(2,1)S(1)}, u32[]{:S(2)}, u32[]{:S(2)}) collective-permute-start(bf16[256,256]{1,0:T(8,128)(2,1)S(1)} %add_convert_fusion.grad), channel_id=1, source_target_pairs={{8,0},{16,8},{24,16},{32,24},{40,32},{48,40},{56,48},{64,56},{72,6... | collective-permute-start | bytes 393224 | tf_op jit(solution)/shard_map/ppermute | solution.py:247
  95.8 6.3 %collective-permute-start.7 = (bf16[128,256]{1,0:T(8,128)(2,1)S(1)}, bf16[128,256]{1,0:T(8,128)(2,1)S(1)}, u32[]{:S(2)}, u32[]{:S(2)}) collective-permute-start(bf16[128,256]{1,0:T(8,128)(2,1)S(1)} %slice.16), channel_id=1, source_target_pairs={{16,0},{24,8},{32,16},{40,24},{48,32},{56,40},{64,48},{72,56},{80,... | collective-permute-start | bytes 196616 | tf_op jit(solution)/shard_map/ppermute | solution.py:247
  102.1 2.3 %shard_map.99.signed = f32[2,384,256]{2,1,0:T(8,128)S(1)} custom-call(s32[128,128]{1,0:T(8,128)S(1)} %copy-done.11, s32[1]{0:T(128)S(6)} %copy.10.seed, bf16[256,256]{1,0:T(8,128)(2,1)S(1)} %copy-done.3, bf16[256,640]{1,0:T(8,128)(2,1)S(1)} %collective-permute-done.2.near, bf16[128,640]{1,0:T(8,128)(2,1)S(1)} %collective-permute-done.3.far), custom_call_target="tpu_custom_call" | custom-call | flops 100663296 | bytes 1474564 | tf_op jit(solution)/shard_map/pallas_call | solution.py:234
  104.5 0.0 copy-done.6
  104.5 0.0 copy-done.8
  104.5 0.0 copy-done.10
  104.5 1.4 %shard_map.98 = (bf16[256,256]{1,0:T(8,128)(2,1)}, f32[256,256]{1,0:T(8,128)S(1)}, f32[256,256]{1,0:T(8,128)S(1)}) custom-call(f32[2,256,640]{2,1,0:T(8,128)S(1)} %copy-done.6, bf16[256,640]{1,0:T(8,128)(2,1)S(1)} %get-tuple-element.16.message, bf16[256,256]{1,0:T(8,128)(2,1)S(1)} %add_convert_fusion.grad, bf16[640,256]{1,0:T(8,128)(2,1)S(1)} %copy-done.8, ...), custom_call_target="tpu_custom_call" | custom-call | flops 335544320 | bytes 3080192 | tf_op jit(solution)/shard_map/pallas_call | solution.py:234
  105.9 0.0 collective-permute-done.7.grad_far
  105.9 0.0 collective-permute-done.6.grad_near
  105.9 1.7 %shard_map.100 = (bf16[256,256]{1,0:T(8,128)(2,1)}, bf16[256,256]{1,0:T(8,128)(2,1)}) custom-call(f32[2,384,256]{2,1,0:T(8,128)S(1)} %shard_map.99.signed, bf16[256,256]{1,0:T(8,128)(2,1)S(1)} %copy-done.3, bf16[256,256]{1,0:T(8,128)(2,1)S(1)} %copy-done.4, bf16[256,640]{1,0:T(8,128)(2,1)S(1)} %collective-permute-done.2.near, ...), custom_call_target="tpu_custom_call" | custom-call | flops 167772160 | bytes 2523136 | tf_op jit(solution)/shard_map/pallas_call | solution.py:234
  (13 shorter events, 0.1 us)
Async XLA Ops:
  7.2 6.0 %copy-start.3 = (bf16[256,256]{1,0:T(8,128)(2,1)S(1)}, bf16[256,256]{1,0:T(8,128)(2,1)}, u32[]{:S(2)}) copy-start(bf16[256,256]{1,0:T(8,128)(2,1)} %key.5) | copy-start | bytes 393220
  7.2 10.2 %slice-start = ((bf16[256,256]{1,0:T(8,128)(2,1)}), bf16[128,256]{1,0:T(8,128)(2,1)S(1)}, s32[]{:S(2)}) async-start(bf16[256,256]{1,0:T(8,128)(2,1)} %key.5), calls=%async_computation.1 | async-start | bytes 131072 | tf_op jit(solution)/shard_map/slice | solution.py:262
  7.2 10.2 %slice-start.1 = ((bf16[256,256]{1,0:T(8,128)(2,1)}), bf16[128,256]{1,0:T(8,128)(2,1)S(1)}, s32[]{:S(2)}) async-start(bf16[256,256]{1,0:T(8,128)(2,1)} %value.3), calls=%async_computation.2 | async-start | bytes 131072 | tf_op jit(solution)/shard_map/slice | solution.py:262
  7.2 74.2 %all-gather.3.cloned.1.call-start = ((), (), s32[]{:S(2)}) async-start(), calls=%async_computation | async-start | bytes 1310720 | tf_op jit(solution)/shard_map/all_gather | solution.py:259
  7.9 1.6 %copy-start = (bf16[256,4096]{1,0:T(8,128)(2,1)S(1)}, bf16[256,4096]{1,0:T(8,128)(2,1)}, u32[]{:S(2)}) copy-start(bf16[256,4096]{1,0:T(8,128)(2,1)} %weight.3) | copy-start | bytes 6291460
  9.5 3.7 %copy-start.4 = (bf16[256,256]{1,0:T(8,128)(2,1)S(1)}, bf16[256,256]{1,0:T(8,128)(2,1)}, u32[]{:S(2)}) copy-start(bf16[256,256]{1,0:T(8,128)(2,1)} %value.3) | copy-start | bytes 393220
  9.5 29.5 %copy-start.11 = (s32[128,128]{1,0:T(8,128)S(1)}, s32[128,128]{1,0:T(8,128)}, u32[]{:S(2)}) copy-start(s32[128,128]{1,0:T(8,128)} %table.3) | copy-start | bytes 196612
  9.5 29.5 %copy-start.12 = (bf16[256,256]{1,0:T(8,128)(2,1)S(1)}, bf16[256,256]{1,0:T(8,128)(2,1)}, u32[]{:S(2)}) copy-start(bf16[256,256]{1,0:T(8,128)(2,1)} %query.1) | copy-start | bytes 393220
  10.6 70.8 %collective-permute-start.4 = (bf16[256,2048]{1,0:T(8,128)(2,1)}, bf16[256,2048]{1,0:T(8,128)(2,1)}, u32[]{:S(2)}, u32[]{:S(2)}) collective-permute-start(bf16[256,2048]{1,0:T(8,128)(2,1)} %shard_map.96), channel_id=1, source_target_pairs={{0,1},{1,0},{2,3},{3,2},{4,5},{5,4},{6,7},{7,6},{8,9},{9,8},{10,11... | collective-permute-start | bytes 3145736 | tf_op jit(solution)/shard_map/ppermute | solution.py:252
  13.2 73.7 %copy-start.1 = (bf16[256,4096]{1,0:T(8,128)(2,1)S(1)}, bf16[256,4096]{1,0:T(8,128)(2,1)}, u32[]{:S(2)}) copy-start(bf16[256,4096]{1,0:T(8,128)(2,1)} %weight.3) | copy-start | bytes 6291460
  13.2 25.8 %collective-permute-start = (bf16[512,256]{1,0:T(8,128)(2,1)S(1)}, bf16[512,256]{1,0:T(8,128)(2,1)S(1)}, u32[]{:S(2)}, u32[]{:S(2)}) collective-permute-start(bf16[512,256]{1,0:T(8,128)(2,1)S(1)} %pad_maximum_fusion), channel_id=1, source_target_pairs={{0,8},{8,16},{16,24},{24,32},{32,40},{40,48},{48,56},{56,64},{64,7... | collective-permute-start | bytes 786440 | tf_op jit(solution)/shard_map/ppermute | solution.py:247
  17.4 20.9 %collective-permute-start.1 = (bf16[256,256]{1,0:T(8,128)(2,1)S(1)}, bf16[256,256]{1,0:T(8,128)(2,1)S(1)}, u32[]{:S(2)}, u32[]{:S(2)}) collective-permute-start(bf16[256,256]{1,0:T(8,128)(2,1)S(1)} %pad_maximum_fusion.1), channel_id=1, source_target_pairs={{0,16},{8,24},{16,32},{24,40},{32,48},{40,56},{48,64},{56,72},{64,... | collective-permute-start | bytes 393224 | tf_op jit(solution)/shard_map/ppermute | solution.py:247
  42.7 1.1 copy-start.5
  43.8 0.7 copy-start.7
  44.5 36.9 %copy-start.9 = (bf16[640,256]{1,0:T(8,128)(2,1)}, bf16[640,256]{1,0:T(8,128)(2,1)S(1)}, u32[]{:S(2)}) copy-start(bf16[640,256]{1,0:T(8,128)(2,1)S(1)} %get-tuple-element.19.value_win) | copy-start | bytes 983044
  44.5 36.9 %collective-permute-start.2 = (bf16[256,640]{1,0:T(8,128)(2,1)S(1)}, bf16[256,640]{1,0:T(8,128)(2,1)S(1)}, u32[]{:S(2)}, u32[]{:S(2)}) collective-permute-start(bf16[256,640]{1,0:T(8,128)(2,1)S(1)} %get-tuple-element.16.message), channel_id=1, source_target_pairs={{8,0},{16,8},{24,16},{32,24},{40,32},{48,40},{56,48},{64,56},{72,6... | collective-permute-start | bytes 983048 | tf_op jit(solution)/shard_map/ppermute | solution.py:247
  57.0 24.4 %collective-permute-start.3 = (bf16[128,640]{1,0:T(8,128)(2,1)S(1)}, bf16[128,640]{1,0:T(8,128)(2,1)S(1)}, u32[]{:S(2)}, u32[]{:S(2)}) collective-permute-start(bf16[128,640]{1,0:T(8,128)(2,1)S(1)} %slice.14), channel_id=1, source_target_pairs={{16,0},{24,8},{32,16},{40,24},{48,32},{56,40},{64,48},{72,56},{80,... | collective-permute-start | bytes 491528 | tf_op jit(solution)/shard_map/ppermute | solution.py:247
  81.4 1.2 %copy-start.2 = (bf16[1024,512]{1,0:T(8,128)(2,1)S(1)}, bf16[1024,512]{1,0:T(8,128)(2,1)}, u32[]{:S(2)}) copy-start(bf16[1024,512]{1,0:T(8,128)(2,1)} %all-gather.3.cloned.1.call-done) | copy-start | bytes 3145732
  84.4 20.1 %copy-start.6 = (f32[2,256,640]{2,1,0:T(8,128)S(1)}, f32[2,256,640]{2,1,0:T(8,128)}, u32[]{:S(2)}) copy-start(f32[2,256,640]{2,1,0:T(8,128)} %copy-done.5) | copy-start | bytes 3932164
  84.4 20.1 %copy-start.8 = (bf16[640,256]{1,0:T(8,128)(2,1)S(1)}, bf16[640,256]{1,0:T(8,128)(2,1)}, u32[]{:S(2)}) copy-start(bf16[640,256]{1,0:T(8,128)(2,1)} %copy-done.7) | copy-start | bytes 983044
  84.4 20.1 %copy-start.10 = (bf16[640,256]{1,0:T(8,128)(2,1)S(1)}, bf16[640,256]{1,0:T(8,128)(2,1)}, u32[]{:S(2)}) copy-start(bf16[640,256]{1,0:T(8,128)(2,1)} %copy-done.9) | copy-start | bytes 983044
  84.4 3.7 %collective-permute-start.5 = (f32[256,256]{1,0:T(8,128)S(1)}, f32[256,256]{1,0:T(8,128)S(1)}, u32[]{:S(2)}, u32[]{:S(2)}) collective-permute-start(f32[256,256]{1,0:T(8,128)S(1)} %shard_map.97), channel_id=1, source_target_pairs={{0,1},{1,0},{2,3},{3,2},{4,5},{5,4},{6,7},{7,6},{8,9},{9,8},{10,11... | collective-permute-start | bytes 786440 | tf_op jit(solution)/shard_map/ppermute | solution.py:252
  88.1 17.8 %collective-permute-start.6 = (bf16[256,256]{1,0:T(8,128)(2,1)S(1)}, bf16[256,256]{1,0:T(8,128)(2,1)S(1)}, u32[]{:S(2)}, u32[]{:S(2)}) collective-permute-start(bf16[256,256]{1,0:T(8,128)(2,1)S(1)} %add_convert_fusion.grad), channel_id=1, source_target_pairs={{8,0},{16,8},{24,16},{32,24},{40,32},{48,40},{56,48},{64,56},{72,6... | collective-permute-start | bytes 393224 | tf_op jit(solution)/shard_map/ppermute | solution.py:247
  95.8 10.1 %collective-permute-start.7 = (bf16[128,256]{1,0:T(8,128)(2,1)S(1)}, bf16[128,256]{1,0:T(8,128)(2,1)S(1)}, u32[]{:S(2)}, u32[]{:S(2)}) collective-permute-start(bf16[128,256]{1,0:T(8,128)(2,1)S(1)} %slice.16), channel_id=1, source_target_pairs={{16,0},{24,8},{32,16},{40,24},{48,32},{56,40},{64,48},{72,56},{80,... | collective-permute-start | bytes 196616 | tf_op jit(solution)/shard_map/ppermute | solution.py:247
Sparse Core Ops, SparseCore 0:
  10.1 38.6 all-gather.2

commit v3 on v2

v3 whole, which is shorter than its diff:
```python
import jax
import jax.numpy as jnp
from jax import lax
from jax.experimental import pallas as pl
from jax.experimental.pallas import tpu as pltpu
from jax.sharding import PartitionSpec as P

DH = 128
MB = 128
HEADS = 2
ROWS = 256
SLOTS = 5
WIN = SLOTS * MB
FAR = 3 * MB
WIDE = HEADS * DH
EXTRA = 16

drop_level = 6554
keep_scale = 65536.0 / 58982.0
mix_one = 73244475
mix_two = 295559667
mix_three = 668265263
score_scale = DH**-0.5
hidden = -1e30

VMEM = pl.BlockSpec(memory_space=pltpu.VMEM)
HBM = pl.BlockSpec(memory_space=pltpu.MemorySpace.HBM)
SMEM = pl.BlockSpec(memory_space=pltpu.SMEM)


def bf16(value):
    return value.astype(jnp.bfloat16)


def f32(value):
    return value.astype(jnp.float32)


def dot_last(left, right):
    return lax.dot_general(
        left, right, (((1,), (1,)), ((), ())), preferred_element_type=jnp.float32
    )


def dot_first(left, right):
    return lax.dot_general(
        left, right, (((0,), (0,)), ((), ())), preferred_element_type=jnp.float32
    )


def dot(left, right):
    return jnp.dot(left, right, preferred_element_type=jnp.float32)


def bound_of(table, query_block, key_block):
    last = table.shape[0] - 1
    inside = (key_block >= 0) & (query_block <= last)
    kind = table[jnp.minimum(query_block, last), jnp.maximum(key_block, 0)]
    far = jnp.int32(1 << 20)
    bound = jnp.where(kind == 2, far, jnp.where(kind == 1, (query_block - key_block) * MB, -far))
    return jnp.where(inside, bound, -far)


def kept(seed, head, query_block, key_block, query_axis):
    base = query_block * MB * mix_one + key_block * MB * mix_two + head * mix_three + seed
    rows = lax.broadcasted_iota(jnp.int32, (MB, MB), query_axis) * mix_one
    cols = lax.broadcasted_iota(jnp.int32, (MB, MB), 1 - query_axis) * mix_two
    hashed = (rows + cols) + base
    for _ in range(2):
        hashed = hashed ^ lax.shift_right_logical(hashed, jnp.int32(16))
        hashed = hashed * mix_one
    hashed = hashed ^ lax.shift_right_logical(hashed, jnp.int32(16))
    return (hashed & 65535) >= drop_level


def key_minus_query(query_axis):
    return lax.broadcasted_iota(jnp.int32, (MB, MB), 1 - query_axis) - lax.broadcasted_iota(
        jnp.int32, (MB, MB), query_axis
    )


def put_parts(stats, lane, first, column):
    rest = column
    for part in range(3):
        piece = f32(bf16(rest))
        stats = jnp.where(lane == first + part, piece, stats)
        rest = rest - piece
    return stats


def take_parts(stats, first):
    return stats[first : first + 1] + stats[first + 1 : first + 2] + stats[first + 2 : first + 3]


def forward_kernel(
    table, seed, query, key, value, near, far, signed, attended, stats, key_win, value_win
):
    shard = lax.axis_index("blk")
    first_head = lax.axis_index("head") * HEADS
    key_win[0:MB] = far[0:MB]
    key_win[MB:FAR] = near[0:ROWS]
    key_win[FAR:] = key[...]
    value_win[0:MB] = far[MB:]
    value_win[MB:FAR] = near[ROWS:]
    value_win[FAR:] = value[...]
    ahead = key_minus_query(0)
    lane = lax.broadcasted_iota(jnp.int32, (MB, MB), 1)
    for block in range(2):
        rows = pl.ds(block * MB, MB)
        query_block = shard * 2 + block
        parts = jnp.zeros((MB, MB), jnp.float32)
        for head in range(HEADS):
            cols = pl.ds(head * DH, DH)
            scores = dot_last(query[rows, cols], key_win[:, cols])
            tiles = []
            for slot in range(block, SLOTS):
                bound = bound_of(table, query_block, shard * 2 - 3 + slot)
                tile = scores[:, slot * MB : (slot + 1) * MB] * score_scale
                tiles.append(jnp.where(ahead <= bound, tile, hidden))
            top = tiles[0]
            for tile in tiles[1:]:
                top = jnp.maximum(top, tile)
            top = jnp.max(top, axis=1, keepdims=True)
            tiles = [jnp.exp(tile - top) for tile in tiles]
            total = tiles[0]
            for tile in tiles[1:]:
                total = total + tile
            total = jnp.sum(total, axis=1, keepdims=True)
            inverse = 1.0 / total
            log_total = top + jnp.log(total)
            drops = []
            for slot in range(block, SLOTS):
                prob = tiles[slot - block] * inverse
                keep = kept(seed[0], first_head + head, query_block, shard * 2 - 3 + slot, 0)
                signed[head, rows, slot * MB : (slot + 1) * MB] = jnp.where(keep, prob, -prob)
                drops.append(bf16(jnp.where(keep, prob * keep_scale, 0.0)))
            if block > 0:
                signed[head, rows, 0:MB] = jnp.zeros((MB, MB), jnp.float32)
            mixed = dot(jnp.concatenate(drops, axis=1), value_win[block * MB :, cols])
            attended[rows, cols] = bf16(mixed)
            parts = put_parts(parts, lane, 3 * head, log_total)
        stats[rows] = parts


def later_kernel(table, seed, key, near, far, scores, keeps):
    shard = lax.axis_index("blk")
    first_head = lax.axis_index("head") * HEADS
    ahead = key_minus_query(1)
    for block in range(3):
        source, first = (near, block * MB) if block < 2 else (far, 0)
        across = slice(block * MB, (block + 1) * MB)
        query_block = shard * 2 + 2 + block
        for head in range(HEADS):
            cols = pl.ds(head * DH, DH)
            tiles = dot_last(key[:, cols], source[first : first + MB, cols]) * score_scale
            for slot in range(2):
                down = slice(slot * MB, (slot + 1) * MB)
                bound = bound_of(table, query_block, shard * 2 + slot)
                scores[head, down, across] = jnp.where(ahead <= bound, tiles[down], hidden)
                keep = kept(seed[0], first_head + head, query_block, shard * 2 + slot, 1)
                keeps[head, down, across] = jnp.where(keep, jnp.float32(keep_scale), 0.0)


def cut_kernel(weight, out):
    core = lax.rem(lax.axis_index("head"), 2)
    parts = lax.axis_size("head") // 2
    width = out.shape[1] // parts
    for part in range(parts):
        first = pl.multiple_of((part * 2 + 1 - core) * width, width)
        out[:, part * width : (part + 1) * width] = weight[:, pl.ds(first, width)]


def project_other_kernel(gathered, weight, out, held, theirs, sems, weight_sem):
    parts, _, width = gathered.shape
    copies = [
        pltpu.make_async_copy(gathered.at[part], held.at[part], sems.at[part])
        for part in range(parts)
    ]
    whole = pltpu.make_async_copy(weight, theirs, weight_sem)
    whole.start()
    for copy in copies:
        copy.start()
    whole.wait()
    total = None
    for part in range(parts):
        copies[part].wait()
        term = dot_last(held[part], theirs[:, part * width : (part + 1) * width])
        total = term if total is None else total + term
    out[...] = total


def project_own_kernel(gathered, weight, out):
    parts, _, width = gathered.shape
    core = lax.rem(lax.axis_index("head"), 2)
    total = None
    for part in range(parts):
        first = pl.multiple_of((part * 2 + core) * width, width)
        term = dot_last(gathered[part], weight[:, pl.ds(first, width)])
        total = term if total is None else total + term
    out[...] = total


def rows_kernel(own, received, attended, stats, near, far):
    grad = bf16(own[...] + received[...])
    near[0:ROWS] = grad
    far[0:MB] = grad[0:MB]
    lane = lax.broadcasted_iota(jnp.int32, (MB, MB), 1)
    for block in range(2):
        rows = slice(block * MB, (block + 1) * MB)
        parts = stats[rows]
        for head in range(HEADS):
            cols = slice(head * DH, (head + 1) * DH)
            row_dot = jnp.sum(
                f32(grad[rows, cols]) * f32(attended[rows, cols]), axis=1, keepdims=True
            )
            parts = put_parts(parts, lane, 6 + 3 * head, row_dot)
        across = bf16(parts.T[0:EXTRA])
        near[ROWS:, rows] = across
        far[MB:, rows] = across


def own_kernel(
    signed, attended, query, grad, key_win, value_win, grad_query, key_part, value_part
):
    for head in range(HEADS):
        cols = pl.ds(head * DH, DH)
        grad_head = grad[0:ROWS, cols]
        row_dot = jnp.sum(f32(grad_head) * f32(attended[:, cols]), axis=1, keepdims=True)
        grad_prob = dot_last(grad_head, value_win[:, cols])
        probs = signed[head]
        scaled = jnp.where(probs > 0.0, grad_prob * keep_scale, 0.0)
        dscore = bf16(jnp.abs(probs) * (scaled - row_dot))
        dropped = bf16(jnp.maximum(probs[:, FAR:], 0.0) * keep_scale)
        grad_query[:, cols] = bf16(dot(dscore, key_win[:, cols]) * score_scale)
        key_part[:, cols] = dot_first(dscore[:, FAR:], query[:, cols])
        value_part[:, cols] = dot_first(dropped, grad_head)


def finish_kernel(
    scores, keeps, value, near_query, far_query, near_grad, far_grad, key_part, value_part,
    grad_key, grad_value,
):
    for head in range(HEADS):
        cols = pl.ds(head * DH, DH)
        key_sum = key_part[:, cols]
        value_sum = value_part[:, cols]
        for queries, grads, first, count in (
            (near_query, near_grad, 0, ROWS), (far_query, far_grad, ROWS, MB)
        ):
            across = slice(first, first + count)
            grad_head = grads[0:count, cols]
            stats = f32(grads[count:, 0:count])
            prob = jnp.exp(scores[head, :, across] - take_parts(stats, 3 * head))
            keep = keeps[head, :, across]
            grad_prob = dot_last(value[:, cols], grad_head)
            dscore = bf16(prob * (grad_prob * keep - take_parts(stats, 6 + 3 * head)))
            key_sum = key_sum + dot(dscore, queries[:, cols])
            value_sum = value_sum + dot(bf16(prob * keep), grad_head)
        grad_key[:, cols] = bf16(key_sum * score_scale)
        grad_value[:, cols] = bf16(value_sum)


def call(kernel, specs, outs, flops, *args, scratch=(), grant=16):
    shapes = [jax.ShapeDtypeStruct(shape, dtype) for shape, dtype in outs]
    moved = sum(a.size * a.dtype.itemsize for a in args)
    moved += sum(s.size * s.dtype.itemsize for s in shapes)
    return pl.pallas_call(
        kernel,
        out_shape=shapes,
        in_specs=specs,
        out_specs=[VMEM] * len(shapes),
        scratch_shapes=scratch,
        compiler_params=pltpu.CompilerParams(vmem_limit_bytes=grant << 20),
        cost_estimate=pl.CostEstimate(flops=flops, bytes_accessed=moved, transcendentals=0),
    )(*args)


def shifted(value, steps):
    count = lax.axis_size("blk")
    pairs = [(source, source + steps) for source in range(count) if 0 <= source + steps < count]
    return lax.ppermute(value, "blk", pairs)


def other_core(value):
    count = lax.axis_size("head")
    return lax.ppermute(value, "head", [(source, source ^ 1) for source in range(count)])


def on_device(query_rows, key_rows, value_rows, grad_out, out_weight, mask_types, drop_seed):
    half, full = jnp.bfloat16, jnp.float32
    count = lax.axis_size("head")
    parts, width = count // 2, grad_out.shape[1]
    groups = [list(range(first, count, 2)) for first in range(2)]
    gathered = lax.all_gather(grad_out, "head", axis=0, axis_index_groups=groups)
    near_keys = shifted(jnp.concatenate((key_rows, value_rows)), 1)
    far_keys = shifted(jnp.concatenate((key_rows[MB:], value_rows[MB:])), 2)
    near_query = shifted(query_rows, -1)
    far_query = shifted(query_rows[:MB], -2)
    (theirs,) = call(cut_kernel, [VMEM], [((WIDE, parts * width), half)], 0, out_weight)
    other_weight = other_core(theirs)
    tile = 2 * MB * MB * DH
    signed, attended, stats, key_win, value_win = call(
        forward_kernel,
        [SMEM, SMEM] + [VMEM] * 5,
        [
            ((HEADS, ROWS, WIN), full),
            ((ROWS, WIDE), half),
            ((ROWS, MB), full),
            ((WIN, WIDE), half),
            ((WIN, WIDE), half),
        ],
        40 * tile,
        mask_types, drop_seed, query_rows, key_rows, value_rows, near_keys, far_keys,
    )
    scores, keeps = call(
        later_kernel,
        [SMEM, SMEM] + [VMEM] * 3,
        [((HEADS, ROWS, FAR), full), ((HEADS, ROWS, FAR), full)],
        24 * tile,
        mask_types, drop_seed, key_rows, near_query, far_query,
    )
    gathered, attended, scores = lax.optimization_barrier((gathered, attended, scores))
    flops = 2 * ROWS * WIDE * width * parts
    (sent,) = call(
        project_other_kernel,
        [HBM] * 2,
        [((ROWS, WIDE), full)],
        flops,
        gathered, other_weight,
        scratch=[
            pltpu.VMEM((parts, ROWS, width), half),
            pltpu.VMEM((WIDE, parts * width), half),
            pltpu.SemaphoreType.DMA((parts,)),
            pltpu.SemaphoreType.DMA,
        ],
        grant=56,
    )
    received = other_core(sent)
    (own,) = call(
        project_own_kernel, [VMEM] * 2, [((ROWS, WIDE), full)], flops, gathered, out_weight
    )
    near_rows, far_rows = call(
        rows_kernel,
        [VMEM] * 4,
        [((ROWS + EXTRA, WIDE), half), ((MB + EXTRA, WIDE), half)],
        0,
        own, received, attended, stats,
    )
    near_grad = shifted(near_rows, -1)
    far_grad = shifted(far_rows, -2)
    grad_query, key_part, value_part = call(
        own_kernel,
        [VMEM] * 6,
        [((ROWS, WIDE), half), ((ROWS, WIDE), full), ((ROWS, WIDE), full)],
        80 * tile,
        signed, attended, query_rows, near_rows, key_win, value_win,
    )
    grad_key, grad_value = call(
        finish_kernel,
        [VMEM] * 9,
        [((ROWS, WIDE), half), ((ROWS, WIDE), half)],
        40 * tile,
        scores, keeps, value_rows, near_query, far_query, near_grad, far_grad, key_part, value_part,
    )
    return (grad_query, grad_key, grad_value)


def solution(mesh):
    split = P("blk", "head")
    return jax.shard_map(
        on_device,
        mesh=mesh,
        in_specs=(split, split, split, split, P("head", None), P(), P()),
        out_specs=(split, split, split),
        check_vma=False,
    )
```

time: 115 us -> 95 us (0.83)
  the two profiles are of different devices: /device:TPU:15 before, /device:TPU:6 now
where the time goes in v3:
time: 95 us; the launch traced here: 94.4 us
  starting transfers between devices  50.7 us (53%)
  between operations  15 us (16%)
  Pallas kernels  13.8 us (15%)
  waiting for transfers between devices  8.7 us (9%)
  local copies, waits for them, and re-layouts  6.21 us (7%)
    ppermute x6, starting transfers between devices, shifted(): return lax.ppermute(value, 'blk', pairs)  46.7 us
    pallas_call x8, Pallas kernels, call(): pl.pallas_call(kernel, out_shape=shapes, in_specs=specs, out_specs=[VMEM]...  13.8 us
    ppermute x6, waiting for transfers between devices, shifted(): return lax.ppermute(value, 'blk', pairs)  6.85 us
    unnamed x48, local copies, waits for them, and re-layouts  6.2 us
    ppermute x2, starting transfers between devices, other_core(): lax.ppermute(value, 'head', [(source, source ^ 1) for source in range(cou...  3.96 us
  transfers between devices with their start and end apart: 9, of which 3 were waited for; matrix products, arithmetic and copies ran while one was open for 0% of the time, Pallas kernels for 9%

profile of v3, /device:TPU:6, one launch (start us, length us, event | category | flops | bytes accessed | tf_op | source)
XLA Modules:
  0.0 94.4 jit_solution(13812935336196660524)
XLA Ops:
  7.2 0.0 copy-start.3
  7.2 0.0 slice-start
  7.2 0.0 slice-start.1
  7.2 0.0 all-gather.3.cloned.1.call-start
  7.2 0.7 all-gather.3.cloned.1.call-update
  7.9 0.0 copy-start
  7.9 1.6 %copy-done = bf16[256,4096]{1,0:T(8,128)(2,1)S(1)} copy-done((bf16[256,4096]{1,0:T(8,128)(2,1)S(1)}, bf16[256,4096]{1,0:T(8,128)(2,1)}, u32[]{:S(2)}) %copy-start) | copy-done | bytes 2097176
  9.5 1.1 %shard_map.97 = bf16[256,2048]{1,0:T(8,128)(2,1)} custom-call(bf16[256,4096]{1,0:T(8,128)(2,1)S(1)} %copy-done), custom_call_target="tpu_custom_call" | custom-call | bytes 3145728 | tf_op jit(solution)/shard_map/pallas_call | solution.py:267
  10.6 1.9 %collective-permute-start.4 = (bf16[256,2048]{1,0:T(8,128)(2,1)}, bf16[256,2048]{1,0:T(8,128)(2,1)}, u32[]{:S(2)}, u32[]{:S(2)}) collective-permute-start(bf16[256,2048]{1,0:T(8,128)(2,1)} %shard_map.97), channel_id=1, source_target_pairs={{0,1},{1,0},{2,3},{3,2},{4,5},{5,4},{6,7},{7,6},{8,9},{9,8},{10,11... | collective-permute-start | bytes 3145736 | tf_op jit(solution)/shard_map/ppermute | solution.py:286
  12.5 0.0 copy-done.3
  12.5 0.0 copy-done.4
  12.6 4.3 %collective-permute-start = (bf16[512,256]{1,0:T(8,128)(2,1)S(1)}, bf16[512,256]{1,0:T(8,128)(2,1)S(1)}, u32[]{:S(2)}, u32[]{:S(2)}) collective-permute-start(bf16[512,256]{1,0:T(8,128)(2,1)S(1)} %pad_maximum_fusion), channel_id=1, source_target_pairs={{0,8},{8,16},{16,24},{24,32},{32,40},{40,48},{48,56},{56,64},{64,7... | collective-permute-start | bytes 786440 | tf_op jit(solution)/shard_map/ppermute | solution.py:281
  16.9 0.0 copy-done.5
  16.9 14.1 %collective-permute-start.2 = (bf16[256,256]{1,0:T(8,128)(2,1)S(1)}, bf16[256,256]{1,0:T(8,128)(2,1)S(1)}, u32[]{:S(2)}, u32[]{:S(2)}) collective-permute-start(bf16[256,256]{1,0:T(8,128)(2,1)S(1)} %copy-done.5), channel_id=1, source_target_pairs={{8,0},{16,8},{24,16},{32,24},{40,32},{48,40},{56,48},{64,56},{72,6... | collective-permute-start | bytes 393224 | tf_op jit(solution)/shard_map/ppermute | solution.py:281
  31.0 0.0 copy-start.1
  31.0 0.0 slice-done
  31.0 2.1 %collective-permute-start.1 = (bf16[256,256]{1,0:T(8,128)(2,1)S(1)}, bf16[256,256]{1,0:T(8,128)(2,1)S(1)}, u32[]{:S(2)}, u32[]{:S(2)}) collective-permute-start(bf16[256,256]{1,0:T(8,128)(2,1)S(1)} %pad_maximum_fusion.1), channel_id=1, source_target_pairs={{0,16},{8,24},{16,32},{24,40},{32,48},{40,56},{48,64},{56,72},{64,... | collective-permute-start | bytes 393224 | tf_op jit(solution)/shard_map/ppermute | solution.py:281
  33.1 11.7 %collective-permute-start.3 = (bf16[128,256]{1,0:T(8,128)(2,1)S(1)}, bf16[128,256]{1,0:T(8,128)(2,1)S(1)}, u32[]{:S(2)}, u32[]{:S(2)}) collective-permute-start(bf16[128,256]{1,0:T(8,128)(2,1)S(1)} %slice.11), channel_id=1, source_target_pairs={{16,0},{24,8},{32,16},{40,24},{48,32},{56,40},{64,48},{72,56},{80,... | collective-permute-start | bytes 196616 | tf_op jit(solution)/shard_map/ppermute | solution.py:281
  45.5 3.2 %collective-permute-done.3.far.far_query = bf16[128,256]{1,0:T(8,128)(2,1)S(1)} collective-permute-done((bf16[128,256]{1,0:T(8,128)(2,1)S(1)}, bf16[128,256]{1,0:T(8,128)(2,1)S(1)}, u32[]{:S(2)}, u32[]{:S(2)}) %collective-permute-start.3) | collective-permute-done | bytes 65568 | tf_op jit(solution)/shard_map/ppermute | solution.py:281
  48.7 0.0 collective-permute-done.2.near.near_query
  48.7 2.2 %shard_map.95 = (f32[2,256,384]{2,1,0:T(8,128)S(1)}, f32[2,256,384]{2,1,0:T(8,128)S(1)}) custom-call(s32[128,128]{1,0:T(8,128)S(1)} %copy-done.19, s32[1]{0:T(128)S(6)} %copy.10.seed, bf16[256,256]{1,0:T(8,128)(2,1)S(1)} %copy-done.4, bf16[256,256]{1,0:T(8,128)(2,1)S(1)} %collective-permute-done.2.near.near_query, ...), custom_call_target="tpu_custom_call" | custom-call | flops 100663296 | bytes 1966084 | tf_op jit(solution)/shard_map/pallas_call | solution.py:267
  50.9 0.9 copy-done.7
  51.8 0.9 copy-done.9
  52.7 0.0 collective-permute-done.1.far
  52.7 0.0 collective-permute-done.near
  52.7 0.0 copy-done.20
  52.7 3.6 %shard_map.94 = (f32[2,256,640]{2,1,0:T(8,128)S(1)}, bf16[256,256]{1,0:T(8,128)(2,1)S(1)}, f32[256,128]{1,0:T(8,128)S(1)}, bf16[640,256]{1,0:T(8,128)(2,1)S(1)}, bf16[640,256]{1,0:T(8,128)(2,1)S(1)}) custom-call(s32[128,128]{1,0:T(8,128)S(1)} %copy-done.19, s32[1]{0:T(128)S(6)} %copy.10.seed, bf16[256,256]{1,0:T(8,128)(2,1)S(1)} %copy-done.5, ...), custom_call_target="tpu_custom_call" | custom-call | flops 167772160 | bytes 3080196 | tf_op jit(solution)/shard_map/pallas_call | solution.py:267
  56.3 0.0 copy-start.13
  56.4 0.7 copy-done.13
  57.0 0.7 copy-done.15
  57.7 0.7 copy-done.17
  58.5 0.7 copy-done.22
  59.1 0.0 collective-permute-done.4.weight
  59.1 3.3 %shard_map.98 = f32[256,256]{1,0:T(8,128)} custom-call(bf16[4,256,512]{2,1,0:T(8,128)(2,1)} %bitcast.1, bf16[256,2048]{1,0:T(8,128)(2,1)} %collective-permute-done.4.weight), custom_call_target="tpu_custom_call" | custom-call | flops 268435456 | bytes 2359296 | tf_op jit(solution)/shard_map/pallas_call | solution.py:267
  62.5 0.0 copy-start.14
  62.5 0.0 copy-start.23
  62.5 0.0 copy-start.6
  62.5 2.1 %collective-permute-start.5 = (f32[256,256]{1,0:T(8,128)}, f32[256,256]{1,0:T(8,128)S(1)}, u32[]{:S(2)}, u32[]{:S(2)}) collective-permute-start(f32[256,256]{1,0:T(8,128)} %shard_map.98), channel_id=1, source_target_pairs={{0,1},{1,0},{2,3},{3,2},{4,5},{5,4},{6,7},{7,6},{8,9},{9,8},{10,11... | collective-permute-start | bytes 786440 | tf_op jit(solution)/shard_map/ppermute | solution.py:286
  64.6 0.5 shard_map.96.own
  65.1 1.2 %collective-permute-done.5.received = f32[256,256]{1,0:T(8,128)S(1)} collective-permute-done((f32[256,256]{1,0:T(8,128)}, f32[256,256]{1,0:T(8,128)S(1)}, u32[]{:S(2)}, u32[]{:S(2)}) %collective-permute-start.5) | collective-permute-done | bytes 262176 | tf_op jit(solution)/shard_map/ppermute | solution.py:286
  66.3 0.0 copy-done.23
  66.3 0.2 shard_map.99
  66.5 7.9 %collective-permute-start.6 = (bf16[272,256]{1,0:T(8,128)(2,1)S(1)}, bf16[272,256]{1,0:T(8,128)(2,1)S(1)}, u32[]{:S(2)}, u32[]{:S(2)}) collective-permute-start(bf16[272,256]{1,0:T(8,128)(2,1)S(1)} %get-tuple-element.26.grad), channel_id=1, source_target_pairs={{8,0},{16,8},{24,16},{32,24},{40,32},{48,40},{56,48},{64,56},{72,6... | collective-permute-start | bytes 417800 | tf_op jit(solution)/shard_map/ppermute | solution.py:281
  74.4 6.6 %collective-permute-start.7 = (bf16[144,256]{1,0:T(8,128)(2,1)S(1)}, bf16[144,256]{1,0:T(8,128)(2,1)S(1)}, u32[]{:S(2)}, u32[]{:S(2)}) collective-permute-start(bf16[144,256]{1,0:T(8,128)(2,1)S(1)} %get-tuple-element.32), channel_id=1, source_target_pairs={{16,0},{24,8},{32,16},{40,24},{48,32},{56,40},{64,48},{72,56},{80,... | collective-permute-start | bytes 221192 | tf_op jit(solution)/shard_map/ppermute | solution.py:281
  81.0 1.4 %shard_map.100 = (bf16[256,256]{1,0:T(8,128)(2,1)}, f32[256,256]{1,0:T(8,128)S(1)}, f32[256,256]{1,0:T(8,128)S(1)}) custom-call(f32[2,256,640]{2,1,0:T(8,128)S(1)} %get-tuple-element.20.signed, bf16[256,256]{1,0:T(8,128)(2,1)S(1)} %copy-done.14, bf16[256,256]{1,0:T(8,128)(2,1)S(1)} %copy-done.6, bf16[272,256]{1,0:T(8,128)(2,1)S(1)} %get-tuple-element.26.grad, ...), custom_call_target="tpu_custom_call" | custom-call | flops 335544320 | bytes 3022848 | tf_op jit(solution)/shard_map/pallas_call | solution.py:267
  82.5 3.6 %collective-permute-done.7.far_grad = bf16[144,256]{1,0:T(8,128)(2,1)S(1)} collective-permute-done((bf16[144,256]{1,0:T(8,128)(2,1)S(1)}, bf16[144,256]{1,0:T(8,128)(2,1)S(1)}, u32[]{:S(2)}, u32[]{:S(2)}) %collective-permute-start.7) | collective-permute-done | bytes 73760 | tf_op jit(solution)/shard_map/ppermute | solution.py:281
  86.1 0.0 collective-permute-done.6.near_grad
  86.1 1.5 %shard_map.101 = (bf16[256,256]{1,0:T(8,128)(2,1)}, bf16[256,256]{1,0:T(8,128)(2,1)}) custom-call(f32[2,256,384]{2,1,0:T(8,128)S(1)} %copy-done.8, f32[2,256,384]{2,1,0:T(8,128)S(1)} %copy-done.10, bf16[256,256]{1,0:T(8,128)(2,1)S(1)} %copy-done.3, bf16[256,256]{1,0:T(8,128)(2,1)S(1)} %copy-done.12, bf16[128,256]{1,0:T(8,128)(2,1)S(1)} %copy-done.21, ...), custom_call_target="tpu_custom_call" | custom-call | flops 167772160 | bytes 2899968 | tf_op jit(solution)/shard_map/pallas_call | solution.py:267
  (34 shorter events, 0.1 us)
Async XLA Ops:
  7.2 5.4 %copy-start.3 = (bf16[256,256]{1,0:T(8,128)(2,1)S(1)}, bf16[256,256]{1,0:T(8,128)(2,1)}, u32[]{:S(2)}) copy-start(bf16[256,256]{1,0:T(8,128)(2,1)} %value.3) | copy-start | bytes 393220
  7.2 23.8 %slice-start = ((bf16[256,256]{1,0:T(8,128)(2,1)}), bf16[128,256]{1,0:T(8,128)(2,1)S(1)}, s32[]{:S(2)}) async-start(bf16[256,256]{1,0:T(8,128)(2,1)} %value.3), calls=%async_computation.1 | async-start | bytes 131072 | tf_op jit(solution)/shard_map/slice | solution.py:296
  7.2 23.8 %slice-start.1 = ((bf16[256,256]{1,0:T(8,128)(2,1)}), bf16[128,256]{1,0:T(8,128)(2,1)S(1)}, s32[]{:S(2)}) async-start(bf16[256,256]{1,0:T(8,128)(2,1)} %key.3), calls=%async_computation.2 | async-start | bytes 131072 | tf_op jit(solution)/shard_map/slice | solution.py:296
  7.2 51.9 %all-gather.3.cloned.1.call-start = ((), (), s32[]{:S(2)}) async-start(), calls=%async_computation | async-start | bytes 1310720 | tf_op jit(solution)/shard_map/all_gather | solution.py:294
  7.9 1.6 %copy-start = (bf16[256,4096]{1,0:T(8,128)(2,1)S(1)}, bf16[256,4096]{1,0:T(8,128)(2,1)}, u32[]{:S(2)}) copy-start(bf16[256,4096]{1,0:T(8,128)(2,1)} %weight.3) | copy-start | bytes 6291460
  9.5 3.0 %copy-start.4 = (bf16[256,256]{1,0:T(8,128)(2,1)S(1)}, bf16[256,256]{1,0:T(8,128)(2,1)}, u32[]{:S(2)}) copy-start(bf16[256,256]{1,0:T(8,128)(2,1)} %key.3) | copy-start | bytes 393220
  9.5 7.3 %copy-start.5 = (bf16[256,256]{1,0:T(8,128)(2,1)S(1)}, bf16[256,256]{1,0:T(8,128)(2,1)}, u32[]{:S(2)}) copy-start(bf16[256,256]{1,0:T(8,128)(2,1)} %query.3) | copy-start | bytes 393220
  9.5 39.2 %copy-start.19 = (s32[128,128]{1,0:T(8,128)S(1)}, s32[128,128]{1,0:T(8,128)}, u32[]{:S(2)}) copy-start(s32[128,128]{1,0:T(8,128)} %table.3) | copy-start | bytes 196612
  10.6 48.5 %collective-permute-start.4 = (bf16[256,2048]{1,0:T(8,128)(2,1)}, bf16[256,2048]{1,0:T(8,128)(2,1)}, u32[]{:S(2)}, u32[]{:S(2)}) collective-permute-start(bf16[256,2048]{1,0:T(8,128)(2,1)} %shard_map.97), channel_id=1, source_target_pairs={{0,1},{1,0},{2,3},{3,2},{4,5},{5,4},{6,7},{7,6},{8,9},{9,8},{10,11... | collective-permute-start | bytes 3145736 | tf_op jit(solution)/shard_map/ppermute | solution.py:286
  12.6 40.1 %collective-permute-start = (bf16[512,256]{1,0:T(8,128)(2,1)S(1)}, bf16[512,256]{1,0:T(8,128)(2,1)S(1)}, u32[]{:S(2)}, u32[]{:S(2)}) collective-permute-start(bf16[512,256]{1,0:T(8,128)(2,1)S(1)} %pad_maximum_fusion), channel_id=1, source_target_pairs={{0,8},{8,16},{16,24},{24,32},{32,40},{40,48},{48,56},{56,64},{64,7... | collective-permute-start | bytes 786440 | tf_op jit(solution)/shard_map/ppermute | solution.py:281
  16.9 31.9 %collective-permute-start.2 = (bf16[256,256]{1,0:T(8,128)(2,1)S(1)}, bf16[256,256]{1,0:T(8,128)(2,1)S(1)}, u32[]{:S(2)}, u32[]{:S(2)}) collective-permute-start(bf16[256,256]{1,0:T(8,128)(2,1)S(1)} %copy-done.5), channel_id=1, source_target_pairs={{8,0},{16,8},{24,16},{32,24},{40,32},{48,40},{56,48},{64,56},{72,6... | collective-permute-start | bytes 393224 | tf_op jit(solution)/shard_map/ppermute | solution.py:281
  31.0 33.6 %copy-start.1 = (bf16[256,4096]{1,0:T(8,128)(2,1)S(1)}, bf16[256,4096]{1,0:T(8,128)(2,1)}, u32[]{:S(2)}) copy-start(bf16[256,4096]{1,0:T(8,128)(2,1)} %weight.3) | copy-start | bytes 6291460
  31.0 21.7 %collective-permute-start.1 = (bf16[256,256]{1,0:T(8,128)(2,1)S(1)}, bf16[256,256]{1,0:T(8,128)(2,1)S(1)}, u32[]{:S(2)}, u32[]{:S(2)}) collective-permute-start(bf16[256,256]{1,0:T(8,128)(2,1)S(1)} %pad_maximum_fusion.1), channel_id=1, source_target_pairs={{0,16},{8,24},{16,32},{24,40},{32,48},{40,56},{48,64},{56,72},{64,... | collective-permute-start | bytes 393224 | tf_op jit(solution)/shard_map/ppermute | solution.py:281
  33.1 15.6 %collective-permute-start.3 = (bf16[128,256]{1,0:T(8,128)(2,1)S(1)}, bf16[128,256]{1,0:T(8,128)(2,1)S(1)}, u32[]{:S(2)}, u32[]{:S(2)}) collective-permute-start(bf16[128,256]{1,0:T(8,128)(2,1)S(1)} %slice.11), channel_id=1, source_target_pairs={{16,0},{24,8},{32,16},{40,24},{48,32},{56,40},{64,48},{72,56},{80,... | collective-permute-start | bytes 196616 | tf_op jit(solution)/shard_map/ppermute | solution.py:281
  48.7 4.0 %copy-start.20 = (bf16[128,256]{1,0:T(8,128)(2,1)}, bf16[128,256]{1,0:T(8,128)(2,1)S(1)}, u32[]{:S(2)}) copy-start(bf16[128,256]{1,0:T(8,128)(2,1)S(1)} %collective-permute-done.3.far.far_query) | copy-start | bytes 196612
  48.7 4.0 %copy-start.11 = (bf16[256,256]{1,0:T(8,128)(2,1)}, bf16[256,256]{1,0:T(8,128)(2,1)S(1)}, u32[]{:S(2)}) copy-start(bf16[256,256]{1,0:T(8,128)(2,1)S(1)} %collective-permute-done.2.near.near_query) | copy-start | bytes 393220
  50.9 0.9 copy-start.7
  51.8 0.9 copy-start.9
  56.3 0.7 copy-start.13
  57.0 0.7 copy-start.15
  57.7 0.7 copy-start.17
  58.5 0.7 copy-start.22
  59.1 5.5 %copy-start.2 = (bf16[1024,512]{1,0:T(8,128)(2,1)S(1)}, bf16[1024,512]{1,0:T(8,128)(2,1)}, u32[]{:S(2)}) copy-start(bf16[1024,512]{1,0:T(8,128)(2,1)} %all-gather.3.cloned.1.call-done) | copy-start | bytes 3145732
  62.5 3.8 %copy-start.14 = (bf16[256,256]{1,0:T(8,128)(2,1)S(1)}, bf16[256,256]{1,0:T(8,128)(2,1)}, u32[]{:S(2)}) copy-start(bf16[256,256]{1,0:T(8,128)(2,1)} %copy-done.13) | copy-start | bytes 393220
  62.5 3.8 %copy-start.23 = (f32[256,128]{1,0:T(8,128)S(1)}, f32[256,128]{1,0:T(8,128)}, u32[]{:S(2)}) copy-start(f32[256,128]{1,0:T(8,128)} %copy-done.22) | copy-start | bytes 393220
  62.5 18.5 %copy-start.6 = (bf16[256,256]{1,0:T(8,128)(2,1)S(1)}, bf16[256,256]{1,0:T(8,128)(2,1)}, u32[]{:S(2)}) copy-start(bf16[256,256]{1,0:T(8,128)(2,1)} %query.3) | copy-start | bytes 393220
  62.5 18.5 %copy-start.16 = (bf16[640,256]{1,0:T(8,128)(2,1)S(1)}, bf16[640,256]{1,0:T(8,128)(2,1)}, u32[]{:S(2)}) copy-start(bf16[640,256]{1,0:T(8,128)(2,1)} %copy-done.15) | copy-start | bytes 983044
  62.5 18.5 %copy-start.18 = (bf16[640,256]{1,0:T(8,128)(2,1)S(1)}, bf16[640,256]{1,0:T(8,128)(2,1)}, u32[]{:S(2)}) copy-start(bf16[640,256]{1,0:T(8,128)(2,1)} %copy-done.17) | copy-start | bytes 983044
  62.5 3.8 %collective-permute-start.5 = (f32[256,256]{1,0:T(8,128)}, f32[256,256]{1,0:T(8,128)S(1)}, u32[]{:S(2)}, u32[]{:S(2)}) collective-permute-start(f32[256,256]{1,0:T(8,128)} %shard_map.98), channel_id=1, source_target_pairs={{0,1},{1,0},{2,3},{3,2},{4,5},{5,4},{6,7},{7,6},{8,9},{9,8},{10,11... | collective-permute-start | bytes 786440 | tf_op jit(solution)/shard_map/ppermute | solution.py:286
  65.1 21.0 %copy-start.8 = (f32[2,256,384]{2,1,0:T(8,128)S(1)}, f32[2,256,384]{2,1,0:T(8,128)}, u32[]{:S(2)}) copy-start(f32[2,256,384]{2,1,0:T(8,128)} %copy-done.7) | copy-start | bytes 2359300
  65.1 21.0 %copy-start.10 = (f32[2,256,384]{2,1,0:T(8,128)S(1)}, f32[2,256,384]{2,1,0:T(8,128)}, u32[]{:S(2)}) copy-start(f32[2,256,384]{2,1,0:T(8,128)} %copy-done.9) | copy-start | bytes 2359300
  65.1 21.0 %copy-start.12 = (bf16[256,256]{1,0:T(8,128)(2,1)S(1)}, bf16[256,256]{1,0:T(8,128)(2,1)}, u32[]{:S(2)}) copy-start(bf16[256,256]{1,0:T(8,128)(2,1)} %copy-done.11) | copy-start | bytes 393220
  65.1 21.0 %copy-start.21 = (bf16[128,256]{1,0:T(8,128)(2,1)S(1)}, bf16[128,256]{1,0:T(8,128)(2,1)}, u32[]{:S(2)}) copy-start(bf16[128,256]{1,0:T(8,128)(2,1)} %copy-done.20) | copy-start | bytes 196612
  66.5 19.6 %collective-permute-start.6 = (bf16[272,256]{1,0:T(8,128)(2,1)S(1)}, bf16[272,256]{1,0:T(8,128)(2,1)S(1)}, u32[]{:S(2)}, u32[]{:S(2)}) collective-permute-start(bf16[272,256]{1,0:T(8,128)(2,1)S(1)} %get-tuple-element.26.grad), channel_id=1, source_target_pairs={{8,0},{16,8},{24,16},{32,24},{40,32},{48,40},{56,48},{64,56},{72,6... | collective-permute-start | bytes 417800 | tf_op jit(solution)/shard_map/ppermute | solution.py:281
  74.4 11.7 %collective-permute-start.7 = (bf16[144,256]{1,0:T(8,128)(2,1)S(1)}, bf16[144,256]{1,0:T(8,128)(2,1)S(1)}, u32[]{:S(2)}, u32[]{:S(2)}) collective-permute-start(bf16[144,256]{1,0:T(8,128)(2,1)S(1)} %get-tuple-element.32), channel_id=1, source_target_pairs={{16,0},{24,8},{32,16},{40,24},{48,32},{56,40},{64,48},{72,56},{80,... | collective-permute-start | bytes 221192 | tf_op jit(solution)/shard_map/ppermute | solution.py:281
Sparse Core Ops, SparseCore 0:
  10.1 47.8 all-gather.2

commit v4 on v3

--- a/solution.py
+++ b/solution.py
@@ -24,7 +24,6 @@
 hidden = -1e30
 
 VMEM = pl.BlockSpec(memory_space=pltpu.VMEM)
-HBM = pl.BlockSpec(memory_space=pltpu.MemorySpace.HBM)
 SMEM = pl.BlockSpec(memory_space=pltpu.SMEM)
 
 
@@ -161,61 +160,38 @@
                 keeps[head, down, across] = jnp.where(keep, jnp.float32(keep_scale), 0.0)
 
 
-def cut_kernel(weight, out):
-    core = lax.rem(lax.axis_index("head"), 2)
-    parts = lax.axis_size("head") // 2
-    width = out.shape[1] // parts
-    for part in range(parts):
-        first = pl.multiple_of((part * 2 + 1 - core) * width, width)
-        out[:, part * width : (part + 1) * width] = weight[:, pl.ds(first, width)]
-
-
-def project_other_kernel(gathered, weight, out, held, theirs, sems, weight_sem):
+def project(total, gathered, weight, core):
     parts, _, width = gathered.shape
-    copies = [
-        pltpu.make_async_copy(gathered.at[part], held.at[part], sems.at[part])
-        for part in range(parts)
-    ]
-    whole = pltpu.make_async_copy(weight, theirs, weight_sem)
-    whole.start()
-    for copy in copies:
-        copy.start()
-    whole.wait()
-    total = None
-    for part in range(parts):
-        copies[part].wait()
-        term = dot_last(held[part], theirs[:, part * width : (part + 1) * width])
-        total = term if total is None else total + term
-    out[...] = total
-
-
-def project_own_kernel(gathered, weight, out):
-    parts, _, width = gathered.shape
-    core = lax.rem(lax.axis_index("head"), 2)
-    total = None
     for part in range(parts):
         first = pl.multiple_of((part * 2 + core) * width, width)
         term = dot_last(gathered[part], weight[:, pl.ds(first, width)])
         total = term if total is None else total + term
-    out[...] = total
-
-
-def rows_kernel(own, received, attended, stats, near, far):
-    grad = bf16(own[...] + received[...])
-    near[0:ROWS] = grad
-    far[0:MB] = grad[0:MB]
+    return total
+
+
+def project_kernel(top, top_other, low, weight, out):
+    core = lax.rem(lax.axis_index("head"), 2)
+    out[0:MB] = project(project(None, top, weight, core), top_other, weight, 1 - core)
+    out[MB:] = project(None, low, weight, core)
+
+
+def rows_kernel(partial, low_other, weight, attended, stats, near, far):
+    core = lax.rem(lax.axis_index("head"), 2)
+    low = project(partial[MB:], low_other, weight, 1 - core)
     lane = lax.broadcasted_iota(jnp.int32, (MB, MB), 1)
-    for block in range(2):
+    for block, total in ((0, partial[0:MB]), (1, low)):
         rows = slice(block * MB, (block + 1) * MB)
+        grad = bf16(total)
+        near[rows] = grad
         parts = stats[rows]
         for head in range(HEADS):
             cols = slice(head * DH, (head + 1) * DH)
-            row_dot = jnp.sum(
-                f32(grad[rows, cols]) * f32(attended[rows, cols]), axis=1, keepdims=True
-            )
+            row_dot = jnp.sum(f32(grad[:, cols]) * f32(attended[rows, cols]), axis=1, keepdims=True)
             parts = put_parts(parts, lane, 6 + 3 * head, row_dot)
         across = bf16(parts.T[0:EXTRA])
         near[ROWS:, rows] = across
+        if block == 0:
+            far[0:MB] = grad
         far[MB:, rows] = across
 
 
@@ -260,7 +236,7 @@
         grad_value[:, cols] = bf16(value_sum)
 
 
-def call(kernel, specs, outs, flops, *args, scratch=(), grant=16):
+def call(kernel, specs, outs, flops, *args):
     shapes = [jax.ShapeDtypeStruct(shape, dtype) for shape, dtype in outs]
     moved = sum(a.size * a.dtype.itemsize for a in args)
     moved += sum(s.size * s.dtype.itemsize for s in shapes)
@@ -269,8 +245,7 @@
         out_shape=shapes,
         in_specs=specs,
         out_specs=[VMEM] * len(shapes),
-        scratch_shapes=scratch,
-        compiler_params=pltpu.CompilerParams(vmem_limit_bytes=grant << 20),
+        compiler_params=pltpu.CompilerParams(vmem_limit_bytes=16 << 20),
         cost_estimate=pl.CostEstimate(flops=flops, bytes_accessed=moved, transcendentals=0),
     )(*args)
 
@@ -291,13 +266,16 @@
     count = lax.axis_size("head")
     parts, width = count // 2, grad_out.shape[1]
     groups = [list(range(first, count, 2)) for first in range(2)]
-    gathered = lax.all_gather(grad_out, "head", axis=0, axis_index_groups=groups)
+
+    def gather(rows):
+        return lax.all_gather(rows, "head", axis=0, axis_index_groups=groups)
+
     near_keys = shifted(jnp.concatenate((key_rows, value_rows)), 1)
     far_keys = shifted(jnp.concatenate((key_rows[MB:], value_rows[MB:])), 2)
     near_query = shifted(query_rows, -1)
     far_query = shifted(query_rows[:MB], -2)
-    (theirs,) = call(cut_kernel, [VMEM], [((WIDE, parts * width), half)], 0, out_weight)
-    other_weight = other_core(theirs)
+    top = gather(grad_out[:MB])
+    top_other = other_core(top)
     tile = 2 * MB * MB * DH
     signed, attended, stats, key_win, value_win = call(
         forward_kernel,
@@ -319,32 +297,20 @@
         24 * tile,
         mask_types, drop_seed, key_rows, near_query, far_query,
     )
-    gathered, attended, scores = lax.optimization_barrier((gathered, attended, scores))
-    flops = 2 * ROWS * WIDE * width * parts
-    (sent,) = call(
-        project_other_kernel,
-        [HBM] * 2,
-        [((ROWS, WIDE), full)],
-        flops,
-        gathered, other_weight,
-        scratch=[
-            pltpu.VMEM((parts, ROWS, width), half),
-            pltpu.VMEM((WIDE, parts * width), half),
-            pltpu.SemaphoreType.DMA((parts,)),
-            pltpu.SemaphoreType.DMA,
-        ],
-        grant=56,
-    )
-    received = other_core(sent)
-    (own,) = call(
-        project_own_kernel, [VMEM] * 2, [((ROWS, WIDE), full)], flops, gathered, out_weight
+    low_rows, attended, scores = lax.optimization_barrier((grad_out[MB:], attended, scores))
+    low = gather(low_rows)
+    low_other = other_core(low)
+    flops = 2 * MB * WIDE * width * parts
+    (partial,) = call(
+        project_kernel, [VMEM] * 4, [((ROWS, WIDE), full)], 3 * flops,
+        top, top_other, low, out_weight,
     )
     near_rows, far_rows = call(
         rows_kernel,
-        [VMEM] * 4,
+        [VMEM] * 5,
         [((ROWS + EXTRA, WIDE), half), ((MB + EXTRA, WIDE), half)],
-        0,
-        own, received, attended, stats,
+        flops,
+        partial, low_other, out_weight, attended, stats,
     )
     near_grad = shifted(near_rows, -1)
     far_grad = shifted(far_rows, -2)

time: 95 us -> 106 us (1.12)
  blocking collectives: 0 us -> 32.2 us
  between operations: 15 us -> 1.47 us
  Pallas kernels: 13.8 us -> 10.5 us
  local copies, waits for them, and re-layouts: 6.21 us -> 3.56 us
  starting transfers between devices: 50.7 us -> 48.7 us
    all_gather x0 -> x2, blocking collectives: none -> 32.2 us  [gather(): return lax.all_gather(rows, 'head', axis=0, axis_index_groups=groups)]
    unnamed x48 -> x10, local copies, waits for them, and re-layouts: 6.2 us -> 0.02 us
    pallas_call x8 -> x6, Pallas kernels: 13.8 us -> 10.5 us  [call(): pl.pallas_call(kernel, out_shape=shapes, in_specs=specs, out_specs=[VMEM]...]
    ppermute x6, starting transfers between devices: 46.7 us -> 44.9 us  [shifted(): return lax.ppermute(value, 'blk', pairs)]
    slice x4 -> x2, local copies, waits for them, and re-layouts: 0.01 us -> 1.69 us  [on_device(): far_keys = shifted(jnp.concatenate((key_rows[MB:], value_rows[MB:])), 2)]
  transfers between devices with their start and end apart: 9 -> 8, of which waited for: 3 -> 3; matrix products, arithmetic and copies ran while one was open for 0% -> 4% of each run, Pallas kernels for 9% -> 8%
where the time goes in v4:
time: 106 us; the launch traced here: 105 us
  starting transfers between devices  48.7 us (46%)
  blocking collectives  32.2 us (30%)
  Pallas kernels  10.5 us (10%)
  waiting for transfers between devices  7.87 us (7%)
  local copies, waits for them, and re-layouts  3.56 us (3%)
  between operations  1.47 us (1%)
    ppermute x6, starting transfers between devices, shifted(): return lax.ppermute(value, 'blk', pairs)  44.9 us
    all_gather x2, blocking collectives, gather(): return lax.all_gather(rows, 'head', axis=0, axis_index_groups=groups)  32.2 us
    pallas_call x6, Pallas kernels, call(): pl.pallas_call(kernel, out_shape=shapes, in_specs=specs, out_specs=[VMEM]...  10.5 us
    ppermute x6, waiting for transfers between devices, shifted(): return lax.ppermute(value, 'blk', pairs)  7.2 us
    ppermute x2, starting transfers between devices, other_core(): lax.ppermute(value, 'head', [(source, source ^ 1) for source in range(cou...  3.82 us
  transfers between devices with their start and end apart: 8, of which 3 were waited for; matrix products, arithmetic and copies ran while one was open for 4% of the time, Pallas kernels for 8%

profile of v4, /device:TPU:6, one launch (start us, length us, event | category | flops | bytes accessed | tf_op | source)
XLA Modules:
  0.0 105.3 jit_solution(6104948948719941468)
XLA Ops:
  0.6 0.0 copy-start.3
  0.6 0.0 copy-start.2
  0.7 0.0 copy-start.1
  0.7 0.0 copy-start.4
  0.7 16.6 %collective-permute-start.2 = (bf16[256,256]{1,0:T(8,128)(2,1)}, bf16[256,256]{1,0:T(8,128)(2,1)S(1)}, u32[]{:S(2)}, u32[]{:S(2)}) collective-permute-start(bf16[256,256]{1,0:T(8,128)(2,1)} %query.3), channel_id=1, source_target_pairs={{8,0},{16,8},{24,16},{32,24},{40,32},{48,40},{56,48},{64,56},{72,6... | collective-permute-start | bytes 393224 | tf_op jit(solution)/shard_map/ppermute | solution.py:256
  17.3 0.9 slice.18
  18.1 0.0 copy-start
  18.1 2.6 %collective-permute-start.3 = (bf16[128,256]{1,0:T(8,128)(2,1)S(1)}, bf16[128,256]{1,0:T(8,128)(2,1)S(1)}, u32[]{:S(2)}, u32[]{:S(2)}) collective-permute-start(bf16[128,256]{1,0:T(8,128)(2,1)S(1)} %slice.18), channel_id=1, source_target_pairs={{16,0},{24,8},{32,16},{40,24},{48,32},{56,40},{64,48},{72,56},{80,... | collective-permute-start | bytes 196616 | tf_op jit(solution)/shard_map/ppermute | solution.py:256
  20.7 0.8 slice.15
  21.6 0.8 slice.16
  22.4 4.3 %collective-permute-start.1 = (bf16[256,256]{1,0:T(8,128)(2,1)S(1)}, bf16[256,256]{1,0:T(8,128)(2,1)S(1)}, u32[]{:S(2)}, u32[]{:S(2)}) collective-permute-start(bf16[256,256]{1,0:T(8,128)(2,1)S(1)} %pad_maximum_fusion.1), channel_id=1, source_target_pairs={{0,16},{8,24},{16,32},{24,40},{32,48},{40,56},{48,64},{56,72},{64,... | collective-permute-start | bytes 393224 | tf_op jit(solution)/shard_map/ppermute | solution.py:256
  26.7 1.0 pad_maximum_fusion
  27.7 1.9 %collective-permute-start = (bf16[512,256]{1,0:T(8,128)(2,1)S(1)}, bf16[512,256]{1,0:T(8,128)(2,1)S(1)}, u32[]{:S(2)}, u32[]{:S(2)}) collective-permute-start(bf16[512,256]{1,0:T(8,128)(2,1)S(1)} %pad_maximum_fusion), channel_id=1, source_target_pairs={{0,8},{8,16},{16,24},{24,32},{32,40},{40,48},{48,56},{56,64},{64,7... | collective-permute-start | bytes 786440 | tf_op jit(solution)/shard_map/ppermute | solution.py:256
  29.6 1.0 fusion
  30.6 15.9 %all-gather = bf16[512,512]{1,0:T(8,128)(2,1)S(1)} all-gather(bf16[128,512]{1,0:T(8,128)(2,1)S(1)} %get-tuple-element.37), channel_id=2, replica_groups={{0,2,4,6},{1,3,5,7},{8,10,12,14},{9,11,13,15},{16,18,20,22},{17,19,21,2..., dimensions={0}, use_global_device_ids=true | all-gather | bytes 655360 | tf_op jit(solution)/shard_map/all_gather | solution.py:271
  46.6 1.9 %collective-permute-start.4 = (bf16[4,128,512]{2,1,0:T(8,128)(2,1)S(1)}, bf16[4,128,512]{2,1,0:T(8,128)(2,1)S(1)}, u32[]{:S(2)}, u32[]{:S(2)}) collective-permute-start(bf16[4,128,512]{2,1,0:T(8,128)(2,1)S(1)} %bitcast.2), channel_id=1, source_target_pairs={{0,1},{1,0},{2,3},{3,2},{4,5},{5,4},{6,7},{7,6},{8,9},{9,8},{10,11... | collective-permute-start | bytes 1572872 | tf_op jit(solution)/shard_map/ppermute | solution.py:261
  49.1 0.0 collective-permute-done.3.far.far_query
  49.1 0.0 collective-permute-done.2.near.near_query
  49.2 0.0 copy-done.2
  49.2 0.0 copy-done.4
  49.2 2.2 %shard_map.95 = (f32[2,256,384]{2,1,0:T(8,128)S(1)}, f32[2,256,384]{2,1,0:T(8,128)S(1)}) custom-call(s32[128,128]{1,0:T(8,128)S(1)} %copy-done.4, s32[1]{0:T(128)S(6)} %copy.10.seed, bf16[256,256]{1,0:T(8,128)(2,1)S(1)} %copy-done.2, bf16[256,256]{1,0:T(8,128)(2,1)S(1)} %collective-permute-done.2.near.near_query, ...), custom_call_target="tpu_custom_call" | custom-call | flops 100663296 | bytes 1966084 | tf_op jit(solution)/shard_map/pallas_call | solution.py:243
  51.4 0.0 collective-permute-done.1.far
  51.4 0.6 collective-permute-done.near
  51.9 0.0 copy-done.3
  51.9 0.0 copy-done.1
  51.9 3.6 %shard_map.94 = (f32[2,256,640]{2,1,0:T(8,128)S(1)}, bf16[256,256]{1,0:T(8,128)(2,1)S(1)}, f32[256,128]{1,0:T(8,128)S(1)}, bf16[640,256]{1,0:T(8,128)(2,1)S(1)}, bf16[640,256]{1,0:T(8,128)(2,1)S(1)}) custom-call(s32[128,128]{1,0:T(8,128)S(1)} %copy-done.4, s32[1]{0:T(128)S(6)} %copy.10.seed, bf16[256,256]{1,0:T(8,128)(2,1)S(1)} %copy-done.3, ...), custom_call_target="tpu_custom_call" | custom-call | flops 167772160 | bytes 3080196 | tf_op jit(solution)/shard_map/pallas_call | solution.py:243
  55.6 16.3 %all-gather.1 = bf16[512,512]{1,0:T(8,128)(2,1)S(1)} all-gather(bf16[128,512]{1,0:T(8,128)(2,1)S(1)} %get-tuple-element.24), channel_id=3, replica_groups={{0,2,4,6},{1,3,5,7},{8,10,12,14},{9,11,13,15},{16,18,20,22},{17,19,21,2..., dimensions={0}, use_global_device_ids=true | all-gather | bytes 655360 | tf_op jit(solution)/shard_map/all_gather | solution.py:271
  71.8 1.9 %collective-permute-start.5 = (bf16[4,128,512]{2,1,0:T(8,128)(2,1)S(1)}, bf16[4,128,512]{2,1,0:T(8,128)(2,1)S(1)}, u32[]{:S(2)}, u32[]{:S(2)}) collective-permute-start(bf16[4,128,512]{2,1,0:T(8,128)(2,1)S(1)} %bitcast.4), channel_id=1, source_target_pairs={{0,1},{1,0},{2,3},{3,2},{4,5},{5,4},{6,7},{7,6},{8,9},{9,8},{10,11... | collective-permute-start | bytes 1572872 | tf_op jit(solution)/shard_map/ppermute | solution.py:261
  73.8 0.0 collective-permute-done.4.top_other
  73.8 0.0 copy-done
  73.8 1.2 %shard_map.96.partial = f32[256,256]{1,0:T(8,128)S(1)} custom-call(bf16[4,128,512]{2,1,0:T(8,128)(2,1)S(1)} %bitcast.3, bf16[4,128,512]{2,1,0:T(8,128)(2,1)S(1)} %collective-permute-done.4.top_other, bf16[4,128,512]{2,1,0:T(8,128)(2,1)S(1)} %bitcast.5, bf16[256,4096]{1,0:T(8,128)(2,1)S(1)} %copy-done), custom_call_target="tpu_custom_call" | custom-call | flops 402653184 | bytes 3932160 | tf_op jit(solution)/shard_map/pallas_call | solution.py:243
  75.0 0.7 collective-permute-done.5.low_other
  75.6 0.6 shard_map.97
  76.3 17.6 %collective-permute-start.6 = (bf16[272,256]{1,0:T(8,128)(2,1)S(1)}, bf16[272,256]{1,0:T(8,128)(2,1)S(1)}, u32[]{:S(2)}, u32[]{:S(2)}) collective-permute-start(bf16[272,256]{1,0:T(8,128)(2,1)S(1)} %get-tuple-element.26.grad), channel_id=1, source_target_pairs={{8,0},{16,8},{24,16},{32,24},{40,32},{48,40},{56,48},{64,56},{72,6... | collective-permute-start | bytes 417800 | tf_op jit(solution)/shard_map/ppermute | solution.py:256
  93.9 1.9 %collective-permute-start.7 = (bf16[144,256]{1,0:T(8,128)(2,1)S(1)}, bf16[144,256]{1,0:T(8,128)(2,1)S(1)}, u32[]{:S(2)}, u32[]{:S(2)}) collective-permute-start(bf16[144,256]{1,0:T(8,128)(2,1)S(1)} %get-tuple-element.32), channel_id=1, source_target_pairs={{16,0},{24,8},{32,16},{40,24},{48,32},{56,40},{64,48},{72,56},{80,... | collective-permute-start | bytes 221192 | tf_op jit(solution)/shard_map/ppermute | solution.py:256
  95.8 1.4 %shard_map.98 = (bf16[256,256]{1,0:T(8,128)(2,1)}, f32[256,256]{1,0:T(8,128)S(1)}, f32[256,256]{1,0:T(8,128)S(1)}) custom-call(f32[2,256,640]{2,1,0:T(8,128)S(1)} %get-tuple-element.20.signed, bf16[256,256]{1,0:T(8,128)(2,1)S(1)} %get-tuple-element.23.attended, bf16[256,256]{1,0:T(8,128)(2,1)S(1)} %copy-done.3, bf16[272,256]{1,0:T(8,128)(2,1)S(1)} %get-tuple-element.26.grad, ...), custom_call_target="tpu_custom_call" | custom-call | flops 335544320 | bytes 3022848 | tf_op jit(solution)/shard_map/pallas_call | solution.py:243
  97.2 6.6 %collective-permute-done.7.far_grad = bf16[144,256]{1,0:T(8,128)(2,1)S(1)} collective-permute-done((bf16[144,256]{1,0:T(8,128)(2,1)S(1)}, bf16[144,256]{1,0:T(8,128)(2,1)S(1)}, u32[]{:S(2)}, u32[]{:S(2)}) %collective-permute-start.7) | collective-permute-done | bytes 73760 | tf_op jit(solution)/shard_map/ppermute | solution.py:256
  103.9 0.0 collective-permute-done.6.near_grad
  103.9 1.5 %shard_map.99 = (bf16[256,256]{1,0:T(8,128)(2,1)}, bf16[256,256]{1,0:T(8,128)(2,1)}) custom-call(f32[2,256,384]{2,1,0:T(8,128)S(1)} %get-tuple-element.30.scores, f32[2,256,384]{2,1,0:T(8,128)S(1)} %get-tuple-element.31.keeps, bf16[256,256]{1,0:T(8,128)(2,1)S(1)} %copy-done.1, bf16[256,256]{1,0:T(8,128)(2,1)S(1)} %collective-permute-done.2.near.near_query, ...), custom_call_target="tpu_custom_call" | custom-call | flops 167772160 | bytes 2899968 | tf_op jit(solution)/shard_map/pallas_call | solution.py:243
  (1 shorter events, 0.0 us)
Async XLA Ops:
  0.6 51.3 %copy-start.3 = (bf16[256,256]{1,0:T(8,128)(2,1)S(1)}, bf16[256,256]{1,0:T(8,128)(2,1)}, u32[]{:S(2)}) copy-start(bf16[256,256]{1,0:T(8,128)(2,1)} %query.3) | copy-start | bytes 393220
  0.6 48.5 %copy-start.2 = (bf16[256,256]{1,0:T(8,128)(2,1)S(1)}, bf16[256,256]{1,0:T(8,128)(2,1)}, u32[]{:S(2)}) copy-start(bf16[256,256]{1,0:T(8,128)(2,1)} %key.3) | copy-start | bytes 393220
  0.7 51.3 %copy-start.1 = (bf16[256,256]{1,0:T(8,128)(2,1)S(1)}, bf16[256,256]{1,0:T(8,128)(2,1)}, u32[]{:S(2)}) copy-start(bf16[256,256]{1,0:T(8,128)(2,1)} %value.3) | copy-start | bytes 393220
  0.7 48.5 %copy-start.4 = (s32[128,128]{1,0:T(8,128)S(1)}, s32[128,128]{1,0:T(8,128)}, u32[]{:S(2)}) copy-start(s32[128,128]{1,0:T(8,128)} %table.3) | copy-start | bytes 196612
  0.7 48.5 %collective-permute-start.2 = (bf16[256,256]{1,0:T(8,128)(2,1)}, bf16[256,256]{1,0:T(8,128)(2,1)S(1)}, u32[]{:S(2)}, u32[]{:S(2)}) collective-permute-start(bf16[256,256]{1,0:T(8,128)(2,1)} %query.3), channel_id=1, source_target_pairs={{8,0},{16,8},{24,16},{32,24},{40,32},{48,40},{56,48},{64,56},{72,6... | collective-permute-start | bytes 393224 | tf_op jit(solution)/shard_map/ppermute | solution.py:256
  18.1 55.6 %copy-start = (bf16[256,4096]{1,0:T(8,128)(2,1)S(1)}, bf16[256,4096]{1,0:T(8,128)(2,1)}, u32[]{:S(2)}) copy-start(bf16[256,4096]{1,0:T(8,128)(2,1)} %weight.3) | copy-start | bytes 6291460
  18.1 31.0 %collective-permute-start.3 = (bf16[128,256]{1,0:T(8,128)(2,1)S(1)}, bf16[128,256]{1,0:T(8,128)(2,1)S(1)}, u32[]{:S(2)}, u32[]{:S(2)}) collective-permute-start(bf16[128,256]{1,0:T(8,128)(2,1)S(1)} %slice.18), channel_id=1, source_target_pairs={{16,0},{24,8},{32,16},{40,24},{48,32},{56,40},{64,48},{72,56},{80,... | collective-permute-start | bytes 196616 | tf_op jit(solution)/shard_map/ppermute | solution.py:256
  22.4 28.9 %collective-permute-start.1 = (bf16[256,256]{1,0:T(8,128)(2,1)S(1)}, bf16[256,256]{1,0:T(8,128)(2,1)S(1)}, u32[]{:S(2)}, u32[]{:S(2)}) collective-permute-start(bf16[256,256]{1,0:T(8,128)(2,1)S(1)} %pad_maximum_fusion.1), channel_id=1, source_target_pairs={{0,16},{8,24},{16,32},{24,40},{32,48},{40,56},{48,64},{56,72},{64,... | collective-permute-start | bytes 393224 | tf_op jit(solution)/shard_map/ppermute | solution.py:256
  27.7 24.2 %collective-permute-start = (bf16[512,256]{1,0:T(8,128)(2,1)S(1)}, bf16[512,256]{1,0:T(8,128)(2,1)S(1)}, u32[]{:S(2)}, u32[]{:S(2)}) collective-permute-start(bf16[512,256]{1,0:T(8,128)(2,1)S(1)} %pad_maximum_fusion), channel_id=1, source_target_pairs={{0,8},{8,16},{16,24},{24,32},{32,40},{40,48},{48,56},{56,64},{64,7... | collective-permute-start | bytes 786440 | tf_op jit(solution)/shard_map/ppermute | solution.py:256
  46.6 27.2 %collective-permute-start.4 = (bf16[4,128,512]{2,1,0:T(8,128)(2,1)S(1)}, bf16[4,128,512]{2,1,0:T(8,128)(2,1)S(1)}, u32[]{:S(2)}, u32[]{:S(2)}) collective-permute-start(bf16[4,128,512]{2,1,0:T(8,128)(2,1)S(1)} %bitcast.2), channel_id=1, source_target_pairs={{0,1},{1,0},{2,3},{3,2},{4,5},{5,4},{6,7},{7,6},{8,9},{9,8},{10,11... | collective-permute-start | bytes 1572872 | tf_op jit(solution)/shard_map/ppermute | solution.py:261
  71.8 3.8 %collective-permute-start.5 = (bf16[4,128,512]{2,1,0:T(8,128)(2,1)S(1)}, bf16[4,128,512]{2,1,0:T(8,128)(2,1)S(1)}, u32[]{:S(2)}, u32[]{:S(2)}) collective-permute-start(bf16[4,128,512]{2,1,0:T(8,128)(2,1)S(1)} %bitcast.4), channel_id=1, source_target_pairs={{0,1},{1,0},{2,3},{3,2},{4,5},{5,4},{6,7},{7,6},{8,9},{9,8},{10,11... | collective-permute-start | bytes 1572872 | tf_op jit(solution)/shard_map/ppermute | solution.py:261
  76.3 27.6 %collective-permute-start.6 = (bf16[272,256]{1,0:T(8,128)(2,1)S(1)}, bf16[272,256]{1,0:T(8,128)(2,1)S(1)}, u32[]{:S(2)}, u32[]{:S(2)}) collective-permute-start(bf16[272,256]{1,0:T(8,128)(2,1)S(1)} %get-tuple-element.26.grad), channel_id=1, source_target_pairs={{8,0},{16,8},{24,16},{32,24},{40,32},{48,40},{56,48},{64,56},{72,6... | collective-permute-start | bytes 417800 | tf_op jit(solution)/shard_map/ppermute | solution.py:256
  93.9 10.0 %collective-permute-start.7 = (bf16[144,256]{1,0:T(8,128)(2,1)S(1)}, bf16[144,256]{1,0:T(8,128)(2,1)S(1)}, u32[]{:S(2)}, u32[]{:S(2)}) collective-permute-start(bf16[144,256]{1,0:T(8,128)(2,1)S(1)} %get-tuple-element.32), channel_id=1, source_target_pairs={{16,0},{24,8},{32,16},{40,24},{48,32},{56,40},{64,48},{72,56},{80,... | collective-permute-start | bytes 221192 | tf_op jit(solution)/shard_map/ppermute | solution.py:256

commit v5 on v4

v5 whole, which is shorter than its diff:
```python
import functools

import jax
import jax.numpy as jnp
from jax import lax
from jax.experimental import pallas as pl
from jax.experimental.pallas import tpu as pltpu
from jax.sharding import PartitionSpec as P

DH = 128
MB = 128
HEADS = 2
ROWS = 256
SLOTS = 5
WIN = SLOTS * MB
FAR = 3 * MB
WIDE = HEADS * DH
EXTRA = 16

drop_level = 6554
keep_scale = 65536.0 / 58982.0
mix_one = 73244475
mix_two = 295559667
mix_three = 668265263
score_scale = DH**-0.5
hidden = -1e30

VMEM = pl.BlockSpec(memory_space=pltpu.VMEM)
SMEM = pl.BlockSpec(memory_space=pltpu.SMEM)


def bf16(value):
    return value.astype(jnp.bfloat16)


def f32(value):
    return value.astype(jnp.float32)


def dot_last(left, right):
    return lax.dot_general(
        left, right, (((1,), (1,)), ((), ())), preferred_element_type=jnp.float32
    )


def dot_first(left, right):
    return lax.dot_general(
        left, right, (((0,), (0,)), ((), ())), preferred_element_type=jnp.float32
    )


def dot(left, right):
    return jnp.dot(left, right, preferred_element_type=jnp.float32)


def bound_of(table, query_block, key_block):
    last = table.shape[0] - 1
    inside = (key_block >= 0) & (query_block <= last)
    kind = table[jnp.minimum(query_block, last), jnp.maximum(key_block, 0)]
    far = jnp.int32(1 << 20)
    bound = jnp.where(kind == 2, far, jnp.where(kind == 1, (query_block - key_block) * MB, -far))
    return jnp.where(inside, bound, -far)


def kept(seed, head, query_block, key_block, query_axis):
    base = query_block * MB * mix_one + key_block * MB * mix_two + head * mix_three + seed
    rows = lax.broadcasted_iota(jnp.int32, (MB, MB), query_axis) * mix_one
    cols = lax.broadcasted_iota(jnp.int32, (MB, MB), 1 - query_axis) * mix_two
    hashed = (rows + cols) + base
    for _ in range(2):
        hashed = hashed ^ lax.shift_right_logical(hashed, jnp.int32(16))
        hashed = hashed * mix_one
    hashed = hashed ^ lax.shift_right_logical(hashed, jnp.int32(16))
    return (hashed & 65535) >= drop_level


def key_minus_query(query_axis):
    return lax.broadcasted_iota(jnp.int32, (MB, MB), 1 - query_axis) - lax.broadcasted_iota(
        jnp.int32, (MB, MB), query_axis
    )


def put_parts(stats, lane, first, column):
    rest = column
    for part in range(3):
        piece = f32(bf16(rest))
        stats = jnp.where(lane == first + part, piece, stats)
        rest = rest - piece
    return stats


def take_parts(stats, first):
    return stats[first : first + 1] + stats[first + 1 : first + 2] + stats[first + 2 : first + 3]


def forward(table, seed, block, query, keys, values, signed, attended, stats):
    shard = lax.axis_index("blk")
    first_head = lax.axis_index("head") * HEADS
    count = keys(0).shape[0] // MB
    query_block = shard * 2 + block
    first_block = shard * 2 + 2 - count
    ahead = key_minus_query(0)
    lane = lax.broadcasted_iota(jnp.int32, (MB, MB), 1)
    parts = jnp.zeros((MB, MB), jnp.float32)
    for head in range(HEADS):
        cols = pl.ds(head * DH, DH)
        scores = dot_last(query[block * MB : (block + 1) * MB, cols], keys(head))
        tiles = []
        for slot in range(count):
            bound = bound_of(table, query_block, first_block + slot)
            tile = scores[:, slot * MB : (slot + 1) * MB] * score_scale
            tiles.append(jnp.where(ahead <= bound, tile, hidden))
        top = functools.reduce(jnp.maximum, tiles)
        top = jnp.max(top, axis=1, keepdims=True)
        tiles = [jnp.exp(tile - top) for tile in tiles]
        total = jnp.sum(functools.reduce(jnp.add, tiles), axis=1, keepdims=True)
        inverse = 1.0 / total
        drops = []
        for slot in range(count):
            prob = tiles[slot] * inverse
            keep = kept(seed[0], first_head + head, query_block, first_block + slot, 0)
            signed[head, :, slot * MB : (slot + 1) * MB] = jnp.where(keep, prob, -prob)
            drops.append(bf16(jnp.where(keep, prob * keep_scale, 0.0)))
        attended[:, cols] = bf16(dot(jnp.concatenate(drops, axis=1), values(head)))
        parts = put_parts(parts, lane, 3 * head, top + jnp.log(total))
    stats[...] = parts


def later(table, seed, first_query, first_key, queries, keys, scores, keeps):
    first_head = lax.axis_index("head") * HEADS
    ahead = key_minus_query(1)
    for head in range(HEADS):
        cols = pl.ds(head * DH, DH)
        tiles = dot_last(keys[:, cols], queries[:, cols]) * score_scale
        for block in range(queries.shape[0] // MB):
            across = slice(block * MB, (block + 1) * MB)
            for slot in range(keys.shape[0] // MB):
                down = slice(slot * MB, (slot + 1) * MB)
                bound = bound_of(table, first_query + block, first_key + slot)
                scores[head, down, across] = jnp.where(
                    ahead <= bound, tiles[down, across], hidden
                )
                keep = kept(seed[0], first_head + head, first_query + block, first_key + slot, 1)
                keeps[head, down, across] = jnp.where(keep, jnp.float32(keep_scale), 0.0)


def stacked(*parts):
    def of_head(head):
        cols = slice(head * DH, (head + 1) * DH)
        return jnp.concatenate([ref[rows, cols] for ref, rows in parts], axis=0)

    return of_head


def near_window(key, value, near):
    whole = slice(None)
    keys = ((near, slice(0, ROWS)), (key, whole))
    values = ((near, slice(ROWS, None)), (value, whole))
    return keys, values


def far_window(key, value, near, far):
    keys, values = near_window(key, value, near)
    return ((far, slice(0, MB)), *keys), ((far, slice(MB, None)), *values)


def near_kernel(
    table, seed, query, key, value, near, near_query, signed, attended, stats, scores, keeps
):
    keys, values = near_window(key, value, near)
    forward(table, seed, 1, query, stacked(*keys), stacked(*values), signed, attended, stats)
    shard = lax.axis_index("blk")
    later(table, seed, shard * 2 + 2, shard * 2, near_query, key, scores, keeps)


def far_kernel(
    table, seed, query, key, value, near, far, far_query, signed, attended, stats, scores, keeps
):
    keys, values = far_window(key, value, near, far)
    forward(table, seed, 0, query, stacked(*keys), stacked(*values), signed, attended, stats)
    shard = lax.axis_index("blk")
    later(table, seed, shard * 2 + 4, shard * 2 + 1, far_query, key.at[MB:], scores, keeps)


def project(total, gathered, weight, core):
    parts, _, width = gathered.shape
    for part in range(parts):
        first = pl.multiple_of((part * 2 + core) * width, width)
        term = dot_last(gathered[part], weight[:, pl.ds(first, width)])
        total = term if total is None else total + term
    return total


def project_kernel(top, top_other, low, weight, out):
    core = lax.rem(lax.axis_index("head"), 2)
    out[0:MB] = project(project(None, top, weight, core), top_other, weight, 1 - core)
    out[MB:] = project(None, low, weight, core)


def rows_kernel(
    partial, low_other, weight, attended_top, attended_low, stats_top, stats_low, near, far
):
    core = lax.rem(lax.axis_index("head"), 2)
    low = project(partial[MB:], low_other, weight, 1 - core)
    lane = lax.broadcasted_iota(jnp.int32, (MB, MB), 1)
    for block, total, attended, stats in (
        (0, partial[0:MB], attended_top, stats_top), (1, low, attended_low, stats_low)
    ):
        rows = slice(block * MB, (block + 1) * MB)
        grad = bf16(total)
        near[rows] = grad
        parts = stats[...]
        for head in range(HEADS):
            cols = slice(head * DH, (head + 1) * DH)
            row_dot = jnp.sum(f32(grad[:, cols]) * f32(attended[:, cols]), axis=1, keepdims=True)
            parts = put_parts(parts, lane, 6 + 3 * head, row_dot)
        across = bf16(parts.T[0:EXTRA])
        near[ROWS:, rows] = across
        if block == 0:
            far[0:MB] = grad
        far[MB:, rows] = across


def own_kernel(
    signed_top, signed_low, attended_top, attended_low, query, grad, key, value, near, far,
    grad_query, key_part, value_part,
):
    for head in range(HEADS):
        cols = slice(head * DH, (head + 1) * DH)
        key_sum = value_sum = None
        for block, signed, attended, (keys, values) in (
            (0, signed_top, attended_top, far_window(key, value, near, far)),
            (1, signed_low, attended_low, near_window(key, value, near)),
        ):
            rows = slice(block * MB, (block + 1) * MB)
            grad_head = grad[rows, cols]
            row_dot = jnp.sum(f32(grad_head) * f32(attended[:, cols]), axis=1, keepdims=True)
            grad_prob = dot_last(grad_head, stacked(*values)(head))
            probs = signed[head]
            first = probs.shape[1] - ROWS
            scaled = jnp.where(probs > 0.0, grad_prob * keep_scale, 0.0)
            dscore = bf16(jnp.abs(probs) * (scaled - row_dot))
            dropped = bf16(jnp.maximum(probs[:, first:], 0.0) * keep_scale)
            grad_query[rows, cols] = bf16(dot(dscore, stacked(*keys)(head)) * score_scale)
            key_term = dot_first(dscore[:, first:], query[rows, cols])
            value_term = dot_first(dropped, grad_head)
            key_sum = key_term if key_sum is None else key_sum + key_term
            value_sum = value_term if value_sum is None else value_sum + value_term
        key_part[:, cols] = key_sum
        value_part[:, cols] = value_sum


def finish_kernel(
    near_scores, near_keeps, far_scores, far_keeps, value, near_query, far_query, near_grad,
    far_grad, key_part, value_part, grad_key, grad_value,
):
    for head in range(HEADS):
        cols = pl.ds(head * DH, DH)

        def terms(scores, keeps, values, queries, grads):
            count = queries.shape[0]
            grad_head = grads[0:count, cols]
            stats = f32(grads[count:, 0:count])
            prob = jnp.exp(scores[head] - take_parts(stats, 3 * head))
            keep = keeps[head]
            grad_prob = dot_last(values, grad_head)
            dscore = bf16(prob * (grad_prob * keep - take_parts(stats, 6 + 3 * head)))
            return dot(dscore, queries[:, cols]), dot(bf16(prob * keep), grad_head)

        keys, values = terms(near_scores, near_keeps, value[:, cols], near_query, near_grad)
        far_keys, far_values = terms(far_scores, far_keeps, value[MB:, cols], far_query, far_grad)
        keys = keys + key_part[:, cols]
        values = values + value_part[:, cols]
        grad_key[0:MB, cols] = bf16(keys[0:MB] * score_scale)
        grad_key[MB:, cols] = bf16((keys[MB:] + far_keys) * score_scale)
        grad_value[0:MB, cols] = bf16(values[0:MB])
        grad_value[MB:, cols] = bf16(values[MB:] + far_values)


def call(kernel, specs, outs, flops, *args):
    shapes = [jax.ShapeDtypeStruct(shape, dtype) for shape, dtype in outs]
    moved = sum(a.size * a.dtype.itemsize for a in args)
    moved += sum(s.size * s.dtype.itemsize for s in shapes)
    return pl.pallas_call(
        kernel,
        out_shape=shapes,
        in_specs=specs,
        out_specs=[VMEM] * len(shapes),
        compiler_params=pltpu.CompilerParams(vmem_limit_bytes=16 << 20),
        cost_estimate=pl.CostEstimate(flops=flops, bytes_accessed=moved, transcendentals=0),
    )(*args)


def shifted(value, steps):
    count = lax.axis_size("blk")
    pairs = [(source, source + steps) for source in range(count) if 0 <= source + steps < count]
    return lax.ppermute(value, "blk", pairs)


def other_core(value):
    count = lax.axis_size("head")
    return lax.ppermute(value, "head", [(source, source ^ 1) for source in range(count)])


def on_device(query_rows, key_rows, value_rows, grad_out, out_weight, mask_types, drop_seed):
    half, full = jnp.bfloat16, jnp.float32
    count = lax.axis_size("head")
    parts, width = count // 2, grad_out.shape[1]
    groups = [list(range(first, count, 2)) for first in range(2)]

    def gather(rows):
        return lax.all_gather(rows, "head", axis=0, axis_index_groups=groups)

    near_keys = shifted(jnp.concatenate((key_rows, value_rows)), 1)
    near_query = shifted(query_rows, -1)
    top = gather(grad_out[:MB])
    top_other = other_core(top)
    far_keys = shifted(jnp.concatenate((near_keys[MB:ROWS], near_keys[ROWS + MB :])), 1)
    far_query = shifted(near_query[:MB], -1)
    tile = 2 * MB * MB * DH

    def outs(width, keys, queries):
        return [
            ((HEADS, MB, width), full),
            ((MB, WIDE), half),
            ((MB, MB), full),
            ((HEADS, keys, queries), full),
            ((HEADS, keys, queries), full),
        ]

    signed_low, attended_low, stats_low, near_scores, near_keeps = call(
        near_kernel, [SMEM, SMEM] + [VMEM] * 5, outs(WIN - MB, ROWS, ROWS), 48 * tile,
        mask_types, drop_seed, query_rows, key_rows, value_rows, near_keys, near_query,
    )
    signed_top, attended_top, stats_top, far_scores, far_keeps = call(
        far_kernel, [SMEM, SMEM] + [VMEM] * 6, outs(WIN, MB, MB), 48 * tile,
        mask_types, drop_seed, query_rows, key_rows, value_rows, near_keys, far_keys, far_query,
    )
    low_rows, attended_top, attended_low = lax.optimization_barrier(
        (grad_out[MB:], attended_top, attended_low)
    )
    low = gather(low_rows)
    low_other = other_core(low)
    flops = 2 * MB * WIDE * width * parts
    (partial,) = call(
        project_kernel, [VMEM] * 4, [((ROWS, WIDE), full)], 3 * flops,
        top, top_other, low, out_weight,
    )
    near_rows, far_rows = call(
        rows_kernel,
        [VMEM] * 7,
        [((ROWS + EXTRA, WIDE), half), ((MB + EXTRA, WIDE), half)],
        flops,
        partial, low_other, out_weight, attended_top, attended_low, stats_top, stats_low,
    )
    near_grad = shifted(near_rows, -1)
    far_grad = shifted(far_rows, -2)
    grad_query, key_part, value_part = call(
        own_kernel,
        [VMEM] * 10,
        [((ROWS, WIDE), half), ((ROWS, WIDE), full), ((ROWS, WIDE), full)],
        80 * tile,
        signed_top, signed_low, attended_top, attended_low, query_rows, near_rows, key_rows,
        value_rows, near_keys, far_keys,
    )
    grad_key, grad_value = call(
        finish_kernel,
        [VMEM] * 11,
        [((ROWS, WIDE), half), ((ROWS, WIDE), half)],
        40 * tile,
        near_scores, near_keeps, far_scores, far_keeps, value_rows, near_query, far_query,
        near_grad, far_grad, key_part, value_part,
    )
    return (grad_query, grad_key, grad_value)


def solution(mesh):
    split = P("blk", "head")
    return jax.shard_map(
        on_device,
        mesh=mesh,
        in_specs=(split, split, split, split, P("head", None), P(), P()),
        out_specs=(split, split, split),
        check_vma=False,
    )
```

time: 106 us -> 106 us (level)
  local copies, waits for them, and re-layouts: 3.56 us -> 1.03 us
  waiting for transfers between devices: 7.87 us -> 9.54 us
    slice x3 -> x2, local copies, waits for them, and re-layouts: 2.55 us -> 0.02 us  [the longest x1 0.01 us: on_device(): near_keys[MB:ROWS]]
    ppermute x6, waiting for transfers between devices: 7.2 us -> 8.88 us  [shifted(): return lax.ppermute(value, 'blk', pairs)]
  transfers between devices with their start and end apart: 8 -> 8, of which waited for: 3 -> 3; matrix products, arithmetic and copies ran while one was open for 4% -> 1% of each run, Pallas kernels for 8% -> 8%
where the time goes in v5:
time: 106 us; the launch traced here: 105 us
  starting transfers between devices  49.6 us (47%)
  blocking collectives  32 us (30%)
  Pallas kernels  10.3 us (10%)
  waiting for transfers between devices  9.54 us (9%)
  between operations  1.5 us (1%)
  other arithmetic  1.06 us (1%)
    ppermute x6, starting transfers between devices, shifted(): return lax.ppermute(value, 'blk', pairs)  45.8 us
    all_gather x2, blocking collectives, gather(): return lax.all_gather(rows, 'head', axis=0, axis_index_groups=groups)  32 us
    pallas_call x6, Pallas kernels, call(): pl.pallas_call(kernel, out_shape=shapes, in_specs=specs, out_specs=[VMEM]...  10.3 us
    ppermute x6, waiting for transfers between devices, shifted(): return lax.ppermute(value, 'blk', pairs)  8.88 us
    ppermute x2, starting transfers between devices, other_core(): lax.ppermute(value, 'head', [(source, source ^ 1) for source in range(cou...  3.82 us
  transfers between devices with their start and end apart: 8, of which 3 were waited for; matrix products, arithmetic and copies ran while one was open for 1% of the time, Pallas kernels for 8%

profile of v5, /device:TPU:6, one launch (start us, length us, event | category | flops | bytes accessed | tf_op | source)
XLA Modules:
  0.0 105.1 jit_solution(13147854868152462027)
XLA Ops:
  0.6 0.0 copy-start.1
  0.6 0.0 copy-start.2
  0.7 0.0 copy-start.3
  0.7 0.0 copy-start.4
  0.7 1.0 pad_maximum_fusion
  1.7 0.0 copy-start
  1.7 4.4 %collective-permute-start = (bf16[512,256]{1,0:T(8,128)(2,1)S(1)}, bf16[512,256]{1,0:T(8,128)(2,1)S(1)}, u32[]{:S(2)}, u32[]{:S(2)}) collective-permute-start(bf16[512,256]{1,0:T(8,128)(2,1)S(1)} %pad_maximum_fusion), channel_id=1, source_target_pairs={{0,8},{8,16},{16,24},{24,32},{32,40},{40,48},{48,56},{56,64},{64,7... | collective-permute-start | bytes 786440 | tf_op jit(solution)/shard_map/ppermute | solution.py:297
  6.2 14.1 %collective-permute-start.2 = (bf16[256,256]{1,0:T(8,128)(2,1)}, bf16[256,256]{1,0:T(8,128)(2,1)S(1)}, u32[]{:S(2)}, u32[]{:S(2)}) collective-permute-start(bf16[256,256]{1,0:T(8,128)(2,1)} %query.5), channel_id=1, source_target_pairs={{8,0},{16,8},{24,16},{32,24},{40,32},{48,40},{56,48},{64,56},{72,6... | collective-permute-start | bytes 393224 | tf_op jit(solution)/shard_map/ppermute | solution.py:297
  20.3 1.0 fusion
  21.3 4.9 %collective-permute-done.2.near_query = bf16[256,256]{1,0:T(8,128)(2,1)S(1)} collective-permute-done((bf16[256,256]{1,0:T(8,128)(2,1)}, bf16[256,256]{1,0:T(8,128)(2,1)S(1)}, u32[]{:S(2)}, u32[]{:S(2)}) %collective-permute-start.2) | collective-permute-done | bytes 131104 | tf_op jit(solution)/shard_map/ppermute | solution.py:297
  26.1 11.2 %collective-permute-start.3 = (bf16[128,256]{1,0:T(8,128)(2,1)S(1)}, bf16[128,256]{1,0:T(8,128)(2,1)S(1)}, u32[]{:S(2)}, u32[]{:S(2)}) collective-permute-start(bf16[128,256]{1,0:T(8,128)(2,1)S(1)} %slice.22), channel_id=1, source_target_pairs={{8,0},{16,8},{24,16},{32,24},{40,32},{48,40},{56,48},{64,56},{72,6... | collective-permute-start | bytes 196616 | tf_op jit(solution)/shard_map/ppermute | solution.py:297
  37.3 0.0 collective-permute-done.near
  37.3 1.9 %collective-permute-start.1 = (bf16[256,256]{1,0:T(8,128)(2,1)S(1)}, bf16[256,256]{1,0:T(8,128)(2,1)S(1)}, u32[]{:S(2)}, u32[]{:S(2)}) collective-permute-start(bf16[256,256]{1,0:T(8,128)(2,1)S(1)} %pad_maximum_fusion.1), channel_id=1, source_target_pairs={{0,8},{8,16},{16,24},{24,32},{32,40},{40,48},{48,56},{56,64},{64,7... | collective-permute-start | bytes 393224 | tf_op jit(solution)/shard_map/ppermute | solution.py:297
  39.3 15.9 %all-gather = bf16[512,512]{1,0:T(8,128)(2,1)S(1)} all-gather(bf16[128,512]{1,0:T(8,128)(2,1)S(1)} %get-tuple-element.43), channel_id=2, replica_groups={{0,2,4,6},{1,3,5,7},{8,10,12,14},{9,11,13,15},{16,18,20,22},{17,19,21,2..., dimensions={0}, use_global_device_ids=true | all-gather | bytes 655360 | tf_op jit(solution)/shard_map/all_gather | solution.py:312
  55.2 1.9 %collective-permute-start.4 = (bf16[4,128,512]{2,1,0:T(8,128)(2,1)S(1)}, bf16[4,128,512]{2,1,0:T(8,128)(2,1)S(1)}, u32[]{:S(2)}, u32[]{:S(2)}) collective-permute-start(bf16[4,128,512]{2,1,0:T(8,128)(2,1)S(1)} %bitcast.2), channel_id=1, source_target_pairs={{0,1},{1,0},{2,3},{3,2},{4,5},{5,4},{6,7},{7,6},{8,9},{9,8},{10,11... | collective-permute-start | bytes 1572872 | tf_op jit(solution)/shard_map/ppermute | solution.py:302
  57.7 0.0 copy-done.1
  57.8 0.0 copy-done.2
  57.8 0.0 copy-done.3
  57.8 0.0 copy-done.4
  57.8 2.8 %shard_map.95 = (f32[2,128,512]{2,1,0:T(8,128)S(1)}, bf16[128,256]{1,0:T(8,128)(2,1)S(1)}, f32[128,128]{1,0:T(8,128)S(1)}, f32[2,256,256]{2,1,0:T(8,128)S(1)}, f32[2,256,256]{2,1,0:T(8,128)S(1)}) custom-call(s32[128,128]{1,0:T(8,128)S(1)} %copy-done.4, s32[1]{0:T(128)S(6)} %copy.10.seed, bf16[256,256]{1,0:T(8,128)(2,1)S(1)} %copy-done.3, ...), custom_call_target="tpu_custom_call" | custom-call | flops 201326592 | bytes 2555908 | tf_op jit(solution)/shard_map/pallas_call | solution.py:284
  60.6 0.0 collective-permute-done.3.far_query
  60.6 0.0 collective-permute-done.1.far
  60.6 2.8 %shard_map.94 = (f32[2,128,640]{2,1,0:T(8,128)S(1)}, bf16[128,256]{1,0:T(8,128)(2,1)S(1)}, f32[128,128]{1,0:T(8,128)S(1)}, f32[2,128,128]{2,1,0:T(8,128)S(1)}, f32[2,128,128]{2,1,0:T(8,128)S(1)}) custom-call(s32[128,128]{1,0:T(8,128)S(1)} %copy-done.4, s32[1]{0:T(128)S(6)} %copy.10.seed, bf16[256,256]{1,0:T(8,128)(2,1)S(1)} %copy-done.3, ...), custom_call_target="tpu_custom_call" | custom-call | flops 201326592 | bytes 1966084 | tf_op jit(solution)/shard_map/pallas_call | solution.py:284
  63.4 16.1 %all-gather.1 = bf16[512,512]{1,0:T(8,128)(2,1)S(1)} all-gather(bf16[128,512]{1,0:T(8,128)(2,1)S(1)} %get-tuple-element.29), channel_id=3, replica_groups={{0,2,4,6},{1,3,5,7},{8,10,12,14},{9,11,13,15},{16,18,20,22},{17,19,21,2..., dimensions={0}, use_global_device_ids=true | all-gather | bytes 655360 | tf_op jit(solution)/shard_map/all_gather | solution.py:312
  79.5 1.9 %collective-permute-start.5 = (bf16[4,128,512]{2,1,0:T(8,128)(2,1)S(1)}, bf16[4,128,512]{2,1,0:T(8,128)(2,1)S(1)}, u32[]{:S(2)}, u32[]{:S(2)}) collective-permute-start(bf16[4,128,512]{2,1,0:T(8,128)(2,1)S(1)} %bitcast.4), channel_id=1, source_target_pairs={{0,1},{1,0},{2,3},{3,2},{4,5},{5,4},{6,7},{7,6},{8,9},{9,8},{10,11... | collective-permute-start | bytes 1572872 | tf_op jit(solution)/shard_map/ppermute | solution.py:302
  81.4 0.0 collective-permute-done.4.top_other
  81.4 0.0 copy-done
  81.5 1.2 %shard_map.96.partial = f32[256,256]{1,0:T(8,128)S(1)} custom-call(bf16[4,128,512]{2,1,0:T(8,128)(2,1)S(1)} %bitcast.3, bf16[4,128,512]{2,1,0:T(8,128)(2,1)S(1)} %collective-permute-done.4.top_other, bf16[4,128,512]{2,1,0:T(8,128)(2,1)S(1)} %bitcast.5, bf16[256,4096]{1,0:T(8,128)(2,1)S(1)} %copy-done), custom_call_target="tpu_custom_call" | custom-call | flops 402653184 | bytes 3932160 | tf_op jit(solution)/shard_map/pallas_call | solution.py:284
  82.6 0.7 collective-permute-done.5.low_other
  83.3 0.6 shard_map.97
  84.0 12.3 %collective-permute-start.6 = (bf16[272,256]{1,0:T(8,128)(2,1)S(1)}, bf16[272,256]{1,0:T(8,128)(2,1)S(1)}, u32[]{:S(2)}, u32[]{:S(2)}) collective-permute-start(bf16[272,256]{1,0:T(8,128)(2,1)S(1)} %get-tuple-element.32.grad), channel_id=1, source_target_pairs={{8,0},{16,8},{24,16},{32,24},{40,32},{48,40},{56,48},{64,56},{72,6... | collective-permute-start | bytes 417800 | tf_op jit(solution)/shard_map/ppermute | solution.py:297
  96.2 1.9 %collective-permute-start.7 = (bf16[144,256]{1,0:T(8,128)(2,1)S(1)}, bf16[144,256]{1,0:T(8,128)(2,1)S(1)}, u32[]{:S(2)}, u32[]{:S(2)}) collective-permute-start(bf16[144,256]{1,0:T(8,128)(2,1)S(1)} %get-tuple-element.38), channel_id=1, source_target_pairs={{16,0},{24,8},{32,16},{40,24},{48,32},{56,40},{64,48},{72,56},{80,... | collective-permute-start | bytes 221192 | tf_op jit(solution)/shard_map/ppermute | solution.py:297
  98.2 1.7 %shard_map.98 = (bf16[256,256]{1,0:T(8,128)(2,1)}, f32[256,256]{1,0:T(8,128)S(1)}, f32[256,256]{1,0:T(8,128)S(1)}) custom-call(f32[2,128,640]{2,1,0:T(8,128)S(1)} %get-tuple-element.23.signed_top, f32[2,128,512]{2,1,0:T(8,128)S(1)} %get-tuple-element.24.signed_low, bf16[128,256]{1,0:T(8,128)(2,1)S(1)} %get-tuple-element.27.attended_top, ...), custom_call_target="tpu_custom_call" | custom-call | flops 335544320 | bytes 2891776 | tf_op jit(solution)/shard_map/pallas_call | solution.py:284
  99.9 4.0 %collective-permute-done.7.far_grad = bf16[144,256]{1,0:T(8,128)(2,1)S(1)} collective-permute-done((bf16[144,256]{1,0:T(8,128)(2,1)S(1)}, bf16[144,256]{1,0:T(8,128)(2,1)S(1)}, u32[]{:S(2)}, u32[]{:S(2)}) %collective-permute-start.7) | collective-permute-done | bytes 73760 | tf_op jit(solution)/shard_map/ppermute | solution.py:297
  103.9 0.0 collective-permute-done.6.near_grad
  103.9 1.2 %shard_map.99 = (bf16[256,256]{1,0:T(8,128)(2,1)}, bf16[256,256]{1,0:T(8,128)(2,1)}) custom-call(f32[2,256,256]{2,1,0:T(8,128)S(1)} %get-tuple-element.34.near_scores, f32[2,256,256]{2,1,0:T(8,128)S(1)} %get-tuple-element.35.near_keeps, f32[2,128,128]{2,1,0:T(8,128)S(1)} %get-tuple-element.36.far_scores, f32[2,128,128]{2,1,0:T(8,128)S(1)} %get-tuple-element.37.far_keeps, ...), custom_call_target="tpu_custom_call" | custom-call | flops 167772160 | bytes 2637824 | tf_op jit(solution)/shard_map/pallas_call | solution.py:284
  (3 shorter events, 0.0 us)
Async XLA Ops:
  0.6 57.1 %copy-start.1 = (bf16[256,256]{1,0:T(8,128)(2,1)S(1)}, bf16[256,256]{1,0:T(8,128)(2,1)}, u32[]{:S(2)}) copy-start(bf16[256,256]{1,0:T(8,128)(2,1)} %value.7) | copy-start | bytes 393220
  0.6 57.1 %copy-start.2 = (bf16[256,256]{1,0:T(8,128)(2,1)S(1)}, bf16[256,256]{1,0:T(8,128)(2,1)}, u32[]{:S(2)}) copy-start(bf16[256,256]{1,0:T(8,128)(2,1)} %key.5) | copy-start | bytes 393220
  0.7 57.1 %copy-start.3 = (bf16[256,256]{1,0:T(8,128)(2,1)S(1)}, bf16[256,256]{1,0:T(8,128)(2,1)}, u32[]{:S(2)}) copy-start(bf16[256,256]{1,0:T(8,128)(2,1)} %query.5) | copy-start | bytes 393220
  0.7 57.1 %copy-start.4 = (s32[128,128]{1,0:T(8,128)S(1)}, s32[128,128]{1,0:T(8,128)}, u32[]{:S(2)}) copy-start(s32[128,128]{1,0:T(8,128)} %table.3) | copy-start | bytes 196612
  1.7 79.7 %copy-start = (bf16[256,4096]{1,0:T(8,128)(2,1)S(1)}, bf16[256,4096]{1,0:T(8,128)(2,1)}, u32[]{:S(2)}) copy-start(bf16[256,4096]{1,0:T(8,128)(2,1)} %weight.3) | copy-start | bytes 6291460
  1.7 35.6 %collective-permute-start = (bf16[512,256]{1,0:T(8,128)(2,1)S(1)}, bf16[512,256]{1,0:T(8,128)(2,1)S(1)}, u32[]{:S(2)}, u32[]{:S(2)}) collective-permute-start(bf16[512,256]{1,0:T(8,128)(2,1)S(1)} %pad_maximum_fusion), channel_id=1, source_target_pairs={{0,8},{8,16},{16,24},{24,32},{32,40},{40,48},{48,56},{56,64},{64,7... | collective-permute-start | bytes 786440 | tf_op jit(solution)/shard_map/ppermute | solution.py:297
  6.2 20.0 %collective-permute-start.2 = (bf16[256,256]{1,0:T(8,128)(2,1)}, bf16[256,256]{1,0:T(8,128)(2,1)S(1)}, u32[]{:S(2)}, u32[]{:S(2)}) collective-permute-start(bf16[256,256]{1,0:T(8,128)(2,1)} %query.5), channel_id=1, source_target_pairs={{8,0},{16,8},{24,16},{32,24},{40,32},{48,40},{56,48},{64,56},{72,6... | collective-permute-start | bytes 393224 | tf_op jit(solution)/shard_map/ppermute | solution.py:297
  26.1 34.5 %collective-permute-start.3 = (bf16[128,256]{1,0:T(8,128)(2,1)S(1)}, bf16[128,256]{1,0:T(8,128)(2,1)S(1)}, u32[]{:S(2)}, u32[]{:S(2)}) collective-permute-start(bf16[128,256]{1,0:T(8,128)(2,1)S(1)} %slice.22), channel_id=1, source_target_pairs={{8,0},{16,8},{24,16},{32,24},{40,32},{48,40},{56,48},{64,56},{72,6... | collective-permute-start | bytes 196616 | tf_op jit(solution)/shard_map/ppermute | solution.py:297
  37.3 23.3 %collective-permute-start.1 = (bf16[256,256]{1,0:T(8,128)(2,1)S(1)}, bf16[256,256]{1,0:T(8,128)(2,1)S(1)}, u32[]{:S(2)}, u32[]{:S(2)}) collective-permute-start(bf16[256,256]{1,0:T(8,128)(2,1)S(1)} %pad_maximum_fusion.1), channel_id=1, source_target_pairs={{0,8},{8,16},{16,24},{24,32},{32,40},{40,48},{48,56},{56,64},{64,7... | collective-permute-start | bytes 393224 | tf_op jit(solution)/shard_map/ppermute | solution.py:297
  55.2 26.3 %collective-permute-start.4 = (bf16[4,128,512]{2,1,0:T(8,128)(2,1)S(1)}, bf16[4,128,512]{2,1,0:T(8,128)(2,1)S(1)}, u32[]{:S(2)}, u32[]{:S(2)}) collective-permute-start(bf16[4,128,512]{2,1,0:T(8,128)(2,1)S(1)} %bitcast.2), channel_id=1, source_target_pairs={{0,1},{1,0},{2,3},{3,2},{4,5},{5,4},{6,7},{7,6},{8,9},{9,8},{10,11... | collective-permute-start | bytes 1572872 | tf_op jit(solution)/shard_map/ppermute | solution.py:302
  79.5 3.8 %collective-permute-start.5 = (bf16[4,128,512]{2,1,0:T(8,128)(2,1)S(1)}, bf16[4,128,512]{2,1,0:T(8,128)(2,1)S(1)}, u32[]{:S(2)}, u32[]{:S(2)}) collective-permute-start(bf16[4,128,512]{2,1,0:T(8,128)(2,1)S(1)} %bitcast.4), channel_id=1, source_target_pairs={{0,1},{1,0},{2,3},{3,2},{4,5},{5,4},{6,7},{7,6},{8,9},{9,8},{10,11... | collective-permute-start | bytes 1572872 | tf_op jit(solution)/shard_map/ppermute | solution.py:302
  84.0 19.9 %collective-permute-start.6 = (bf16[272,256]{1,0:T(8,128)(2,1)S(1)}, bf16[272,256]{1,0:T(8,128)(2,1)S(1)}, u32[]{:S(2)}, u32[]{:S(2)}) collective-permute-start(bf16[272,256]{1,0:T(8,128)(2,1)S(1)} %get-tuple-element.32.grad), channel_id=1, source_target_pairs={{8,0},{16,8},{24,16},{32,24},{40,32},{48,40},{56,48},{64,56},{72,6... | collective-permute-start | bytes 417800 | tf_op jit(solution)/shard_map/ppermute | solution.py:297
  96.2 7.6 %collective-permute-start.7 = (bf16[144,256]{1,0:T(8,128)(2,1)S(1)}, bf16[144,256]{1,0:T(8,128)(2,1)S(1)}, u32[]{:S(2)}, u32[]{:S(2)}) collective-permute-start(bf16[144,256]{1,0:T(8,128)(2,1)S(1)} %get-tuple-element.38), channel_id=1, source_target_pairs={{16,0},{24,8},{32,16},{40,24},{48,32},{56,40},{64,48},{72,56},{80,... | collective-permute-start | bytes 221192 | tf_op jit(solution)/shard_map/ppermute | solution.py:297

commit v6 on v5

--- a/solution.py
+++ b/solution.py
@@ -164,22 +164,22 @@
     return ((far, slice(0, MB)), *keys), ((far, slice(MB, None)), *values)
 
 
-def near_kernel(
-    table, seed, query, key, value, near, near_query, signed, attended, stats, scores, keeps
-):
+def near_kernel(table, seed, query, key, value, near, signed, attended, stats):
     keys, values = near_window(key, value, near)
     forward(table, seed, 1, query, stacked(*keys), stacked(*values), signed, attended, stats)
-    shard = lax.axis_index("blk")
-    later(table, seed, shard * 2 + 2, shard * 2, near_query, key, scores, keeps)
-
-
-def far_kernel(
-    table, seed, query, key, value, near, far, far_query, signed, attended, stats, scores, keeps
-):
+
+
+def far_kernel(table, seed, query, key, value, near, far, signed, attended, stats):
     keys, values = far_window(key, value, near, far)
     forward(table, seed, 0, query, stacked(*keys), stacked(*values), signed, attended, stats)
-    shard = lax.axis_index("blk")
-    later(table, seed, shard * 2 + 4, shard * 2 + 1, far_query, key.at[MB:], scores, keeps)
+
+
+def later_kernel(
+    table, seed, key, near_query, far_query, near_scores, near_keeps, far_scores, far_keeps
+):
+    block = lax.axis_index("blk") * 2
+    later(table, seed, block + 2, block, near_query, key, near_scores, near_keeps)
+    later(table, seed, block + 4, block + 1, far_query, key.at[MB:], far_scores, far_keeps)
 
 
 def project(total, gathered, weight, core):
@@ -277,10 +277,11 @@
         grad_value[MB:, cols] = bf16(values[MB:] + far_values)
 
 
-def call(kernel, specs, outs, flops, *args):
+def call(kernel, specs, outs, microseconds, *args):
     shapes = [jax.ShapeDtypeStruct(shape, dtype) for shape, dtype in outs]
     moved = sum(a.size * a.dtype.itemsize for a in args)
     moved += sum(s.size * s.dtype.itemsize for s in shapes)
+    flops = int(microseconds * 1.15e9)
     return pl.pallas_call(
         kernel,
         out_shape=shapes,
@@ -305,52 +306,43 @@
 def on_device(query_rows, key_rows, value_rows, grad_out, out_weight, mask_types, drop_seed):
     half, full = jnp.bfloat16, jnp.float32
     count = lax.axis_size("head")
-    parts, width = count // 2, grad_out.shape[1]
     groups = [list(range(first, count, 2)) for first in range(2)]
 
     def gather(rows):
         return lax.all_gather(rows, "head", axis=0, axis_index_groups=groups)
 
     near_keys = shifted(jnp.concatenate((key_rows, value_rows)), 1)
-    near_query = shifted(query_rows, -1)
     top = gather(grad_out[:MB])
+    top, sent_query = lax.optimization_barrier((top, query_rows))
+    near_query = shifted(sent_query, -1)
+    far_query = shifted(sent_query[:MB], -2)
+    top, near_keys = lax.optimization_barrier((top, near_keys))
     top_other = other_core(top)
     far_keys = shifted(jnp.concatenate((near_keys[MB:ROWS], near_keys[ROWS + MB :])), 1)
-    far_query = shifted(near_query[:MB], -1)
-    tile = 2 * MB * MB * DH
-
-    def outs(width, keys, queries):
-        return [
-            ((HEADS, MB, width), full),
-            ((MB, WIDE), half),
-            ((MB, MB), full),
-            ((HEADS, keys, queries), full),
-            ((HEADS, keys, queries), full),
-        ]
-
-    signed_low, attended_low, stats_low, near_scores, near_keeps = call(
-        near_kernel, [SMEM, SMEM] + [VMEM] * 5, outs(WIN - MB, ROWS, ROWS), 48 * tile,
-        mask_types, drop_seed, query_rows, key_rows, value_rows, near_keys, near_query,
-    )
-    signed_top, attended_top, stats_top, far_scores, far_keeps = call(
-        far_kernel, [SMEM, SMEM] + [VMEM] * 6, outs(WIN, MB, MB), 48 * tile,
-        mask_types, drop_seed, query_rows, key_rows, value_rows, near_keys, far_keys, far_query,
-    )
-    low_rows, attended_top, attended_low = lax.optimization_barrier(
-        (grad_out[MB:], attended_top, attended_low)
-    )
+    low_rows, near_keys = lax.optimization_barrier((grad_out[MB:], near_keys))
     low = gather(low_rows)
+    low, near_keys = lax.optimization_barrier((low, near_keys))
     low_other = other_core(low)
-    flops = 2 * MB * WIDE * width * parts
+
+    def outs(keys):
+        return [((HEADS, MB, keys), full), ((MB, WIDE), half), ((MB, MB), full)]
+
+    signed_low, attended_low, stats_low = call(
+        near_kernel, [SMEM, SMEM] + [VMEM] * 4, outs(WIN - MB), 1.8,
+        mask_types, drop_seed, query_rows, key_rows, value_rows, near_keys,
+    )
+    signed_top, attended_top, stats_top = call(
+        far_kernel, [SMEM, SMEM] + [VMEM] * 5, outs(WIN), 2.0,
+        mask_types, drop_seed, query_rows, key_rows, value_rows, near_keys, far_keys,
+    )
     (partial,) = call(
-        project_kernel, [VMEM] * 4, [((ROWS, WIDE), full)], 3 * flops,
-        top, top_other, low, out_weight,
+        project_kernel, [VMEM] * 4, [((ROWS, WIDE), full)], 1.2, top, top_other, low, out_weight
     )
     near_rows, far_rows = call(
         rows_kernel,
         [VMEM] * 7,
         [((ROWS + EXTRA, WIDE), half), ((MB + EXTRA, WIDE), half)],
-        flops,
+        0.7,
         partial, low_other, out_weight, attended_top, attended_low, stats_top, stats_low,
     )
     near_grad = shifted(near_rows, -1)
@@ -359,17 +351,22 @@
         own_kernel,
         [VMEM] * 10,
         [((ROWS, WIDE), half), ((ROWS, WIDE), full), ((ROWS, WIDE), full)],
-        80 * tile,
+        1.7,
         signed_top, signed_low, attended_top, attended_low, query_rows, near_rows, key_rows,
         value_rows, near_keys, far_keys,
+    )
+    later_key, _ = lax.optimization_barrier((key_rows, near_rows))
+    scores = call(
+        later_kernel, [SMEM, SMEM] + [VMEM] * 3,
+        [((HEADS, ROWS, ROWS), full)] * 2 + [((HEADS, MB, MB), full)] * 2, 2.0,
+        mask_types, drop_seed, later_key, near_query, far_query,
     )
     grad_key, grad_value = call(
         finish_kernel,
         [VMEM] * 11,
         [((ROWS, WIDE), half), ((ROWS, WIDE), half)],
-        40 * tile,
-        near_scores, near_keeps, far_scores, far_keeps, value_rows, near_query, far_query,
-        near_grad, far_grad, key_part, value_part,
+        1.3,
+        *scores, value_rows, near_query, far_query, near_grad, far_grad, key_part, value_part,
     )
     return (grad_query, grad_key, grad_value)
 

time: 106 us -> 99.2 us (0.936)
  the two profiles are of different devices: /device:TPU:6 before, /device:TPU:5 now
where the time goes in v6:
time: 99.2 us; the launch traced here: 98.8 us
  starting transfers between devices  48.9 us (49%)
  blocking collectives  28.8 us (29%)
  Pallas kernels  12.2 us (12%)
  waiting for transfers between devices  4.48 us (5%)
  local copies, waits for them, and re-layouts  1.88 us (2%)
  between operations  1.52 us (2%)
  other arithmetic  1.06 us (1%)
    ppermute x6, starting transfers between devices, shifted(): return lax.ppermute(value, 'blk', pairs)  40.3 us
    all_gather x2, blocking collectives, gather(): return lax.all_gather(rows, 'head', axis=0, axis_index_groups=groups)  28.8 us
    pallas_call x7, Pallas kernels, call(): pl.pallas_call(kernel, out_shape=shapes, in_specs=specs, out_specs=[VMEM]...  12.2 us
    ppermute x2, starting transfers between devices, other_core(): lax.ppermute(value, 'head', [(source, source ^ 1) for source in range(cou...  8.57 us
    ppermute x6, waiting for transfers between devices, shifted(): return lax.ppermute(value, 'blk', pairs)  4.48 us
  transfers between devices with their start and end apart: 8, of which 1 were waited for; matrix products, arithmetic and copies ran while one was open for 2% of the time, Pallas kernels for 11%

profile of v6, /device:TPU:5, one launch (start us, length us, event | category | flops | bytes accessed | tf_op | source)
XLA Modules:
  0.0 98.8 jit_solution(16804693272581638309)
XLA Ops:
  0.6 0.0 copy-start.2
  0.6 0.0 copy-start.1
  0.7 0.0 copy-start.3
  0.7 0.0 copy-start.4
  0.7 1.0 %pad_maximum_fusion = bf16[512,256]{1,0:T(8,128)(2,1)S(1)} fusion(bf16[256,256]{1,0:T(8,128)(2,1)} %value.7, bf16[256,256]{1,0:T(8,128)(2,1)} %key.6), kind=kLoop, calls=%fused_computation | loop fusion | flops 524288 | bytes 524288 | tf_op jit(solution)/shard_map/concatenate | solution.py:314
  1.7 4.0 %collective-permute-start = (bf16[512,256]{1,0:T(8,128)(2,1)S(1)}, bf16[512,256]{1,0:T(8,128)(2,1)S(1)}, u32[]{:S(2)}, u32[]{:S(2)}) collective-permute-start(bf16[512,256]{1,0:T(8,128)(2,1)S(1)} %pad_maximum_fusion), channel_id=1, source_target_pairs={{0,8},{8,16},{16,24},{24,32},{32,40},{40,48},{48,56},{56,64},{64,7... | collective-permute-start | bytes 786440 | tf_op jit(solution)/shard_map/ppermute | solution.py:298
  5.7 1.0 fusion.1
  6.7 14.2 %all-gather = bf16[512,512]{1,0:T(8,128)(2,1)S(1)} all-gather(bf16[128,512]{1,0:T(8,128)(2,1)S(1)} %get-tuple-element.57), channel_id=2, replica_groups={{0,2,4,6},{1,3,5,7},{8,10,12,14},{9,11,13,15},{16,18,20,22},{17,19,21,2..., dimensions={0}, use_global_device_ids=true | all-gather | bytes 655360 | tf_op jit(solution)/shard_map/all_gather | solution.py:312
  20.9 20.3 %collective-permute-start.4 = (bf16[256,256]{1,0:T(8,128)(2,1)}, bf16[256,256]{1,0:T(8,128)(2,1)S(1)}, u32[]{:S(2)}, u32[]{:S(2)}) collective-permute-start(bf16[256,256]{1,0:T(8,128)(2,1)} %query.5), channel_id=1, source_target_pairs={{8,0},{16,8},{24,16},{32,24},{40,32},{48,40},{56,48},{64,56},{72,6... | collective-permute-start | bytes 393224 | tf_op jit(solution)/shard_map/ppermute | solution.py:298
  41.3 0.9 slice.19
  42.1 1.9 %collective-permute-start.5 = (bf16[128,256]{1,0:T(8,128)(2,1)S(1)}, bf16[128,256]{1,0:T(8,128)(2,1)S(1)}, u32[]{:S(2)}, u32[]{:S(2)}) collective-permute-start(bf16[128,256]{1,0:T(8,128)(2,1)S(1)} %slice.19), channel_id=1, source_target_pairs={{16,0},{24,8},{32,16},{40,24},{48,32},{56,40},{64,48},{72,56},{80,... | collective-permute-start | bytes 196616 | tf_op jit(solution)/shard_map/ppermute | solution.py:298
  44.7 0.0 collective-permute-done.near
  44.7 3.1 %collective-permute-start.1 = (bf16[256,256]{1,0:T(8,128)(2,1)S(1)}, bf16[256,256]{1,0:T(8,128)(2,1)S(1)}, u32[]{:S(2)}, u32[]{:S(2)}) collective-permute-start(bf16[256,256]{1,0:T(8,128)(2,1)S(1)} %pad_maximum_fusion.1), channel_id=1, source_target_pairs={{0,8},{8,16},{16,24},{24,32},{32,40},{40,48},{48,56},{56,64},{64,7... | collective-permute-start | bytes 393224 | tf_op jit(solution)/shard_map/ppermute | solution.py:298
  47.8 5.4 %collective-permute-start.2 = (bf16[4,128,512]{2,1,0:T(8,128)(2,1)S(1)}, bf16[4,128,512]{2,1,0:T(8,128)(2,1)S(1)}, u32[]{:S(2)}, u32[]{:S(2)}) collective-permute-start(bf16[4,128,512]{2,1,0:T(8,128)(2,1)S(1)} %bitcast.2), channel_id=1, source_target_pairs={{0,1},{1,0},{2,3},{3,2},{4,5},{5,4},{6,7},{7,6},{8,9},{9,8},{10,11... | collective-permute-start | bytes 1572872 | tf_op jit(solution)/shard_map/ppermute | solution.py:303
  53.2 14.5 %all-gather.1 = bf16[512,512]{1,0:T(8,128)(2,1)S(1)} all-gather(bf16[128,512]{1,0:T(8,128)(2,1)S(1)} %get-tuple-element.31), channel_id=3, replica_groups={{0,2,4,6},{1,3,5,7},{8,10,12,14},{9,11,13,15},{16,18,20,22},{17,19,21,2..., dimensions={0}, use_global_device_ids=true | all-gather | bytes 655360 | tf_op jit(solution)/shard_map/all_gather | solution.py:312
  67.8 3.2 %collective-permute-start.3 = (bf16[4,128,512]{2,1,0:T(8,128)(2,1)S(1)}, bf16[4,128,512]{2,1,0:T(8,128)(2,1)S(1)}, u32[]{:S(2)}, u32[]{:S(2)}) collective-permute-start(bf16[4,128,512]{2,1,0:T(8,128)(2,1)S(1)} %bitcast.4), channel_id=1, source_target_pairs={{0,1},{1,0},{2,3},{3,2},{4,5},{5,4},{6,7},{7,6},{8,9},{9,8},{10,11... | collective-permute-start | bytes 1572872 | tf_op jit(solution)/shard_map/ppermute | solution.py:303
  71.0 0.0 copy-done.2
  71.0 0.0 copy-done.1
  71.0 0.0 copy-done.3
  71.0 0.0 copy-done.4
  71.0 2.6 %shard_map.95 = (f32[2,128,512]{2,1,0:T(8,128)S(1)}, bf16[128,256]{1,0:T(8,128)(2,1)S(1)}, f32[128,128]{1,0:T(8,128)S(1)}) custom-call(s32[128,128]{1,0:T(8,128)S(1)} %copy-done.4, s32[1]{0:T(128)S(6)} %copy.10.seed, bf16[256,256]{1,0:T(8,128)(2,1)S(1)} %copy-done.3, bf16[256,256]{1,0:T(8,128)(2,1)S(1)} %copy-done.1, bf16[256,256]{1,0:T(8,128)(2,1)S(1)} %copy-done.2, ...), custom_call_target="tpu_custom_call" | custom-call | flops 2070000000 | bytes 1376260 | tf_op jit(solution)/shard_map/pallas_call | solution.py:285
  73.6 0.0 copy-start
  73.6 0.0 collective-permute-done.1.far
  73.6 2.7 %shard_map.94 = (f32[2,128,640]{2,1,0:T(8,128)S(1)}, bf16[128,256]{1,0:T(8,128)(2,1)S(1)}, f32[128,128]{1,0:T(8,128)S(1)}) custom-call(s32[128,128]{1,0:T(8,128)S(1)} %copy-done.4, s32[1]{0:T(128)S(6)} %copy.10.seed, bf16[256,256]{1,0:T(8,128)(2,1)S(1)} %copy-done.3, bf16[256,256]{1,0:T(8,128)(2,1)S(1)} %copy-done.1, bf16[256,256]{1,0:T(8,128)(2,1)S(1)} %copy-done.2, ...), custom_call_target="tpu_custom_call" | custom-call | flops 2300000000 | bytes 1638404 | tf_op jit(solution)/shard_map/pallas_call | solution.py:285
  76.4 0.0 collective-permute-done.2.top_other
  76.4 0.0 copy-done
  76.4 1.2 %shard_map.96.partial = f32[256,256]{1,0:T(8,128)S(1)} custom-call(bf16[4,128,512]{2,1,0:T(8,128)(2,1)S(1)} %bitcast.3, bf16[4,128,512]{2,1,0:T(8,128)(2,1)S(1)} %collective-permute-done.2.top_other, bf16[4,128,512]{2,1,0:T(8,128)(2,1)S(1)} %bitcast.5, bf16[256,4096]{1,0:T(8,128)(2,1)S(1)} %copy-done), custom_call_target="tpu_custom_call" | custom-call | flops 1380000000 | bytes 3932160 | tf_op jit(solution)/shard_map/pallas_call | solution.py:285
  77.6 0.0 collective-permute-done.3.low_other
  77.6 0.7 shard_map.97
  78.3 9.1 %collective-permute-start.6 = (bf16[272,256]{1,0:T(8,128)(2,1)S(1)}, bf16[272,256]{1,0:T(8,128)(2,1)S(1)}, u32[]{:S(2)}, u32[]{:S(2)}) collective-permute-start(bf16[272,256]{1,0:T(8,128)(2,1)S(1)} %get-tuple-element.42.grad), channel_id=1, source_target_pairs={{8,0},{16,8},{24,16},{32,24},{40,32},{48,40},{56,48},{64,56},{72,6... | collective-permute-start | bytes 417800 | tf_op jit(solution)/shard_map/ppermute | solution.py:298
  87.4 1.9 %collective-permute-start.7 = (bf16[144,256]{1,0:T(8,128)(2,1)S(1)}, bf16[144,256]{1,0:T(8,128)(2,1)S(1)}, u32[]{:S(2)}, u32[]{:S(2)}) collective-permute-start(bf16[144,256]{1,0:T(8,128)(2,1)S(1)} %get-tuple-element.50), channel_id=1, source_target_pairs={{16,0},{24,8},{32,16},{40,24},{48,32},{56,40},{64,48},{72,56},{80,... | collective-permute-start | bytes 221192 | tf_op jit(solution)/shard_map/ppermute | solution.py:298
  89.3 0.0 collective-permute-done.5.far_query
  89.3 0.0 collective-permute-done.4.near_query
  89.3 2.1 %shard_map.99 = (f32[2,256,256]{2,1,0:T(8,128)S(1)}, f32[2,256,256]{2,1,0:T(8,128)S(1)}, f32[2,128,128]{2,1,0:T(8,128)S(1)}, f32[2,128,128]{2,1,0:T(8,128)S(1)}) custom-call(s32[128,128]{1,0:T(8,128)S(1)} %copy-done.4, s32[1]{0:T(128)S(6)} %copy.10.seed, bf16[256,256]{1,0:T(8,128)(2,1)S(1)} %copy-done.1, ...), custom_call_target="tpu_custom_call" | custom-call | flops 2300000000 | bytes 1703940 | tf_op jit(solution)/shard_map/pallas_call | solution.py:285
  91.4 1.7 %shard_map.98 = (bf16[256,256]{1,0:T(8,128)(2,1)}, f32[256,256]{1,0:T(8,128)S(1)}, f32[256,256]{1,0:T(8,128)S(1)}) custom-call(f32[2,128,640]{2,1,0:T(8,128)S(1)} %get-tuple-element.34.signed_top, f32[2,128,512]{2,1,0:T(8,128)S(1)} %get-tuple-element.35.signed_low, bf16[128,256]{1,0:T(8,128)(2,1)S(1)} %get-tuple-element.36.attended_top, ...), custom_call_target="tpu_custom_call" | custom-call | flops 1955000064 | bytes 2891776 | tf_op jit(solution)/shard_map/pallas_call | solution.py:285
  93.1 4.5 %collective-permute-done.7.far_grad = bf16[144,256]{1,0:T(8,128)(2,1)S(1)} collective-permute-done((bf16[144,256]{1,0:T(8,128)(2,1)S(1)}, bf16[144,256]{1,0:T(8,128)(2,1)S(1)}, u32[]{:S(2)}, u32[]{:S(2)}) %collective-permute-start.7) | collective-permute-done | bytes 73760 | tf_op jit(solution)/shard_map/ppermute | solution.py:298
  97.6 0.0 collective-permute-done.6.near_grad
  97.6 1.3 %shard_map.100 = (bf16[256,256]{1,0:T(8,128)(2,1)}, bf16[256,256]{1,0:T(8,128)(2,1)}) custom-call(f32[2,256,256]{2,1,0:T(8,128)S(1)} %get-tuple-element.46.near_scores, f32[2,256,256]{2,1,0:T(8,128)S(1)} %get-tuple-element.47.near_keeps, f32[2,128,128]{2,1,0:T(8,128)S(1)} %get-tuple-element.48.far_scores, f32[2,128,128]{2,1,0:T(8,128)S(1)} %get-tuple-element.49.far_keeps, ...), custom_call_target="tpu_custom_call" | custom-call | flops 1495000064 | bytes 2637824 | tf_op jit(solution)/shard_map/pallas_call | solution.py:285
  (2 shorter events, 0.0 us)
Async XLA Ops:
  0.6 70.3 %copy-start.2 = (bf16[256,256]{1,0:T(8,128)(2,1)S(1)}, bf16[256,256]{1,0:T(8,128)(2,1)}, u32[]{:S(2)}) copy-start(bf16[256,256]{1,0:T(8,128)(2,1)} %value.7) | copy-start | bytes 393220
  0.6 70.3 %copy-start.1 = (bf16[256,256]{1,0:T(8,128)(2,1)S(1)}, bf16[256,256]{1,0:T(8,128)(2,1)}, u32[]{:S(2)}) copy-start(bf16[256,256]{1,0:T(8,128)(2,1)} %key.6) | copy-start | bytes 393220
  0.7 70.3 %copy-start.3 = (bf16[256,256]{1,0:T(8,128)(2,1)S(1)}, bf16[256,256]{1,0:T(8,128)(2,1)}, u32[]{:S(2)}) copy-start(bf16[256,256]{1,0:T(8,128)(2,1)} %query.5) | copy-start | bytes 393220
  0.7 70.3 %copy-start.4 = (s32[128,128]{1,0:T(8,128)S(1)}, s32[128,128]{1,0:T(8,128)}, u32[]{:S(2)}) copy-start(s32[128,128]{1,0:T(8,128)} %table.5) | copy-start | bytes 196612
  1.7 43.0 %collective-permute-start = (bf16[512,256]{1,0:T(8,128)(2,1)S(1)}, bf16[512,256]{1,0:T(8,128)(2,1)S(1)}, u32[]{:S(2)}, u32[]{:S(2)}) collective-permute-start(bf16[512,256]{1,0:T(8,128)(2,1)S(1)} %pad_maximum_fusion), channel_id=1, source_target_pairs={{0,8},{8,16},{16,24},{24,32},{32,40},{40,48},{48,56},{56,64},{64,7... | collective-permute-start | bytes 786440 | tf_op jit(solution)/shard_map/ppermute | solution.py:298
  20.9 68.4 %collective-permute-start.4 = (bf16[256,256]{1,0:T(8,128)(2,1)}, bf16[256,256]{1,0:T(8,128)(2,1)S(1)}, u32[]{:S(2)}, u32[]{:S(2)}) collective-permute-start(bf16[256,256]{1,0:T(8,128)(2,1)} %query.5), channel_id=1, source_target_pairs={{8,0},{16,8},{24,16},{32,24},{40,32},{48,40},{56,48},{64,56},{72,6... | collective-permute-start | bytes 393224 | tf_op jit(solution)/shard_map/ppermute | solution.py:298
  42.1 47.2 %collective-permute-start.5 = (bf16[128,256]{1,0:T(8,128)(2,1)S(1)}, bf16[128,256]{1,0:T(8,128)(2,1)S(1)}, u32[]{:S(2)}, u32[]{:S(2)}) collective-permute-start(bf16[128,256]{1,0:T(8,128)(2,1)S(1)} %slice.19), channel_id=1, source_target_pairs={{16,0},{24,8},{32,16},{40,24},{48,32},{56,40},{64,48},{72,56},{80,... | collective-permute-start | bytes 196616 | tf_op jit(solution)/shard_map/ppermute | solution.py:298
  44.7 28.9 %collective-permute-start.1 = (bf16[256,256]{1,0:T(8,128)(2,1)S(1)}, bf16[256,256]{1,0:T(8,128)(2,1)S(1)}, u32[]{:S(2)}, u32[]{:S(2)}) collective-permute-start(bf16[256,256]{1,0:T(8,128)(2,1)S(1)} %pad_maximum_fusion.1), channel_id=1, source_target_pairs={{0,8},{8,16},{16,24},{24,32},{32,40},{40,48},{48,56},{56,64},{64,7... | collective-permute-start | bytes 393224 | tf_op jit(solution)/shard_map/ppermute | solution.py:298
  47.8 28.5 %collective-permute-start.2 = (bf16[4,128,512]{2,1,0:T(8,128)(2,1)S(1)}, bf16[4,128,512]{2,1,0:T(8,128)(2,1)S(1)}, u32[]{:S(2)}, u32[]{:S(2)}) collective-permute-start(bf16[4,128,512]{2,1,0:T(8,128)(2,1)S(1)} %bitcast.2), channel_id=1, source_target_pairs={{0,1},{1,0},{2,3},{3,2},{4,5},{5,4},{6,7},{7,6},{8,9},{9,8},{10,11... | collective-permute-start | bytes 1572872 | tf_op jit(solution)/shard_map/ppermute | solution.py:303
  67.8 9.8 %collective-permute-start.3 = (bf16[4,128,512]{2,1,0:T(8,128)(2,1)S(1)}, bf16[4,128,512]{2,1,0:T(8,128)(2,1)S(1)}, u32[]{:S(2)}, u32[]{:S(2)}) collective-permute-start(bf16[4,128,512]{2,1,0:T(8,128)(2,1)S(1)} %bitcast.4), channel_id=1, source_target_pairs={{0,1},{1,0},{2,3},{3,2},{4,5},{5,4},{6,7},{7,6},{8,9},{9,8},{10,11... | collective-permute-start | bytes 1572872 | tf_op jit(solution)/shard_map/ppermute | solution.py:303
  73.6 2.8 %copy-start = (bf16[256,4096]{1,0:T(8,128)(2,1)S(1)}, bf16[256,4096]{1,0:T(8,128)(2,1)}, u32[]{:S(2)}) copy-start(bf16[256,4096]{1,0:T(8,128)(2,1)} %weight.3) | copy-start | bytes 6291460
  78.3 19.3 %collective-permute-start.6 = (bf16[272,256]{1,0:T(8,128)(2,1)S(1)}, bf16[272,256]{1,0:T(8,128)(2,1)S(1)}, u32[]{:S(2)}, u32[]{:S(2)}) collective-permute-start(bf16[272,256]{1,0:T(8,128)(2,1)S(1)} %get-tuple-element.42.grad), channel_id=1, source_target_pairs={{8,0},{16,8},{24,16},{32,24},{40,32},{48,40},{56,48},{64,56},{72,6... | collective-permute-start | bytes 417800 | tf_op jit(solution)/shard_map/ppermute | solution.py:298
  87.4 10.2 %collective-permute-start.7 = (bf16[144,256]{1,0:T(8,128)(2,1)S(1)}, bf16[144,256]{1,0:T(8,128)(2,1)S(1)}, u32[]{:S(2)}, u32[]{:S(2)}) collective-permute-start(bf16[144,256]{1,0:T(8,128)(2,1)S(1)} %get-tuple-element.50), channel_id=1, source_target_pairs={{16,0},{24,8},{32,16},{40,24},{48,32},{56,40},{64,48},{72,56},{80,... | collective-permute-start | bytes 221192 | tf_op jit(solution)/shard_map/ppermute | solution.py:298

commit v7 on v6

--- a/solution.py
+++ b/solution.py
@@ -191,20 +191,18 @@
     return total
 
 
-def project_kernel(top, top_other, low, weight, out):
-    core = lax.rem(lax.axis_index("head"), 2)
-    out[0:MB] = project(project(None, top, weight, core), top_other, weight, 1 - core)
-    out[MB:] = project(None, low, weight, core)
+def project_kernel(gathered, weight, out):
+    out[...] = project(None, gathered, weight, lax.rem(lax.axis_index("head"), 2))
 
 
 def rows_kernel(
-    partial, low_other, weight, attended_top, attended_low, stats_top, stats_low, near, far
+    partial, other, weight, attended_top, attended_low, stats_top, stats_low, near, far
 ):
     core = lax.rem(lax.axis_index("head"), 2)
-    low = project(partial[MB:], low_other, weight, 1 - core)
+    whole = project(partial[...], other, weight, 1 - core)
     lane = lax.broadcasted_iota(jnp.int32, (MB, MB), 1)
     for block, total, attended, stats in (
-        (0, partial[0:MB], attended_top, stats_top), (1, low, attended_low, stats_low)
+        (0, whole[0:MB], attended_top, stats_top), (1, whole[MB:], attended_low, stats_low)
     ):
         rows = slice(block * MB, (block + 1) * MB)
         grad = bf16(total)
@@ -308,21 +306,12 @@
     count = lax.axis_size("head")
     groups = [list(range(first, count, 2)) for first in range(2)]
 
-    def gather(rows):
-        return lax.all_gather(rows, "head", axis=0, axis_index_groups=groups)
-
+    copies = jnp.broadcast_to(grad_out[None], (count // 2, *grad_out.shape))
+    gathered = lax.all_to_all(copies, "head", 0, 0, axis_index_groups=groups)
     near_keys = shifted(jnp.concatenate((key_rows, value_rows)), 1)
-    top = gather(grad_out[:MB])
-    top, sent_query = lax.optimization_barrier((top, query_rows))
-    near_query = shifted(sent_query, -1)
-    far_query = shifted(sent_query[:MB], -2)
-    top, near_keys = lax.optimization_barrier((top, near_keys))
-    top_other = other_core(top)
-    far_keys = shifted(jnp.concatenate((near_keys[MB:ROWS], near_keys[ROWS + MB :])), 1)
-    low_rows, near_keys = lax.optimization_barrier((grad_out[MB:], near_keys))
-    low = gather(low_rows)
-    low, near_keys = lax.optimization_barrier((low, near_keys))
-    low_other = other_core(low)
+    near_query = shifted(query_rows, -1)
+    far_keys = shifted(jnp.concatenate((key_rows[MB:], value_rows[MB:])), 2)
+    far_query = shifted(query_rows[:MB], -2)
 
     def outs(keys):
         return [((HEADS, MB, keys), full), ((MB, WIDE), half), ((MB, MB), full)]
@@ -335,15 +324,19 @@
         far_kernel, [SMEM, SMEM] + [VMEM] * 5, outs(WIN), 2.0,
         mask_types, drop_seed, query_rows, key_rows, value_rows, near_keys, far_keys,
     )
+    gathered, attended_low, attended_top, near_query, far_query = lax.optimization_barrier(
+        (gathered, attended_low, attended_top, near_query, far_query)
+    )
+    other = other_core(gathered)
     (partial,) = call(
-        project_kernel, [VMEM] * 4, [((ROWS, WIDE), full)], 1.2, top, top_other, low, out_weight
+        project_kernel, [VMEM] * 2, [((ROWS, WIDE), full)], 0.7, gathered, out_weight
     )
     near_rows, far_rows = call(
         rows_kernel,
         [VMEM] * 7,
         [((ROWS + EXTRA, WIDE), half), ((MB + EXTRA, WIDE), half)],
-        0.7,
-        partial, low_other, out_weight, attended_top, attended_low, stats_top, stats_low,
+        1.0,
+        partial, other, out_weight, attended_top, attended_low, stats_top, stats_low,
     )
     near_grad = shifted(near_rows, -1)
     far_grad = shifted(far_rows, -2)

time: 99.2 us -> 84.9 us (0.86)
  the two profiles are of different devices: /device:TPU:5 before, /device:TPU:6 now
where the time goes in v7:
time: 84.9 us; the launch traced here: 83.9 us
  starting transfers between devices  36.2 us (43%)
  waiting for transfers between devices  26.5 us (31%)
  Pallas kernels  12.4 us (15%)
  local copies, waits for them, and re-layouts  7.19 us (8%)
  between operations  1.61 us (2%)
    ppermute x6, starting transfers between devices, shifted(): return lax.ppermute(value, 'blk', pairs)  29.2 us
    ppermute x6, waiting for transfers between devices, shifted(): return lax.ppermute(value, 'blk', pairs)  24.4 us
    pallas_call x7, Pallas kernels, call(): pl.pallas_call(kernel, out_shape=shapes, in_specs=specs, out_specs=[VMEM]...  12.4 us
    all_to_all x1, starting transfers between devices, on_device(): gathered = lax.all_to_all(copies, 'head', 0, 0, axis_index_groups=groups)  4.87 us
    unnamed x46, local copies, waits for them, and re-layouts  4.24 us
    ppermute x1, waiting for transfers between devices, other_core(): lax.ppermute(value, 'head', [(source, source ^ 1) for source in range(cou...  2.13 us
    broadcast_in_dim x1, local copies, waits for them, and re-layouts, on_device(): copies = jnp.broadcast_to(grad_out[None], (count // 2, *grad_out.shape))  2.09 us
    ppermute x1, starting transfers between devices, other_core(): lax.ppermute(value, 'head', [(source, source ^ 1) for source in range(cou...  2.05 us
  transfers between devices with their start and end apart: 8, of which 4 were waited for; matrix products, arithmetic and copies ran while one was open for 1% of the time, Pallas kernels for 12%

profile of v7, /device:TPU:6, one launch (start us, length us, event | category | flops | bytes accessed | tf_op | source)
XLA Modules:
  0.0 83.9 jit_solution(11351149802169013569)
XLA Ops:
  0.6 0.0 copy-start.1
  0.6 0.0 slice-start
  0.7 0.0 copy-start.2
  0.7 0.0 slice-start.1
  0.7 0.0 copy-start.9
  0.7 2.1 %broadcast_in_dim.2 = bf16[4,256,512]{2,1,0:T(8,128)(2,1)} broadcast(bf16[256,512]{1,0:T(8,128)(2,1)} %param.10), dimensions={1,2} | broadcast | bytes 1310720 | tf_op jit(solution)/shard_map/broadcast_in_dim | solution.py:309
  2.8 4.9 %all-to-all-start = ((bf16[4,256,512]{2,1,0:T(8,128)(2,1)}), bf16[4,256,512]{2,1,0:T(8,128)(2,1)S(1)}, u32[]{:S(2)}, u32[]{:S(2)}) async-start(bf16[4,256,512]{2,1,0:T(8,128)(2,1)} %broadcast_in_dim.2), calls=%async_computation | async-start | bytes 2097152 | tf_op jit(solution)/shard_map/all_to_all | solution.py:310
  7.6 0.0 copy-done.1
  7.7 4.3 %collective-permute-start = (bf16[512,256]{1,0:T(8,128)(2,1)S(1)}, bf16[512,256]{1,0:T(8,128)(2,1)S(1)}, u32[]{:S(2)}, u32[]{:S(2)}) collective-permute-start(bf16[512,256]{1,0:T(8,128)(2,1)S(1)} %pad_maximum_fusion), channel_id=1, source_target_pairs={{0,8},{8,16},{16,24},{24,32},{32,40},{40,48},{48,56},{56,64},{64,7... | collective-permute-start | bytes 786440 | tf_op jit(solution)/shard_map/ppermute | solution.py:296
  12.0 6.1 %collective-permute-start.1 = (bf16[256,256]{1,0:T(8,128)(2,1)S(1)}, bf16[256,256]{1,0:T(8,128)(2,1)S(1)}, u32[]{:S(2)}, u32[]{:S(2)}) collective-permute-start(bf16[256,256]{1,0:T(8,128)(2,1)S(1)} %pad_maximum_fusion.1), channel_id=1, source_target_pairs={{0,16},{8,24},{16,32},{24,40},{32,48},{40,56},{48,64},{56,72},{64,... | collective-permute-start | bytes 393224 | tf_op jit(solution)/shard_map/ppermute | solution.py:296
  18.1 8.6 %collective-permute-start.2 = (bf16[256,256]{1,0:T(8,128)(2,1)}, bf16[256,256]{1,0:T(8,128)(2,1)S(1)}, u32[]{:S(2)}, u32[]{:S(2)}) collective-permute-start(bf16[256,256]{1,0:T(8,128)(2,1)} %query.5), channel_id=1, source_target_pairs={{8,0},{16,8},{24,16},{32,24},{40,32},{48,40},{56,48},{64,56},{72,6... | collective-permute-start | bytes 393224 | tf_op jit(solution)/shard_map/ppermute | solution.py:296
  26.7 0.9 %slice.11 = bf16[128,256]{1,0:T(8,128)(2,1)S(1)} slice(bf16[256,256]{1,0:T(8,128)(2,1)} %query.5), slice={[0:128], [0:256]} | slice | bytes 131072 | tf_op jit(solution)/shard_map/slice | solution.py:314
  27.6 4.8 %collective-permute-start.3 = (bf16[128,256]{1,0:T(8,128)(2,1)S(1)}, bf16[128,256]{1,0:T(8,128)(2,1)S(1)}, u32[]{:S(2)}, u32[]{:S(2)}) collective-permute-start(bf16[128,256]{1,0:T(8,128)(2,1)S(1)} %slice.11), channel_id=1, source_target_pairs={{16,0},{24,8},{32,16},{40,24},{48,32},{56,40},{64,48},{72,56},{80,... | collective-permute-start | bytes 196616 | tf_op jit(solution)/shard_map/ppermute | solution.py:296
  33.0 0.0 copy-start.10
  33.1 11.6 %collective-permute-done.1.far = bf16[256,256]{1,0:T(8,128)(2,1)S(1)} collective-permute-done((bf16[256,256]{1,0:T(8,128)(2,1)S(1)}, bf16[256,256]{1,0:T(8,128)(2,1)S(1)}, u32[]{:S(2)}, u32[]{:S(2)}) %collective-permute-start.1) | collective-permute-done | bytes 131104 | tf_op jit(solution)/shard_map/ppermute | solution.py:296
  44.7 9.4 %collective-permute-done.near = bf16[512,256]{1,0:T(8,128)(2,1)S(1)} collective-permute-done((bf16[512,256]{1,0:T(8,128)(2,1)S(1)}, bf16[512,256]{1,0:T(8,128)(2,1)S(1)}, u32[]{:S(2)}, u32[]{:S(2)}) %collective-permute-start) | collective-permute-done | bytes 262176 | tf_op jit(solution)/shard_map/ppermute | solution.py:296
  54.0 0.0 copy-done.9
  54.0 2.7 %shard_map.94 = (f32[2,128,640]{2,1,0:T(8,128)S(1)}, bf16[128,256]{1,0:T(8,128)(2,1)S(1)}, f32[128,128]{1,0:T(8,128)S(1)}) custom-call(s32[128,128]{1,0:T(8,128)S(1)} %copy-done.9, s32[1]{0:T(128)S(6)} %copy.10.seed, bf16[256,256]{1,0:T(8,128)(2,1)} %query.5, bf16[256,256]{1,0:T(8,128)(2,1)S(1)} %copy-done.1, bf16[256,256]{1,0:T(8,128)(2,1)S(1)} %copy-done.2, ...), custom_call_target="tpu_custom_call" | custom-call | flops 2300000000 | bytes 1638404 | tf_op jit(solution)/shard_map/pallas_call | solution.py:283
  56.8 0.6 copy-done.15
  57.4 0.9 %copy-done.19 = f32[2,128,640]{2,1,0:T(8,128)} copy-done((f32[2,128,640]{2,1,0:T(8,128)}, f32[2,128,640]{2,1,0:T(8,128)S(1)}, u32[]{:S(2)}) %copy-start.19) | copy-done | bytes 655384
  58.3 2.6 %shard_map.95 = (f32[2,128,512]{2,1,0:T(8,128)S(1)}, bf16[128,256]{1,0:T(8,128)(2,1)S(1)}, f32[128,128]{1,0:T(8,128)S(1)}) custom-call(s32[128,128]{1,0:T(8,128)S(1)} %copy-done.10, s32[1]{0:T(128)S(6)} %copy.10.seed, bf16[256,256]{1,0:T(8,128)(2,1)} %query.5, bf16[256,256]{1,0:T(8,128)(2,1)S(1)} %copy-done.1, bf16[256,256]{1,0:T(8,128)(2,1)S(1)} %copy-done.2, ...), custom_call_target="tpu_custom_call" | custom-call | flops 2070000000 | bytes 1376260 | tf_op jit(solution)/shard_map/pallas_call | solution.py:283
  60.9 0.6 copy-done.13
  61.5 0.6 copy-done.17
  62.1 0.8 copy-done.21
  62.9 0.0 collective-permute-done.3.far_query
  62.9 0.0 collective-permute-done.2.near_query
  62.9 0.7 copy-done.5
  63.6 0.0 all-to-all-done.gathered
  63.6 0.0 copy-start.18
  63.6 2.1 %collective-permute-start.4 = (bf16[4,256,512]{2,1,0:T(8,128)(2,1)S(1)}, bf16[4,256,512]{2,1,0:T(8,128)(2,1)S(1)}, u32[]{:S(2)}, u32[]{:S(2)}) collective-permute-start(bf16[4,256,512]{2,1,0:T(8,128)(2,1)S(1)} %all-to-all-done.gathered), channel_id=1, source_target_pairs={{0,1},{1,0},{2,3},{3,2},{4,5},{5,4},{6,7},{7,6},{8,9},{9,8},{10,11... | collective-permute-start | bytes 3145736 | tf_op jit(solution)/shard_map/ppermute | solution.py:301
  65.7 0.0 copy-done
  65.7 0.5 shard_map.96.partial
  66.2 2.1 %collective-permute-done.4.other = bf16[4,256,512]{2,1,0:T(8,128)(2,1)S(1)} collective-permute-done((bf16[4,256,512]{2,1,0:T(8,128)(2,1)S(1)}, bf16[4,256,512]{2,1,0:T(8,128)(2,1)S(1)}, u32[]{:S(2)}, u32[]{:S(2)}) %collective-permute-start.4) | collective-permute-done | bytes 1048608 | tf_op jit(solution)/shard_map/ppermute | solution.py:301
  68.3 0.0 copy-done.16
  68.3 0.0 copy-done.18
  68.3 0.0 copy-start.6
  68.3 0.6 shard_map.97
  69.0 3.4 %collective-permute-start.5 = (bf16[272,256]{1,0:T(8,128)(2,1)S(1)}, bf16[272,256]{1,0:T(8,128)(2,1)S(1)}, u32[]{:S(2)}, u32[]{:S(2)}) collective-permute-start(bf16[272,256]{1,0:T(8,128)(2,1)S(1)} %get-tuple-element.35.grad), channel_id=1, source_target_pairs={{8,0},{16,8},{24,16},{32,24},{40,32},{48,40},{56,48},{64,56},{72,6... | collective-permute-start | bytes 417800 | tf_op jit(solution)/shard_map/ppermute | solution.py:296
  72.4 0.0 copy-start.8
  72.4 0.0 copy-start.20
  72.4 0.0 copy-start.22
  72.4 2.1 %collective-permute-start.6 = (bf16[144,256]{1,0:T(8,128)(2,1)S(1)}, bf16[144,256]{1,0:T(8,128)(2,1)S(1)}, u32[]{:S(2)}, u32[]{:S(2)}) collective-permute-start(bf16[144,256]{1,0:T(8,128)(2,1)S(1)} %get-tuple-element.44), channel_id=1, source_target_pairs={{16,0},{24,8},{32,16},{40,24},{48,32},{56,40},{64,48},{72,56},{80,... | collective-permute-start | bytes 221192 | tf_op jit(solution)/shard_map/ppermute | solution.py:296
  74.5 0.0 copy-done.6
  74.5 2.1 %shard_map.99 = (f32[2,256,256]{2,1,0:T(8,128)S(1)}, f32[2,256,256]{2,1,0:T(8,128)S(1)}, f32[2,128,128]{2,1,0:T(8,128)S(1)}, f32[2,128,128]{2,1,0:T(8,128)S(1)}) custom-call(s32[128,128]{1,0:T(8,128)S(1)} %copy-done.10, s32[1]{0:T(128)S(6)} %copy.10.seed, bf16[256,256]{1,0:T(8,128)(2,1)S(1)} %copy-done.1, bf16[256,256]{1,0:T(8,128)(2,1)S(1)} %copy-done.6, ...), custom_call_target="tpu_custom_call" | custom-call | flops 2300000000 | bytes 1703940 | tf_op jit(solution)/shard_map/pallas_call | solution.py:283
  76.6 2.6 %shard_map.98 = (bf16[256,256]{1,0:T(8,128)(2,1)}, f32[256,256]{1,0:T(8,128)S(1)}, f32[256,256]{1,0:T(8,128)S(1)}) custom-call(f32[2,128,640]{2,1,0:T(8,128)S(1)} %copy-done.20, f32[2,128,512]{2,1,0:T(8,128)S(1)} %copy-done.22, bf16[128,256]{1,0:T(8,128)(2,1)S(1)} %copy-done.12, bf16[128,256]{1,0:T(8,128)(2,1)S(1)} %copy-done.14, bf16[256,256]{1,0:T(8,128)(2,1)} %query.5, ...), custom_call_target="tpu_custom_call" | custom-call | flops 1955000064 | bytes 2891776 | tf_op jit(solution)/shard_map/pallas_call | solution.py:283
  79.2 3.4 %collective-permute-done.6.far_grad = bf16[144,256]{1,0:T(8,128)(2,1)S(1)} collective-permute-done((bf16[144,256]{1,0:T(8,128)(2,1)S(1)}, bf16[144,256]{1,0:T(8,128)(2,1)S(1)}, u32[]{:S(2)}, u32[]{:S(2)}) %collective-permute-start.6) | collective-permute-done | bytes 73760 | tf_op jit(solution)/shard_map/ppermute | solution.py:296
  82.6 0.0 collective-permute-done.5.near_grad
  82.6 1.3 %shard_map.100 = (bf16[256,256]{1,0:T(8,128)(2,1)}, bf16[256,256]{1,0:T(8,128)(2,1)}) custom-call(f32[2,256,256]{2,1,0:T(8,128)S(1)} %get-tuple-element.40.near_scores, f32[2,256,256]{2,1,0:T(8,128)S(1)} %get-tuple-element.41.near_keeps, f32[2,128,128]{2,1,0:T(8,128)S(1)} %get-tuple-element.42.far_scores, f32[2,128,128]{2,1,0:T(8,128)S(1)} %get-tuple-element.43.far_keeps, ...), custom_call_target="tpu_custom_call" | custom-call | flops 1495000064 | bytes 2637824 | tf_op jit(solution)/shard_map/pallas_call | solution.py:283
  (29 shorter events, 0.1 us)
Async XLA Ops:
  0.6 7.0 %copy-start.1 = (bf16[256,256]{1,0:T(8,128)(2,1)S(1)}, bf16[256,256]{1,0:T(8,128)(2,1)}, u32[]{:S(2)}) copy-start(bf16[256,256]{1,0:T(8,128)(2,1)} %key.6) | copy-start | bytes 393220
  0.6 11.3 %slice-start = ((bf16[256,256]{1,0:T(8,128)(2,1)}), bf16[128,256]{1,0:T(8,128)(2,1)S(1)}, s32[]{:S(2)}) async-start(bf16[256,256]{1,0:T(8,128)(2,1)} %key.6), calls=%async_computation.1 | async-start | bytes 131072 | tf_op jit(solution)/shard_map/slice | solution.py:313
  0.7 7.0 %copy-start.2 = (bf16[256,256]{1,0:T(8,128)(2,1)S(1)}, bf16[256,256]{1,0:T(8,128)(2,1)}, u32[]{:S(2)}) copy-start(bf16[256,256]{1,0:T(8,128)(2,1)} %value.7) | copy-start | bytes 393220
  0.7 11.3 %slice-start.1 = ((bf16[256,256]{1,0:T(8,128)(2,1)}), bf16[128,256]{1,0:T(8,128)(2,1)S(1)}, s32[]{:S(2)}) async-start(bf16[256,256]{1,0:T(8,128)(2,1)} %value.7), calls=%async_computation.2 | async-start | bytes 131072 | tf_op jit(solution)/shard_map/slice | solution.py:313
  0.7 53.4 %copy-start.9 = (s32[128,128]{1,0:T(8,128)S(1)}, s32[128,128]{1,0:T(8,128)}, u32[]{:S(2)}) copy-start(s32[128,128]{1,0:T(8,128)} %table.5) | copy-start | bytes 196612
  2.8 60.8 %all-to-all-start = ((bf16[4,256,512]{2,1,0:T(8,128)(2,1)}), bf16[4,256,512]{2,1,0:T(8,128)(2,1)S(1)}, u32[]{:S(2)}, u32[]{:S(2)}) async-start(bf16[4,256,512]{2,1,0:T(8,128)(2,1)} %broadcast_in_dim.2), calls=%async_computation | async-start | bytes 2097152 | tf_op jit(solution)/shard_map/all_to_all | solution.py:310
  7.7 46.4 %collective-permute-start = (bf16[512,256]{1,0:T(8,128)(2,1)S(1)}, bf16[512,256]{1,0:T(8,128)(2,1)S(1)}, u32[]{:S(2)}, u32[]{:S(2)}) collective-permute-start(bf16[512,256]{1,0:T(8,128)(2,1)S(1)} %pad_maximum_fusion), channel_id=1, source_target_pairs={{0,8},{8,16},{16,24},{24,32},{32,40},{40,48},{48,56},{56,64},{64,7... | collective-permute-start | bytes 786440 | tf_op jit(solution)/shard_map/ppermute | solution.py:296
  12.0 32.7 %collective-permute-start.1 = (bf16[256,256]{1,0:T(8,128)(2,1)S(1)}, bf16[256,256]{1,0:T(8,128)(2,1)S(1)}, u32[]{:S(2)}, u32[]{:S(2)}) collective-permute-start(bf16[256,256]{1,0:T(8,128)(2,1)S(1)} %pad_maximum_fusion.1), channel_id=1, source_target_pairs={{0,16},{8,24},{16,32},{24,40},{32,48},{40,56},{48,64},{56,72},{64,... | collective-permute-start | bytes 393224 | tf_op jit(solution)/shard_map/ppermute | solution.py:296
  18.1 44.8 %collective-permute-start.2 = (bf16[256,256]{1,0:T(8,128)(2,1)}, bf16[256,256]{1,0:T(8,128)(2,1)S(1)}, u32[]{:S(2)}, u32[]{:S(2)}) collective-permute-start(bf16[256,256]{1,0:T(8,128)(2,1)} %query.5), channel_id=1, source_target_pairs={{8,0},{16,8},{24,16},{32,24},{40,32},{48,40},{56,48},{64,56},{72,6... | collective-permute-start | bytes 393224 | tf_op jit(solution)/shard_map/ppermute | solution.py:296
  27.6 35.3 %collective-permute-start.3 = (bf16[128,256]{1,0:T(8,128)(2,1)S(1)}, bf16[128,256]{1,0:T(8,128)(2,1)S(1)}, u32[]{:S(2)}, u32[]{:S(2)}) collective-permute-start(bf16[128,256]{1,0:T(8,128)(2,1)S(1)} %slice.11), channel_id=1, source_target_pairs={{16,0},{24,8},{32,16},{40,24},{48,32},{56,40},{64,48},{72,56},{80,... | collective-permute-start | bytes 196616 | tf_op jit(solution)/shard_map/ppermute | solution.py:296
  33.0 25.2 %copy-start.10 = (s32[128,128]{1,0:T(8,128)S(1)}, s32[128,128]{1,0:T(8,128)}, u32[]{:S(2)}) copy-start(s32[128,128]{1,0:T(8,128)} %table.5) | copy-start | bytes 196612
  44.7 12.1 %copy-start.7 = (bf16[256,256]{1,0:T(8,128)(2,1)}, bf16[256,256]{1,0:T(8,128)(2,1)S(1)}, u32[]{:S(2)}) copy-start(bf16[256,256]{1,0:T(8,128)(2,1)S(1)} %collective-permute-done.1.far) | copy-start | bytes 393220
  54.0 2.8 %copy-start.3 = (bf16[512,256]{1,0:T(8,128)(2,1)}, bf16[512,256]{1,0:T(8,128)(2,1)S(1)}, u32[]{:S(2)}) copy-start(bf16[512,256]{1,0:T(8,128)(2,1)S(1)} %collective-permute-done.near) | copy-start | bytes 786436
  56.8 0.6 copy-start.15
  57.4 0.9 %copy-start.19 = (f32[2,128,640]{2,1,0:T(8,128)}, f32[2,128,640]{2,1,0:T(8,128)S(1)}, u32[]{:S(2)}) copy-start(f32[2,128,640]{2,1,0:T(8,128)S(1)} %get-tuple-element.26.signed_top) | copy-start | bytes 1966084
  58.3 2.6 %copy-start.11 = (bf16[128,256]{1,0:T(8,128)(2,1)}, bf16[128,256]{1,0:T(8,128)(2,1)S(1)}, u32[]{:S(2)}) copy-start(bf16[128,256]{1,0:T(8,128)(2,1)S(1)} %get-tuple-element.30.attended_top) | copy-start | bytes 196612
  58.3 7.4 %copy-start = (bf16[256,4096]{1,0:T(8,128)(2,1)S(1)}, bf16[256,4096]{1,0:T(8,128)(2,1)}, u32[]{:S(2)}) copy-start(bf16[256,4096]{1,0:T(8,128)(2,1)} %weight.3) | copy-start | bytes 6291460
  60.9 0.6 copy-start.13
  61.5 0.6 copy-start.17
  62.1 0.8 copy-start.21
  62.9 0.7 copy-start.5
  63.6 4.7 %copy-start.12 = (bf16[128,256]{1,0:T(8,128)(2,1)S(1)}, bf16[128,256]{1,0:T(8,128)(2,1)}, u32[]{:S(2)}) copy-start(bf16[128,256]{1,0:T(8,128)(2,1)} %copy-done.11) | copy-start | bytes 196612
  63.6 4.7 %copy-start.14 = (bf16[128,256]{1,0:T(8,128)(2,1)S(1)}, bf16[128,256]{1,0:T(8,128)(2,1)}, u32[]{:S(2)}) copy-start(bf16[128,256]{1,0:T(8,128)(2,1)} %copy-done.13) | copy-start | bytes 196612
  63.6 4.7 %copy-start.16 = (f32[128,128]{1,0:T(8,128)S(1)}, f32[128,128]{1,0:T(8,128)}, u32[]{:S(2)}) copy-start(f32[128,128]{1,0:T(8,128)} %copy-done.15) | copy-start | bytes 196612
  63.6 4.7 %copy-start.18 = (f32[128,128]{1,0:T(8,128)S(1)}, f32[128,128]{1,0:T(8,128)}, u32[]{:S(2)}) copy-start(f32[128,128]{1,0:T(8,128)} %copy-done.17) | copy-start | bytes 196612
  63.6 4.7 %collective-permute-start.4 = (bf16[4,256,512]{2,1,0:T(8,128)(2,1)S(1)}, bf16[4,256,512]{2,1,0:T(8,128)(2,1)S(1)}, u32[]{:S(2)}, u32[]{:S(2)}) collective-permute-start(bf16[4,256,512]{2,1,0:T(8,128)(2,1)S(1)} %all-to-all-done.gathered), channel_id=1, source_target_pairs={{0,1},{1,0},{2,3},{3,2},{4,5},{5,4},{6,7},{7,6},{8,9},{9,8},{10,11... | collective-permute-start | bytes 3145736 | tf_op jit(solution)/shard_map/ppermute | solution.py:301
  68.3 6.2 %copy-start.6 = (bf16[256,256]{1,0:T(8,128)(2,1)S(1)}, bf16[256,256]{1,0:T(8,128)(2,1)}, u32[]{:S(2)}) copy-start(bf16[256,256]{1,0:T(8,128)(2,1)} %copy-done.5) | copy-start | bytes 393220
  69.0 13.7 %collective-permute-start.5 = (bf16[272,256]{1,0:T(8,128)(2,1)S(1)}, bf16[272,256]{1,0:T(8,128)(2,1)S(1)}, u32[]{:S(2)}, u32[]{:S(2)}) collective-permute-start(bf16[272,256]{1,0:T(8,128)(2,1)S(1)} %get-tuple-element.35.grad), channel_id=1, source_target_pairs={{8,0},{16,8},{24,16},{32,24},{40,32},{48,40},{56,48},{64,56},{72,6... | collective-permute-start | bytes 417800 | tf_op jit(solution)/shard_map/ppermute | solution.py:296
  72.4 4.2 %copy-start.4 = (bf16[512,256]{1,0:T(8,128)(2,1)S(1)}, bf16[512,256]{1,0:T(8,128)(2,1)}, u32[]{:S(2)}) copy-start(bf16[512,256]{1,0:T(8,128)(2,1)} %copy-done.3) | copy-start | bytes 786436
  72.4 4.2 %copy-start.8 = (bf16[256,256]{1,0:T(8,128)(2,1)S(1)}, bf16[256,256]{1,0:T(8,128)(2,1)}, u32[]{:S(2)}) copy-start(bf16[256,256]{1,0:T(8,128)(2,1)} %copy-done.7) | copy-start | bytes 393220
  72.4 4.2 %copy-start.20 = (f32[2,128,640]{2,1,0:T(8,128)S(1)}, f32[2,128,640]{2,1,0:T(8,128)}, u32[]{:S(2)}) copy-start(f32[2,128,640]{2,1,0:T(8,128)} %copy-done.19) | copy-start | bytes 1966084
  72.4 4.2 %copy-start.22 = (f32[2,128,512]{2,1,0:T(8,128)S(1)}, f32[2,128,512]{2,1,0:T(8,128)}, u32[]{:S(2)}) copy-start(f32[2,128,512]{2,1,0:T(8,128)} %copy-done.21) | copy-start | bytes 1572868
  72.4 10.2 %collective-permute-start.6 = (bf16[144,256]{1,0:T(8,128)(2,1)S(1)}, bf16[144,256]{1,0:T(8,128)(2,1)S(1)}, u32[]{:S(2)}, u32[]{:S(2)}) collective-permute-start(bf16[144,256]{1,0:T(8,128)(2,1)S(1)} %get-tuple-element.44), channel_id=1, source_target_pairs={{16,0},{24,8},{32,16},{40,24},{48,32},{56,40},{64,48},{72,56},{80,... | collective-permute-start | bytes 221192 | tf_op jit(solution)/shard_map/ppermute | solution.py:296

commit v8 on v7

--- a/solution.py
+++ b/solution.py
@@ -306,12 +306,18 @@
     count = lax.axis_size("head")
     groups = [list(range(first, count, 2)) for first in range(2)]
 
-    copies = jnp.broadcast_to(grad_out[None], (count // 2, *grad_out.shape))
+    own_keys, own_grad = lax.optimization_barrier(
+        (jnp.concatenate((key_rows, value_rows)), grad_out)
+    )
+    near_keys = shifted(own_keys, 1)
+    copies = jnp.broadcast_to(own_grad[None], (count // 2, *grad_out.shape))
     gathered = lax.all_to_all(copies, "head", 0, 0, axis_index_groups=groups)
-    near_keys = shifted(jnp.concatenate((key_rows, value_rows)), 1)
     near_query = shifted(query_rows, -1)
     far_keys = shifted(jnp.concatenate((key_rows[MB:], value_rows[MB:])), 2)
     far_query = shifted(query_rows[:MB], -2)
+    gathered, near_keys, far_keys, near_query, far_query = lax.optimization_barrier(
+        (gathered, near_keys, far_keys, near_query, far_query)
+    )
 
     def outs(keys):
         return [((HEADS, MB, keys), full), ((MB, WIDE), half), ((MB, MB), full)]
@@ -323,9 +329,6 @@
     signed_top, attended_top, stats_top = call(
         far_kernel, [SMEM, SMEM] + [VMEM] * 5, outs(WIN), 2.0,
         mask_types, drop_seed, query_rows, key_rows, value_rows, near_keys, far_keys,
-    )
-    gathered, attended_low, attended_top, near_query, far_query = lax.optimization_barrier(
-        (gathered, attended_low, attended_top, near_query, far_query)
     )
     other = other_core(gathered)
     (partial,) = call(

time: 84.9 us -> 89.3 us (1.052)
  starting transfers between devices: 36.2 us -> 43.6 us
  waiting for transfers between devices: 26.5 us -> 23.4 us
  other arithmetic: 0.03 us -> 1.74 us
  Pallas kernels: 12.4 us -> 11.5 us
    ppermute x6, starting transfers between devices: 29.2 us -> 36.7 us  [shifted(): return lax.ppermute(value, 'blk', pairs)]
    ppermute x1, waiting for transfers between devices: 2.13 us -> 0.01 us  [other_core(): lax.ppermute(value, 'head', [(source, source ^ 1) for source in range(cou...]
    concatenate x1, other arithmetic: 0.02 us -> 1.73 us  [on_device(): jnp.concatenate((key_rows, value_rows))]
    ppermute x6, waiting for transfers between devices: 24.4 us -> 23.4 us  [shifted(): return lax.ppermute(value, 'blk', pairs)]
    pallas_call x7, Pallas kernels: 12.4 us -> 11.5 us  [call(): pl.pallas_call(kernel, out_shape=shapes, in_specs=specs, out_specs=[VMEM]...]
    unnamed x46 -> x24, local copies, waits for them, and re-layouts: 4.24 us -> 3.79 us
  transfers between devices with their start and end apart: 8 -> 8, of which waited for: 4 -> 4; matrix products, arithmetic and copies ran while one was open for 1% -> 1% of each run, Pallas kernels for 12% -> 11%
where the time goes in v8:
time: 89.3 us; the launch traced here: 88.5 us
  starting transfers between devices  43.6 us (49%)
  waiting for transfers between devices  23.4 us (26%)
  Pallas kernels  11.5 us (13%)
  local copies, waits for them, and re-layouts  6.83 us (8%)
  other arithmetic  1.74 us (2%)
  between operations  1.5 us (2%)
    ppermute x6, starting transfers between devices, shifted(): return lax.ppermute(value, 'blk', pairs)  36.7 us
    ppermute x6, waiting for transfers between devices, shifted(): return lax.ppermute(value, 'blk', pairs)  23.4 us
    pallas_call x7, Pallas kernels, call(): pl.pallas_call(kernel, out_shape=shapes, in_specs=specs, out_specs=[VMEM]...  11.5 us
    all_to_all x1, starting transfers between devices, on_device(): gathered = lax.all_to_all(copies, 'head', 0, 0, axis_index_groups=groups)  4.87 us
    unnamed x24, local copies, waits for them, and re-layouts  3.79 us
    broadcast_in_dim x1, local copies, waits for them, and re-layouts, on_device(): copies = jnp.broadcast_to(own_grad[None], (count // 2, *grad_out.shape))  2.17 us
    ppermute x1, starting transfers between devices, other_core(): lax.ppermute(value, 'head', [(source, source ^ 1) for source in range(cou...  2.04 us
  transfers between devices with their start and end apart: 8, of which 4 were waited for; matrix products, arithmetic and copies ran while one was open for 1% of the time, Pallas kernels for 11%

profile of v8, /device:TPU:6, one launch (start us, length us, event | category | flops | bytes accessed | tf_op | source)
XLA Modules:
  0.0 88.5 jit_solution(10518364249077171959)
XLA Ops:
  0.6 0.0 slice-start
  0.6 0.0 slice-start.1
  0.7 1.7 %pad_maximum_fusion = bf16[512,256]{1,0:T(8,128)(2,1)} fusion(bf16[256,256]{1,0:T(8,128)(2,1)} %value.7, bf16[256,256]{1,0:T(8,128)(2,1)} %key.6), kind=kLoop, calls=%fused_computation | loop fusion | flops 524288 | bytes 524288 | tf_op jit(solution)/shard_map/concatenate | solution.py:310
  2.4 0.0 copy-start
  2.4 2.2 %broadcast_in_dim.2 = bf16[4,256,512]{2,1,0:T(8,128)(2,1)} broadcast(bf16[256,512]{1,0:T(8,128)(2,1)} %param.10), dimensions={1,2} | broadcast | bytes 1310720 | tf_op jit(solution)/shard_map/broadcast_in_dim | solution.py:313
  4.6 4.9 %all-to-all-start = ((bf16[4,256,512]{2,1,0:T(8,128)(2,1)}), bf16[4,256,512]{2,1,0:T(8,128)(2,1)S(1)}, u32[]{:S(2)}, u32[]{:S(2)}) async-start(bf16[4,256,512]{2,1,0:T(8,128)(2,1)} %broadcast_in_dim.2), calls=%async_computation | async-start | bytes 2097152 | tf_op jit(solution)/shard_map/all_to_all | solution.py:314
  9.4 0.0 copy-start.1
  9.4 0.0 copy-start.2
  9.4 4.4 %collective-permute-start = (bf16[512,256]{1,0:T(8,128)(2,1)}, bf16[512,256]{1,0:T(8,128)(2,1)S(1)}, u32[]{:S(2)}, u32[]{:S(2)}) collective-permute-start(bf16[512,256]{1,0:T(8,128)(2,1)} %pad_maximum_fusion), channel_id=1, source_target_pairs={{0,8},{8,16},{16,24},{24,32},{32,40},{40,48},{48,56},{56,64},{64,7... | collective-permute-start | bytes 786440 | tf_op jit(solution)/shard_map/ppermute | solution.py:296
  13.8 0.0 slice-done
  13.8 0.0 slice-done.1
  13.9 6.1 %collective-permute-start.1 = (bf16[256,256]{1,0:T(8,128)(2,1)S(1)}, bf16[256,256]{1,0:T(8,128)(2,1)S(1)}, u32[]{:S(2)}, u32[]{:S(2)}) collective-permute-start(bf16[256,256]{1,0:T(8,128)(2,1)S(1)} %pad_maximum_fusion.1), channel_id=1, source_target_pairs={{0,16},{8,24},{16,32},{24,40},{32,48},{40,56},{48,64},{56,72},{64,... | collective-permute-start | bytes 393224 | tf_op jit(solution)/shard_map/ppermute | solution.py:296
  20.0 8.6 %collective-permute-start.2 = (bf16[256,256]{1,0:T(8,128)(2,1)}, bf16[256,256]{1,0:T(8,128)(2,1)S(1)}, u32[]{:S(2)}, u32[]{:S(2)}) collective-permute-start(bf16[256,256]{1,0:T(8,128)(2,1)} %query.5), channel_id=1, source_target_pairs={{8,0},{16,8},{24,16},{32,24},{40,32},{48,40},{56,48},{64,56},{72,6... | collective-permute-start | bytes 393224 | tf_op jit(solution)/shard_map/ppermute | solution.py:296
  28.6 0.9 slice.11
  29.5 4.8 %collective-permute-start.3 = (bf16[128,256]{1,0:T(8,128)(2,1)S(1)}, bf16[128,256]{1,0:T(8,128)(2,1)S(1)}, u32[]{:S(2)}, u32[]{:S(2)}) collective-permute-start(bf16[128,256]{1,0:T(8,128)(2,1)S(1)} %slice.11), channel_id=1, source_target_pairs={{16,0},{24,8},{32,16},{40,24},{48,32},{56,40},{64,48},{72,56},{80,... | collective-permute-start | bytes 196616 | tf_op jit(solution)/shard_map/ppermute | solution.py:296
  34.3 2.8 %collective-permute-done.3.far_query = bf16[128,256]{1,0:T(8,128)(2,1)S(1)} collective-permute-done((bf16[128,256]{1,0:T(8,128)(2,1)S(1)}, bf16[128,256]{1,0:T(8,128)(2,1)S(1)}, u32[]{:S(2)}, u32[]{:S(2)}) %collective-permute-start.3) | collective-permute-done | bytes 65568 | tf_op jit(solution)/shard_map/ppermute | solution.py:296
  37.1 9.4 %collective-permute-done.1.far = bf16[256,256]{1,0:T(8,128)(2,1)S(1)} collective-permute-done((bf16[256,256]{1,0:T(8,128)(2,1)S(1)}, bf16[256,256]{1,0:T(8,128)(2,1)S(1)}, u32[]{:S(2)}, u32[]{:S(2)}) %collective-permute-start.1) | collective-permute-done | bytes 131104 | tf_op jit(solution)/shard_map/ppermute | solution.py:296
  46.4 0.0 copy-start.9
  46.4 0.7 copy-done.9
  47.1 0.0 collective-permute-done.2.near_query
  47.1 0.7 copy-done.7
  47.7 8.1 %collective-permute-done.near = bf16[512,256]{1,0:T(8,128)(2,1)S(1)} collective-permute-done((bf16[512,256]{1,0:T(8,128)(2,1)}, bf16[512,256]{1,0:T(8,128)(2,1)S(1)}, u32[]{:S(2)}, u32[]{:S(2)}) %collective-permute-start) | collective-permute-done | bytes 262176 | tf_op jit(solution)/shard_map/ppermute | solution.py:296
  55.8 0.7 copy-done.5
  56.5 0.0 all-to-all-done.gathered
  56.5 2.0 %collective-permute-start.4 = (bf16[4,256,512]{2,1,0:T(8,128)(2,1)S(1)}, bf16[4,256,512]{2,1,0:T(8,128)(2,1)S(1)}, u32[]{:S(2)}, u32[]{:S(2)}) collective-permute-start(bf16[4,256,512]{2,1,0:T(8,128)(2,1)S(1)} %all-to-all-done.gathered), channel_id=1, source_target_pairs={{0,1},{1,0},{2,3},{3,2},{4,5},{5,4},{6,7},{7,6},{8,9},{9,8},{10,11... | collective-permute-start | bytes 3145736 | tf_op jit(solution)/shard_map/ppermute | solution.py:301
  59.2 0.0 copy-done
  59.3 0.5 shard_map.96.partial
  59.7 0.0 copy-done.1
  59.8 0.0 copy-done.2
  59.8 0.0 copy-done.6
  59.8 0.0 copy-start.3
  59.8 0.9 %copy-done.3 = bf16[256,256]{1,0:T(8,128)(2,1)S(1)} copy-done((bf16[256,256]{1,0:T(8,128)(2,1)S(1)}, bf16[256,256]{1,0:T(8,128)(2,1)}, u32[]{:S(2)}) %copy-start.3) | copy-done | bytes 131096
  60.7 0.8 copy-done.11
  61.5 2.6 %shard_map.95 = (f32[2,128,512]{2,1,0:T(8,128)S(1)}, bf16[128,256]{1,0:T(8,128)(2,1)S(1)}, f32[128,128]{1,0:T(8,128)S(1)}) custom-call(s32[128,128]{1,0:T(8,128)S(1)} %copy-done.11, s32[1]{0:T(128)S(6)} %copy.10.seed, bf16[256,256]{1,0:T(8,128)(2,1)S(1)} %copy-done.3, bf16[256,256]{1,0:T(8,128)(2,1)S(1)} %copy-done.1, bf16[256,256]{1,0:T(8,128)(2,1)S(1)} %copy-done.2, ...), custom_call_target="tpu_custom_call" | custom-call | flops 2070000000 | bytes 1376260 | tf_op jit(solution)/shard_map/pallas_call | solution.py:283
  64.1 0.0 copy-done.4
  64.1 0.0 copy-done.10
  64.1 2.7 %shard_map.94 = (f32[2,128,640]{2,1,0:T(8,128)S(1)}, bf16[128,256]{1,0:T(8,128)(2,1)S(1)}, f32[128,128]{1,0:T(8,128)S(1)}) custom-call(s32[128,128]{1,0:T(8,128)S(1)} %copy-done.11, s32[1]{0:T(128)S(6)} %copy.10.seed, bf16[256,256]{1,0:T(8,128)(2,1)S(1)} %copy-done.4, bf16[256,256]{1,0:T(8,128)(2,1)S(1)} %copy-done.1, bf16[256,256]{1,0:T(8,128)(2,1)S(1)} %copy-done.2, ...), custom_call_target="tpu_custom_call" | custom-call | flops 2300000000 | bytes 1638404 | tf_op jit(solution)/shard_map/pallas_call | solution.py:283
  66.9 0.0 collective-permute-done.4.other
  66.9 0.0 copy-start.8
  66.9 0.6 shard_map.97
  67.5 10.8 %collective-permute-start.5 = (bf16[272,256]{1,0:T(8,128)(2,1)S(1)}, bf16[272,256]{1,0:T(8,128)(2,1)S(1)}, u32[]{:S(2)}, u32[]{:S(2)}) collective-permute-start(bf16[272,256]{1,0:T(8,128)(2,1)S(1)} %get-tuple-element.39.grad), channel_id=1, source_target_pairs={{8,0},{16,8},{24,16},{32,24},{40,32},{48,40},{56,48},{64,56},{72,6... | collective-permute-start | bytes 417800 | tf_op jit(solution)/shard_map/ppermute | solution.py:296
  78.4 1.9 %collective-permute-start.6 = (bf16[144,256]{1,0:T(8,128)(2,1)S(1)}, bf16[144,256]{1,0:T(8,128)(2,1)S(1)}, u32[]{:S(2)}, u32[]{:S(2)}) collective-permute-start(bf16[144,256]{1,0:T(8,128)(2,1)S(1)} %get-tuple-element.48), channel_id=1, source_target_pairs={{16,0},{24,8},{32,16},{40,24},{48,32},{56,40},{64,48},{72,56},{80,... | collective-permute-start | bytes 221192 | tf_op jit(solution)/shard_map/ppermute | solution.py:296
  80.3 0.0 copy-done.8
  80.3 2.1 %shard_map.99 = (f32[2,256,256]{2,1,0:T(8,128)S(1)}, f32[2,256,256]{2,1,0:T(8,128)S(1)}, f32[2,128,128]{2,1,0:T(8,128)S(1)}, f32[2,128,128]{2,1,0:T(8,128)S(1)}) custom-call(s32[128,128]{1,0:T(8,128)S(1)} %copy-done.11, s32[1]{0:T(128)S(6)} %copy.10.seed, bf16[256,256]{1,0:T(8,128)(2,1)S(1)} %copy-done.1, bf16[256,256]{1,0:T(8,128)(2,1)S(1)} %copy-done.8, ...), custom_call_target="tpu_custom_call" | custom-call | flops 2300000000 | bytes 1703940 | tf_op jit(solution)/shard_map/pallas_call | solution.py:283
  82.4 1.7 %shard_map.98 = (bf16[256,256]{1,0:T(8,128)(2,1)}, f32[256,256]{1,0:T(8,128)S(1)}, f32[256,256]{1,0:T(8,128)S(1)}) custom-call(f32[2,128,640]{2,1,0:T(8,128)S(1)} %get-tuple-element.32.signed_top, f32[2,128,512]{2,1,0:T(8,128)S(1)} %get-tuple-element.33.signed_low, bf16[128,256]{1,0:T(8,128)(2,1)S(1)} %get-tuple-element.34.attended_top, ...), custom_call_target="tpu_custom_call" | custom-call | flops 1955000064 | bytes 2891776 | tf_op jit(solution)/shard_map/pallas_call | solution.py:283
  84.1 3.2 %collective-permute-done.6.far_grad = bf16[144,256]{1,0:T(8,128)(2,1)S(1)} collective-permute-done((bf16[144,256]{1,0:T(8,128)(2,1)S(1)}, bf16[144,256]{1,0:T(8,128)(2,1)S(1)}, u32[]{:S(2)}, u32[]{:S(2)}) %collective-permute-start.6) | collective-permute-done | bytes 73760 | tf_op jit(solution)/shard_map/ppermute | solution.py:296
  87.3 0.0 collective-permute-done.5.near_grad
  87.3 1.3 %shard_map.100 = (bf16[256,256]{1,0:T(8,128)(2,1)}, bf16[256,256]{1,0:T(8,128)(2,1)}) custom-call(f32[2,256,256]{2,1,0:T(8,128)S(1)} %get-tuple-element.44.near_scores, f32[2,256,256]{2,1,0:T(8,128)S(1)} %get-tuple-element.45.near_keeps, f32[2,128,128]{2,1,0:T(8,128)S(1)} %get-tuple-element.46.far_scores, f32[2,128,128]{2,1,0:T(8,128)S(1)} %get-tuple-element.47.far_keeps, ...), custom_call_target="tpu_custom_call" | custom-call | flops 1495000064 | bytes 2637824 | tf_op jit(solution)/shard_map/pallas_call | solution.py:283
  (7 shorter events, 0.0 us)
Async XLA Ops:
  0.6 13.2 %slice-start = ((bf16[256,256]{1,0:T(8,128)(2,1)}), bf16[128,256]{1,0:T(8,128)(2,1)S(1)}, s32[]{:S(2)}) async-start(bf16[256,256]{1,0:T(8,128)(2,1)} %key.6), calls=%async_computation.1 | async-start | bytes 131072 | tf_op jit(solution)/shard_map/slice | solution.py:316
  0.6 13.2 %slice-start.1 = ((bf16[256,256]{1,0:T(8,128)(2,1)}), bf16[128,256]{1,0:T(8,128)(2,1)S(1)}, s32[]{:S(2)}) async-start(bf16[256,256]{1,0:T(8,128)(2,1)} %value.7), calls=%async_computation.2 | async-start | bytes 131072 | tf_op jit(solution)/shard_map/slice | solution.py:316
  2.4 56.9 %copy-start = (bf16[256,4096]{1,0:T(8,128)(2,1)S(1)}, bf16[256,4096]{1,0:T(8,128)(2,1)}, u32[]{:S(2)}) copy-start(bf16[256,4096]{1,0:T(8,128)(2,1)} %weight.3) | copy-start | bytes 6291460
  4.6 52.0 %all-to-all-start = ((bf16[4,256,512]{2,1,0:T(8,128)(2,1)}), bf16[4,256,512]{2,1,0:T(8,128)(2,1)S(1)}, u32[]{:S(2)}, u32[]{:S(2)}) async-start(bf16[4,256,512]{2,1,0:T(8,128)(2,1)} %broadcast_in_dim.2), calls=%async_computation | async-start | bytes 2097152 | tf_op jit(solution)/shard_map/all_to_all | solution.py:314
  9.4 50.3 %copy-start.1 = (bf16[256,256]{1,0:T(8,128)(2,1)S(1)}, bf16[256,256]{1,0:T(8,128)(2,1)}, u32[]{:S(2)}) copy-start(bf16[256,256]{1,0:T(8,128)(2,1)} %key.6) | copy-start | bytes 393220
  9.4 50.3 %copy-start.2 = (bf16[256,256]{1,0:T(8,128)(2,1)S(1)}, bf16[256,256]{1,0:T(8,128)(2,1)}, u32[]{:S(2)}) copy-start(bf16[256,256]{1,0:T(8,128)(2,1)} %value.7) | copy-start | bytes 393220
  9.4 46.4 %collective-permute-start = (bf16[512,256]{1,0:T(8,128)(2,1)}, bf16[512,256]{1,0:T(8,128)(2,1)S(1)}, u32[]{:S(2)}, u32[]{:S(2)}) collective-permute-start(bf16[512,256]{1,0:T(8,128)(2,1)} %pad_maximum_fusion), channel_id=1, source_target_pairs={{0,8},{8,16},{16,24},{24,32},{32,40},{40,48},{48,56},{56,64},{64,7... | collective-permute-start | bytes 786440 | tf_op jit(solution)/shard_map/ppermute | solution.py:296
  13.9 32.5 %collective-permute-start.1 = (bf16[256,256]{1,0:T(8,128)(2,1)S(1)}, bf16[256,256]{1,0:T(8,128)(2,1)S(1)}, u32[]{:S(2)}, u32[]{:S(2)}) collective-permute-start(bf16[256,256]{1,0:T(8,128)(2,1)S(1)} %pad_maximum_fusion.1), channel_id=1, source_target_pairs={{0,16},{8,24},{16,32},{24,40},{32,48},{40,56},{48,64},{56,72},{64,... | collective-permute-start | bytes 393224 | tf_op jit(solution)/shard_map/ppermute | solution.py:296
  20.0 27.1 %collective-permute-start.2 = (bf16[256,256]{1,0:T(8,128)(2,1)}, bf16[256,256]{1,0:T(8,128)(2,1)S(1)}, u32[]{:S(2)}, u32[]{:S(2)}) collective-permute-start(bf16[256,256]{1,0:T(8,128)(2,1)} %query.5), channel_id=1, source_target_pairs={{8,0},{16,8},{24,16},{32,24},{40,32},{48,40},{56,48},{64,56},{72,6... | collective-permute-start | bytes 393224 | tf_op jit(solution)/shard_map/ppermute | solution.py:296
  29.5 7.6 %collective-permute-start.3 = (bf16[128,256]{1,0:T(8,128)(2,1)S(1)}, bf16[128,256]{1,0:T(8,128)(2,1)S(1)}, u32[]{:S(2)}, u32[]{:S(2)}) collective-permute-start(bf16[128,256]{1,0:T(8,128)(2,1)S(1)} %slice.11), channel_id=1, source_target_pairs={{16,0},{24,8},{32,16},{40,24},{48,32},{56,40},{64,48},{72,56},{80,... | collective-permute-start | bytes 196616 | tf_op jit(solution)/shard_map/ppermute | solution.py:296
  46.4 0.7 copy-start.9
  47.1 0.7 copy-start.7
  55.8 0.7 copy-start.5
  56.5 3.2 %copy-start.6 = (bf16[512,256]{1,0:T(8,128)(2,1)S(1)}, bf16[512,256]{1,0:T(8,128)(2,1)}, u32[]{:S(2)}) copy-start(bf16[512,256]{1,0:T(8,128)(2,1)} %copy-done.5) | copy-start | bytes 786436
  56.5 10.3 %collective-permute-start.4 = (bf16[4,256,512]{2,1,0:T(8,128)(2,1)S(1)}, bf16[4,256,512]{2,1,0:T(8,128)(2,1)S(1)}, u32[]{:S(2)}, u32[]{:S(2)}) collective-permute-start(bf16[4,256,512]{2,1,0:T(8,128)(2,1)S(1)} %all-to-all-done.gathered), channel_id=1, source_target_pairs={{0,1},{1,0},{2,3},{3,2},{4,5},{5,4},{6,7},{7,6},{8,9},{9,8},{10,11... | collective-permute-start | bytes 3145736 | tf_op jit(solution)/shard_map/ppermute | solution.py:301
  59.8 0.9 %copy-start.3 = (bf16[256,256]{1,0:T(8,128)(2,1)S(1)}, bf16[256,256]{1,0:T(8,128)(2,1)}, u32[]{:S(2)}) copy-start(bf16[256,256]{1,0:T(8,128)(2,1)} %query.5) | copy-start | bytes 393220
  60.7 0.8 copy-start.11
  61.5 2.6 %copy-start.4 = (bf16[256,256]{1,0:T(8,128)(2,1)S(1)}, bf16[256,256]{1,0:T(8,128)(2,1)}, u32[]{:S(2)}) copy-start(bf16[256,256]{1,0:T(8,128)(2,1)} %query.5) | copy-start | bytes 393220
  61.5 2.6 %copy-start.10 = (bf16[256,256]{1,0:T(8,128)(2,1)S(1)}, bf16[256,256]{1,0:T(8,128)(2,1)}, u32[]{:S(2)}) copy-start(bf16[256,256]{1,0:T(8,128)(2,1)} %copy-done.9) | copy-start | bytes 393220
  66.9 13.4 %copy-start.8 = (bf16[256,256]{1,0:T(8,128)(2,1)S(1)}, bf16[256,256]{1,0:T(8,128)(2,1)}, u32[]{:S(2)}) copy-start(bf16[256,256]{1,0:T(8,128)(2,1)} %copy-done.7) | copy-start | bytes 393220
  67.5 19.7 %collective-permute-start.5 = (bf16[272,256]{1,0:T(8,128)(2,1)S(1)}, bf16[272,256]{1,0:T(8,128)(2,1)S(1)}, u32[]{:S(2)}, u32[]{:S(2)}) collective-permute-start(bf16[272,256]{1,0:T(8,128)(2,1)S(1)} %get-tuple-element.39.grad), channel_id=1, source_target_pairs={{8,0},{16,8},{24,16},{32,24},{40,32},{48,40},{56,48},{64,56},{72,6... | collective-permute-start | bytes 417800 | tf_op jit(solution)/shard_map/ppermute | solution.py:296
  78.4 8.9 %collective-permute-start.6 = (bf16[144,256]{1,0:T(8,128)(2,1)S(1)}, bf16[144,256]{1,0:T(8,128)(2,1)S(1)}, u32[]{:S(2)}, u32[]{:S(2)}) collective-permute-start(bf16[144,256]{1,0:T(8,128)(2,1)S(1)} %get-tuple-element.48), channel_id=1, source_target_pairs={{16,0},{24,8},{32,16},{40,24},{48,32},{56,40},{64,48},{72,56},{80,... | collective-permute-start | bytes 221192 | tf_op jit(solution)/shard_map/ppermute | solution.py:296

commit v9 on v7

--- a/solution.py
+++ b/solution.py
@@ -15,7 +15,7 @@
 WIN = SLOTS * MB
 FAR = 3 * MB
 WIDE = HEADS * DH
-EXTRA = 16
+STATS = 8
 
 drop_level = 6554
 keep_scale = 65536.0 / 58982.0
@@ -80,20 +80,7 @@
     )
 
 
-def put_parts(stats, lane, first, column):
-    rest = column
-    for part in range(3):
-        piece = f32(bf16(rest))
-        stats = jnp.where(lane == first + part, piece, stats)
-        rest = rest - piece
-    return stats
-
-
-def take_parts(stats, first):
-    return stats[first : first + 1] + stats[first + 1 : first + 2] + stats[first + 2 : first + 3]
-
-
-def forward(table, seed, block, query, keys, values, signed, attended, stats):
+def forward(table, seed, block, query, keys, values, grad, signed, attended):
     shard = lax.axis_index("blk")
     first_head = lax.axis_index("head") * HEADS
     count = keys(0).shape[0] // MB
@@ -101,10 +88,11 @@
     first_block = shard * 2 + 2 - count
     ahead = key_minus_query(0)
     lane = lax.broadcasted_iota(jnp.int32, (MB, MB), 1)
-    parts = jnp.zeros((MB, MB), jnp.float32)
+    rows = slice(block * MB, (block + 1) * MB)
+    stats = jnp.zeros((MB, MB), jnp.float32)
     for head in range(HEADS):
         cols = pl.ds(head * DH, DH)
-        scores = dot_last(query[block * MB : (block + 1) * MB, cols], keys(head))
+        scores = dot_last(query[rows, cols], keys(head))
         tiles = []
         for slot in range(count):
             bound = bound_of(table, query_block, first_block + slot)
@@ -121,9 +109,12 @@
             keep = kept(seed[0], first_head + head, query_block, first_block + slot, 0)
             signed[head, :, slot * MB : (slot + 1) * MB] = jnp.where(keep, prob, -prob)
             drops.append(bf16(jnp.where(keep, prob * keep_scale, 0.0)))
-        attended[:, cols] = bf16(dot(jnp.concatenate(drops, axis=1), values(head)))
-        parts = put_parts(parts, lane, 3 * head, top + jnp.log(total))
-    stats[...] = parts
+        mixed = bf16(dot(jnp.concatenate(drops, axis=1), values(head)))
+        attended[rows, cols] = mixed
+        row_dot = jnp.sum(f32(grad[rows, cols]) * f32(mixed), axis=1, keepdims=True)
+        stats = jnp.where(lane == head, top + jnp.log(total), stats)
+        stats = jnp.where(lane == HEADS + head, row_dot, stats)
+    return stats.T[0:STATS]
 
 
 def later(table, seed, first_query, first_key, queries, keys, scores, keeps):
@@ -164,14 +155,20 @@
     return ((far, slice(0, MB)), *keys), ((far, slice(MB, None)), *values)
 
 
-def near_kernel(table, seed, query, key, value, near, signed, attended, stats):
+def forward_kernel(
+    table, seed, query, key, value, near, far, grad,
+    signed_top, signed_low, attended, near_stats, far_stats,
+):
+    keys, values = far_window(key, value, near, far)
+    stats = forward(
+        table, seed, 0, query, stacked(*keys), stacked(*values), grad, signed_top, attended
+    )
+    near_stats[:, 0:MB] = stats
+    far_stats[...] = stats
     keys, values = near_window(key, value, near)
-    forward(table, seed, 1, query, stacked(*keys), stacked(*values), signed, attended, stats)
-
-
-def far_kernel(table, seed, query, key, value, near, far, signed, attended, stats):
-    keys, values = far_window(key, value, near, far)
-    forward(table, seed, 0, query, stacked(*keys), stacked(*values), signed, attended, stats)
+    near_stats[:, MB:] = forward(
+        table, seed, 1, query, stacked(*keys), stacked(*values), grad, signed_low, attended
+    )
 
 
 def later_kernel(
@@ -191,48 +188,47 @@
     return total
 
 
-def project_kernel(gathered, weight, out):
+def cut_kernel(weight, out):
+    core = lax.rem(lax.axis_index("head"), 2)
+    parts = lax.axis_size("head") // 2
+    width = out.shape[1] // parts
+    for part in range(parts):
+        first = pl.multiple_of((part * 2 + 1 - core) * width, width)
+        out[:, part * width : (part + 1) * width] = weight[:, pl.ds(first, width)]
+
+
+def project_other_kernel(gathered, weight, out):
+    parts, _, width = gathered.shape
+    total = dot_last(gathered[0], weight[:, 0:width])
+    for part in range(1, parts):
+        total = total + dot_last(gathered[part], weight[:, part * width : (part + 1) * width])
+    out[...] = bf16(total)
+
+
+def project_own_kernel(gathered, weight, out):
     out[...] = project(None, gathered, weight, lax.rem(lax.axis_index("head"), 2))
 
 
-def rows_kernel(
-    partial, other, weight, attended_top, attended_low, stats_top, stats_low, near, far
-):
-    core = lax.rem(lax.axis_index("head"), 2)
-    whole = project(partial[...], other, weight, 1 - core)
-    lane = lax.broadcasted_iota(jnp.int32, (MB, MB), 1)
-    for block, total, attended, stats in (
-        (0, whole[0:MB], attended_top, stats_top), (1, whole[MB:], attended_low, stats_low)
-    ):
-        rows = slice(block * MB, (block + 1) * MB)
-        grad = bf16(total)
-        near[rows] = grad
-        parts = stats[...]
-        for head in range(HEADS):
-            cols = slice(head * DH, (head + 1) * DH)
-            row_dot = jnp.sum(f32(grad[:, cols]) * f32(attended[:, cols]), axis=1, keepdims=True)
-            parts = put_parts(parts, lane, 6 + 3 * head, row_dot)
-        across = bf16(parts.T[0:EXTRA])
-        near[ROWS:, rows] = across
-        if block == 0:
-            far[0:MB] = grad
-        far[MB:, rows] = across
+def rows_kernel(own, received, grad, grad_top):
+    whole = bf16(own[...] + f32(received[...]))
+    grad[...] = whole
+    grad_top[...] = whole[0:MB]
 
 
 def own_kernel(
-    signed_top, signed_low, attended_top, attended_low, query, grad, key, value, near, far,
+    signed_top, signed_low, attended, query, grad, key, value, near, far,
     grad_query, key_part, value_part,
 ):
     for head in range(HEADS):
         cols = slice(head * DH, (head + 1) * DH)
         key_sum = value_sum = None
-        for block, signed, attended, (keys, values) in (
-            (0, signed_top, attended_top, far_window(key, value, near, far)),
-            (1, signed_low, attended_low, near_window(key, value, near)),
+        for block, signed, (keys, values) in (
+            (0, signed_top, far_window(key, value, near, far)),
+            (1, signed_low, near_window(key, value, near)),
         ):
             rows = slice(block * MB, (block + 1) * MB)
             grad_head = grad[rows, cols]
-            row_dot = jnp.sum(f32(grad_head) * f32(attended[:, cols]), axis=1, keepdims=True)
+            row_dot = jnp.sum(f32(grad_head) * f32(attended[rows, cols]), axis=1, keepdims=True)
             grad_prob = dot_last(grad_head, stacked(*values)(head))
             probs = signed[head]
             first = probs.shape[1] - ROWS
@@ -250,23 +246,25 @@
 
 def finish_kernel(
     near_scores, near_keeps, far_scores, far_keeps, value, near_query, far_query, near_grad,
-    far_grad, key_part, value_part, grad_key, grad_value,
+    far_grad, near_stats, far_stats, key_part, value_part, grad_key, grad_value,
 ):
     for head in range(HEADS):
         cols = pl.ds(head * DH, DH)
 
-        def terms(scores, keeps, values, queries, grads):
-            count = queries.shape[0]
-            grad_head = grads[0:count, cols]
-            stats = f32(grads[count:, 0:count])
-            prob = jnp.exp(scores[head] - take_parts(stats, 3 * head))
+        def terms(scores, keeps, values, queries, grads, stats):
+            grad_head = grads[:, cols]
+            prob = jnp.exp(scores[head] - stats[head : head + 1])
             keep = keeps[head]
             grad_prob = dot_last(values, grad_head)
-            dscore = bf16(prob * (grad_prob * keep - take_parts(stats, 6 + 3 * head)))
+            dscore = bf16(prob * (grad_prob * keep - stats[HEADS + head : HEADS + head + 1]))
             return dot(dscore, queries[:, cols]), dot(bf16(prob * keep), grad_head)
 
-        keys, values = terms(near_scores, near_keeps, value[:, cols], near_query, near_grad)
-        far_keys, far_values = terms(far_scores, far_keeps, value[MB:, cols], far_query, far_grad)
+        keys, values = terms(
+            near_scores, near_keeps, value[:, cols], near_query, near_grad, near_stats
+        )
+        far_keys, far_values = terms(
+            far_scores, far_keeps, value[MB:, cols], far_query, far_grad, far_stats
+        )
         keys = keys + key_part[:, cols]
         values = values + value_part[:, cols]
         grad_key[0:MB, cols] = bf16(keys[0:MB] * score_scale)
@@ -286,7 +284,7 @@
         in_specs=specs,
         out_specs=[VMEM] * len(shapes),
         compiler_params=pltpu.CompilerParams(vmem_limit_bytes=16 << 20),
-        cost_estimate=pl.CostEstimate(flops=flops, bytes_accessed=moved, transcendentals=0),
+        cost_estimate=pl.CostEstimate(flops=flops, bytes_accessed=min(moved, flops), transcendentals=0),
     )(*args)
 
 
@@ -313,53 +311,60 @@
     far_keys = shifted(jnp.concatenate((key_rows[MB:], value_rows[MB:])), 2)
     far_query = shifted(query_rows[:MB], -2)
 
-    def outs(keys):
-        return [((HEADS, MB, keys), full), ((MB, WIDE), half), ((MB, MB), full)]
-
-    signed_low, attended_low, stats_low = call(
-        near_kernel, [SMEM, SMEM] + [VMEM] * 4, outs(WIN - MB), 1.8,
-        mask_types, drop_seed, query_rows, key_rows, value_rows, near_keys,
-    )
-    signed_top, attended_top, stats_top = call(
-        far_kernel, [SMEM, SMEM] + [VMEM] * 5, outs(WIN), 2.0,
-        mask_types, drop_seed, query_rows, key_rows, value_rows, near_keys, far_keys,
-    )
-    gathered, attended_low, attended_top, near_query, far_query = lax.optimization_barrier(
-        (gathered, attended_low, attended_top, near_query, far_query)
-    )
-    other = other_core(gathered)
-    (partial,) = call(
-        project_kernel, [VMEM] * 2, [((ROWS, WIDE), full)], 0.7, gathered, out_weight
-    )
-    near_rows, far_rows = call(
-        rows_kernel,
-        [VMEM] * 7,
-        [((ROWS + EXTRA, WIDE), half), ((MB + EXTRA, WIDE), half)],
-        1.0,
-        partial, other, out_weight, attended_top, attended_low, stats_top, stats_low,
-    )
-    near_grad = shifted(near_rows, -1)
-    far_grad = shifted(far_rows, -2)
+    width = (count // 2) * grad_out.shape[1]
+    (theirs,) = call(cut_kernel, [VMEM], [((WIDE, width), half)], 0.0, out_weight)
+    other_weight = other_core(theirs)
+    gathered, other_weight, far_keys, near_query, far_query = lax.optimization_barrier(
+        (gathered, other_weight, far_keys, near_query, far_query)
+    )
+    (sent,) = call(
+        project_other_kernel, [VMEM] * 2, [((ROWS, WIDE), half)], 0.0, gathered, other_weight
+    )
+    received = other_core(sent)
+    (own,) = call(
+        project_own_kernel, [VMEM] * 2, [((ROWS, WIDE), full)], 0.0, gathered, out_weight
+    )
+    grad, grad_top = call(
+        rows_kernel, [VMEM] * 2, [((ROWS, WIDE), half), ((MB, WIDE), half)], 0.0, own, received
+    )
+    near_grad = shifted(grad, -1)
+    far_grad = shifted(grad_top, -2)
+    signed_top, signed_low, attended, near_sums, far_sums = call(
+        forward_kernel,
+        [SMEM, SMEM] + [VMEM] * 6,
+        [
+            ((HEADS, MB, WIN), full),
+            ((HEADS, MB, WIN - MB), full),
+            ((ROWS, WIDE), half),
+            ((STATS, ROWS), full),
+            ((STATS, MB), full),
+        ],
+        0.0,
+        mask_types, drop_seed, query_rows, key_rows, value_rows, near_keys, far_keys, grad,
+    )
+    near_stats = shifted(near_sums, -1)
+    far_stats = shifted(far_sums, -2)
     grad_query, key_part, value_part = call(
         own_kernel,
-        [VMEM] * 10,
+        [VMEM] * 9,
         [((ROWS, WIDE), half), ((ROWS, WIDE), full), ((ROWS, WIDE), full)],
-        1.7,
-        signed_top, signed_low, attended_top, attended_low, query_rows, near_rows, key_rows,
-        value_rows, near_keys, far_keys,
-    )
-    later_key, _ = lax.optimization_barrier((key_rows, near_rows))
+        0.0,
+        signed_top, signed_low, attended, query_rows, grad, key_rows, value_rows, near_keys,
+        far_keys,
+    )
+    later_key, _ = lax.optimization_barrier((key_rows, near_sums))
     scores = call(
         later_kernel, [SMEM, SMEM] + [VMEM] * 3,
-        [((HEADS, ROWS, ROWS), full)] * 2 + [((HEADS, MB, MB), full)] * 2, 2.0,
+        [((HEADS, ROWS, ROWS), full)] * 2 + [((HEADS, MB, MB), full)] * 2, 0.0,
         mask_types, drop_seed, later_key, near_query, far_query,
     )
     grad_key, grad_value = call(
         finish_kernel,
-        [VMEM] * 11,
+        [VMEM] * 13,
         [((ROWS, WIDE), half), ((ROWS, WIDE), half)],
         1.3,
-        *scores, value_rows, near_query, far_query, near_grad, far_grad, key_part, value_part,
+        *scores, value_rows, near_query, far_query, near_grad, far_grad, near_stats, far_stats,
+        key_part, value_part,
     )
     return (grad_query, grad_key, grad_value)
 

time: 84.9 us -> 89 us (1.048)
  starting transfers between devices: 36.2 us -> 56.9 us
  waiting for transfers between devices: 26.5 us -> 12.8 us
  Pallas kernels: 12.4 us -> 10.6 us
  local copies, waits for them, and re-layouts: 7.19 us -> 5.73 us
    ppermute x6 -> x8, starting transfers between devices: 29.2 us -> 47.9 us  [shifted(): return lax.ppermute(value, 'blk', pairs)]
    ppermute x6 -> x8, waiting for transfers between devices: 24.4 us -> 12 us  [shifted(): return lax.ppermute(value, 'blk', pairs)]
    ppermute x1 -> x2, starting transfers between devices: 2.05 us -> 4.1 us  [other_core(): lax.ppermute(value, 'head', [(source, source ^ 1) for source in range(cou...]
    pallas_call x7 -> x8, Pallas kernels: 12.4 us -> 10.6 us  [call(): pl.pallas_call(kernel, out_shape=shapes, in_specs=specs, out_specs=[VMEM]...]
    ppermute x1 -> x2, waiting for transfers between devices: 2.13 us -> 0.83 us  [other_core(): lax.ppermute(value, 'head', [(source, source ^ 1) for source in range(cou...]
    unnamed x46 -> x24, local copies, waits for them, and re-layouts: 4.24 us -> 3.56 us
  transfers between devices with their start and end apart: 8 -> 11, of which waited for: 4 -> 3; matrix products, arithmetic and copies ran while one was open for 1% -> 1% of each run, Pallas kernels for 12% -> 11%
where the time goes in v9:
time: 89 us; the launch traced here: 88.4 us
  starting transfers between devices  56.9 us (64%)
  waiting for transfers between devices  12.8 us (14%)
  Pallas kernels  10.6 us (12%)
  local copies, waits for them, and re-layouts  5.73 us (6%)
  between operations  1.58 us (2%)
    ppermute x8, starting transfers between devices, shifted(): return lax.ppermute(value, 'blk', pairs)  47.9 us
    ppermute x8, waiting for transfers between devices, shifted(): return lax.ppermute(value, 'blk', pairs)  12 us
    pallas_call x8, Pallas kernels, call(): pl.pallas_call(kernel, out_shape=shapes, in_specs=specs, out_specs=[VMEM]...  10.6 us
    all_to_all x1, starting transfers between devices, on_device(): gathered = lax.all_to_all(copies, 'head', 0, 0, axis_index_groups=groups)  4.87 us
    ppermute x2, starting transfers between devices, other_core(): lax.ppermute(value, 'head', [(source, source ^ 1) for source in range(cou...  4.1 us
    unnamed x24, local copies, waits for them, and re-layouts  3.56 us
    broadcast_in_dim x1, local copies, waits for them, and re-layouts, on_device(): copies = jnp.broadcast_to(grad_out[None], (count // 2, *grad_out.shape))  2.16 us
  transfers between devices with their start and end apart: 11, of which 3 were waited for; matrix products, arithmetic and copies ran while one was open for 1% of the time, Pallas kernels for 11%

profile of v9, /device:TPU:6, one launch (start us, length us, event | category | flops | bytes accessed | tf_op | source)
XLA Modules:
  0.0 88.4 jit_solution(10085237610516121080)
XLA Ops:
  0.6 0.0 copy-start
  0.6 2.2 %broadcast_in_dim.2 = bf16[4,256,512]{2,1,0:T(8,128)(2,1)} broadcast(bf16[256,512]{1,0:T(8,128)(2,1)} %param.10), dimensions={1,2} | broadcast | bytes 1310720 | tf_op jit(solution)/shard_map/broadcast_in_dim | solution.py:307
  2.8 4.9 %all-to-all-start = ((bf16[4,256,512]{2,1,0:T(8,128)(2,1)}), bf16[4,256,512]{2,1,0:T(8,128)(2,1)S(1)}, u32[]{:S(2)}, u32[]{:S(2)}) async-start(bf16[4,256,512]{2,1,0:T(8,128)(2,1)} %broadcast_in_dim.2), calls=%async_computation | async-start | bytes 2097152 | tf_op jit(solution)/shard_map/all_to_all | solution.py:308
  7.7 0.0 copy-start.5
  7.7 0.0 copy-start.1
  7.7 0.0 copy-start.2
  7.7 0.1 shard_map.94
  7.8 2.1 %collective-permute-start.1 = (bf16[256,2048]{1,0:T(8,128)(2,1)S(1)}, bf16[256,2048]{1,0:T(8,128)(2,1)S(1)}, u32[]{:S(2)}, u32[]{:S(2)}) collective-permute-start(bf16[256,2048]{1,0:T(8,128)(2,1)S(1)} %shard_map.94), channel_id=1, source_target_pairs={{0,1},{1,0},{2,3},{3,2},{4,5},{5,4},{6,7},{7,6},{8,9},{9,8},{10,11... | collective-permute-start | bytes 3145736 | tf_op jit(solution)/shard_map/ppermute | solution.py:299
  9.9 0.0 slice-done
  9.9 0.0 slice-done.1
  9.9 6.1 %collective-permute-start.2 = (bf16[256,256]{1,0:T(8,128)(2,1)S(1)}, bf16[256,256]{1,0:T(8,128)(2,1)S(1)}, u32[]{:S(2)}, u32[]{:S(2)}) collective-permute-start(bf16[256,256]{1,0:T(8,128)(2,1)S(1)} %pad_maximum_fusion.1), channel_id=1, source_target_pairs={{0,16},{8,24},{16,32},{24,40},{32,48},{40,56},{48,64},{56,72},{64,... | collective-permute-start | bytes 393224 | tf_op jit(solution)/shard_map/ppermute | solution.py:294
  16.0 11.0 %collective-permute-start.3 = (bf16[256,256]{1,0:T(8,128)(2,1)S(1)}, bf16[256,256]{1,0:T(8,128)(2,1)S(1)}, u32[]{:S(2)}, u32[]{:S(2)}) collective-permute-start(bf16[256,256]{1,0:T(8,128)(2,1)S(1)} %copy-done.5), channel_id=1, source_target_pairs={{8,0},{16,8},{24,16},{32,24},{40,32},{48,40},{56,48},{64,56},{72,6... | collective-permute-start | bytes 393224 | tf_op jit(solution)/shard_map/ppermute | solution.py:294
  27.0 4.8 %collective-permute-start.4 = (bf16[128,256]{1,0:T(8,128)(2,1)S(1)}, bf16[128,256]{1,0:T(8,128)(2,1)S(1)}, u32[]{:S(2)}, u32[]{:S(2)}) collective-permute-start(bf16[128,256]{1,0:T(8,128)(2,1)S(1)} %slice.11), channel_id=1, source_target_pairs={{16,0},{24,8},{32,16},{40,24},{48,32},{56,40},{64,48},{72,56},{80,... | collective-permute-start | bytes 196616 | tf_op jit(solution)/shard_map/ppermute | solution.py:294
  31.9 0.7 pad_maximum_fusion
  32.6 1.9 %collective-permute-start = (bf16[512,256]{1,0:T(8,128)(2,1)}, bf16[512,256]{1,0:T(8,128)(2,1)}, u32[]{:S(2)}, u32[]{:S(2)}) collective-permute-start(bf16[512,256]{1,0:T(8,128)(2,1)} %pad_maximum_fusion), channel_id=1, source_target_pairs={{0,8},{8,16},{16,24},{24,32},{32,40},{40,48},{48,56},{56,64},{64,7... | collective-permute-start | bytes 786440 | tf_op jit(solution)/shard_map/ppermute | solution.py:294
  34.5 0.7 collective-permute-done.4.far_query
  35.2 11.3 %collective-permute-done.2.far = bf16[256,256]{1,0:T(8,128)(2,1)S(1)} collective-permute-done((bf16[256,256]{1,0:T(8,128)(2,1)S(1)}, bf16[256,256]{1,0:T(8,128)(2,1)S(1)}, u32[]{:S(2)}, u32[]{:S(2)}) %collective-permute-start.2) | collective-permute-done | bytes 131104 | tf_op jit(solution)/shard_map/ppermute | solution.py:294
  46.5 0.7 copy-done.7
  47.2 0.0 collective-permute-done.3.near_query
  47.2 0.7 copy-done.10
  47.8 0.0 collective-permute-done.1.weight
  47.8 1.0 %copy-done.3 = bf16[256,2048]{1,0:T(8,128)(2,1)} copy-done((bf16[256,2048]{1,0:T(8,128)(2,1)}, bf16[256,2048]{1,0:T(8,128)(2,1)S(1)}, u32[]{:S(2)}) %copy-start.3) | copy-done | bytes 1048600
  48.8 0.0 all-to-all-done.gathered
  48.8 1.2 %copy-done.4 = bf16[256,2048]{1,0:T(8,128)(2,1)S(1)} copy-done((bf16[256,2048]{1,0:T(8,128)(2,1)S(1)}, bf16[256,2048]{1,0:T(8,128)(2,1)}, u32[]{:S(2)}) %copy-start.4) | copy-done | bytes 1048600
  50.0 0.5 shard_map.96
  50.5 0.0 copy-start.6
  50.5 0.0 copy-start.8
  50.5 0.0 copy-start.9
  50.5 0.0 copy-start.11
  50.5 2.1 %collective-permute-start.5 = (bf16[256,256]{1,0:T(8,128)(2,1)S(1)}, bf16[256,256]{1,0:T(8,128)(2,1)S(1)}, u32[]{:S(2)}, u32[]{:S(2)}) collective-permute-start(bf16[256,256]{1,0:T(8,128)(2,1)S(1)} %shard_map.96), channel_id=1, source_target_pairs={{0,1},{1,0},{2,3},{3,2},{4,5},{5,4},{6,7},{7,6},{8,9},{9,8},{10,11... | collective-permute-start | bytes 393224 | tf_op jit(solution)/shard_map/ppermute | solution.py:299
  52.6 0.5 shard_map.95.own
  53.1 0.8 collective-permute-done.5.received
  54.0 18.4 %collective-permute-start.6 = (bf16[256,256]{1,0:T(8,128)(2,1)S(1)}, bf16[256,256]{1,0:T(8,128)(2,1)S(1)}, u32[]{:S(2)}, u32[]{:S(2)}) collective-permute-start(bf16[256,256]{1,0:T(8,128)(2,1)S(1)} %get-tuple-element.28.grad), channel_id=1, source_target_pairs={{8,0},{16,8},{24,16},{32,24},{40,32},{48,40},{56,48},{64,56},{72,6... | collective-permute-start | bytes 393224 | tf_op jit(solution)/shard_map/ppermute | solution.py:294
  72.3 1.9 %collective-permute-start.7 = (bf16[128,256]{1,0:T(8,128)(2,1)S(1)}, bf16[128,256]{1,0:T(8,128)(2,1)S(1)}, u32[]{:S(2)}, u32[]{:S(2)}) collective-permute-start(bf16[128,256]{1,0:T(8,128)(2,1)S(1)} %get-tuple-element.41), channel_id=1, source_target_pairs={{16,0},{24,8},{32,16},{40,24},{48,32},{56,40},{64,48},{72,56},{80,... | collective-permute-start | bytes 196616 | tf_op jit(solution)/shard_map/ppermute | solution.py:294
  74.9 0.0 collective-permute-done.near
  74.9 0.0 copy-done.6
  74.9 0.0 copy-done.8
  74.9 0.0 copy-done.9
  75.0 3.6 %shard_map.98 = (f32[2,128,640]{2,1,0:T(8,128)S(1)}, f32[2,128,512]{2,1,0:T(8,128)S(1)}, bf16[256,256]{1,0:T(8,128)(2,1)S(1)}, f32[8,256]{1,0:T(8,128)S(1)}, f32[8,128]{1,0:T(8,128)S(1)}) custom-call(s32[128,128]{1,0:T(8,128)S(1)} %copy-done.9, s32[1]{0:T(128)S(6)} %copy.10.seed, bf16[256,256]{1,0:T(8,128)(2,1)S(1)} %copy-done.6, ...), custom_call_target="tpu_custom_call" | custom-call | tf_op jit(solution)/shard_map/pallas_call | solution.py:281
  78.6 1.9 %collective-permute-start.8 = (f32[8,256]{1,0:T(8,128)S(1)}, f32[8,256]{1,0:T(8,128)S(1)}, u32[]{:S(2)}, u32[]{:S(2)}) collective-permute-start(f32[8,256]{1,0:T(8,128)S(1)} %get-tuple-element.33), channel_id=1, source_target_pairs={{8,0},{16,8},{24,16},{32,24},{40,32},{48,40},{56,48},{64,56},{72,6... | collective-permute-start | bytes 24584 | tf_op jit(solution)/shard_map/ppermute | solution.py:294
  80.5 1.9 %collective-permute-start.9 = (f32[8,128]{1,0:T(8,128)S(1)}, f32[8,128]{1,0:T(8,128)S(1)}, u32[]{:S(2)}, u32[]{:S(2)}) collective-permute-start(f32[8,128]{1,0:T(8,128)S(1)} %get-tuple-element.42), channel_id=1, source_target_pairs={{16,0},{24,8},{32,16},{40,24},{48,32},{56,40},{64,48},{72,56},{80,... | collective-permute-start | bytes 12296 | tf_op jit(solution)/shard_map/ppermute | solution.py:294
  82.4 2.1 %shard_map.100 = (f32[2,256,256]{2,1,0:T(8,128)S(1)}, f32[2,256,256]{2,1,0:T(8,128)S(1)}, f32[2,128,128]{2,1,0:T(8,128)S(1)}, f32[2,128,128]{2,1,0:T(8,128)S(1)}) custom-call(s32[128,128]{1,0:T(8,128)S(1)} %copy-done.9, s32[1]{0:T(128)S(6)} %copy.10.seed, bf16[256,256]{1,0:T(8,128)(2,1)S(1)} %copy-done.1, bf16[256,256]{1,0:T(8,128)(2,1)S(1)} %copy-done.11, ...), custom_call_target="tpu_custom_call" | custom-call | tf_op jit(solution)/shard_map/pallas_call | solution.py:281
  84.5 2.6 %shard_map.99 = (bf16[256,256]{1,0:T(8,128)(2,1)}, f32[256,256]{1,0:T(8,128)S(1)}, f32[256,256]{1,0:T(8,128)S(1)}) custom-call(f32[2,128,640]{2,1,0:T(8,128)S(1)} %get-tuple-element.29.signed_top, f32[2,128,512]{2,1,0:T(8,128)S(1)} %get-tuple-element.30.signed_low, bf16[256,256]{1,0:T(8,128)(2,1)S(1)} %get-tuple-element.31.attended, ...), custom_call_target="tpu_custom_call" | custom-call | tf_op jit(solution)/shard_map/pallas_call | solution.py:281
  87.2 0.0 collective-permute-done.9.far_stats
  87.2 0.0 collective-permute-done.8.near_stats
  87.2 0.0 collective-permute-done.7.far_grad
  87.2 0.0 collective-permute-done.6.near_grad
  87.2 1.2 %shard_map.101 = (bf16[256,256]{1,0:T(8,128)(2,1)}, bf16[256,256]{1,0:T(8,128)(2,1)}) custom-call(f32[2,256,256]{2,1,0:T(8,128)S(1)} %get-tuple-element.37.near_scores, f32[2,256,256]{2,1,0:T(8,128)S(1)} %get-tuple-element.38.near_keeps, f32[2,128,128]{2,1,0:T(8,128)S(1)} %get-tuple-element.39.far_scores, f32[2,128,128]{2,1,0:T(8,128)S(1)} %get-tuple-element.40.far_keeps, ...), custom_call_target="tpu_custom_call" | custom-call | flops 1495000064 | bytes 2633728 | tf_op jit(solution)/shard_map/pallas_call | solution.py:281
  (14 shorter events, 0.1 us)
Async XLA Ops:
  0.6 7.0 %copy-start = (bf16[256,4096]{1,0:T(8,128)(2,1)S(1)}, bf16[256,4096]{1,0:T(8,128)(2,1)}, u32[]{:S(2)}) copy-start(bf16[256,4096]{1,0:T(8,128)(2,1)} %weight.3) | copy-start | bytes 6291460
  2.8 46.0 %all-to-all-start = ((bf16[4,256,512]{2,1,0:T(8,128)(2,1)}), bf16[4,256,512]{2,1,0:T(8,128)(2,1)S(1)}, u32[]{:S(2)}, u32[]{:S(2)}) async-start(bf16[4,256,512]{2,1,0:T(8,128)(2,1)} %broadcast_in_dim.2), calls=%async_computation | async-start | bytes 2097152 | tf_op jit(solution)/shard_map/all_to_all | solution.py:308
  7.7 2.2 %slice-start = ((bf16[256,256]{1,0:T(8,128)(2,1)}), bf16[128,256]{1,0:T(8,128)(2,1)S(1)}, s32[]{:S(2)}) async-start(bf16[256,256]{1,0:T(8,128)(2,1)} %key.4), calls=%async_computation.1 | async-start | bytes 131072 | tf_op jit(solution)/shard_map/slice | solution.py:311
  7.7 2.2 %slice-start.1 = ((bf16[256,256]{1,0:T(8,128)(2,1)}), bf16[128,256]{1,0:T(8,128)(2,1)S(1)}, s32[]{:S(2)}) async-start(bf16[256,256]{1,0:T(8,128)(2,1)} %value.5), calls=%async_computation.2 | async-start | bytes 131072 | tf_op jit(solution)/shard_map/slice | solution.py:311
  7.7 8.3 %copy-start.5 = (bf16[256,256]{1,0:T(8,128)(2,1)S(1)}, bf16[256,256]{1,0:T(8,128)(2,1)}, u32[]{:S(2)}) copy-start(bf16[256,256]{1,0:T(8,128)(2,1)} %query.3) | copy-start | bytes 393220
  7.7 24.2 %copy-start.1 = (bf16[256,256]{1,0:T(8,128)(2,1)S(1)}, bf16[256,256]{1,0:T(8,128)(2,1)}, u32[]{:S(2)}) copy-start(bf16[256,256]{1,0:T(8,128)(2,1)} %key.4) | copy-start | bytes 393220
  7.7 24.2 %copy-start.2 = (bf16[256,256]{1,0:T(8,128)(2,1)S(1)}, bf16[256,256]{1,0:T(8,128)(2,1)}, u32[]{:S(2)}) copy-start(bf16[256,256]{1,0:T(8,128)(2,1)} %value.5) | copy-start | bytes 393220
  7.8 40.0 %collective-permute-start.1 = (bf16[256,2048]{1,0:T(8,128)(2,1)S(1)}, bf16[256,2048]{1,0:T(8,128)(2,1)S(1)}, u32[]{:S(2)}, u32[]{:S(2)}) collective-permute-start(bf16[256,2048]{1,0:T(8,128)(2,1)S(1)} %shard_map.94), channel_id=1, source_target_pairs={{0,1},{1,0},{2,3},{3,2},{4,5},{5,4},{6,7},{7,6},{8,9},{9,8},{10,11... | collective-permute-start | bytes 3145736 | tf_op jit(solution)/shard_map/ppermute | solution.py:299
  9.9 36.6 %collective-permute-start.2 = (bf16[256,256]{1,0:T(8,128)(2,1)S(1)}, bf16[256,256]{1,0:T(8,128)(2,1)S(1)}, u32[]{:S(2)}, u32[]{:S(2)}) collective-permute-start(bf16[256,256]{1,0:T(8,128)(2,1)S(1)} %pad_maximum_fusion.1), channel_id=1, source_target_pairs={{0,16},{8,24},{16,32},{24,40},{32,48},{40,56},{48,64},{56,72},{64,... | collective-permute-start | bytes 393224 | tf_op jit(solution)/shard_map/ppermute | solution.py:294
  16.0 31.1 %collective-permute-start.3 = (bf16[256,256]{1,0:T(8,128)(2,1)S(1)}, bf16[256,256]{1,0:T(8,128)(2,1)S(1)}, u32[]{:S(2)}, u32[]{:S(2)}) collective-permute-start(bf16[256,256]{1,0:T(8,128)(2,1)S(1)} %copy-done.5), channel_id=1, source_target_pairs={{8,0},{16,8},{24,16},{32,24},{40,32},{48,40},{56,48},{64,56},{72,6... | collective-permute-start | bytes 393224 | tf_op jit(solution)/shard_map/ppermute | solution.py:294
  27.0 8.2 %collective-permute-start.4 = (bf16[128,256]{1,0:T(8,128)(2,1)S(1)}, bf16[128,256]{1,0:T(8,128)(2,1)S(1)}, u32[]{:S(2)}, u32[]{:S(2)}) collective-permute-start(bf16[128,256]{1,0:T(8,128)(2,1)S(1)} %slice.11), channel_id=1, source_target_pairs={{16,0},{24,8},{32,16},{40,24},{48,32},{56,40},{64,48},{72,56},{80,... | collective-permute-start | bytes 196616 | tf_op jit(solution)/shard_map/ppermute | solution.py:294
  32.6 42.3 %collective-permute-start = (bf16[512,256]{1,0:T(8,128)(2,1)}, bf16[512,256]{1,0:T(8,128)(2,1)}, u32[]{:S(2)}, u32[]{:S(2)}) collective-permute-start(bf16[512,256]{1,0:T(8,128)(2,1)} %pad_maximum_fusion), channel_id=1, source_target_pairs={{0,8},{8,16},{16,24},{24,32},{32,40},{40,48},{48,56},{56,64},{64,7... | collective-permute-start | bytes 786440 | tf_op jit(solution)/shard_map/ppermute | solution.py:294
  46.5 0.7 copy-start.7
  47.2 0.7 copy-start.10
  47.8 1.0 %copy-start.3 = (bf16[256,2048]{1,0:T(8,128)(2,1)}, bf16[256,2048]{1,0:T(8,128)(2,1)S(1)}, u32[]{:S(2)}) copy-start(bf16[256,2048]{1,0:T(8,128)(2,1)S(1)} %collective-permute-done.1.weight) | copy-start | bytes 3145732
  48.8 1.2 %copy-start.4 = (bf16[256,2048]{1,0:T(8,128)(2,1)S(1)}, bf16[256,2048]{1,0:T(8,128)(2,1)}, u32[]{:S(2)}) copy-start(bf16[256,2048]{1,0:T(8,128)(2,1)} %copy-done.3) | copy-start | bytes 3145732
  50.5 24.4 %copy-start.6 = (bf16[256,256]{1,0:T(8,128)(2,1)S(1)}, bf16[256,256]{1,0:T(8,128)(2,1)}, u32[]{:S(2)}) copy-start(bf16[256,256]{1,0:T(8,128)(2,1)} %query.3) | copy-start | bytes 393220
  50.5 24.4 %copy-start.8 = (bf16[256,256]{1,0:T(8,128)(2,1)S(1)}, bf16[256,256]{1,0:T(8,128)(2,1)}, u32[]{:S(2)}) copy-start(bf16[256,256]{1,0:T(8,128)(2,1)} %copy-done.7) | copy-start | bytes 393220
  50.5 24.4 %copy-start.9 = (s32[128,128]{1,0:T(8,128)S(1)}, s32[128,128]{1,0:T(8,128)}, u32[]{:S(2)}) copy-start(s32[128,128]{1,0:T(8,128)} %table.3) | copy-start | bytes 196612
  50.5 31.9 %copy-start.11 = (bf16[256,256]{1,0:T(8,128)(2,1)S(1)}, bf16[256,256]{1,0:T(8,128)(2,1)}, u32[]{:S(2)}) copy-start(bf16[256,256]{1,0:T(8,128)(2,1)} %copy-done.10) | copy-start | bytes 393220
  50.5 3.4 %collective-permute-start.5 = (bf16[256,256]{1,0:T(8,128)(2,1)S(1)}, bf16[256,256]{1,0:T(8,128)(2,1)S(1)}, u32[]{:S(2)}, u32[]{:S(2)}) collective-permute-start(bf16[256,256]{1,0:T(8,128)(2,1)S(1)} %shard_map.96), channel_id=1, source_target_pairs={{0,1},{1,0},{2,3},{3,2},{4,5},{5,4},{6,7},{7,6},{8,9},{9,8},{10,11... | collective-permute-start | bytes 393224 | tf_op jit(solution)/shard_map/ppermute | solution.py:299
  54.0 33.2 %collective-permute-start.6 = (bf16[256,256]{1,0:T(8,128)(2,1)S(1)}, bf16[256,256]{1,0:T(8,128)(2,1)S(1)}, u32[]{:S(2)}, u32[]{:S(2)}) collective-permute-start(bf16[256,256]{1,0:T(8,128)(2,1)S(1)} %get-tuple-element.28.grad), channel_id=1, source_target_pairs={{8,0},{16,8},{24,16},{32,24},{40,32},{48,40},{56,48},{64,56},{72,6... | collective-permute-start | bytes 393224 | tf_op jit(solution)/shard_map/ppermute | solution.py:294
  72.3 14.8 %collective-permute-start.7 = (bf16[128,256]{1,0:T(8,128)(2,1)S(1)}, bf16[128,256]{1,0:T(8,128)(2,1)S(1)}, u32[]{:S(2)}, u32[]{:S(2)}) collective-permute-start(bf16[128,256]{1,0:T(8,128)(2,1)S(1)} %get-tuple-element.41), channel_id=1, source_target_pairs={{16,0},{24,8},{32,16},{40,24},{48,32},{56,40},{64,48},{72,56},{80,... | collective-permute-start | bytes 196616 | tf_op jit(solution)/shard_map/ppermute | solution.py:294
  78.6 8.6 %collective-permute-start.8 = (f32[8,256]{1,0:T(8,128)S(1)}, f32[8,256]{1,0:T(8,128)S(1)}, u32[]{:S(2)}, u32[]{:S(2)}) collective-permute-start(f32[8,256]{1,0:T(8,128)S(1)} %get-tuple-element.33), channel_id=1, source_target_pairs={{8,0},{16,8},{24,16},{32,24},{40,32},{48,40},{56,48},{64,56},{72,6... | collective-permute-start | bytes 24584 | tf_op jit(solution)/shard_map/ppermute | solution.py:294
  80.5 6.7 %collective-permute-start.9 = (f32[8,128]{1,0:T(8,128)S(1)}, f32[8,128]{1,0:T(8,128)S(1)}, u32[]{:S(2)}, u32[]{:S(2)}) collective-permute-start(f32[8,128]{1,0:T(8,128)S(1)} %get-tuple-element.42), channel_id=1, source_target_pairs={{16,0},{24,8},{32,16},{40,24},{48,32},{56,40},{64,48},{72,56},{80,... | collective-permute-start | bytes 12296 | tf_op jit(solution)/shard_map/ppermute | solution.py:294

commit v10 on v9

--- a/solution.py
+++ b/solution.py
@@ -306,7 +306,6 @@
 
     copies = jnp.broadcast_to(grad_out[None], (count // 2, *grad_out.shape))
     gathered = lax.all_to_all(copies, "head", 0, 0, axis_index_groups=groups)
-    near_keys = shifted(jnp.concatenate((key_rows, value_rows)), 1)
     near_query = shifted(query_rows, -1)
     far_keys = shifted(jnp.concatenate((key_rows[MB:], value_rows[MB:])), 2)
     far_query = shifted(query_rows[:MB], -2)
@@ -314,9 +313,11 @@
     width = (count // 2) * grad_out.shape[1]
     (theirs,) = call(cut_kernel, [VMEM], [((WIDE, width), half)], 0.0, out_weight)
     other_weight = other_core(theirs)
-    gathered, other_weight, far_keys, near_query, far_query = lax.optimization_barrier(
-        (gathered, other_weight, far_keys, near_query, far_query)
-    )
+    own_keys = jnp.concatenate((key_rows, value_rows))
+    gathered, other_weight, far_keys, near_query, far_query, own_keys = lax.optimization_barrier(
+        (gathered, other_weight, far_keys, near_query, far_query, own_keys)
+    )
+    near_keys = shifted(own_keys, 1)
     (sent,) = call(
         project_other_kernel, [VMEM] * 2, [((ROWS, WIDE), half)], 0.0, gathered, other_weight
     )

time: 89 us -> 82.9 us (0.931)
  starting transfers between devices: 56.9 us -> 49.4 us
  waiting for transfers between devices: 12.8 us -> 15.3 us
  Pallas kernels: 10.6 us -> 9.69 us
    ppermute x8, starting transfers between devices: 47.9 us -> 40.4 us  [shifted(): return lax.ppermute(value, 'blk', pairs)]
    ppermute x8, waiting for transfers between devices: 12 us -> 14.5 us  [shifted(): return lax.ppermute(value, 'blk', pairs)]
    pallas_call x8, Pallas kernels: 10.6 us -> 9.69 us  [call(): pl.pallas_call(kernel, out_shape=shapes, in_specs=specs, out_specs=[VMEM]...]
  transfers between devices with their start and end apart: 11 -> 11, of which waited for: 3 -> 4; matrix products, arithmetic and copies ran while one was open for 1% -> 1% of each run, Pallas kernels for 11% -> 10%
where the time goes in v10:
time: 82.9 us; the launch traced here: 82.4 us
  starting transfers between devices  49.4 us (60%)
  waiting for transfers between devices  15.3 us (18%)
  Pallas kernels  9.69 us (12%)
  local copies, waits for them, and re-layouts  5.72 us (7%)
  between operations  1.58 us (2%)
    ppermute x8, starting transfers between devices, shifted(): return lax.ppermute(value, 'blk', pairs)  40.4 us
    ppermute x8, waiting for transfers between devices, shifted(): return lax.ppermute(value, 'blk', pairs)  14.5 us
    pallas_call x8, Pallas kernels, call(): pl.pallas_call(kernel, out_shape=shapes, in_specs=specs, out_specs=[VMEM]...  9.69 us
    all_to_all x1, starting transfers between devices, on_device(): gathered = lax.all_to_all(copies, 'head', 0, 0, axis_index_groups=groups)  4.87 us
    ppermute x2, starting transfers between devices, other_core(): lax.ppermute(value, 'head', [(source, source ^ 1) for source in range(cou...  4.1 us
    unnamed x24, local copies, waits for them, and re-layouts  3.55 us
    broadcast_in_dim x1, local copies, waits for them, and re-layouts, on_device(): copies = jnp.broadcast_to(grad_out[None], (count // 2, *grad_out.shape))  2.16 us
  transfers between devices with their start and end apart: 11, of which 4 were waited for; matrix products, arithmetic and copies ran while one was open for 1% of the time, Pallas kernels for 10%

profile of v10, /device:TPU:6, one launch (start us, length us, event | category | flops | bytes accessed | tf_op | source)
XLA Modules:
  0.0 82.4 jit_solution(1795746154152989143)
XLA Ops:
  0.6 0.0 copy-start
  0.6 2.2 %broadcast_in_dim.2 = bf16[4,256,512]{2,1,0:T(8,128)(2,1)} broadcast(bf16[256,512]{1,0:T(8,128)(2,1)} %param.10), dimensions={1,2} | broadcast | bytes 1310720 | tf_op jit(solution)/shard_map/broadcast_in_dim | solution.py:307
  2.8 4.9 %all-to-all-start = ((bf16[4,256,512]{2,1,0:T(8,128)(2,1)}), bf16[4,256,512]{2,1,0:T(8,128)(2,1)S(1)}, u32[]{:S(2)}, u32[]{:S(2)}) async-start(bf16[4,256,512]{2,1,0:T(8,128)(2,1)} %broadcast_in_dim.2), calls=%async_computation | async-start | bytes 2097152 | tf_op jit(solution)/shard_map/all_to_all | solution.py:308
  7.7 0.0 copy-start.5
  7.7 0.0 copy-start.1
  7.7 0.0 copy-start.2
  7.7 0.1 shard_map.94
  7.8 2.1 %collective-permute-start = (bf16[256,2048]{1,0:T(8,128)(2,1)S(1)}, bf16[256,2048]{1,0:T(8,128)(2,1)S(1)}, u32[]{:S(2)}, u32[]{:S(2)}) collective-permute-start(bf16[256,2048]{1,0:T(8,128)(2,1)S(1)} %shard_map.94), channel_id=1, source_target_pairs={{0,1},{1,0},{2,3},{3,2},{4,5},{5,4},{6,7},{7,6},{8,9},{9,8},{10,11... | collective-permute-start | bytes 3145736 | tf_op jit(solution)/shard_map/ppermute | solution.py:299
  9.9 0.0 slice-done
  9.9 0.0 slice-done.1
  9.9 6.1 %collective-permute-start.1 = (bf16[256,256]{1,0:T(8,128)(2,1)S(1)}, bf16[256,256]{1,0:T(8,128)(2,1)S(1)}, u32[]{:S(2)}, u32[]{:S(2)}) collective-permute-start(bf16[256,256]{1,0:T(8,128)(2,1)S(1)} %pad_maximum_fusion.1), channel_id=1, source_target_pairs={{0,16},{8,24},{16,32},{24,40},{32,48},{40,56},{48,64},{56,72},{64,... | collective-permute-start | bytes 393224 | tf_op jit(solution)/shard_map/ppermute | solution.py:294
  16.0 11.0 %collective-permute-start.2 = (bf16[256,256]{1,0:T(8,128)(2,1)S(1)}, bf16[256,256]{1,0:T(8,128)(2,1)S(1)}, u32[]{:S(2)}, u32[]{:S(2)}) collective-permute-start(bf16[256,256]{1,0:T(8,128)(2,1)S(1)} %copy-done.5), channel_id=1, source_target_pairs={{8,0},{16,8},{24,16},{32,24},{40,32},{48,40},{56,48},{64,56},{72,6... | collective-permute-start | bytes 393224 | tf_op jit(solution)/shard_map/ppermute | solution.py:294
  27.0 4.8 %collective-permute-start.3 = (bf16[128,256]{1,0:T(8,128)(2,1)S(1)}, bf16[128,256]{1,0:T(8,128)(2,1)S(1)}, u32[]{:S(2)}, u32[]{:S(2)}) collective-permute-start(bf16[128,256]{1,0:T(8,128)(2,1)S(1)} %slice.11), channel_id=1, source_target_pairs={{16,0},{24,8},{32,16},{40,24},{48,32},{56,40},{64,48},{72,56},{80,... | collective-permute-start | bytes 196616 | tf_op jit(solution)/shard_map/ppermute | solution.py:294
  31.9 0.7 pad_maximum_fusion
  32.6 2.6 %collective-permute-done.3.far_query = bf16[128,256]{1,0:T(8,128)(2,1)S(1)} collective-permute-done((bf16[128,256]{1,0:T(8,128)(2,1)S(1)}, bf16[128,256]{1,0:T(8,128)(2,1)S(1)}, u32[]{:S(2)}, u32[]{:S(2)}) %collective-permute-start.3) | collective-permute-done | bytes 65568 | tf_op jit(solution)/shard_map/ppermute | solution.py:294
  35.2 11.2 %collective-permute-done.1.far = bf16[256,256]{1,0:T(8,128)(2,1)S(1)} collective-permute-done((bf16[256,256]{1,0:T(8,128)(2,1)S(1)}, bf16[256,256]{1,0:T(8,128)(2,1)S(1)}, u32[]{:S(2)}, u32[]{:S(2)}) %collective-permute-start.1) | collective-permute-done | bytes 131104 | tf_op jit(solution)/shard_map/ppermute | solution.py:294
  46.4 0.7 copy-done.7
  47.0 0.0 collective-permute-done.2.near_query
  47.1 0.7 copy-done.10
  47.7 0.0 collective-permute-done.weight
  47.7 1.0 %copy-done.3 = bf16[256,2048]{1,0:T(8,128)(2,1)} copy-done((bf16[256,2048]{1,0:T(8,128)(2,1)}, bf16[256,2048]{1,0:T(8,128)(2,1)S(1)}, u32[]{:S(2)}) %copy-start.3) | copy-done | bytes 1048600
  48.7 0.0 all-to-all-done.gathered
  48.7 3.3 %collective-permute-start.4 = (bf16[512,256]{1,0:T(8,128)(2,1)}, bf16[512,256]{1,0:T(8,128)(2,1)S(1)}, u32[]{:S(2)}, u32[]{:S(2)}) collective-permute-start(bf16[512,256]{1,0:T(8,128)(2,1)} %pad_maximum_fusion), channel_id=1, source_target_pairs={{0,8},{8,16},{16,24},{24,32},{32,40},{40,48},{48,56},{56,64},{64,7... | collective-permute-start | bytes 786440 | tf_op jit(solution)/shard_map/ppermute | solution.py:294
  52.0 1.2 %copy-done.4 = bf16[256,2048]{1,0:T(8,128)(2,1)S(1)} copy-done((bf16[256,2048]{1,0:T(8,128)(2,1)S(1)}, bf16[256,2048]{1,0:T(8,128)(2,1)}, u32[]{:S(2)}) %copy-start.4) | copy-done | bytes 1048600
  53.2 0.5 shard_map.96
  53.7 0.0 copy-start.6
  53.7 0.0 copy-start.8
  53.7 0.0 copy-start.9
  53.7 0.0 copy-start.11
  53.7 2.1 %collective-permute-start.5 = (bf16[256,256]{1,0:T(8,128)(2,1)S(1)}, bf16[256,256]{1,0:T(8,128)(2,1)S(1)}, u32[]{:S(2)}, u32[]{:S(2)}) collective-permute-start(bf16[256,256]{1,0:T(8,128)(2,1)S(1)} %shard_map.96), channel_id=1, source_target_pairs={{0,1},{1,0},{2,3},{3,2},{4,5},{5,4},{6,7},{7,6},{8,9},{9,8},{10,11... | collective-permute-start | bytes 393224 | tf_op jit(solution)/shard_map/ppermute | solution.py:299
  55.8 0.5 shard_map.95.own
  56.3 0.8 collective-permute-done.5.received
  57.1 9.5 %collective-permute-start.6 = (bf16[256,256]{1,0:T(8,128)(2,1)S(1)}, bf16[256,256]{1,0:T(8,128)(2,1)S(1)}, u32[]{:S(2)}, u32[]{:S(2)}) collective-permute-start(bf16[256,256]{1,0:T(8,128)(2,1)S(1)} %get-tuple-element.30.grad), channel_id=1, source_target_pairs={{8,0},{16,8},{24,16},{32,24},{40,32},{48,40},{56,48},{64,56},{72,6... | collective-permute-start | bytes 393224 | tf_op jit(solution)/shard_map/ppermute | solution.py:294
  66.6 1.9 %collective-permute-start.7 = (bf16[128,256]{1,0:T(8,128)(2,1)S(1)}, bf16[128,256]{1,0:T(8,128)(2,1)S(1)}, u32[]{:S(2)}, u32[]{:S(2)}) collective-permute-start(bf16[128,256]{1,0:T(8,128)(2,1)S(1)} %get-tuple-element.43), channel_id=1, source_target_pairs={{16,0},{24,8},{32,16},{40,24},{48,32},{56,40},{64,48},{72,56},{80,... | collective-permute-start | bytes 196616 | tf_op jit(solution)/shard_map/ppermute | solution.py:294
  69.2 0.0 collective-permute-done.4.near
  69.2 0.0 copy-done.6
  69.2 0.0 copy-done.8
  69.2 0.0 copy-done.9
  69.2 3.6 %shard_map.98 = (f32[2,128,640]{2,1,0:T(8,128)S(1)}, f32[2,128,512]{2,1,0:T(8,128)S(1)}, bf16[256,256]{1,0:T(8,128)(2,1)S(1)}, f32[8,256]{1,0:T(8,128)S(1)}, f32[8,128]{1,0:T(8,128)S(1)}) custom-call(s32[128,128]{1,0:T(8,128)S(1)} %copy-done.9, s32[1]{0:T(128)S(6)} %copy.10.seed, bf16[256,256]{1,0:T(8,128)(2,1)S(1)} %copy-done.6, ...), custom_call_target="tpu_custom_call" | custom-call | tf_op jit(solution)/shard_map/pallas_call | solution.py:281
  72.8 1.9 %collective-permute-start.8 = (f32[8,256]{1,0:T(8,128)S(1)}, f32[8,256]{1,0:T(8,128)S(1)}, u32[]{:S(2)}, u32[]{:S(2)}) collective-permute-start(f32[8,256]{1,0:T(8,128)S(1)} %get-tuple-element.35), channel_id=1, source_target_pairs={{8,0},{16,8},{24,16},{32,24},{40,32},{48,40},{56,48},{64,56},{72,6... | collective-permute-start | bytes 24584 | tf_op jit(solution)/shard_map/ppermute | solution.py:294
  74.7 1.9 %collective-permute-start.9 = (f32[8,128]{1,0:T(8,128)S(1)}, f32[8,128]{1,0:T(8,128)S(1)}, u32[]{:S(2)}, u32[]{:S(2)}) collective-permute-start(f32[8,128]{1,0:T(8,128)S(1)} %get-tuple-element.44), channel_id=1, source_target_pairs={{16,0},{24,8},{32,16},{40,24},{48,32},{56,40},{64,48},{72,56},{80,... | collective-permute-start | bytes 12296 | tf_op jit(solution)/shard_map/ppermute | solution.py:294
  76.7 2.1 %shard_map.100 = (f32[2,256,256]{2,1,0:T(8,128)S(1)}, f32[2,256,256]{2,1,0:T(8,128)S(1)}, f32[2,128,128]{2,1,0:T(8,128)S(1)}, f32[2,128,128]{2,1,0:T(8,128)S(1)}) custom-call(s32[128,128]{1,0:T(8,128)S(1)} %copy-done.9, s32[1]{0:T(128)S(6)} %copy.10.seed, bf16[256,256]{1,0:T(8,128)(2,1)S(1)} %copy-done.1, bf16[256,256]{1,0:T(8,128)(2,1)S(1)} %copy-done.11, ...), custom_call_target="tpu_custom_call" | custom-call | tf_op jit(solution)/shard_map/pallas_call | solution.py:281
  78.8 1.7 %shard_map.99 = (bf16[256,256]{1,0:T(8,128)(2,1)}, f32[256,256]{1,0:T(8,128)S(1)}, f32[256,256]{1,0:T(8,128)S(1)}) custom-call(f32[2,128,640]{2,1,0:T(8,128)S(1)} %get-tuple-element.31.signed_top, f32[2,128,512]{2,1,0:T(8,128)S(1)} %get-tuple-element.32.signed_low, bf16[256,256]{1,0:T(8,128)(2,1)S(1)} %get-tuple-element.33.attended, ...), custom_call_target="tpu_custom_call" | custom-call | tf_op jit(solution)/shard_map/pallas_call | solution.py:281
  80.5 0.0 collective-permute-done.7.far_grad
  80.5 0.0 collective-permute-done.6.near_grad
  80.5 0.7 collective-permute-done.9.far_stats
  81.1 0.0 collective-permute-done.8.near_stats
  81.1 1.2 %shard_map.101 = (bf16[256,256]{1,0:T(8,128)(2,1)}, bf16[256,256]{1,0:T(8,128)(2,1)}) custom-call(f32[2,256,256]{2,1,0:T(8,128)S(1)} %get-tuple-element.39.near_scores, f32[2,256,256]{2,1,0:T(8,128)S(1)} %get-tuple-element.40.near_keeps, f32[2,128,128]{2,1,0:T(8,128)S(1)} %get-tuple-element.41.far_scores, f32[2,128,128]{2,1,0:T(8,128)S(1)} %get-tuple-element.42.far_keeps, ...), custom_call_target="tpu_custom_call" | custom-call | flops 1495000064 | bytes 2633728 | tf_op jit(solution)/shard_map/pallas_call | solution.py:281
  (14 shorter events, 0.1 us)
Async XLA Ops:
  0.6 7.0 %copy-start = (bf16[256,4096]{1,0:T(8,128)(2,1)S(1)}, bf16[256,4096]{1,0:T(8,128)(2,1)}, u32[]{:S(2)}) copy-start(bf16[256,4096]{1,0:T(8,128)(2,1)} %weight.3) | copy-start | bytes 6291460
  2.8 45.9 %all-to-all-start = ((bf16[4,256,512]{2,1,0:T(8,128)(2,1)}), bf16[4,256,512]{2,1,0:T(8,128)(2,1)S(1)}, u32[]{:S(2)}, u32[]{:S(2)}) async-start(bf16[4,256,512]{2,1,0:T(8,128)(2,1)} %broadcast_in_dim.2), calls=%async_computation | async-start | bytes 2097152 | tf_op jit(solution)/shard_map/all_to_all | solution.py:308
  7.7 2.2 %slice-start = ((bf16[256,256]{1,0:T(8,128)(2,1)}), bf16[128,256]{1,0:T(8,128)(2,1)S(1)}, s32[]{:S(2)}) async-start(bf16[256,256]{1,0:T(8,128)(2,1)} %key.4), calls=%async_computation.1 | async-start | bytes 131072 | tf_op jit(solution)/shard_map/slice | solution.py:310
  7.7 2.2 %slice-start.1 = ((bf16[256,256]{1,0:T(8,128)(2,1)}), bf16[128,256]{1,0:T(8,128)(2,1)S(1)}, s32[]{:S(2)}) async-start(bf16[256,256]{1,0:T(8,128)(2,1)} %value.5), calls=%async_computation.2 | async-start | bytes 131072 | tf_op jit(solution)/shard_map/slice | solution.py:310
  7.7 8.3 %copy-start.5 = (bf16[256,256]{1,0:T(8,128)(2,1)S(1)}, bf16[256,256]{1,0:T(8,128)(2,1)}, u32[]{:S(2)}) copy-start(bf16[256,256]{1,0:T(8,128)(2,1)} %query.3) | copy-start | bytes 393220
  7.7 24.2 %copy-start.1 = (bf16[256,256]{1,0:T(8,128)(2,1)S(1)}, bf16[256,256]{1,0:T(8,128)(2,1)}, u32[]{:S(2)}) copy-start(bf16[256,256]{1,0:T(8,128)(2,1)} %key.4) | copy-start | bytes 393220
  7.7 24.2 %copy-start.2 = (bf16[256,256]{1,0:T(8,128)(2,1)S(1)}, bf16[256,256]{1,0:T(8,128)(2,1)}, u32[]{:S(2)}) copy-start(bf16[256,256]{1,0:T(8,128)(2,1)} %value.5) | copy-start | bytes 393220
  7.8 39.9 %collective-permute-start = (bf16[256,2048]{1,0:T(8,128)(2,1)S(1)}, bf16[256,2048]{1,0:T(8,128)(2,1)S(1)}, u32[]{:S(2)}, u32[]{:S(2)}) collective-permute-start(bf16[256,2048]{1,0:T(8,128)(2,1)S(1)} %shard_map.94), channel_id=1, source_target_pairs={{0,1},{1,0},{2,3},{3,2},{4,5},{5,4},{6,7},{7,6},{8,9},{9,8},{10,11... | collective-permute-start | bytes 3145736 | tf_op jit(solution)/shard_map/ppermute | solution.py:299
  9.9 36.5 %collective-permute-start.1 = (bf16[256,256]{1,0:T(8,128)(2,1)S(1)}, bf16[256,256]{1,0:T(8,128)(2,1)S(1)}, u32[]{:S(2)}, u32[]{:S(2)}) collective-permute-start(bf16[256,256]{1,0:T(8,128)(2,1)S(1)} %pad_maximum_fusion.1), channel_id=1, source_target_pairs={{0,16},{8,24},{16,32},{24,40},{32,48},{40,56},{48,64},{56,72},{64,... | collective-permute-start | bytes 393224 | tf_op jit(solution)/shard_map/ppermute | solution.py:294
  16.0 31.0 %collective-permute-start.2 = (bf16[256,256]{1,0:T(8,128)(2,1)S(1)}, bf16[256,256]{1,0:T(8,128)(2,1)S(1)}, u32[]{:S(2)}, u32[]{:S(2)}) collective-permute-start(bf16[256,256]{1,0:T(8,128)(2,1)S(1)} %copy-done.5), channel_id=1, source_target_pairs={{8,0},{16,8},{24,16},{32,24},{40,32},{48,40},{56,48},{64,56},{72,6... | collective-permute-start | bytes 393224 | tf_op jit(solution)/shard_map/ppermute | solution.py:294
  27.0 8.2 %collective-permute-start.3 = (bf16[128,256]{1,0:T(8,128)(2,1)S(1)}, bf16[128,256]{1,0:T(8,128)(2,1)S(1)}, u32[]{:S(2)}, u32[]{:S(2)}) collective-permute-start(bf16[128,256]{1,0:T(8,128)(2,1)S(1)} %slice.11), channel_id=1, source_target_pairs={{16,0},{24,8},{32,16},{40,24},{48,32},{56,40},{64,48},{72,56},{80,... | collective-permute-start | bytes 196616 | tf_op jit(solution)/shard_map/ppermute | solution.py:294
  46.4 0.7 copy-start.7
  47.0 0.7 copy-start.10
  47.7 1.0 %copy-start.3 = (bf16[256,2048]{1,0:T(8,128)(2,1)}, bf16[256,2048]{1,0:T(8,128)(2,1)S(1)}, u32[]{:S(2)}) copy-start(bf16[256,2048]{1,0:T(8,128)(2,1)S(1)} %collective-permute-done.weight) | copy-start | bytes 3145732
  48.7 20.5 %collective-permute-start.4 = (bf16[512,256]{1,0:T(8,128)(2,1)}, bf16[512,256]{1,0:T(8,128)(2,1)S(1)}, u32[]{:S(2)}, u32[]{:S(2)}) collective-permute-start(bf16[512,256]{1,0:T(8,128)(2,1)} %pad_maximum_fusion), channel_id=1, source_target_pairs={{0,8},{8,16},{16,24},{24,32},{32,40},{40,48},{48,56},{56,64},{64,7... | collective-permute-start | bytes 786440 | tf_op jit(solution)/shard_map/ppermute | solution.py:294
  52.0 1.2 %copy-start.4 = (bf16[256,2048]{1,0:T(8,128)(2,1)S(1)}, bf16[256,2048]{1,0:T(8,128)(2,1)}, u32[]{:S(2)}) copy-start(bf16[256,2048]{1,0:T(8,128)(2,1)} %copy-done.3) | copy-start | bytes 3145732
  53.7 15.5 %copy-start.6 = (bf16[256,256]{1,0:T(8,128)(2,1)S(1)}, bf16[256,256]{1,0:T(8,128)(2,1)}, u32[]{:S(2)}) copy-start(bf16[256,256]{1,0:T(8,128)(2,1)} %query.3) | copy-start | bytes 393220
  53.7 15.5 %copy-start.8 = (bf16[256,256]{1,0:T(8,128)(2,1)S(1)}, bf16[256,256]{1,0:T(8,128)(2,1)}, u32[]{:S(2)}) copy-start(bf16[256,256]{1,0:T(8,128)(2,1)} %copy-done.7) | copy-start | bytes 393220
  53.7 15.5 %copy-start.9 = (s32[128,128]{1,0:T(8,128)S(1)}, s32[128,128]{1,0:T(8,128)}, u32[]{:S(2)}) copy-start(s32[128,128]{1,0:T(8,128)} %table.3) | copy-start | bytes 196612
  53.7 23.0 %copy-start.11 = (bf16[256,256]{1,0:T(8,128)(2,1)S(1)}, bf16[256,256]{1,0:T(8,128)(2,1)}, u32[]{:S(2)}) copy-start(bf16[256,256]{1,0:T(8,128)(2,1)} %copy-done.10) | copy-start | bytes 393220
  53.7 3.4 %collective-permute-start.5 = (bf16[256,256]{1,0:T(8,128)(2,1)S(1)}, bf16[256,256]{1,0:T(8,128)(2,1)S(1)}, u32[]{:S(2)}, u32[]{:S(2)}) collective-permute-start(bf16[256,256]{1,0:T(8,128)(2,1)S(1)} %shard_map.96), channel_id=1, source_target_pairs={{0,1},{1,0},{2,3},{3,2},{4,5},{5,4},{6,7},{7,6},{8,9},{9,8},{10,11... | collective-permute-start | bytes 393224 | tf_op jit(solution)/shard_map/ppermute | solution.py:299
  57.1 23.3 %collective-permute-start.6 = (bf16[256,256]{1,0:T(8,128)(2,1)S(1)}, bf16[256,256]{1,0:T(8,128)(2,1)S(1)}, u32[]{:S(2)}, u32[]{:S(2)}) collective-permute-start(bf16[256,256]{1,0:T(8,128)(2,1)S(1)} %get-tuple-element.30.grad), channel_id=1, source_target_pairs={{8,0},{16,8},{24,16},{32,24},{40,32},{48,40},{56,48},{64,56},{72,6... | collective-permute-start | bytes 393224 | tf_op jit(solution)/shard_map/ppermute | solution.py:294
  66.6 13.9 %collective-permute-start.7 = (bf16[128,256]{1,0:T(8,128)(2,1)S(1)}, bf16[128,256]{1,0:T(8,128)(2,1)S(1)}, u32[]{:S(2)}, u32[]{:S(2)}) collective-permute-start(bf16[128,256]{1,0:T(8,128)(2,1)S(1)} %get-tuple-element.43), channel_id=1, source_target_pairs={{16,0},{24,8},{32,16},{40,24},{48,32},{56,40},{64,48},{72,56},{80,... | collective-permute-start | bytes 196616 | tf_op jit(solution)/shard_map/ppermute | solution.py:294
  72.8 8.3 %collective-permute-start.8 = (f32[8,256]{1,0:T(8,128)S(1)}, f32[8,256]{1,0:T(8,128)S(1)}, u32[]{:S(2)}, u32[]{:S(2)}) collective-permute-start(f32[8,256]{1,0:T(8,128)S(1)} %get-tuple-element.35), channel_id=1, source_target_pairs={{8,0},{16,8},{24,16},{32,24},{40,32},{48,40},{56,48},{64,56},{72,6... | collective-permute-start | bytes 24584 | tf_op jit(solution)/shard_map/ppermute | solution.py:294
  74.7 6.4 %collective-permute-start.9 = (f32[8,128]{1,0:T(8,128)S(1)}, f32[8,128]{1,0:T(8,128)S(1)}, u32[]{:S(2)}, u32[]{:S(2)}) collective-permute-start(f32[8,128]{1,0:T(8,128)S(1)} %get-tuple-element.44), channel_id=1, source_target_pairs={{16,0},{24,8},{32,16},{40,24},{48,32},{56,40},{64,48},{72,56},{80,... | collective-permute-start | bytes 12296 | tf_op jit(solution)/shard_map/ppermute | solution.py:294

commit v11 on v10

--- a/solution.py
+++ b/solution.py
@@ -314,10 +314,13 @@
     (theirs,) = call(cut_kernel, [VMEM], [((WIDE, width), half)], 0.0, out_weight)
     other_weight = other_core(theirs)
     own_keys = jnp.concatenate((key_rows, value_rows))
-    gathered, other_weight, far_keys, near_query, far_query, own_keys = lax.optimization_barrier(
-        (gathered, other_weight, far_keys, near_query, far_query, own_keys)
+    far_keys, near_query, far_query, own_keys = lax.optimization_barrier(
+        (far_keys, near_query, far_query, own_keys)
     )
     near_keys = shifted(own_keys, 1)
+    gathered, other_weight, far_keys = lax.optimization_barrier(
+        (gathered, other_weight, far_keys)
+    )
     (sent,) = call(
         project_other_kernel, [VMEM] * 2, [((ROWS, WIDE), half)], 0.0, gathered, other_weight
     )

time: 82.9 us -> 83.3 us (level)
  Pallas kernels: 9.69 us -> 10.6 us
    pallas_call x8, Pallas kernels: 9.69 us -> 10.6 us  [call(): pl.pallas_call(kernel, out_shape=shapes, in_specs=specs, out_specs=[VMEM]...]
  transfers between devices with their start and end apart: 11 -> 11, of which waited for: 4 -> 3; matrix products, arithmetic and copies ran while one was open for 1% -> 1% of each run, Pallas kernels for 10% -> 11%
where the time goes in v11:
time: 83.3 us; the launch traced here: 82.7 us
  starting transfers between devices  49.4 us (59%)
  waiting for transfers between devices  14.6 us (18%)
  Pallas kernels  10.6 us (13%)
  local copies, waits for them, and re-layouts  5.72 us (7%)
  between operations  1.6 us (2%)
    ppermute x8, starting transfers between devices, shifted(): return lax.ppermute(value, 'blk', pairs)  40.4 us
    ppermute x8, waiting for transfers between devices, shifted(): return lax.ppermute(value, 'blk', pairs)  13.8 us
    pallas_call x8, Pallas kernels, call(): pl.pallas_call(kernel, out_shape=shapes, in_specs=specs, out_specs=[VMEM]...  10.6 us
    all_to_all x1, starting transfers between devices, on_device(): gathered = lax.all_to_all(copies, 'head', 0, 0, axis_index_groups=groups)  4.87 us
    ppermute x2, starting transfers between devices, other_core(): lax.ppermute(value, 'head', [(source, source ^ 1) for source in range(cou...  4.1 us
    unnamed x24, local copies, waits for them, and re-layouts  3.55 us
    broadcast_in_dim x1, local copies, waits for them, and re-layouts, on_device(): copies = jnp.broadcast_to(grad_out[None], (count // 2, *grad_out.shape))  2.16 us
  transfers between devices with their start and end apart: 11, of which 3 were waited for; matrix products, arithmetic and copies ran while one was open for 1% of the time, Pallas kernels for 11%

profile of v11, /device:TPU:6, one launch (start us, length us, event | category | flops | bytes accessed | tf_op | source)
XLA Modules:
  0.0 82.7 jit_solution(16647762099801760742)
XLA Ops:
  0.6 0.0 copy-start
  0.6 2.2 %broadcast_in_dim.2 = bf16[4,256,512]{2,1,0:T(8,128)(2,1)} broadcast(bf16[256,512]{1,0:T(8,128)(2,1)} %param.10), dimensions={1,2} | broadcast | bytes 1310720 | tf_op jit(solution)/shard_map/broadcast_in_dim | solution.py:307
  2.8 4.9 %all-to-all-start = ((bf16[4,256,512]{2,1,0:T(8,128)(2,1)}), bf16[4,256,512]{2,1,0:T(8,128)(2,1)S(1)}, u32[]{:S(2)}, u32[]{:S(2)}) async-start(bf16[4,256,512]{2,1,0:T(8,128)(2,1)} %broadcast_in_dim.2), calls=%async_computation | async-start | bytes 2097152 | tf_op jit(solution)/shard_map/all_to_all | solution.py:308
  7.7 0.0 copy-done
  7.7 0.0 copy-start.5
  7.7 0.0 copy-start.1
  7.7 0.0 copy-start.2
  7.7 0.1 shard_map.94
  7.8 2.1 %collective-permute-start.4 = (bf16[256,2048]{1,0:T(8,128)(2,1)S(1)}, bf16[256,2048]{1,0:T(8,128)(2,1)S(1)}, u32[]{:S(2)}, u32[]{:S(2)}) collective-permute-start(bf16[256,2048]{1,0:T(8,128)(2,1)S(1)} %shard_map.94), channel_id=1, source_target_pairs={{0,1},{1,0},{2,3},{3,2},{4,5},{5,4},{6,7},{7,6},{8,9},{9,8},{10,11... | collective-permute-start | bytes 3145736 | tf_op jit(solution)/shard_map/ppermute | solution.py:299
  9.9 0.0 slice-done
  9.9 0.0 slice-done.1
  9.9 6.1 %collective-permute-start = (bf16[256,256]{1,0:T(8,128)(2,1)S(1)}, bf16[256,256]{1,0:T(8,128)(2,1)S(1)}, u32[]{:S(2)}, u32[]{:S(2)}) collective-permute-start(bf16[256,256]{1,0:T(8,128)(2,1)S(1)} %pad_maximum_fusion.1), channel_id=1, source_target_pairs={{0,16},{8,24},{16,32},{24,40},{32,48},{40,56},{48,64},{56,72},{64,... | collective-permute-start | bytes 393224 | tf_op jit(solution)/shard_map/ppermute | solution.py:294
  16.0 11.0 %collective-permute-start.1 = (bf16[256,256]{1,0:T(8,128)(2,1)S(1)}, bf16[256,256]{1,0:T(8,128)(2,1)S(1)}, u32[]{:S(2)}, u32[]{:S(2)}) collective-permute-start(bf16[256,256]{1,0:T(8,128)(2,1)S(1)} %copy-done.5), channel_id=1, source_target_pairs={{8,0},{16,8},{24,16},{32,24},{40,32},{48,40},{56,48},{64,56},{72,6... | collective-permute-start | bytes 393224 | tf_op jit(solution)/shard_map/ppermute | solution.py:294
  27.0 4.8 %collective-permute-start.2 = (bf16[128,256]{1,0:T(8,128)(2,1)S(1)}, bf16[128,256]{1,0:T(8,128)(2,1)S(1)}, u32[]{:S(2)}, u32[]{:S(2)}) collective-permute-start(bf16[128,256]{1,0:T(8,128)(2,1)S(1)} %slice.11), channel_id=1, source_target_pairs={{16,0},{24,8},{32,16},{40,24},{48,32},{56,40},{64,48},{72,56},{80,... | collective-permute-start | bytes 196616 | tf_op jit(solution)/shard_map/ppermute | solution.py:294
  31.9 0.7 pad_maximum_fusion
  32.6 2.6 %collective-permute-done.2.far_query = bf16[128,256]{1,0:T(8,128)(2,1)S(1)} collective-permute-done((bf16[128,256]{1,0:T(8,128)(2,1)S(1)}, bf16[128,256]{1,0:T(8,128)(2,1)S(1)}, u32[]{:S(2)}, u32[]{:S(2)}) %collective-permute-start.2) | collective-permute-done | bytes 65568 | tf_op jit(solution)/shard_map/ppermute | solution.py:294
  35.2 11.2 %collective-permute-done.far = bf16[256,256]{1,0:T(8,128)(2,1)S(1)} collective-permute-done((bf16[256,256]{1,0:T(8,128)(2,1)S(1)}, bf16[256,256]{1,0:T(8,128)(2,1)S(1)}, u32[]{:S(2)}, u32[]{:S(2)}) %collective-permute-start) | collective-permute-done | bytes 131104 | tf_op jit(solution)/shard_map/ppermute | solution.py:294
  46.4 0.7 copy-done.7
  47.0 0.0 collective-permute-done.1.near_query
  47.1 0.7 copy-done.10
  47.7 3.3 %collective-permute-start.3 = (bf16[512,256]{1,0:T(8,128)(2,1)}, bf16[512,256]{1,0:T(8,128)(2,1)}, u32[]{:S(2)}, u32[]{:S(2)}) collective-permute-start(bf16[512,256]{1,0:T(8,128)(2,1)} %pad_maximum_fusion), channel_id=1, source_target_pairs={{0,8},{8,16},{16,24},{24,32},{32,40},{40,48},{48,56},{56,64},{64,7... | collective-permute-start | bytes 786440 | tf_op jit(solution)/shard_map/ppermute | solution.py:294
  51.0 0.0 collective-permute-done.4.weight
  51.0 0.0 copy-start.3
  51.0 1.0 %copy-done.3 = bf16[256,2048]{1,0:T(8,128)(2,1)} copy-done((bf16[256,2048]{1,0:T(8,128)(2,1)}, bf16[256,2048]{1,0:T(8,128)(2,1)S(1)}, u32[]{:S(2)}) %copy-start.3) | copy-done | bytes 1048600
  52.0 0.0 all-to-all-done.gathered
  52.0 1.2 %copy-done.4 = bf16[256,2048]{1,0:T(8,128)(2,1)S(1)} copy-done((bf16[256,2048]{1,0:T(8,128)(2,1)S(1)}, bf16[256,2048]{1,0:T(8,128)(2,1)}, u32[]{:S(2)}) %copy-start.4) | copy-done | bytes 1048600
  53.2 0.5 shard_map.96
  53.7 0.0 copy-start.6
  53.7 0.0 copy-start.8
  53.7 0.0 copy-start.9
  53.7 0.0 copy-start.11
  53.7 2.1 %collective-permute-start.5 = (bf16[256,256]{1,0:T(8,128)(2,1)S(1)}, bf16[256,256]{1,0:T(8,128)(2,1)S(1)}, u32[]{:S(2)}, u32[]{:S(2)}) collective-permute-start(bf16[256,256]{1,0:T(8,128)(2,1)S(1)} %shard_map.96), channel_id=1, source_target_pairs={{0,1},{1,0},{2,3},{3,2},{4,5},{5,4},{6,7},{7,6},{8,9},{9,8},{10,11... | collective-permute-start | bytes 393224 | tf_op jit(solution)/shard_map/ppermute | solution.py:299
  55.8 0.5 shard_map.95.own
  56.3 0.8 collective-permute-done.5.received
  57.1 9.5 %collective-permute-start.6 = (bf16[256,256]{1,0:T(8,128)(2,1)S(1)}, bf16[256,256]{1,0:T(8,128)(2,1)S(1)}, u32[]{:S(2)}, u32[]{:S(2)}) collective-permute-start(bf16[256,256]{1,0:T(8,128)(2,1)S(1)} %get-tuple-element.32.grad), channel_id=1, source_target_pairs={{8,0},{16,8},{24,16},{32,24},{40,32},{48,40},{56,48},{64,56},{72,6... | collective-permute-start | bytes 393224 | tf_op jit(solution)/shard_map/ppermute | solution.py:294
  66.6 1.9 %collective-permute-start.7 = (bf16[128,256]{1,0:T(8,128)(2,1)S(1)}, bf16[128,256]{1,0:T(8,128)(2,1)S(1)}, u32[]{:S(2)}, u32[]{:S(2)}) collective-permute-start(bf16[128,256]{1,0:T(8,128)(2,1)S(1)} %get-tuple-element.45), channel_id=1, source_target_pairs={{16,0},{24,8},{32,16},{40,24},{48,32},{56,40},{64,48},{72,56},{80,... | collective-permute-start | bytes 196616 | tf_op jit(solution)/shard_map/ppermute | solution.py:294
  69.2 0.0 collective-permute-done.3.near
  69.2 3.6 %shard_map.98 = (f32[2,128,640]{2,1,0:T(8,128)S(1)}, f32[2,128,512]{2,1,0:T(8,128)S(1)}, bf16[256,256]{1,0:T(8,128)(2,1)S(1)}, f32[8,256]{1,0:T(8,128)S(1)}, f32[8,128]{1,0:T(8,128)S(1)}) custom-call(s32[128,128]{1,0:T(8,128)S(1)} %copy-done.9, s32[1]{0:T(128)S(6)} %copy.10.seed, bf16[256,256]{1,0:T(8,128)(2,1)S(1)} %copy-done.6, ...), custom_call_target="tpu_custom_call" | custom-call | tf_op jit(solution)/shard_map/pallas_call | solution.py:281
  72.8 1.9 %collective-permute-start.8 = (f32[8,256]{1,0:T(8,128)S(1)}, f32[8,256]{1,0:T(8,128)S(1)}, u32[]{:S(2)}, u32[]{:S(2)}) collective-permute-start(f32[8,256]{1,0:T(8,128)S(1)} %get-tuple-element.37), channel_id=1, source_target_pairs={{8,0},{16,8},{24,16},{32,24},{40,32},{48,40},{56,48},{64,56},{72,6... | collective-permute-start | bytes 24584 | tf_op jit(solution)/shard_map/ppermute | solution.py:294
  74.8 1.9 %collective-permute-start.9 = (f32[8,128]{1,0:T(8,128)S(1)}, f32[8,128]{1,0:T(8,128)S(1)}, u32[]{:S(2)}, u32[]{:S(2)}) collective-permute-start(f32[8,128]{1,0:T(8,128)S(1)} %get-tuple-element.46), channel_id=1, source_target_pairs={{16,0},{24,8},{32,16},{40,24},{48,32},{56,40},{64,48},{72,56},{80,... | collective-permute-start | bytes 12296 | tf_op jit(solution)/shard_map/ppermute | solution.py:294
  76.7 0.0 copy-done.11
  76.7 2.1 %shard_map.100 = (f32[2,256,256]{2,1,0:T(8,128)S(1)}, f32[2,256,256]{2,1,0:T(8,128)S(1)}, f32[2,128,128]{2,1,0:T(8,128)S(1)}, f32[2,128,128]{2,1,0:T(8,128)S(1)}) custom-call(s32[128,128]{1,0:T(8,128)S(1)} %copy-done.9, s32[1]{0:T(128)S(6)} %copy.10.seed, bf16[256,256]{1,0:T(8,128)(2,1)S(1)} %copy-done.1, bf16[256,256]{1,0:T(8,128)(2,1)S(1)} %copy-done.11, ...), custom_call_target="tpu_custom_call" | custom-call | tf_op jit(solution)/shard_map/pallas_call | solution.py:281
  78.8 2.6 %shard_map.99 = (bf16[256,256]{1,0:T(8,128)(2,1)}, f32[256,256]{1,0:T(8,128)S(1)}, f32[256,256]{1,0:T(8,128)S(1)}) custom-call(f32[2,128,640]{2,1,0:T(8,128)S(1)} %get-tuple-element.33.signed_top, f32[2,128,512]{2,1,0:T(8,128)S(1)} %get-tuple-element.34.signed_low, bf16[256,256]{1,0:T(8,128)(2,1)S(1)} %get-tuple-element.35.attended, ...), custom_call_target="tpu_custom_call" | custom-call | tf_op jit(solution)/shard_map/pallas_call | solution.py:281
  81.4 0.0 collective-permute-done.9.far_stats
  81.4 0.0 collective-permute-done.8.near_stats
  81.4 0.0 collective-permute-done.7.far_grad
  81.4 0.0 collective-permute-done.6.near_grad
  81.5 1.2 %shard_map.101 = (bf16[256,256]{1,0:T(8,128)(2,1)}, bf16[256,256]{1,0:T(8,128)(2,1)}) custom-call(f32[2,256,256]{2,1,0:T(8,128)S(1)} %get-tuple-element.41.near_scores, f32[2,256,256]{2,1,0:T(8,128)S(1)} %get-tuple-element.42.near_keeps, f32[2,128,128]{2,1,0:T(8,128)S(1)} %get-tuple-element.43.far_scores, f32[2,128,128]{2,1,0:T(8,128)S(1)} %get-tuple-element.44.far_keeps, ...), custom_call_target="tpu_custom_call" | custom-call | flops 1495000064 | bytes 2633728 | tf_op jit(solution)/shard_map/pallas_call | solution.py:281
  (14 shorter events, 0.1 us)
Async XLA Ops:
  0.6 7.0 %copy-start = (bf16[256,4096]{1,0:T(8,128)(2,1)S(1)}, bf16[256,4096]{1,0:T(8,128)(2,1)}, u32[]{:S(2)}) copy-start(bf16[256,4096]{1,0:T(8,128)(2,1)} %weight.3) | copy-start | bytes 6291460
  2.8 49.2 %all-to-all-start = ((bf16[4,256,512]{2,1,0:T(8,128)(2,1)}), bf16[4,256,512]{2,1,0:T(8,128)(2,1)S(1)}, u32[]{:S(2)}, u32[]{:S(2)}) async-start(bf16[4,256,512]{2,1,0:T(8,128)(2,1)} %broadcast_in_dim.2), calls=%async_computation | async-start | bytes 2097152 | tf_op jit(solution)/shard_map/all_to_all | solution.py:308
  7.7 2.2 %slice-start = ((bf16[256,256]{1,0:T(8,128)(2,1)}), bf16[128,256]{1,0:T(8,128)(2,1)S(1)}, s32[]{:S(2)}) async-start(bf16[256,256]{1,0:T(8,128)(2,1)} %key.4), calls=%async_computation.1 | async-start | bytes 131072 | tf_op jit(solution)/shard_map/slice | solution.py:310
  7.7 2.2 %slice-start.1 = ((bf16[256,256]{1,0:T(8,128)(2,1)}), bf16[128,256]{1,0:T(8,128)(2,1)S(1)}, s32[]{:S(2)}) async-start(bf16[256,256]{1,0:T(8,128)(2,1)} %value.5), calls=%async_computation.2 | async-start | bytes 131072 | tf_op jit(solution)/shard_map/slice | solution.py:310
  7.7 8.3 %copy-start.5 = (bf16[256,256]{1,0:T(8,128)(2,1)S(1)}, bf16[256,256]{1,0:T(8,128)(2,1)}, u32[]{:S(2)}) copy-start(bf16[256,256]{1,0:T(8,128)(2,1)} %query.3) | copy-start | bytes 393220
  7.7 24.2 %copy-start.1 = (bf16[256,256]{1,0:T(8,128)(2,1)S(1)}, bf16[256,256]{1,0:T(8,128)(2,1)}, u32[]{:S(2)}) copy-start(bf16[256,256]{1,0:T(8,128)(2,1)} %key.4) | copy-start | bytes 393220
  7.7 24.2 %copy-start.2 = (bf16[256,256]{1,0:T(8,128)(2,1)S(1)}, bf16[256,256]{1,0:T(8,128)(2,1)}, u32[]{:S(2)}) copy-start(bf16[256,256]{1,0:T(8,128)(2,1)} %value.5) | copy-start | bytes 393220
  7.8 43.2 %collective-permute-start.4 = (bf16[256,2048]{1,0:T(8,128)(2,1)S(1)}, bf16[256,2048]{1,0:T(8,128)(2,1)S(1)}, u32[]{:S(2)}, u32[]{:S(2)}) collective-permute-start(bf16[256,2048]{1,0:T(8,128)(2,1)S(1)} %shard_map.94), channel_id=1, source_target_pairs={{0,1},{1,0},{2,3},{3,2},{4,5},{5,4},{6,7},{7,6},{8,9},{9,8},{10,11... | collective-permute-start | bytes 3145736 | tf_op jit(solution)/shard_map/ppermute | solution.py:299
  9.9 36.5 %collective-permute-start = (bf16[256,256]{1,0:T(8,128)(2,1)S(1)}, bf16[256,256]{1,0:T(8,128)(2,1)S(1)}, u32[]{:S(2)}, u32[]{:S(2)}) collective-permute-start(bf16[256,256]{1,0:T(8,128)(2,1)S(1)} %pad_maximum_fusion.1), channel_id=1, source_target_pairs={{0,16},{8,24},{16,32},{24,40},{32,48},{40,56},{48,64},{56,72},{64,... | collective-permute-start | bytes 393224 | tf_op jit(solution)/shard_map/ppermute | solution.py:294
  16.0 31.0 %collective-permute-start.1 = (bf16[256,256]{1,0:T(8,128)(2,1)S(1)}, bf16[256,256]{1,0:T(8,128)(2,1)S(1)}, u32[]{:S(2)}, u32[]{:S(2)}) collective-permute-start(bf16[256,256]{1,0:T(8,128)(2,1)S(1)} %copy-done.5), channel_id=1, source_target_pairs={{8,0},{16,8},{24,16},{32,24},{40,32},{48,40},{56,48},{64,56},{72,6... | collective-permute-start | bytes 393224 | tf_op jit(solution)/shard_map/ppermute | solution.py:294
  27.0 8.2 %collective-permute-start.2 = (bf16[128,256]{1,0:T(8,128)(2,1)S(1)}, bf16[128,256]{1,0:T(8,128)(2,1)S(1)}, u32[]{:S(2)}, u32[]{:S(2)}) collective-permute-start(bf16[128,256]{1,0:T(8,128)(2,1)S(1)} %slice.11), channel_id=1, source_target_pairs={{16,0},{24,8},{32,16},{40,24},{48,32},{56,40},{64,48},{72,56},{80,... | collective-permute-start | bytes 196616 | tf_op jit(solution)/shard_map/ppermute | solution.py:294
  46.4 0.7 copy-start.7
  47.0 0.7 copy-start.10
  47.7 21.5 %collective-permute-start.3 = (bf16[512,256]{1,0:T(8,128)(2,1)}, bf16[512,256]{1,0:T(8,128)(2,1)}, u32[]{:S(2)}, u32[]{:S(2)}) collective-permute-start(bf16[512,256]{1,0:T(8,128)(2,1)} %pad_maximum_fusion), channel_id=1, source_target_pairs={{0,8},{8,16},{16,24},{24,32},{32,40},{40,48},{48,56},{56,64},{64,7... | collective-permute-start | bytes 786440 | tf_op jit(solution)/shard_map/ppermute | solution.py:294
  51.0 1.0 %copy-start.3 = (bf16[256,2048]{1,0:T(8,128)(2,1)}, bf16[256,2048]{1,0:T(8,128)(2,1)S(1)}, u32[]{:S(2)}) copy-start(bf16[256,2048]{1,0:T(8,128)(2,1)S(1)} %collective-permute-done.4.weight) | copy-start | bytes 3145732
  52.0 1.2 %copy-start.4 = (bf16[256,2048]{1,0:T(8,128)(2,1)S(1)}, bf16[256,2048]{1,0:T(8,128)(2,1)}, u32[]{:S(2)}) copy-start(bf16[256,2048]{1,0:T(8,128)(2,1)} %copy-done.3) | copy-start | bytes 3145732
  53.7 15.5 %copy-start.6 = (bf16[256,256]{1,0:T(8,128)(2,1)S(1)}, bf16[256,256]{1,0:T(8,128)(2,1)}, u32[]{:S(2)}) copy-start(bf16[256,256]{1,0:T(8,128)(2,1)} %query.3) | copy-start | bytes 393220
  53.7 15.5 %copy-start.8 = (bf16[256,256]{1,0:T(8,128)(2,1)S(1)}, bf16[256,256]{1,0:T(8,128)(2,1)}, u32[]{:S(2)}) copy-start(bf16[256,256]{1,0:T(8,128)(2,1)} %copy-done.7) | copy-start | bytes 393220
  53.7 15.5 %copy-start.9 = (s32[128,128]{1,0:T(8,128)S(1)}, s32[128,128]{1,0:T(8,128)}, u32[]{:S(2)}) copy-start(s32[128,128]{1,0:T(8,128)} %table.3) | copy-start | bytes 196612
  53.7 23.0 %copy-start.11 = (bf16[256,256]{1,0:T(8,128)(2,1)S(1)}, bf16[256,256]{1,0:T(8,128)(2,1)}, u32[]{:S(2)}) copy-start(bf16[256,256]{1,0:T(8,128)(2,1)} %copy-done.10) | copy-start | bytes 393220
  53.7 3.4 %collective-permute-start.5 = (bf16[256,256]{1,0:T(8,128)(2,1)S(1)}, bf16[256,256]{1,0:T(8,128)(2,1)S(1)}, u32[]{:S(2)}, u32[]{:S(2)}) collective-permute-start(bf16[256,256]{1,0:T(8,128)(2,1)S(1)} %shard_map.96), channel_id=1, source_target_pairs={{0,1},{1,0},{2,3},{3,2},{4,5},{5,4},{6,7},{7,6},{8,9},{9,8},{10,11... | collective-permute-start | bytes 393224 | tf_op jit(solution)/shard_map/ppermute | solution.py:299
  57.1 24.3 %collective-permute-start.6 = (bf16[256,256]{1,0:T(8,128)(2,1)S(1)}, bf16[256,256]{1,0:T(8,128)(2,1)S(1)}, u32[]{:S(2)}, u32[]{:S(2)}) collective-permute-start(bf16[256,256]{1,0:T(8,128)(2,1)S(1)} %get-tuple-element.32.grad), channel_id=1, source_target_pairs={{8,0},{16,8},{24,16},{32,24},{40,32},{48,40},{56,48},{64,56},{72,6... | collective-permute-start | bytes 393224 | tf_op jit(solution)/shard_map/ppermute | solution.py:294
  66.6 14.8 %collective-permute-start.7 = (bf16[128,256]{1,0:T(8,128)(2,1)S(1)}, bf16[128,256]{1,0:T(8,128)(2,1)S(1)}, u32[]{:S(2)}, u32[]{:S(2)}) collective-permute-start(bf16[128,256]{1,0:T(8,128)(2,1)S(1)} %get-tuple-element.45), channel_id=1, source_target_pairs={{16,0},{24,8},{32,16},{40,24},{48,32},{56,40},{64,48},{72,56},{80,... | collective-permute-start | bytes 196616 | tf_op jit(solution)/shard_map/ppermute | solution.py:294
  72.8 8.6 %collective-permute-start.8 = (f32[8,256]{1,0:T(8,128)S(1)}, f32[8,256]{1,0:T(8,128)S(1)}, u32[]{:S(2)}, u32[]{:S(2)}) collective-permute-start(f32[8,256]{1,0:T(8,128)S(1)} %get-tuple-element.37), channel_id=1, source_target_pairs={{8,0},{16,8},{24,16},{32,24},{40,32},{48,40},{56,48},{64,56},{72,6... | collective-permute-start | bytes 24584 | tf_op jit(solution)/shard_map/ppermute | solution.py:294
  74.8 6.7 %collective-permute-start.9 = (f32[8,128]{1,0:T(8,128)S(1)}, f32[8,128]{1,0:T(8,128)S(1)}, u32[]{:S(2)}, u32[]{:S(2)}) collective-permute-start(f32[8,128]{1,0:T(8,128)S(1)} %get-tuple-element.46), channel_id=1, source_target_pairs={{16,0},{24,8},{32,16},{40,24},{48,32},{56,40},{64,48},{72,56},{80,... | collective-permute-start | bytes 12296 | tf_op jit(solution)/shard_map/ppermute | solution.py:294

commit v12 on v11

--- a/solution.py
+++ b/solution.py
@@ -314,9 +314,7 @@
     (theirs,) = call(cut_kernel, [VMEM], [((WIDE, width), half)], 0.0, out_weight)
     other_weight = other_core(theirs)
     own_keys = jnp.concatenate((key_rows, value_rows))
-    far_keys, near_query, far_query, own_keys = lax.optimization_barrier(
-        (far_keys, near_query, far_query, own_keys)
-    )
+    near_query, far_query, own_keys = lax.optimization_barrier((near_query, far_query, own_keys))
     near_keys = shifted(own_keys, 1)
     gathered, other_weight, far_keys = lax.optimization_barrier(
         (gathered, other_weight, far_keys)

time: 83.3 us -> 81.6 us (0.980)
  waiting for transfers between devices: 14.6 us -> 4.24 us
  starting transfers between devices: 49.4 us -> 57.3 us
    ppermute x8, waiting for transfers between devices: 13.8 us -> 3.41 us  [shifted(): return lax.ppermute(value, 'blk', pairs)]
    ppermute x8, starting transfers between devices: 40.4 us -> 48.3 us  [shifted(): return lax.ppermute(value, 'blk', pairs)]
  transfers between devices with their start and end apart: 11 -> 11, of which waited for: 3 -> 3; matrix products, arithmetic and copies ran while one was open for 1% -> 1% of each run, Pallas kernels for 11% -> 12%
where the time goes in v12:
time: 81.6 us; the launch traced here: 80.2 us
  starting transfers between devices  57.3 us (70%)
  Pallas kernels  10.6 us (13%)
  local copies, waits for them, and re-layouts  5.73 us (7%)
  waiting for transfers between devices  4.24 us (5%)
  between operations  1.58 us (2%)
    ppermute x8, starting transfers between devices, shifted(): return lax.ppermute(value, 'blk', pairs)  48.3 us
    pallas_call x8, Pallas kernels, call(): pl.pallas_call(kernel, out_shape=shapes, in_specs=specs, out_specs=[VMEM]...  10.6 us
    all_to_all x1, starting transfers between devices, on_device(): gathered = lax.all_to_all(copies, 'head', 0, 0, axis_index_groups=groups)  4.87 us
    ppermute x2, starting transfers between devices, other_core(): lax.ppermute(value, 'head', [(source, source ^ 1) for source in range(cou...  4.1 us
    unnamed x24, local copies, waits for them, and re-layouts  3.55 us
    ppermute x8, waiting for transfers between devices, shifted(): return lax.ppermute(value, 'blk', pairs)  3.41 us
    broadcast_in_dim x1, local copies, waits for them, and re-layouts, on_device(): copies = jnp.broadcast_to(grad_out[None], (count // 2, *grad_out.shape))  2.16 us
  transfers between devices with their start and end apart: 11, of which 3 were waited for; matrix products, arithmetic and copies ran while one was open for 1% of the time, Pallas kernels for 12%

profile of v12, /device:TPU:6, one launch (start us, length us, event | category | flops | bytes accessed | tf_op | source)
XLA Modules:
  0.0 80.2 jit_solution(14854652747173587171)
XLA Ops:
  0.6 0.0 copy-start
  0.6 2.2 %broadcast_in_dim.2 = bf16[4,256,512]{2,1,0:T(8,128)(2,1)} broadcast(bf16[256,512]{1,0:T(8,128)(2,1)} %param.10), dimensions={1,2} | broadcast | bytes 1310720 | tf_op jit(solution)/shard_map/broadcast_in_dim | solution.py:307
  2.8 4.9 %all-to-all-start = ((bf16[4,256,512]{2,1,0:T(8,128)(2,1)}), bf16[4,256,512]{2,1,0:T(8,128)(2,1)S(1)}, u32[]{:S(2)}, u32[]{:S(2)}) async-start(bf16[4,256,512]{2,1,0:T(8,128)(2,1)} %broadcast_in_dim.2), calls=%async_computation | async-start | bytes 2097152 | tf_op jit(solution)/shard_map/all_to_all | solution.py:308
  7.7 0.0 copy-done
  7.7 0.0 slice-start.1
  7.7 0.0 copy-start.1
  7.7 0.0 copy-start.2
  7.7 0.1 shard_map.94
  7.8 2.1 %collective-permute-start.3 = (bf16[256,2048]{1,0:T(8,128)(2,1)S(1)}, bf16[256,2048]{1,0:T(8,128)(2,1)S(1)}, u32[]{:S(2)}, u32[]{:S(2)}) collective-permute-start(bf16[256,2048]{1,0:T(8,128)(2,1)S(1)} %shard_map.94), channel_id=1, source_target_pairs={{0,1},{1,0},{2,3},{3,2},{4,5},{5,4},{6,7},{7,6},{8,9},{9,8},{10,11... | collective-permute-start | bytes 3145736 | tf_op jit(solution)/shard_map/ppermute | solution.py:299
  9.9 0.0 copy-done.5
  9.9 15.1 %collective-permute-start = (bf16[256,256]{1,0:T(8,128)(2,1)S(1)}, bf16[256,256]{1,0:T(8,128)(2,1)S(1)}, u32[]{:S(2)}, u32[]{:S(2)}) collective-permute-start(bf16[256,256]{1,0:T(8,128)(2,1)S(1)} %copy-done.5), channel_id=1, source_target_pairs={{8,0},{16,8},{24,16},{32,24},{40,32},{48,40},{56,48},{64,56},{72,6... | collective-permute-start | bytes 393224 | tf_op jit(solution)/shard_map/ppermute | solution.py:294
  25.0 0.0 slice-done
  25.0 0.0 slice-done.1
  25.1 1.9 %collective-permute-start.4 = (bf16[256,256]{1,0:T(8,128)(2,1)S(1)}, bf16[256,256]{1,0:T(8,128)(2,1)S(1)}, u32[]{:S(2)}, u32[]{:S(2)}) collective-permute-start(bf16[256,256]{1,0:T(8,128)(2,1)S(1)} %pad_maximum_fusion.1), channel_id=1, source_target_pairs={{0,16},{8,24},{16,32},{24,40},{32,48},{40,56},{48,64},{56,72},{64,... | collective-permute-start | bytes 393224 | tf_op jit(solution)/shard_map/ppermute | solution.py:294
  27.0 11.7 %collective-permute-start.1 = (bf16[128,256]{1,0:T(8,128)(2,1)S(1)}, bf16[128,256]{1,0:T(8,128)(2,1)S(1)}, u32[]{:S(2)}, u32[]{:S(2)}) collective-permute-start(bf16[128,256]{1,0:T(8,128)(2,1)S(1)} %slice.9), channel_id=1, source_target_pairs={{16,0},{24,8},{32,16},{40,24},{48,32},{56,40},{64,48},{72,56},{80,... | collective-permute-start | bytes 196616 | tf_op jit(solution)/shard_map/ppermute | solution.py:294
  38.8 0.0 copy-done.1
  38.8 0.7 pad_maximum_fusion
  39.5 1.1 %collective-permute-done.1.far_query = bf16[128,256]{1,0:T(8,128)(2,1)S(1)} collective-permute-done((bf16[128,256]{1,0:T(8,128)(2,1)S(1)}, bf16[128,256]{1,0:T(8,128)(2,1)S(1)}, u32[]{:S(2)}, u32[]{:S(2)}) %collective-permute-start.1) | collective-permute-done | bytes 65568 | tf_op jit(solution)/shard_map/ppermute | solution.py:294
  40.6 0.0 collective-permute-done.near_query
  40.7 0.7 copy-done.10
  41.3 1.9 %collective-permute-start.2 = (bf16[512,256]{1,0:T(8,128)(2,1)}, bf16[512,256]{1,0:T(8,128)(2,1)}, u32[]{:S(2)}, u32[]{:S(2)}) collective-permute-start(bf16[512,256]{1,0:T(8,128)(2,1)} %pad_maximum_fusion), channel_id=1, source_target_pairs={{0,8},{8,16},{16,24},{24,32},{32,40},{40,48},{48,56},{56,64},{64,7... | collective-permute-start | bytes 786440 | tf_op jit(solution)/shard_map/ppermute | solution.py:294
  43.2 2.3 %collective-permute-done.4.far = bf16[256,256]{1,0:T(8,128)(2,1)S(1)} collective-permute-done((bf16[256,256]{1,0:T(8,128)(2,1)S(1)}, bf16[256,256]{1,0:T(8,128)(2,1)S(1)}, u32[]{:S(2)}, u32[]{:S(2)}) %collective-permute-start.4) | collective-permute-done | bytes 131104 | tf_op jit(solution)/shard_map/ppermute | solution.py:294
  45.5 0.7 copy-done.7
  46.1 0.0 collective-permute-done.3.weight
  46.2 1.0 %copy-done.3 = bf16[256,2048]{1,0:T(8,128)(2,1)} copy-done((bf16[256,2048]{1,0:T(8,128)(2,1)}, bf16[256,2048]{1,0:T(8,128)(2,1)S(1)}, u32[]{:S(2)}) %copy-start.3) | copy-done | bytes 1048600
  47.1 0.0 all-to-all-done.gathered
  47.1 1.2 %copy-done.4 = bf16[256,2048]{1,0:T(8,128)(2,1)S(1)} copy-done((bf16[256,2048]{1,0:T(8,128)(2,1)S(1)}, bf16[256,2048]{1,0:T(8,128)(2,1)}, u32[]{:S(2)}) %copy-start.4) | copy-done | bytes 1048600
  48.4 0.5 shard_map.96
  48.8 0.0 copy-start.6
  48.8 0.0 copy-start.8
  48.9 0.0 copy-start.9
  48.9 0.0 copy-start.11
  48.9 2.1 %collective-permute-start.5 = (bf16[256,256]{1,0:T(8,128)(2,1)S(1)}, bf16[256,256]{1,0:T(8,128)(2,1)S(1)}, u32[]{:S(2)}, u32[]{:S(2)}) collective-permute-start(bf16[256,256]{1,0:T(8,128)(2,1)S(1)} %shard_map.96), channel_id=1, source_target_pairs={{0,1},{1,0},{2,3},{3,2},{4,5},{5,4},{6,7},{7,6},{8,9},{9,8},{10,11... | collective-permute-start | bytes 393224 | tf_op jit(solution)/shard_map/ppermute | solution.py:299
  50.9 0.5 shard_map.95.own
  51.4 0.8 %collective-permute-done.5.received = bf16[256,256]{1,0:T(8,128)(2,1)S(1)} collective-permute-done((bf16[256,256]{1,0:T(8,128)(2,1)S(1)}, bf16[256,256]{1,0:T(8,128)(2,1)S(1)}, u32[]{:S(2)}, u32[]{:S(2)}) %collective-permute-start.5) | collective-permute-done | bytes 131104 | tf_op jit(solution)/shard_map/ppermute | solution.py:299
  52.3 8.6 %collective-permute-start.6 = (bf16[256,256]{1,0:T(8,128)(2,1)S(1)}, bf16[256,256]{1,0:T(8,128)(2,1)S(1)}, u32[]{:S(2)}, u32[]{:S(2)}) collective-permute-start(bf16[256,256]{1,0:T(8,128)(2,1)S(1)} %get-tuple-element.30.grad), channel_id=1, source_target_pairs={{8,0},{16,8},{24,16},{32,24},{40,32},{48,40},{56,48},{64,56},{72,6... | collective-permute-start | bytes 393224 | tf_op jit(solution)/shard_map/ppermute | solution.py:294
  60.9 5.2 %collective-permute-start.7 = (bf16[128,256]{1,0:T(8,128)(2,1)S(1)}, bf16[128,256]{1,0:T(8,128)(2,1)S(1)}, u32[]{:S(2)}, u32[]{:S(2)}) collective-permute-start(bf16[128,256]{1,0:T(8,128)(2,1)S(1)} %get-tuple-element.43), channel_id=1, source_target_pairs={{16,0},{24,8},{32,16},{40,24},{48,32},{56,40},{64,48},{72,56},{80,... | collective-permute-start | bytes 196616 | tf_op jit(solution)/shard_map/ppermute | solution.py:294
  66.7 0.0 collective-permute-done.2.near
  66.8 3.6 %shard_map.98 = (f32[2,128,640]{2,1,0:T(8,128)S(1)}, f32[2,128,512]{2,1,0:T(8,128)S(1)}, bf16[256,256]{1,0:T(8,128)(2,1)S(1)}, f32[8,256]{1,0:T(8,128)S(1)}, f32[8,128]{1,0:T(8,128)S(1)}) custom-call(s32[128,128]{1,0:T(8,128)S(1)} %copy-done.9, s32[1]{0:T(128)S(6)} %copy.10.seed, bf16[256,256]{1,0:T(8,128)(2,1)S(1)} %copy-done.6, ...), custom_call_target="tpu_custom_call" | custom-call | tf_op jit(solution)/shard_map/pallas_call | solution.py:281
  70.4 1.9 %collective-permute-start.8 = (f32[8,256]{1,0:T(8,128)S(1)}, f32[8,256]{1,0:T(8,128)S(1)}, u32[]{:S(2)}, u32[]{:S(2)}) collective-permute-start(f32[8,256]{1,0:T(8,128)S(1)} %get-tuple-element.35), channel_id=1, source_target_pairs={{8,0},{16,8},{24,16},{32,24},{40,32},{48,40},{56,48},{64,56},{72,6... | collective-permute-start | bytes 24584 | tf_op jit(solution)/shard_map/ppermute | solution.py:294
  72.3 1.9 %collective-permute-start.9 = (f32[8,128]{1,0:T(8,128)S(1)}, f32[8,128]{1,0:T(8,128)S(1)}, u32[]{:S(2)}, u32[]{:S(2)}) collective-permute-start(f32[8,128]{1,0:T(8,128)S(1)} %get-tuple-element.44), channel_id=1, source_target_pairs={{16,0},{24,8},{32,16},{40,24},{48,32},{56,40},{64,48},{72,56},{80,... | collective-permute-start | bytes 12296 | tf_op jit(solution)/shard_map/ppermute | solution.py:294
  74.2 2.1 %shard_map.100 = (f32[2,256,256]{2,1,0:T(8,128)S(1)}, f32[2,256,256]{2,1,0:T(8,128)S(1)}, f32[2,128,128]{2,1,0:T(8,128)S(1)}, f32[2,128,128]{2,1,0:T(8,128)S(1)}) custom-call(s32[128,128]{1,0:T(8,128)S(1)} %copy-done.9, s32[1]{0:T(128)S(6)} %copy.10.seed, bf16[256,256]{1,0:T(8,128)(2,1)S(1)} %copy-done.1, bf16[256,256]{1,0:T(8,128)(2,1)S(1)} %copy-done.11, ...), custom_call_target="tpu_custom_call" | custom-call | tf_op jit(solution)/shard_map/pallas_call | solution.py:281
  76.3 2.6 %shard_map.99 = (bf16[256,256]{1,0:T(8,128)(2,1)}, f32[256,256]{1,0:T(8,128)S(1)}, f32[256,256]{1,0:T(8,128)S(1)}) custom-call(f32[2,128,640]{2,1,0:T(8,128)S(1)} %get-tuple-element.31.signed_top, f32[2,128,512]{2,1,0:T(8,128)S(1)} %get-tuple-element.32.signed_low, bf16[256,256]{1,0:T(8,128)(2,1)S(1)} %get-tuple-element.33.attended, ...), custom_call_target="tpu_custom_call" | custom-call | tf_op jit(solution)/shard_map/pallas_call | solution.py:281
  79.0 0.0 collective-permute-done.9.far_stats
  79.0 0.0 collective-permute-done.8.near_stats
  79.0 0.0 collective-permute-done.7.far_grad
  79.0 0.0 collective-permute-done.6.near_grad
  79.0 1.2 %shard_map.101 = (bf16[256,256]{1,0:T(8,128)(2,1)}, bf16[256,256]{1,0:T(8,128)(2,1)}) custom-call(f32[2,256,256]{2,1,0:T(8,128)S(1)} %get-tuple-element.39.near_scores, f32[2,256,256]{2,1,0:T(8,128)S(1)} %get-tuple-element.40.near_keeps, f32[2,128,128]{2,1,0:T(8,128)S(1)} %get-tuple-element.41.far_scores, f32[2,128,128]{2,1,0:T(8,128)S(1)} %get-tuple-element.42.far_keeps, ...), custom_call_target="tpu_custom_call" | custom-call | flops 1495000064 | bytes 2633728 | tf_op jit(solution)/shard_map/pallas_call | solution.py:281
  (14 shorter events, 0.1 us)
Async XLA Ops:
  0.6 7.0 %copy-start = (bf16[256,4096]{1,0:T(8,128)(2,1)S(1)}, bf16[256,4096]{1,0:T(8,128)(2,1)}, u32[]{:S(2)}) copy-start(bf16[256,4096]{1,0:T(8,128)(2,1)} %weight.3) | copy-start | bytes 6291460
  2.8 44.3 %all-to-all-start = ((bf16[4,256,512]{2,1,0:T(8,128)(2,1)}), bf16[4,256,512]{2,1,0:T(8,128)(2,1)S(1)}, u32[]{:S(2)}, u32[]{:S(2)}) async-start(bf16[4,256,512]{2,1,0:T(8,128)(2,1)} %broadcast_in_dim.2), calls=%async_computation | async-start | bytes 2097152 | tf_op jit(solution)/shard_map/all_to_all | solution.py:308
  7.7 2.2 %copy-start.5 = (bf16[256,256]{1,0:T(8,128)(2,1)S(1)}, bf16[256,256]{1,0:T(8,128)(2,1)}, u32[]{:S(2)}) copy-start(bf16[256,256]{1,0:T(8,128)(2,1)} %query.3) | copy-start | bytes 393220
  7.7 17.4 %slice-start = ((bf16[256,256]{1,0:T(8,128)(2,1)}), bf16[128,256]{1,0:T(8,128)(2,1)S(1)}, s32[]{:S(2)}) async-start(bf16[256,256]{1,0:T(8,128)(2,1)} %key.4), calls=%async_computation.1 | async-start | bytes 131072 | tf_op jit(solution)/shard_map/slice | solution.py:310
  7.7 17.4 %slice-start.1 = ((bf16[256,256]{1,0:T(8,128)(2,1)}), bf16[128,256]{1,0:T(8,128)(2,1)S(1)}, s32[]{:S(2)}) async-start(bf16[256,256]{1,0:T(8,128)(2,1)} %value.5), calls=%async_computation.2 | async-start | bytes 131072 | tf_op jit(solution)/shard_map/slice | solution.py:310
  7.7 31.1 %copy-start.1 = (bf16[256,256]{1,0:T(8,128)(2,1)S(1)}, bf16[256,256]{1,0:T(8,128)(2,1)}, u32[]{:S(2)}) copy-start(bf16[256,256]{1,0:T(8,128)(2,1)} %key.4) | copy-start | bytes 393220
  7.7 31.1 %copy-start.2 = (bf16[256,256]{1,0:T(8,128)(2,1)S(1)}, bf16[256,256]{1,0:T(8,128)(2,1)}, u32[]{:S(2)}) copy-start(bf16[256,256]{1,0:T(8,128)(2,1)} %value.5) | copy-start | bytes 393220
  7.8 38.3 %collective-permute-start.3 = (bf16[256,2048]{1,0:T(8,128)(2,1)S(1)}, bf16[256,2048]{1,0:T(8,128)(2,1)S(1)}, u32[]{:S(2)}, u32[]{:S(2)}) collective-permute-start(bf16[256,2048]{1,0:T(8,128)(2,1)S(1)} %shard_map.94), channel_id=1, source_target_pairs={{0,1},{1,0},{2,3},{3,2},{4,5},{5,4},{6,7},{7,6},{8,9},{9,8},{10,11... | collective-permute-start | bytes 3145736 | tf_op jit(solution)/shard_map/ppermute | solution.py:299
  9.9 30.8 %collective-permute-start = (bf16[256,256]{1,0:T(8,128)(2,1)S(1)}, bf16[256,256]{1,0:T(8,128)(2,1)S(1)}, u32[]{:S(2)}, u32[]{:S(2)}) collective-permute-start(bf16[256,256]{1,0:T(8,128)(2,1)S(1)} %copy-done.5), channel_id=1, source_target_pairs={{8,0},{16,8},{24,16},{32,24},{40,32},{48,40},{56,48},{64,56},{72,6... | collective-permute-start | bytes 393224 | tf_op jit(solution)/shard_map/ppermute | solution.py:294
  25.1 20.4 %collective-permute-start.4 = (bf16[256,256]{1,0:T(8,128)(2,1)S(1)}, bf16[256,256]{1,0:T(8,128)(2,1)S(1)}, u32[]{:S(2)}, u32[]{:S(2)}) collective-permute-start(bf16[256,256]{1,0:T(8,128)(2,1)S(1)} %pad_maximum_fusion.1), channel_id=1, source_target_pairs={{0,16},{8,24},{16,32},{24,40},{32,48},{40,56},{48,64},{56,72},{64,... | collective-permute-start | bytes 393224 | tf_op jit(solution)/shard_map/ppermute | solution.py:294
  27.0 13.6 %collective-permute-start.1 = (bf16[128,256]{1,0:T(8,128)(2,1)S(1)}, bf16[128,256]{1,0:T(8,128)(2,1)S(1)}, u32[]{:S(2)}, u32[]{:S(2)}) collective-permute-start(bf16[128,256]{1,0:T(8,128)(2,1)S(1)} %slice.9), channel_id=1, source_target_pairs={{16,0},{24,8},{32,16},{40,24},{48,32},{56,40},{64,48},{72,56},{80,... | collective-permute-start | bytes 196616 | tf_op jit(solution)/shard_map/ppermute | solution.py:294
  40.7 0.7 copy-start.10
  41.3 25.4 %collective-permute-start.2 = (bf16[512,256]{1,0:T(8,128)(2,1)}, bf16[512,256]{1,0:T(8,128)(2,1)}, u32[]{:S(2)}, u32[]{:S(2)}) collective-permute-start(bf16[512,256]{1,0:T(8,128)(2,1)} %pad_maximum_fusion), channel_id=1, source_target_pairs={{0,8},{8,16},{16,24},{24,32},{32,40},{40,48},{48,56},{56,64},{64,7... | collective-permute-start | bytes 786440 | tf_op jit(solution)/shard_map/ppermute | solution.py:294
  45.5 0.7 copy-start.7
  46.1 1.0 %copy-start.3 = (bf16[256,2048]{1,0:T(8,128)(2,1)}, bf16[256,2048]{1,0:T(8,128)(2,1)S(1)}, u32[]{:S(2)}) copy-start(bf16[256,2048]{1,0:T(8,128)(2,1)S(1)} %collective-permute-done.3.weight) | copy-start | bytes 3145732
  47.1 1.2 %copy-start.4 = (bf16[256,2048]{1,0:T(8,128)(2,1)S(1)}, bf16[256,2048]{1,0:T(8,128)(2,1)}, u32[]{:S(2)}) copy-start(bf16[256,2048]{1,0:T(8,128)(2,1)} %copy-done.3) | copy-start | bytes 3145732
  48.8 17.9 %copy-start.6 = (bf16[256,256]{1,0:T(8,128)(2,1)S(1)}, bf16[256,256]{1,0:T(8,128)(2,1)}, u32[]{:S(2)}) copy-start(bf16[256,256]{1,0:T(8,128)(2,1)} %query.3) | copy-start | bytes 393220
  48.8 17.9 %copy-start.8 = (bf16[256,256]{1,0:T(8,128)(2,1)S(1)}, bf16[256,256]{1,0:T(8,128)(2,1)}, u32[]{:S(2)}) copy-start(bf16[256,256]{1,0:T(8,128)(2,1)} %copy-done.7) | copy-start | bytes 393220
  48.9 17.9 %copy-start.9 = (s32[128,128]{1,0:T(8,128)S(1)}, s32[128,128]{1,0:T(8,128)}, u32[]{:S(2)}) copy-start(s32[128,128]{1,0:T(8,128)} %table.3) | copy-start | bytes 196612
  48.9 25.4 %copy-start.11 = (bf16[256,256]{1,0:T(8,128)(2,1)S(1)}, bf16[256,256]{1,0:T(8,128)(2,1)}, u32[]{:S(2)}) copy-start(bf16[256,256]{1,0:T(8,128)(2,1)} %copy-done.10) | copy-start | bytes 393220
  48.9 3.4 %collective-permute-start.5 = (bf16[256,256]{1,0:T(8,128)(2,1)S(1)}, bf16[256,256]{1,0:T(8,128)(2,1)S(1)}, u32[]{:S(2)}, u32[]{:S(2)}) collective-permute-start(bf16[256,256]{1,0:T(8,128)(2,1)S(1)} %shard_map.96), channel_id=1, source_target_pairs={{0,1},{1,0},{2,3},{3,2},{4,5},{5,4},{6,7},{7,6},{8,9},{9,8},{10,11... | collective-permute-start | bytes 393224 | tf_op jit(solution)/shard_map/ppermute | solution.py:299
  52.3 26.7 %collective-permute-start.6 = (bf16[256,256]{1,0:T(8,128)(2,1)S(1)}, bf16[256,256]{1,0:T(8,128)(2,1)S(1)}, u32[]{:S(2)}, u32[]{:S(2)}) collective-permute-start(bf16[256,256]{1,0:T(8,128)(2,1)S(1)} %get-tuple-element.30.grad), channel_id=1, source_target_pairs={{8,0},{16,8},{24,16},{32,24},{40,32},{48,40},{56,48},{64,56},{72,6... | collective-permute-start | bytes 393224 | tf_op jit(solution)/shard_map/ppermute | solution.py:294
  60.9 18.1 %collective-permute-start.7 = (bf16[128,256]{1,0:T(8,128)(2,1)S(1)}, bf16[128,256]{1,0:T(8,128)(2,1)S(1)}, u32[]{:S(2)}, u32[]{:S(2)}) collective-permute-start(bf16[128,256]{1,0:T(8,128)(2,1)S(1)} %get-tuple-element.43), channel_id=1, source_target_pairs={{16,0},{24,8},{32,16},{40,24},{48,32},{56,40},{64,48},{72,56},{80,... | collective-permute-start | bytes 196616 | tf_op jit(solution)/shard_map/ppermute | solution.py:294
  70.4 8.6 %collective-permute-start.8 = (f32[8,256]{1,0:T(8,128)S(1)}, f32[8,256]{1,0:T(8,128)S(1)}, u32[]{:S(2)}, u32[]{:S(2)}) collective-permute-start(f32[8,256]{1,0:T(8,128)S(1)} %get-tuple-element.35), channel_id=1, source_target_pairs={{8,0},{16,8},{24,16},{32,24},{40,32},{48,40},{56,48},{64,56},{72,6... | collective-permute-start | bytes 24584 | tf_op jit(solution)/shard_map/ppermute | solution.py:294
  72.3 6.7 %collective-permute-start.9 = (f32[8,128]{1,0:T(8,128)S(1)}, f32[8,128]{1,0:T(8,128)S(1)}, u32[]{:S(2)}, u32[]{:S(2)}) collective-permute-start(f32[8,128]{1,0:T(8,128)S(1)} %get-tuple-element.44), channel_id=1, source_target_pairs={{16,0},{24,8},{32,16},{40,24},{48,32},{56,40},{64,48},{72,56},{80,... | collective-permute-start | bytes 12296 | tf_op jit(solution)/shard_map/ppermute | solution.py:294

commit v13 on v10

--- a/solution.py
+++ b/solution.py
@@ -311,13 +311,14 @@
     far_query = shifted(query_rows[:MB], -2)
 
     width = (count // 2) * grad_out.shape[1]
-    (theirs,) = call(cut_kernel, [VMEM], [((WIDE, width), half)], 0.0, out_weight)
+    own_keys = jnp.concatenate((key_rows, value_rows))
+    near_query, far_query, own_keys, weight = lax.optimization_barrier(
+        (near_query, far_query, own_keys, out_weight)
+    )
+    (theirs,) = call(cut_kernel, [VMEM], [((WIDE, width), half)], 0.0, weight)
     other_weight = other_core(theirs)
-    own_keys = jnp.concatenate((key_rows, value_rows))
-    gathered, other_weight, far_keys, near_query, far_query, own_keys = lax.optimization_barrier(
-        (gathered, other_weight, far_keys, near_query, far_query, own_keys)
-    )
     near_keys = shifted(own_keys, 1)
+    gathered, other_weight = lax.optimization_barrier((gathered, other_weight))
     (sent,) = call(
         project_other_kernel, [VMEM] * 2, [((ROWS, WIDE), half)], 0.0, gathered, other_weight
     )

time: 82.9 us -> 81.6 us (0.984)
  waiting for transfers between devices: 15.3 us -> 12.5 us
  Pallas kernels: 9.69 us -> 10.6 us
  starting transfers between devices: 49.4 us -> 48.5 us
    ppermute x8, waiting for transfers between devices: 14.5 us -> 10 us  [shifted(): return lax.ppermute(value, 'blk', pairs)]
    all_to_all x1, waiting for transfers between devices: 0.01 us -> 1.78 us  [on_device(): gathered = lax.all_to_all(copies, 'head', 0, 0, axis_index_groups=groups)]
    pallas_call x8, Pallas kernels: 9.69 us -> 10.6 us  [call(): pl.pallas_call(kernel, out_shape=shapes, in_specs=specs, out_specs=[VMEM]...]
    slice x1, local copies, waits for them, and re-layouts: 0.01 us -> 0.86 us  [on_device(): far_query = shifted(query_rows[:MB], -2)]
    unnamed x24 -> x22, local copies, waits for them, and re-layouts: 3.55 us -> 3.51 us
  transfers between devices with their start and end apart: 11 -> 11, of which waited for: 4 -> 4; matrix products, arithmetic and copies ran while one was open for 1% -> 2% of each run, Pallas kernels for 10% -> 12%
where the time goes in v13:
time: 81.6 us; the launch traced here: 80.4 us
  starting transfers between devices  48.5 us (59%)
  waiting for transfers between devices  12.5 us (15%)
  Pallas kernels  10.6 us (13%)
  local copies, waits for them, and re-layouts  6.54 us (8%)
  between operations  1.54 us (2%)
    ppermute x8, starting transfers between devices, shifted(): return lax.ppermute(value, 'blk', pairs)  39.7 us
    pallas_call x8, Pallas kernels, call(): pl.pallas_call(kernel, out_shape=shapes, in_specs=specs, out_specs=[VMEM]...  10.6 us
    ppermute x8, waiting for transfers between devices, shifted(): return lax.ppermute(value, 'blk', pairs)  10 us
    all_to_all x1, starting transfers between devices, on_device(): gathered = lax.all_to_all(copies, 'head', 0, 0, axis_index_groups=groups)  4.87 us
    ppermute x2, starting transfers between devices, other_core(): lax.ppermute(value, 'head', [(source, source ^ 1) for source in range(cou...  3.84 us
    unnamed x22, local copies, waits for them, and re-layouts  3.51 us
    broadcast_in_dim x1, local copies, waits for them, and re-layouts, on_device(): copies = jnp.broadcast_to(grad_out[None], (count // 2, *grad_out.shape))  2.17 us
    all_to_all x1, waiting for transfers between devices, on_device(): gathered = lax.all_to_all(copies, 'head', 0, 0, axis_index_groups=groups)  1.78 us
  transfers between devices with their start and end apart: 11, of which 4 were waited for; matrix products, arithmetic and copies ran while one was open for 2% of the time, Pallas kernels for 12%

profile of v13, /device:TPU:6, one launch (start us, length us, event | category | flops | bytes accessed | tf_op | source)
XLA Modules:
  0.0 80.4 jit_solution(3627967127940090085)
XLA Ops:
  0.6 0.0 copy-start.1
  0.6 0.0 copy-start.2
  0.7 0.0 copy-start
  0.7 2.2 %broadcast_in_dim.2 = bf16[4,256,512]{2,1,0:T(8,128)(2,1)} broadcast(bf16[256,512]{1,0:T(8,128)(2,1)} %param.10), dimensions={1,2} | broadcast | bytes 1310720 | tf_op jit(solution)/shard_map/broadcast_in_dim | solution.py:307
  2.8 4.9 %all-to-all-start = ((bf16[4,256,512]{2,1,0:T(8,128)(2,1)}), bf16[4,256,512]{2,1,0:T(8,128)(2,1)S(1)}, u32[]{:S(2)}, u32[]{:S(2)}) async-start(bf16[4,256,512]{2,1,0:T(8,128)(2,1)} %broadcast_in_dim.2), calls=%async_computation | async-start | bytes 2097152 | tf_op jit(solution)/shard_map/all_to_all | solution.py:308
  7.7 15.1 %collective-permute-start = (bf16[256,256]{1,0:T(8,128)(2,1)}, bf16[256,256]{1,0:T(8,128)(2,1)S(1)}, u32[]{:S(2)}, u32[]{:S(2)}) collective-permute-start(bf16[256,256]{1,0:T(8,128)(2,1)} %query.3), channel_id=1, source_target_pairs={{8,0},{16,8},{24,16},{32,24},{40,32},{48,40},{56,48},{64,56},{72,6... | collective-permute-start | bytes 393224 | tf_op jit(solution)/shard_map/ppermute | solution.py:294
  22.8 0.9 %slice.9 = bf16[128,256]{1,0:T(8,128)(2,1)S(1)} slice(bf16[256,256]{1,0:T(8,128)(2,1)} %query.3), slice={[0:128], [0:256]} | slice | bytes 131072 | tf_op jit(solution)/shard_map/slice | solution.py:311
  23.7 2.4 %collective-permute-start.1 = (bf16[128,256]{1,0:T(8,128)(2,1)S(1)}, bf16[128,256]{1,0:T(8,128)(2,1)S(1)}, u32[]{:S(2)}, u32[]{:S(2)}) collective-permute-start(bf16[128,256]{1,0:T(8,128)(2,1)S(1)} %slice.9), channel_id=1, source_target_pairs={{16,0},{24,8},{32,16},{40,24},{48,32},{56,40},{64,48},{72,56},{80,... | collective-permute-start | bytes 196616 | tf_op jit(solution)/shard_map/ppermute | solution.py:294
  26.1 0.0 copy-done.1
  26.1 0.0 copy-done.2
  26.2 0.7 pad_maximum_fusion
  26.9 6.3 %collective-permute-done.1.far_query = bf16[128,256]{1,0:T(8,128)(2,1)S(1)} collective-permute-done((bf16[128,256]{1,0:T(8,128)(2,1)S(1)}, bf16[128,256]{1,0:T(8,128)(2,1)S(1)}, u32[]{:S(2)}, u32[]{:S(2)}) %collective-permute-start.1) | collective-permute-done | bytes 65568 | tf_op jit(solution)/shard_map/ppermute | solution.py:294
  33.2 0.6 copy-done.9
  33.8 0.0 collective-permute-done.near_query
  33.8 0.7 copy-done.7
  34.5 0.0 copy-done
  34.5 0.1 shard_map.94
  34.6 1.9 %collective-permute-start.4 = (bf16[256,2048]{1,0:T(8,128)(2,1)S(1)}, bf16[256,2048]{1,0:T(8,128)(2,1)S(1)}, u32[]{:S(2)}, u32[]{:S(2)}) collective-permute-start(bf16[256,2048]{1,0:T(8,128)(2,1)S(1)} %shard_map.94), channel_id=1, source_target_pairs={{0,1},{1,0},{2,3},{3,2},{4,5},{5,4},{6,7},{7,6},{8,9},{9,8},{10,11... | collective-permute-start | bytes 3145736 | tf_op jit(solution)/shard_map/ppermute | solution.py:299
  36.5 1.9 %collective-permute-start.2 = (bf16[512,256]{1,0:T(8,128)(2,1)}, bf16[512,256]{1,0:T(8,128)(2,1)}, u32[]{:S(2)}, u32[]{:S(2)}) collective-permute-start(bf16[512,256]{1,0:T(8,128)(2,1)} %pad_maximum_fusion), channel_id=1, source_target_pairs={{0,8},{8,16},{16,24},{24,32},{32,40},{40,48},{48,56},{56,64},{64,7... | collective-permute-start | bytes 786440 | tf_op jit(solution)/shard_map/ppermute | solution.py:294
  38.4 0.7 collective-permute-done.4.weight
  39.1 1.0 %copy-done.3 = bf16[256,2048]{1,0:T(8,128)(2,1)} copy-done((bf16[256,2048]{1,0:T(8,128)(2,1)}, bf16[256,2048]{1,0:T(8,128)(2,1)S(1)}, u32[]{:S(2)}) %copy-start.3) | copy-done | bytes 1048600
  40.1 1.8 %all-to-all-done.gathered = bf16[4,256,512]{2,1,0:T(8,128)(2,1)S(1)} async-done(((bf16[4,256,512]{2,1,0:T(8,128)(2,1)}), bf16[4,256,512]{2,1,0:T(8,128)(2,1)S(1)}, u32[]{:S(2)}, u32[]{:S(2)}) %all-to-all-start) | async-done | bytes 1048608 | tf_op jit(solution)/shard_map/all_to_all | solution.py:308
  41.9 1.2 %copy-done.4 = bf16[256,2048]{1,0:T(8,128)(2,1)S(1)} copy-done((bf16[256,2048]{1,0:T(8,128)(2,1)S(1)}, bf16[256,2048]{1,0:T(8,128)(2,1)}, u32[]{:S(2)}) %copy-start.4) | copy-done | bytes 1048600
  43.1 0.5 shard_map.96
  43.5 1.9 %collective-permute-start.5 = (bf16[256,256]{1,0:T(8,128)(2,1)S(1)}, bf16[256,256]{1,0:T(8,128)(2,1)S(1)}, u32[]{:S(2)}, u32[]{:S(2)}) collective-permute-start(bf16[256,256]{1,0:T(8,128)(2,1)S(1)} %shard_map.96), channel_id=1, source_target_pairs={{0,1},{1,0},{2,3},{3,2},{4,5},{5,4},{6,7},{7,6},{8,9},{9,8},{10,11... | collective-permute-start | bytes 393224 | tf_op jit(solution)/shard_map/ppermute | solution.py:299
  45.5 0.0 copy-start.5
  45.5 0.0 copy-start.6
  45.5 0.0 slice-done
  45.5 0.0 copy-start.8
  45.6 0.0 copy-start.10
  45.6 2.1 %collective-permute-start.3 = (bf16[256,256]{1,0:T(8,128)(2,1)S(1)}, bf16[256,256]{1,0:T(8,128)(2,1)S(1)}, u32[]{:S(2)}, u32[]{:S(2)}) collective-permute-start(bf16[256,256]{1,0:T(8,128)(2,1)S(1)} %pad_maximum_fusion.1), channel_id=1, source_target_pairs={{0,16},{8,24},{16,32},{24,40},{32,48},{40,56},{48,64},{56,72},{64,... | collective-permute-start | bytes 393224 | tf_op jit(solution)/shard_map/ppermute | solution.py:294
  47.6 0.5 shard_map.95.own
  48.1 0.0 collective-permute-done.5.received
  48.2 8.6 %collective-permute-start.6 = (bf16[256,256]{1,0:T(8,128)(2,1)S(1)}, bf16[256,256]{1,0:T(8,128)(2,1)S(1)}, u32[]{:S(2)}, u32[]{:S(2)}) collective-permute-start(bf16[256,256]{1,0:T(8,128)(2,1)S(1)} %get-tuple-element.30.grad), channel_id=1, source_target_pairs={{8,0},{16,8},{24,16},{32,24},{40,32},{48,40},{56,48},{64,56},{72,6... | collective-permute-start | bytes 393224 | tf_op jit(solution)/shard_map/ppermute | solution.py:294
  56.7 5.3 %collective-permute-start.7 = (bf16[128,256]{1,0:T(8,128)(2,1)S(1)}, bf16[128,256]{1,0:T(8,128)(2,1)S(1)}, u32[]{:S(2)}, u32[]{:S(2)}) collective-permute-start(bf16[128,256]{1,0:T(8,128)(2,1)S(1)} %get-tuple-element.43), channel_id=1, source_target_pairs={{16,0},{24,8},{32,16},{40,24},{48,32},{56,40},{64,48},{72,56},{80,... | collective-permute-start | bytes 196616 | tf_op jit(solution)/shard_map/ppermute | solution.py:294
  62.8 3.7 %collective-permute-done.3.far = bf16[256,256]{1,0:T(8,128)(2,1)S(1)} collective-permute-done((bf16[256,256]{1,0:T(8,128)(2,1)S(1)}, bf16[256,256]{1,0:T(8,128)(2,1)S(1)}, u32[]{:S(2)}, u32[]{:S(2)}) %collective-permute-start.3) | collective-permute-done | bytes 131104 | tf_op jit(solution)/shard_map/ppermute | solution.py:294
  66.5 0.0 collective-permute-done.2.near
  66.5 0.0 copy-done.5
  66.5 3.6 %shard_map.98 = (f32[2,128,640]{2,1,0:T(8,128)S(1)}, f32[2,128,512]{2,1,0:T(8,128)S(1)}, bf16[256,256]{1,0:T(8,128)(2,1)S(1)}, f32[8,256]{1,0:T(8,128)S(1)}, f32[8,128]{1,0:T(8,128)S(1)}) custom-call(s32[128,128]{1,0:T(8,128)S(1)} %copy-done.6, s32[1]{0:T(128)S(6)} %copy.10.seed, bf16[256,256]{1,0:T(8,128)(2,1)S(1)} %copy-done.5, ...), custom_call_target="tpu_custom_call" | custom-call | tf_op jit(solution)/shard_map/pallas_call | solution.py:281
  70.1 1.9 %collective-permute-start.8 = (f32[8,256]{1,0:T(8,128)S(1)}, f32[8,256]{1,0:T(8,128)S(1)}, u32[]{:S(2)}, u32[]{:S(2)}) collective-permute-start(f32[8,256]{1,0:T(8,128)S(1)} %get-tuple-element.35), channel_id=1, source_target_pairs={{8,0},{16,8},{24,16},{32,24},{40,32},{48,40},{56,48},{64,56},{72,6... | collective-permute-start | bytes 24584 | tf_op jit(solution)/shard_map/ppermute | solution.py:294
  72.0 2.4 %collective-permute-start.9 = (f32[8,128]{1,0:T(8,128)S(1)}, f32[8,128]{1,0:T(8,128)S(1)}, u32[]{:S(2)}, u32[]{:S(2)}) collective-permute-start(f32[8,128]{1,0:T(8,128)S(1)} %get-tuple-element.44), channel_id=1, source_target_pairs={{16,0},{24,8},{32,16},{40,24},{48,32},{56,40},{64,48},{72,56},{80,... | collective-permute-start | bytes 12296 | tf_op jit(solution)/shard_map/ppermute | solution.py:294
  74.4 2.1 %shard_map.100 = (f32[2,256,256]{2,1,0:T(8,128)S(1)}, f32[2,256,256]{2,1,0:T(8,128)S(1)}, f32[2,128,128]{2,1,0:T(8,128)S(1)}, f32[2,128,128]{2,1,0:T(8,128)S(1)}) custom-call(s32[128,128]{1,0:T(8,128)S(1)} %copy-done.6, s32[1]{0:T(128)S(6)} %copy.10.seed, bf16[256,256]{1,0:T(8,128)(2,1)S(1)} %copy-done.1, bf16[256,256]{1,0:T(8,128)(2,1)S(1)} %copy-done.8, ...), custom_call_target="tpu_custom_call" | custom-call | tf_op jit(solution)/shard_map/pallas_call | solution.py:281
  76.5 2.6 %shard_map.99 = (bf16[256,256]{1,0:T(8,128)(2,1)}, f32[256,256]{1,0:T(8,128)S(1)}, f32[256,256]{1,0:T(8,128)S(1)}) custom-call(f32[2,128,640]{2,1,0:T(8,128)S(1)} %get-tuple-element.31.signed_top, f32[2,128,512]{2,1,0:T(8,128)S(1)} %get-tuple-element.32.signed_low, bf16[256,256]{1,0:T(8,128)(2,1)S(1)} %get-tuple-element.33.attended, ...), custom_call_target="tpu_custom_call" | custom-call | tf_op jit(solution)/shard_map/pallas_call | solution.py:281
  79.1 0.0 collective-permute-done.9.far_stats
  79.1 0.0 collective-permute-done.8.near_stats
  79.1 0.0 collective-permute-done.7.far_grad
  79.1 0.0 collective-permute-done.6.near_grad
  79.1 1.2 %shard_map.101 = (bf16[256,256]{1,0:T(8,128)(2,1)}, bf16[256,256]{1,0:T(8,128)(2,1)}) custom-call(f32[2,256,256]{2,1,0:T(8,128)S(1)} %get-tuple-element.39.near_scores, f32[2,256,256]{2,1,0:T(8,128)S(1)} %get-tuple-element.40.near_keeps, f32[2,128,128]{2,1,0:T(8,128)S(1)} %get-tuple-element.41.far_scores, f32[2,128,128]{2,1,0:T(8,128)S(1)} %get-tuple-element.42.far_keeps, ...), custom_call_target="tpu_custom_call" | custom-call | flops 1495000064 | bytes 2633728 | tf_op jit(solution)/shard_map/pallas_call | solution.py:281
  (12 shorter events, 0.1 us)
Async XLA Ops:
  0.6 25.5 %copy-start.1 = (bf16[256,256]{1,0:T(8,128)(2,1)S(1)}, bf16[256,256]{1,0:T(8,128)(2,1)}, u32[]{:S(2)}) copy-start(bf16[256,256]{1,0:T(8,128)(2,1)} %key.4) | copy-start | bytes 393220
  0.6 25.5 %copy-start.2 = (bf16[256,256]{1,0:T(8,128)(2,1)S(1)}, bf16[256,256]{1,0:T(8,128)(2,1)}, u32[]{:S(2)}) copy-start(bf16[256,256]{1,0:T(8,128)(2,1)} %value.5) | copy-start | bytes 393220
  0.7 33.8 %copy-start = (bf16[256,4096]{1,0:T(8,128)(2,1)S(1)}, bf16[256,4096]{1,0:T(8,128)(2,1)}, u32[]{:S(2)}) copy-start(bf16[256,4096]{1,0:T(8,128)(2,1)} %weight.2) | copy-start | bytes 6291460
  2.8 39.0 %all-to-all-start = ((bf16[4,256,512]{2,1,0:T(8,128)(2,1)}), bf16[4,256,512]{2,1,0:T(8,128)(2,1)S(1)}, u32[]{:S(2)}, u32[]{:S(2)}) async-start(bf16[4,256,512]{2,1,0:T(8,128)(2,1)} %broadcast_in_dim.2), calls=%async_computation | async-start | bytes 2097152 | tf_op jit(solution)/shard_map/all_to_all | solution.py:308
  7.7 26.1 %collective-permute-start = (bf16[256,256]{1,0:T(8,128)(2,1)}, bf16[256,256]{1,0:T(8,128)(2,1)S(1)}, u32[]{:S(2)}, u32[]{:S(2)}) collective-permute-start(bf16[256,256]{1,0:T(8,128)(2,1)} %query.3), channel_id=1, source_target_pairs={{8,0},{16,8},{24,16},{32,24},{40,32},{48,40},{56,48},{64,56},{72,6... | collective-permute-start | bytes 393224 | tf_op jit(solution)/shard_map/ppermute | solution.py:294
  23.7 9.5 %collective-permute-start.1 = (bf16[128,256]{1,0:T(8,128)(2,1)S(1)}, bf16[128,256]{1,0:T(8,128)(2,1)S(1)}, u32[]{:S(2)}, u32[]{:S(2)}) collective-permute-start(bf16[128,256]{1,0:T(8,128)(2,1)S(1)} %slice.9), channel_id=1, source_target_pairs={{16,0},{24,8},{32,16},{40,24},{48,32},{56,40},{64,48},{72,56},{80,... | collective-permute-start | bytes 196616 | tf_op jit(solution)/shard_map/ppermute | solution.py:294
  26.9 18.6 %slice-start = ((bf16[256,256]{1,0:T(8,128)(2,1)}), bf16[128,256]{1,0:T(8,128)(2,1)S(1)}, s32[]{:S(2)}) async-start(bf16[256,256]{1,0:T(8,128)(2,1)} %key.4), calls=%async_computation.1 | async-start | bytes 131072 | tf_op jit(solution)/shard_map/slice | solution.py:310
  26.9 18.6 %slice-start.1 = ((bf16[256,256]{1,0:T(8,128)(2,1)}), bf16[128,256]{1,0:T(8,128)(2,1)S(1)}, s32[]{:S(2)}) async-start(bf16[256,256]{1,0:T(8,128)(2,1)} %value.5), calls=%async_computation.2 | async-start | bytes 131072 | tf_op jit(solution)/shard_map/slice | solution.py:310
  33.2 0.6 copy-start.9
  33.8 0.7 copy-start.7
  34.6 4.6 %collective-permute-start.4 = (bf16[256,2048]{1,0:T(8,128)(2,1)S(1)}, bf16[256,2048]{1,0:T(8,128)(2,1)S(1)}, u32[]{:S(2)}, u32[]{:S(2)}) collective-permute-start(bf16[256,2048]{1,0:T(8,128)(2,1)S(1)} %shard_map.94), channel_id=1, source_target_pairs={{0,1},{1,0},{2,3},{3,2},{4,5},{5,4},{6,7},{7,6},{8,9},{9,8},{10,11... | collective-permute-start | bytes 3145736 | tf_op jit(solution)/shard_map/ppermute | solution.py:299
  36.5 30.0 %collective-permute-start.2 = (bf16[512,256]{1,0:T(8,128)(2,1)}, bf16[512,256]{1,0:T(8,128)(2,1)}, u32[]{:S(2)}, u32[]{:S(2)}) collective-permute-start(bf16[512,256]{1,0:T(8,128)(2,1)} %pad_maximum_fusion), channel_id=1, source_target_pairs={{0,8},{8,16},{16,24},{24,32},{32,40},{40,48},{48,56},{56,64},{64,7... | collective-permute-start | bytes 786440 | tf_op jit(solution)/shard_map/ppermute | solution.py:294
  39.1 1.0 %copy-start.3 = (bf16[256,2048]{1,0:T(8,128)(2,1)}, bf16[256,2048]{1,0:T(8,128)(2,1)S(1)}, u32[]{:S(2)}) copy-start(bf16[256,2048]{1,0:T(8,128)(2,1)S(1)} %collective-permute-done.4.weight) | copy-start | bytes 3145732
  41.9 1.2 %copy-start.4 = (bf16[256,2048]{1,0:T(8,128)(2,1)S(1)}, bf16[256,2048]{1,0:T(8,128)(2,1)}, u32[]{:S(2)}) copy-start(bf16[256,2048]{1,0:T(8,128)(2,1)} %copy-done.3) | copy-start | bytes 3145732
  43.5 4.6 %collective-permute-start.5 = (bf16[256,256]{1,0:T(8,128)(2,1)S(1)}, bf16[256,256]{1,0:T(8,128)(2,1)S(1)}, u32[]{:S(2)}, u32[]{:S(2)}) collective-permute-start(bf16[256,256]{1,0:T(8,128)(2,1)S(1)} %shard_map.96), channel_id=1, source_target_pairs={{0,1},{1,0},{2,3},{3,2},{4,5},{5,4},{6,7},{7,6},{8,9},{9,8},{10,11... | collective-permute-start | bytes 393224 | tf_op jit(solution)/shard_map/ppermute | solution.py:299
  45.5 21.0 %copy-start.5 = (bf16[256,256]{1,0:T(8,128)(2,1)S(1)}, bf16[256,256]{1,0:T(8,128)(2,1)}, u32[]{:S(2)}) copy-start(bf16[256,256]{1,0:T(8,128)(2,1)} %query.3) | copy-start | bytes 393220
  45.5 21.0 %copy-start.6 = (s32[128,128]{1,0:T(8,128)S(1)}, s32[128,128]{1,0:T(8,128)}, u32[]{:S(2)}) copy-start(s32[128,128]{1,0:T(8,128)} %table.3) | copy-start | bytes 196612
  45.5 28.8 %copy-start.8 = (bf16[256,256]{1,0:T(8,128)(2,1)S(1)}, bf16[256,256]{1,0:T(8,128)(2,1)}, u32[]{:S(2)}) copy-start(bf16[256,256]{1,0:T(8,128)(2,1)} %copy-done.7) | copy-start | bytes 393220
  45.6 28.8 %copy-start.10 = (bf16[128,256]{1,0:T(8,128)(2,1)S(1)}, bf16[128,256]{1,0:T(8,128)(2,1)}, u32[]{:S(2)}) copy-start(bf16[128,256]{1,0:T(8,128)(2,1)} %copy-done.9) | copy-start | bytes 196612
  45.6 20.9 %collective-permute-start.3 = (bf16[256,256]{1,0:T(8,128)(2,1)S(1)}, bf16[256,256]{1,0:T(8,128)(2,1)S(1)}, u32[]{:S(2)}, u32[]{:S(2)}) collective-permute-start(bf16[256,256]{1,0:T(8,128)(2,1)S(1)} %pad_maximum_fusion.1), channel_id=1, source_target_pairs={{0,16},{8,24},{16,32},{24,40},{32,48},{40,56},{48,64},{56,72},{64,... | collective-permute-start | bytes 393224 | tf_op jit(solution)/shard_map/ppermute | solution.py:294
  48.2 31.0 %collective-permute-start.6 = (bf16[256,256]{1,0:T(8,128)(2,1)S(1)}, bf16[256,256]{1,0:T(8,128)(2,1)S(1)}, u32[]{:S(2)}, u32[]{:S(2)}) collective-permute-start(bf16[256,256]{1,0:T(8,128)(2,1)S(1)} %get-tuple-element.30.grad), channel_id=1, source_target_pairs={{8,0},{16,8},{24,16},{32,24},{40,32},{48,40},{56,48},{64,56},{72,6... | collective-permute-start | bytes 393224 | tf_op jit(solution)/shard_map/ppermute | solution.py:294
  56.7 22.4 %collective-permute-start.7 = (bf16[128,256]{1,0:T(8,128)(2,1)S(1)}, bf16[128,256]{1,0:T(8,128)(2,1)S(1)}, u32[]{:S(2)}, u32[]{:S(2)}) collective-permute-start(bf16[128,256]{1,0:T(8,128)(2,1)S(1)} %get-tuple-element.43), channel_id=1, source_target_pairs={{16,0},{24,8},{32,16},{40,24},{48,32},{56,40},{64,48},{72,56},{80,... | collective-permute-start | bytes 196616 | tf_op jit(solution)/shard_map/ppermute | solution.py:294
  70.1 9.1 %collective-permute-start.8 = (f32[8,256]{1,0:T(8,128)S(1)}, f32[8,256]{1,0:T(8,128)S(1)}, u32[]{:S(2)}, u32[]{:S(2)}) collective-permute-start(f32[8,256]{1,0:T(8,128)S(1)} %get-tuple-element.35), channel_id=1, source_target_pairs={{8,0},{16,8},{24,16},{32,24},{40,32},{48,40},{56,48},{64,56},{72,6... | collective-permute-start | bytes 24584 | tf_op jit(solution)/shard_map/ppermute | solution.py:294
  72.0 7.1 %collective-permute-start.9 = (f32[8,128]{1,0:T(8,128)S(1)}, f32[8,128]{1,0:T(8,128)S(1)}, u32[]{:S(2)}, u32[]{:S(2)}) collective-permute-start(f32[8,128]{1,0:T(8,128)S(1)} %get-tuple-element.44), channel_id=1, source_target_pairs={{16,0},{24,8},{32,16},{40,24},{48,32},{56,40},{64,48},{72,56},{80,... | collective-permute-start | bytes 12296 | tf_op jit(solution)/shard_map/ppermute | solution.py:294
